TPU v7x, 128 devices: a whole 4x4x4 slice. The times are simulated.
128 devices in a mesh: wide: 32 (over z, y_lo, x), narrow: 4 (over y_hi, core).
Axes of the slice: x: 4, y: 4 (y_hi: 2, y_lo: 2; y = y_hi * 2 + y_lo), z: 4, core: 2. Of those that a mesh axis runs over, the one named last changes fastest.
Arguments:
- hidden: bfloat16 [512, 4, 8192], P('narrow', None, 'wide'), may hold values from -0.1796875 to 0.1796875
- grad_out: bfloat16 [512, 8192], P('narrow', 'wide'), may hold values from -6 to 6
- weight_base: bfloat16 [32768, 8192], P('narrow', 'wide'), may hold values from -0.0625 to 0.0625
- block_scale: bfloat16 [2048, 512], P('narrow', 'wide'), may hold values from 0.25 to 4
Outputs:
- grad_hidden: bfloat16 [512, 4, 8192], P('narrow', None, 'wide')
- grad_weight: bfloat16 [8192, 4, 8192], P('narrow', None, 'wide')
All inputs are finite; a program needn't handle non-finite values.
Results may differ from a plain program's by a relative error of at most 0.0049.
Values may be sent and summed in bfloat16 or wider, within the bound.
No kernel may reach another device: no remote copies, remote signals or barrier semaphores. Data moves between devices by JAX's collectives and lax.ppermute only.
A program may use at most 192 MiB of HBM per device.

v0:
```python
import jax
import jax.numpy as jnp
from jax import lax
from jax.sharding import PartitionSpec as P


def from_everyone(shard, axis):
    length = lax.axis_size(axis)
    return lax.all_to_all(
        jnp.broadcast_to(shard[None], (length, *shard.shape)), axis, 0, 0, tiled=True
    )


def joined_along(parts, dim):
    shape = list(parts.shape[1:])
    shape[dim] *= parts.shape[0]
    return jnp.moveaxis(parts, 0, dim).reshape(shape)


def gathered_copies(shard, axis, dim):
    parts = from_everyone(shard, axis)
    return joined_along(parts, dim)


def apply_scales(values, scales):
    height, breadth = values.shape
    widened = jnp.repeat(scales, 16, axis=1).astype(jnp.float32)
    blocked = values.reshape(height // 16, 16, breadth).astype(jnp.float32)
    blocked = blocked * widened[:, None, :]
    return blocked.reshape(height, breadth).astype(jnp.bfloat16)


def per_device(hidden, grad_out, weight_base, block_scale):
    tokens_here, groups, slice_width = hidden.shape
    row_values, row_scales = (
        lax.all_to_all(weight_base, "wide", split_axis=0, concat_axis=1, tiled=True),
        lax.all_to_all(block_scale, "wide", split_axis=0, concat_axis=1, tiled=True),
    )
    values_all, scales_all = (
        lax.all_gather(row_values, "narrow", axis=0, tiled=True),
        lax.all_gather(row_scales, "narrow", axis=0, tiled=True),
    )
    effective = apply_scales(values_all, scales_all)
    contract_last = (((1,), (1,)), ((), ()))
    incoming = gathered_copies(grad_out, "wide", 1)
    summed = lax.dot_general(incoming, effective, contract_last, preferred_element_type=jnp.float32)
    summed, gathered = (summed, incoming)
    grad_hidden = summed.astype(jnp.bfloat16).reshape(tokens_here, groups, slice_width)
    columns_mine = lax.all_to_all(gathered, "narrow", split_axis=1, concat_axis=0, tiled=True)
    hidden_all = lax.all_gather(
        hidden.reshape(tokens_here, groups * slice_width), "narrow", axis=0, tiled=True
    )
    product = lax.dot_general(
        columns_mine, hidden_all, (((0,), (0,)), ((), ())), preferred_element_type=jnp.float32
    )
    grad_weight = product.astype(jnp.bfloat16).reshape(product.shape[0], groups, slice_width)
    return (grad_hidden, grad_weight)


def solution(mesh):
    return jax.shard_map(
        per_device,
        mesh=mesh,
        in_specs=(
            P("narrow", None, "wide"),
            P("narrow", "wide"),
            P("narrow", "wide"),
            P("narrow", "wide"),
        ),
        out_specs=(P("narrow", None, "wide"), P("narrow", None, "wide")),
        check_vma=False,
    )
```

profile of v0, /device:TPU:1, one launch (start us, length us, event | category | flops | bytes accessed | tf_op | source)
XLA Modules:
  0.0 282.5 jit_solution(4466259191748090938)
XLA Ops:
  7.2 0.0 copy-start
  7.2 10.0 %all-to-all-start = ((bf16[32,256,256]{2,1,0:T(8,128)(2,1)}), bf16[32,256,256]{2,1,0:T(8,128)(2,1)}, u32[]{:S(2)}, u32[]{:S(2)}) async-start(bf16[32,256,256]{2,1,0:T(8,128)(2,1)} %bitcast.33), calls=%async_computation | async-start | bytes 8388608 | tf_op jit(solution)/shard_map/all_to_all | solution.py:36
  17.2 0.0 all-gather.5.cloned.1.call-start
  17.2 0.0 copy-done
  17.2 0.7 copy.34
  18.0 0.0 all-gather.5.cloned.1.call-update
  18.0 0.0 all-gather.3.cloned.1.call-start
  18.1 53.2 %all-to-all-done = bf16[32,256,256]{2,1,0:T(8,128)(2,1)} async-done(((bf16[32,256,256]{2,1,0:T(8,128)(2,1)}), bf16[32,256,256]{2,1,0:T(8,128)(2,1)}, u32[]{:S(2)}, u32[]{:S(2)}) %all-to-all-start) | async-done | bytes 4194336 | tf_op jit(solution)/shard_map/all_to_all | solution.py:36
  71.2 6.5 %copy.23 = bf16[256,32,256]{0,2,1:T(8,128)(2,1)} copy(bf16[256,32,256]{2,0,1:T(8,128)(2,1)} %bitcast.1) | data formatting | bytes 8388608 | tf_op jit(solution)/shard_map/all_to_all | solution.py:36
  77.7 0.0 copy-start.2
  77.7 0.0 copy-start.1
  77.7 0.0 all-gather.3.cloned.1.call-update
  77.8 0.7 copy-done.2
  78.5 0.1 all_to_all.49
  78.6 0.1 copy.36
  78.7 0.7 reshape.41
  79.4 10.3 %all-to-all-start.1 = ((bf16[32,2,128]{2,1,0:T(2,128)(2,1)}), bf16[32,2,128]{2,1,0:T(2,128)(2,1)S(1)}, u32[]{:S(2)}, u32[]{:S(2)}) async-start(bf16[32,2,128]{2,1,0:T(2,128)(2,1)} %reshape.41), calls=%async_computation.1 | async-start | bytes 32768 | tf_op jit(solution)/shard_map/all_to_all | solution.py:37
  89.8 0.0 copy-done.1
  89.8 0.1 copy.29
  89.9 6.9 %all-to-all-done.1 = bf16[32,2,128]{2,1,0:T(2,128)(2,1)S(1)} async-done(((bf16[32,2,128]{2,1,0:T(2,128)(2,1)}), bf16[32,2,128]{2,1,0:T(2,128)(2,1)S(1)}, u32[]{:S(2)}, u32[]{:S(2)}) %all-to-all-start.1) | async-done | bytes 16416 | tf_op jit(solution)/shard_map/all_to_all | solution.py:37
  96.8 0.5 broadcast_in_dim.5
  97.3 33.7 %all_to_all.62 = bf16[32,128,256]{1,2,0:T(8,128)(2,1)} all-to-all(bf16[32,128,256]{1,2,0:T(8,128)(2,1)S(1)} %broadcast_in_dim.5), channel_id=1, replica_groups=mesh['wide'=32,'narrow'=4] {'wide'}, dimensions={0} | all-to-all | bytes 4194304 | tf_op jit(solution)/shard_map/all_to_all | solution.py:9
  131.0 6.6 %all-to-all-start.3 = ((bf16[128,4,2048]{0,2,1:T(8,128)(2,1)}), bf16[128,4,2048]{0,2,1:T(8,128)(2,1)}, u32[]{:S(2)}, u32[]{:S(2)}) async-start(bf16[128,4,2048]{0,2,1:T(8,128)(2,1)} %bitcast.11), calls=%async_computation.3 | async-start | bytes 4194304 | tf_op jit(solution)/shard_map/all_to_all | solution.py:49
  137.7 0.1 reshape.42
  137.8 0.1 copy.33
  137.9 51.1 %all_gather.10 = bf16[64,512]{1,0:T(8,128)(2,1)S(1)} all-gather(bf16[16,512]{1,0:T(8,128)(2,1)S(1)} %copy.33), channel_id=1, replica_groups=mesh['wide'=32,'narrow'=4] {'narrow'}, dimensions={0}, use_global_device_ids=true | all-gather | bytes 81920 | tf_op jit(solution)/shard_map/all_gather | solution.py:41
  189.0 0.1 copy.26
  189.1 2.3 broadcast_in_dim.4
  191.4 3.2 %copy.27 = f32[64,8192]{1,0:T(8,128)S(1)} copy(f32[64,8192]{0,1:T(8,128)} %bitcast.32) | data formatting | bytes 4194304 | tf_op jit(solution)/shard_map/convert_element_type | solution.py:27
  194.6 11.2 %mul.11 = f32[64,16,8192]{2,1,0:T(8,128)} broadcast(f32[64,8192]{1,0:T(8,128)S(1)} %copy.27), dimensions={0,2} | broadcast | bytes 35651584 | tf_op jit(solution)/shard_map/mul | solution.py:29
  205.8 33.5 %copy.28 = f32[1024,8192]{0,1:T(8,128)} copy(f32[1024,8192]{1,0:T(8,128)} %bitcast.30) | data formatting | bytes 67108864 | tf_op jit(solution)/shard_map/mul | solution.py:29
  239.3 0.0 all-to-all-done.3
  239.3 2.9 %copy.30 = bf16[4,128,2048]{2,1,0:T(8,128)(2,1)S(1)} copy(bf16[4,128,2048]{1,2,0:T(8,128)(2,1)} %bitcast.12) | data formatting | bytes 4194304 | tf_op jit(solution)/shard_map/all_to_all | solution.py:49
  242.3 0.0 all-gather.5.cloned.1.call-done
  242.3 5.7 %convolution_convert_fusion = bf16[2048,1024]{0,1:T(8,128)(2,1)} fusion(bf16[512,2048]{1,0:T(8,128)(2,1)S(1)} %bitcast.35, bf16[512,1024]{1,0:T(8,128)(2,1)} %all-gather.5.cloned.1.call-done), kind=kOutput, calls=%fused_computation.2 | convolution fusion | flops 2149580800 | bytes 7340032 | tf_op jit(solution)/shard_map/dot_general | solution.py:53
  248.0 7.4 %copy.32 = bf16[2048,4,256]{2,1,0:T(4,128)(2,1)} copy(bf16[2048,4,256]{0,2,1:T(8,128)(2,1)} %bitcast.34) | data formatting | bytes 8388608
  255.4 0.0 all-gather.3.cloned.1.call-done
  255.4 19.3 %fusion.1 = bf16[1024,128]{1,0:T(8,128)(2,1)S(1)} fusion(bf16[128,8192]{0,1:T(8,128)(2,1)} %bitcast.8, f32[1024,8192]{0,1:T(8,128)} %copy.28, bf16[1024,8192]{0,1:T(8,128)(2,1)} %all-gather.3.cloned.1.call-done), kind=kOutput, calls=%fused_computation.3 | convolution fusion | flops 2172780544 | bytes 52690944 | tf_op jit(solution)/shard_map/dot_general | solution.py:46
  274.7 0.9 copy.31
Async XLA Ops:
  7.2 10.1 %copy-start = (bf16[128,4,256]{2,1,0:T(4,128)(2,1)S(1)}, bf16[128,4,256]{2,1,0:T(4,128)(2,1)}, u32[]{:S(2)}) copy-start(bf16[128,4,256]{2,1,0:T(4,128)(2,1)} %param.4) | copy-start | bytes 786436
  7.2 64.1 %all-to-all-start = ((bf16[32,256,256]{2,1,0:T(8,128)(2,1)}), bf16[32,256,256]{2,1,0:T(8,128)(2,1)}, u32[]{:S(2)}, u32[]{:S(2)}) async-start(bf16[32,256,256]{2,1,0:T(8,128)(2,1)} %bitcast.33), calls=%async_computation | async-start | bytes 8388608 | tf_op jit(solution)/shard_map/all_to_all | solution.py:36
  17.2 225.1 %all-gather.5.cloned.1.call-start = ((), (), s32[]{:S(2)}) async-start(), calls=%async_computation.5 | async-start | bytes 1310720 | tf_op jit(solution)/shard_map/all_gather | solution.py:50
  18.0 237.4 %all-gather.3.cloned.1.call-start = ((), (), s32[]{:S(2)}) async-start(), calls=%async_computation.4 | async-start | bytes 20971520 | tf_op jit(solution)/shard_map/all_gather | solution.py:40
  77.7 0.7 copy-start.2
  77.7 12.0 %copy-start.1 = (bf16[128,256]{1,0:T(8,128)(2,1)S(1)}, bf16[128,256]{1,0:T(8,128)(2,1)}, u32[]{:S(2)}) copy-start(bf16[128,256]{1,0:T(8,128)(2,1)} %param.5) | copy-start | bytes 196612
  79.4 17.4 %all-to-all-start.1 = ((bf16[32,2,128]{2,1,0:T(2,128)(2,1)}), bf16[32,2,128]{2,1,0:T(2,128)(2,1)S(1)}, u32[]{:S(2)}, u32[]{:S(2)}) async-start(bf16[32,2,128]{2,1,0:T(2,128)(2,1)} %reshape.41), calls=%async_computation.1 | async-start | bytes 32768 | tf_op jit(solution)/shard_map/all_to_all | solution.py:37
  131.0 108.3 %all-to-all-start.3 = ((bf16[128,4,2048]{0,2,1:T(8,128)(2,1)}), bf16[128,4,2048]{0,2,1:T(8,128)(2,1)}, u32[]{:S(2)}, u32[]{:S(2)}) async-start(bf16[128,4,2048]{0,2,1:T(8,128)(2,1)} %bitcast.11), calls=%async_computation.3 | async-start | bytes 4194304 | tf_op jit(solution)/shard_map/all_to_all | solution.py:49
Sparse Core Ops, SparseCore 0:
  20.3 52.2 all-gather.4
  77.9 162.2 all-gather.2
where the time goes:
time: 284 us; the launch traced here: 282 us
  blocking collectives  84.9 us (30%)
  local copies, waits for them, and re-layouts  71.2 us (25%)
  waiting for transfers between devices  60.2 us (21%)
  starting transfers between devices  27.1 us (10%)
  matrix products  25 us (9%)
  between operations  14.2 us (5%)
    all_to_all x1, waiting for transfers between devices, per_device(): lax.all_to_all(weight_base, 'wide', split_axis=0, concat_axis=1, tiled=True)  53.2 us
    all_gather x1, blocking collectives, per_device(): lax.all_gather(row_scales, 'narrow', axis=0, tiled=True)  51.1 us
    mul x2, local copies, waits for them, and re-layouts, apply_scales(): blocked = blocked * widened[:, None, :]  44.7 us
    all_to_all x1, blocking collectives, from_everyone(): lax.all_to_all(jnp.broadcast_to(shard[None], (length, *shard.shape)), axi...  33.7 us
    dot_general x1, matrix products, per_device(): lax.dot_general(incoming, effective, contract_last, preferred_element_typ...  19.3 us
    unnamed x12, local copies, waits for them, and re-layouts  10.7 us
    all_to_all x1, starting transfers between devices, per_device(): lax.all_to_all(block_scale, 'wide', split_axis=0, concat_axis=1, tiled=True)  10.3 us
    all_to_all x1, starting transfers between devices, per_device(): lax.all_to_all(weight_base, 'wide', split_axis=0, concat_axis=1, tiled=True)  10 us
  transfers between devices with their start and end apart: 5, of which 2 were waited for; matrix products, arithmetic and copies ran while one was open for 27% of the time, Pallas kernels for 0%

commit v1 on v0

v1 whole, which is shorter than its diff:
```python
import functools

import jax
import jax.numpy as jnp
from jax import lax
from jax.experimental import pallas as pl
from jax.experimental.pallas import tpu as pltpu
from jax.sharding import Mesh, PartitionSpec as P

BF = jnp.bfloat16
F32 = jnp.float32
VM = pltpu.VMEM


def first_axis_steps(k):
    pairs = []
    for z in range(4):
        for x in range(4):
            pairs.append(((z * 4 + x) * 2, (z * 4 + (x + k) % 4) * 2))
            pairs.append(((z * 4 + x) * 2 + 1, (((z + k) % 4) * 4 + x) * 2 + 1))
    return pairs


def second_axis_steps(k):
    pairs = []
    for z in range(4):
        for x in range(4):
            pairs.append(((z * 4 + x) * 2, (((z + k) % 4) * 4 + x) * 2))
            pairs.append(((z * 4 + x) * 2 + 1, (z * 4 + (x + k) % 4) * 2 + 1))
    return pairs


def shift(value, pairs):
    return lax.ppermute(value, ("z", "x", "c"), pairs)


def swap(value, axis):
    return lax.ppermute(value, axis, [(0, 1), (1, 0)])


def place(k, i, m):
    p = (m[1] + k) & 3
    c = m[0]
    return c * p + (1 - c) * i, c * i + (1 - c) * p


def scale_body(k, m, w_ref, s_ref, o_ref, wide_ref):
    i = pl.program_id(0)

    @pl.when(i == 0)
    def _():
        row = lax.broadcasted_iota(jnp.int32, (16, 256), 0)
        col = lax.broadcasted_iota(jnp.int32, (16, 256), 1)
        spread = jnp.where(col // 16 == row, 1.0, 0.0).astype(BF)
        wide_ref[...] = lax.dot_general(
            s_ref[...], spread, (((0,), (0,)), ((), ())), preferred_element_type=F32
        )

    z, x = place(k, i, m)
    for yl in range(2):
        r = pl.multiple_of((z * 8 + yl * 4 + x) * 16, 16)
        s = wide_ref[pl.ds(r, 16), :]
        w = w_ref[0, yl, 0].astype(F32).reshape(16, 16, 256)
        o_ref[pl.ds(yl * 256, 256), :] = (w * s[:, None, :]).reshape(256, 256).astype(BF)


def scaled_rows(k, meta, w5, scales_t):
    def w_map(i, m):
        z, x = place(k, i, m)
        return z, 0, x, 0, 0

    return pl.pallas_call(
        functools.partial(scale_body, k),
        out_shape=jax.ShapeDtypeStruct((2048, 256), BF),
        grid_spec=pltpu.PrefetchScalarGridSpec(
            num_scalar_prefetch=1,
            grid=(4,),
            in_specs=[
                pl.BlockSpec((1, 2, 1, 256, 256), w_map),
                pl.BlockSpec((16, 512), lambda i, m: (0, 0)),
            ],
            out_specs=pl.BlockSpec((512, 256), lambda i, m: (i, 0)),
            scratch_shapes=[VM((512, 256), F32)],
        ),
        name=f"scale{k}",
    )(meta, w5, scales_t)


def partial_body(m, *refs):
    g, w, o_ref = refs[:4], refs[4:8], refs[8]
    total = None
    for a, b in zip(g, w):
        part = lax.dot_general(
            a[...], b[...], (((1,), (1,)), ((), ())), preferred_element_type=F32
        )
        total = part if total is None else total + part
    o_ref[...] = total.astype(o_ref.dtype)


def partial_sums(k, meta, grads, weights, dtype):
    return pl.pallas_call(
        partial_body,
        out_shape=jax.ShapeDtypeStruct((512, 512), dtype),
        grid_spec=pltpu.PrefetchScalarGridSpec(
            num_scalar_prefetch=1,
            grid=(1,),
            in_specs=[pl.BlockSpec((512, 256), lambda i, m: (0, 0))] * 4
            + [pl.BlockSpec((512, 256), lambda i, m: ((m[2] + k) & 3, 0))] * 4,
            out_specs=pl.BlockSpec((512, 512), lambda i, m: (0, 0)),
        ),
        name=f"partial{k}",
    )(meta, *grads, *weights)


def gather_body(a, b, c, d, o_ref):
    total = a[...] + b[...].astype(F32) + c[...].astype(F32) + d[...].astype(F32)
    total = total.astype(BF)
    for yl in range(2):
        for n in range(4):
            o_ref[yl * 4 + n] = total[n * 128 : (n + 1) * 128, yl * 256 : (yl + 1) * 256]


def summed_blocks(parts):
    return pl.pallas_call(
        gather_body,
        out_shape=jax.ShapeDtypeStruct((8, 128, 256), BF),
        name="summed",
    )(*parts)


def finish_body(r_ref, o_ref):
    for n in range(4):
        o_ref[:, n, :] = (r_ref[n].astype(F32) + r_ref[4 + n].astype(F32)).astype(BF)


def finished(blocks):
    return pl.pallas_call(
        finish_body,
        out_shape=jax.ShapeDtypeStruct((128, 4, 256), BF),
        name="finish",
    )(blocks)


def outer_body(m, *refs):
    mine, theirs, h_ref, o_ref = refs[:4], refs[4], refs[5], refs[6]
    i = pl.program_id(0)

    def block(g):
        r = lax.dot_general(
            g, h_ref[...], (((0,), (0,)), ((), ())), preferred_element_type=F32
        ).astype(BF)
        for n in range(4):
            o_ref[:, n, :] = r[:, n * 256 : (n + 1) * 256]

    for k in range(4):

        @pl.when(i == k)
        def _():
            block(mine[k][...])

    @pl.when(i >= 4)
    def _():
        block(theirs[i - 4])


def outer_product(meta, mine, theirs, hidden):
    def o_map(i, m):
        yl = jnp.where(i < 4, m[3], 1 - m[3])
        return yl * 4 + ((m[4] - i) & 3), 0, 0

    full = pl.BlockSpec((512, 256), lambda i, m: (0, 0))
    return pl.pallas_call(
        outer_body,
        out_shape=jax.ShapeDtypeStruct((2048, 4, 256), BF),
        grid_spec=pltpu.PrefetchScalarGridSpec(
            num_scalar_prefetch=1,
            grid=(8,),
            in_specs=[full] * 4
            + [
                pl.BlockSpec((4, 512, 256), lambda i, m: (0, 0, 0)),
                pl.BlockSpec((512, 1024), lambda i, m: (0, 0)),
            ],
            out_specs=pl.BlockSpec((256, 4, 256), o_map),
        ),
        name="outer",
    )(meta, *mine, theirs, hidden)


def joined(a, b, first):
    return jnp.where(first, jnp.concatenate([a, b], 0), jnp.concatenate([b, a], 0))


def per_device(hidden, grad_out, weight_base, block_scale):
    z, yl, x = lax.axis_index("z"), lax.axis_index("yl"), lax.axis_index("x")
    yh, c = lax.axis_index("yh"), lax.axis_index("c")
    pos = jnp.where(c == 0, x, z)
    other = jnp.where(c == 0, z, x)
    meta = jnp.stack([c, pos, other, yl, x]).astype(jnp.int32)

    g2 = joined(grad_out, swap(grad_out, "c"), c == 0)
    g4 = joined(g2, swap(g2, "yh"), yh == 0)

    w5 = weight_base.reshape(4, 2, 4, 256, 256)
    scales_t = block_scale.T
    rows = [None] * 4
    for k in (2, 1, 3):
        rows[k] = shift(scaled_rows(k, meta, w5, scales_t), first_axis_steps(k))
    rows[0] = scaled_rows(0, meta, w5, scales_t)
    grads = [g4] + [shift(g4, first_axis_steps(k)) for k in (1, 2, 3)]

    parts = [None] * 4
    for k in (2, 1, 3):
        parts[k] = shift(partial_sums(k, meta, grads, rows, BF), second_axis_steps(k))
    parts[0] = partial_sums(0, meta, grads, rows, F32)
    blocks = summed_blocks(parts)
    blocks = lax.all_to_all(blocks, ("yl", "yh", "c"), 0, 0, tiled=True)
    grad_hidden = finished(blocks)

    h = hidden.reshape(128, 1024)
    h2 = joined(h, swap(h, "c"), c == 0)
    h4 = joined(h2, swap(h2, "yh"), yh == 0)
    stacked = jnp.stack(grads)
    want = jnp.where(c == 0, yh * 2, yh * 2 + 1)
    give = lax.dynamic_index_in_dim(stacked, (z - yh * 2) & 3, 0, keepdims=False)
    keep = lax.dynamic_index_in_dim(stacked, (z - want) & 3, 0, keepdims=False)
    got = lax.ppermute(give, "c", [(1, 0)])
    seed = jnp.where(c == 0, got, keep)
    ring = lambda k: [(i, (i + k) % 4) for i in range(4)]
    mine = [seed] + [lax.ppermute(seed, "x", ring(k)) for k in (1, 2, 3)]
    theirs = swap(jnp.stack(mine), "yl")
    grad_weight = outer_product(meta, mine, theirs, h4)
    return grad_hidden, grad_weight


def solution(mesh):
    fine = Mesh(mesh.devices.reshape(4, 2, 4, 2, 2), ("z", "yl", "x", "yh", "c"))
    narrow, wide = ("yh", "c"), ("z", "yl", "x")
    return jax.shard_map(
        per_device,
        mesh=fine,
        in_specs=(
            P(narrow, None, wide),
            P(narrow, wide),
            P(narrow, wide),
            P(narrow, wide),
        ),
        out_specs=(P(narrow, None, wide), P(narrow, None, wide)),
        check_vma=False,
    )
```

time: 284 us -> 144 us (0.51)
  blocking collectives: 84.9 us -> 0 us
  local copies, waits for them, and re-layouts: 71.2 us -> 8.96 us
  Pallas kernels: 0 us -> 49.5 us
  matrix products: 25 us -> 0 us
  waiting for transfers between devices: 60.2 us -> 37.7 us
  between operations: 14.2 us -> 0.77 us
  starting transfers between devices: 27.1 us -> 39.4 us
  other arithmetic: 0 us -> 6.24 us
    all_to_all x3 -> x1, waiting for transfers between devices: 60.1 us -> 7.28 us  [per_device(): blocks = lax.all_to_all(blocks, ('yl', 'yh', 'c'), 0, 0, tiled=True)]
    all_gather x1 -> x0, blocking collectives: 51.1 us -> none  [per_device(): lax.all_gather(row_scales, 'narrow', axis=0, tiled=True)]
    pallas_call x0 -> x11, Pallas kernels: none -> 49.5 us  [the longest x4 17.7 us: scaled_rows(): pl.pallas_call(functools.partial(scale_body, k), out_shape=jax.ShapeDtype...]
    mul x2 -> x0, local copies, waits for them, and re-layouts: 44.7 us -> none  [apply_scales(): blocked = blocked * widened[:, None, :]]
    all_to_all x1 -> x0, blocking collectives: 33.7 us -> none  [from_everyone(): lax.all_to_all(jnp.broadcast_to(shard[None], (length, *shard.shape)), axi...]
    ppermute x0 -> x18, starting transfers between devices: none -> 32.7 us  [the longest x9 15.7 us: shift(): return lax.ppermute(value, ('z', 'x', 'c'), pairs)]
    ppermute x0 -> x18, waiting for transfers between devices: none -> 30.5 us  [the longest x3 20 us: per_device(): mine = [seed] + [lax.ppermute(seed, 'x', ring(k)) for k in (1, 2, 3)]]
    dot_general x2 -> x0, matrix products: 25 us -> none  [the longest x1 19.3 us: per_device(): lax.dot_general(incoming, effective, contract_last, preferred_element_typ...]
  transfers between devices with their start and end apart: 5 -> 19, of which waited for: 2 -> 7; matrix products, arithmetic and copies ran while one was open for 27% -> 5% of each run, Pallas kernels for 0% -> 26%
where the time goes in v1:
time: 144 us; the launch traced here: 143 us
  Pallas kernels  49.5 us (34%)
  starting transfers between devices  39.4 us (27%)
  waiting for transfers between devices  37.7 us (26%)
  local copies, waits for them, and re-layouts  8.96 us (6%)
  other arithmetic  6.24 us (4%)
    ppermute x3, waiting for transfers between devices, per_device(): mine = [seed] + [lax.ppermute(seed, 'x', ring(k)) for k in (1, 2, 3)]  20 us
    pallas_call x4, Pallas kernels, scaled_rows(): pl.pallas_call(functools.partial(scale_body, k), out_shape=jax.ShapeDtype...  17.7 us
    ppermute x9, starting transfers between devices, shift(): return lax.ppermute(value, ('z', 'x', 'c'), pairs)  15.7 us
    pallas_call x4, Pallas kernels, partial_sums(): pl.pallas_call(partial_body, out_shape=jax.ShapeDtypeStruct((512, 512), d...  15 us
    pallas_call x1, Pallas kernels, outer_product(): pl.pallas_call(outer_body, out_shape=jax.ShapeDtypeStruct((2048, 4, 256),...  11.8 us
    ppermute x5, starting transfers between devices, swap(): return lax.ppermute(value, axis, [(0, 1), (1, 0)])  10.1 us
    unnamed x33, local copies, waits for them, and re-layouts  7.66 us
    all_to_all x1, waiting for transfers between devices, per_device(): blocks = lax.all_to_all(blocks, ('yl', 'yh', 'c'), 0, 0, tiled=True)  7.28 us
  transfers between devices with their start and end apart: 19, of which 7 were waited for; matrix products, arithmetic and copies ran while one was open for 5% of the time, Pallas kernels for 26%

profile of v1, /device:TPU:1, one launch (start us, length us, event | category | flops | bytes accessed | tf_op | source)
XLA Modules:
  0.0 142.6 jit_solution(7249915133510827240)
XLA Ops:
  0.6 1.5 %collective-permute-start = (bf16[128,256]{1,0:T(8,128)(2,1)}, bf16[128,256]{1,0:T(8,128)(2,1)S(1)}, u32[]{:S(2)}, u32[]{:S(2)}) collective-permute-start(bf16[128,256]{1,0:T(8,128)(2,1)} %param.5), channel_id=1, source_target_pairs={{0,1},{1,0},{2,3},{3,2},{4,5},{5,4},{6,7},{7,6},{8,9},{9,8},{10,11... | collective-permute-start | bytes 196616 | tf_op jit(solution)/shard_map/ppermute | solution.py:38
  2.1 1.1 collective-permute-done
  3.2 1.0 maximum_select_fusion.4
  4.2 3.1 %collective-permute-start.1 = (bf16[256,256]{1,0:T(8,128)(2,1)S(1)}, bf16[256,256]{1,0:T(8,128)(2,1)S(1)}, u32[]{:S(2)}, u32[]{:S(2)}) collective-permute-start(bf16[256,256]{1,0:T(8,128)(2,1)S(1)} %maximum_select_fusion.4), channel_id=1, source_target_pairs={{0,2},{2,0},{1,3},{3,1},{4,6},{6,4},{5,7},{7,5},{8,10},{10,8},{9,1... | collective-permute-start | bytes 393224 | tf_op jit(solution)/shard_map/ppermute | solution.py:38
  7.3 3.3 %collective-permute-done.1 = bf16[256,256]{1,0:T(8,128)(2,1)S(1)} collective-permute-done((bf16[256,256]{1,0:T(8,128)(2,1)S(1)}, bf16[256,256]{1,0:T(8,128)(2,1)S(1)}, u32[]{:S(2)}, u32[]{:S(2)}) %collective-permute-start.1) | collective-permute-done | bytes 131104 | tf_op jit(solution)/shard_map/ppermute | solution.py:38
  10.7 1.7 %collective-permute-start.2 = (bf16[512,256]{1,0:T(8,128)(2,1)S(1)}, bf16[512,256]{1,0:T(8,128)(2,1)S(1)}, u32[]{:S(2)}, u32[]{:S(2)}) collective-permute-start(bf16[512,256]{1,0:T(8,128)(2,1)S(1)} %maximum_select_fusion.2.refs_0_), channel_id=1, source_target_pairs={{0,4},{1,33},{4,8},{5,37},{8,12},{9,41},{12,0},{13,45},{32,36},{33... | collective-permute-start | bytes 786440 | tf_op jit(solution)/shard_map/ppermute | solution.py:34
  12.4 3.3 %collective-permute-start.3 = (bf16[512,256]{1,0:T(8,128)(2,1)S(1)}, bf16[512,256]{1,0:T(8,128)(2,1)S(1)}, u32[]{:S(2)}, u32[]{:S(2)}) collective-permute-start(bf16[512,256]{1,0:T(8,128)(2,1)S(1)} %maximum_select_fusion.2.refs_0_), channel_id=1, source_target_pairs={{0,8},{1,65},{4,12},{5,69},{8,0},{9,73},{12,4},{13,77},{32,40},{33... | collective-permute-start | bytes 786440 | tf_op jit(solution)/shard_map/ppermute | solution.py:34
  15.7 0.7 collective-permute-start.4
  16.6 2.0 %collective-permute-done.2.refs_1_ = bf16[512,256]{1,0:T(8,128)(2,1)S(1)} collective-permute-done((bf16[512,256]{1,0:T(8,128)(2,1)S(1)}, bf16[512,256]{1,0:T(8,128)(2,1)S(1)}, u32[]{:S(2)}, u32[]{:S(2)}) %collective-permute-start.2) | collective-permute-done | bytes 262176 | tf_op jit(solution)/shard_map/ppermute | solution.py:34
  18.6 4.0 %collective-permute-done.3.refs_2_ = bf16[512,256]{1,0:T(8,128)(2,1)S(1)} collective-permute-done((bf16[512,256]{1,0:T(8,128)(2,1)S(1)}, bf16[512,256]{1,0:T(8,128)(2,1)S(1)}, u32[]{:S(2)}, u32[]{:S(2)}) %collective-permute-start.3) | collective-permute-done | bytes 262176 | tf_op jit(solution)/shard_map/ppermute | solution.py:34
  22.7 1.0 copy-done.7
  24.4 3.4 %collective-permute-start.11 = (bf16[512,256]{1,0:T(8,128)(2,1)}, bf16[512,256]{1,0:T(8,128)(2,1)}, u32[]{:S(2)}, u32[]{:S(2)}) collective-permute-start(bf16[512,256]{1,0:T(8,128)(2,1)} %dynamic-slice_bitcast_fusion), channel_id=1, source_target_pairs={{1,0},{3,2},{5,4},{7,6},{9,8},{11,10},{13,12},{15,14},{17,16},{19,... | collective-permute-start | bytes 786440 | tf_op jit(solution)/shard_map/ppermute | solution.py:226
  28.4 4.4 %scale1.1 = bf16[2048,256]{1,0:T(8,128)(2,1)} custom-call(s32[5]{0:T(128)} %stack.51.m, bf16[4,2,4,256,256]{4,3,2,1,0:T(8,128)(2,1)} %bitcast.22, bf16[16,512]{1,0:T(8,128)(2,1)} %bitcast.35), custom_call_target="tpu_custom_call" | custom-call | tf_op jit(solution)/shard_map/scale1/pallas_call | solution.py:72
  32.8 1.6 %collective-permute-start.5 = (bf16[2048,256]{1,0:T(8,128)(2,1)}, bf16[2048,256]{1,0:T(8,128)(2,1)S(1)}, u32[]{:S(2)}, u32[]{:S(2)}) collective-permute-start(bf16[2048,256]{1,0:T(8,128)(2,1)} %scale1.1), channel_id=1, source_target_pairs={{0,4},{1,33},{4,8},{5,37},{8,12},{9,41},{12,0},{13,45},{32,36},{33... | collective-permute-start | bytes 3145736 | tf_op jit(solution)/shard_map/ppermute | solution.py:34
  34.5 4.4 %scale2.1 = bf16[2048,256]{1,0:T(8,128)(2,1)} custom-call(s32[5]{0:T(128)} %stack.51.m, bf16[4,2,4,256,256]{4,3,2,1,0:T(8,128)(2,1)} %bitcast.23, bf16[16,512]{1,0:T(8,128)(2,1)} %bitcast.36), custom_call_target="tpu_custom_call" | custom-call | tf_op jit(solution)/shard_map/scale2/pallas_call | solution.py:72
  38.9 3.3 %collective-permute-start.6 = (bf16[2048,256]{1,0:T(8,128)(2,1)}, bf16[2048,256]{1,0:T(8,128)(2,1)S(1)}, u32[]{:S(2)}, u32[]{:S(2)}) collective-permute-start(bf16[2048,256]{1,0:T(8,128)(2,1)} %scale2.1), channel_id=1, source_target_pairs={{0,8},{1,65},{4,12},{5,69},{8,0},{9,73},{12,4},{13,77},{32,40},{33... | collective-permute-start | bytes 3145736 | tf_op jit(solution)/shard_map/ppermute | solution.py:34
  42.2 4.4 %scale3.1 = bf16[2048,256]{1,0:T(8,128)(2,1)} custom-call(s32[5]{0:T(128)} %stack.51.m, bf16[4,2,4,256,256]{4,3,2,1,0:T(8,128)(2,1)} %bitcast.24, bf16[16,512]{1,0:T(8,128)(2,1)} %bitcast.37), custom_call_target="tpu_custom_call" | custom-call | tf_op jit(solution)/shard_map/scale3/pallas_call | solution.py:72
  46.6 0.7 collective-permute-start.7
  47.3 1.0 bitcast_select_fusion.refs_0_
  48.3 1.7 %collective-permute-start.12 = (bf16[512,256]{1,0:T(8,128)(2,1)S(1)}, bf16[512,256]{1,0:T(8,128)(2,1)S(1)}, u32[]{:S(2)}, u32[]{:S(2)}) collective-permute-start(bf16[512,256]{1,0:T(8,128)(2,1)S(1)} %bitcast_select_fusion.refs_0_), channel_id=1, source_target_pairs={{0,4},{4,8},{8,12},{12,0},{1,5},{5,9},{9,13},{13,1},{2,6},{6,10},{... | collective-permute-start | bytes 786440 | tf_op jit(solution)/shard_map/ppermute | solution.py:229
  50.0 1.8 %collective-permute-start.13 = (bf16[512,256]{1,0:T(8,128)(2,1)S(1)}, bf16[512,256]{1,0:T(8,128)(2,1)S(1)}, u32[]{:S(2)}, u32[]{:S(2)}) collective-permute-start(bf16[512,256]{1,0:T(8,128)(2,1)S(1)} %bitcast_select_fusion.refs_0_), channel_id=1, source_target_pairs={{0,8},{4,12},{8,0},{12,4},{1,9},{5,13},{9,1},{13,5},{2,10},{6,14},... | collective-permute-start | bytes 786440 | tf_op jit(solution)/shard_map/ppermute | solution.py:229
  51.8 15.8 %collective-permute-done.12.refs_1_ = bf16[512,256]{1,0:T(8,128)(2,1)S(1)} collective-permute-done((bf16[512,256]{1,0:T(8,128)(2,1)S(1)}, bf16[512,256]{1,0:T(8,128)(2,1)S(1)}, u32[]{:S(2)}, u32[]{:S(2)}) %collective-permute-start.12) | collective-permute-done | bytes 262176 | tf_op jit(solution)/shard_map/ppermute | solution.py:229
  67.6 1.8 %copy.6 = bf16[16,8,4,256]{3,1,2,0:T(8,128)(2,1)} copy(bf16[16,8,4,256]{3,2,1,0:T(4,128)(2,1)} %bitcast.39) | data formatting | bytes 524288
  69.4 1.5 %collective-permute-start.16 = (bf16[128,1024]{1,0:T(8,128)(2,1)}, bf16[128,1024]{1,0:T(8,128)(2,1)}, u32[]{:S(2)}, u32[]{:S(2)}) collective-permute-start(bf16[128,1024]{1,0:T(8,128)(2,1)} %bitcast.19), channel_id=1, source_target_pairs={{0,1},{1,0},{2,3},{3,2},{4,5},{5,4},{6,7},{7,6},{8,9},{9,8},{10,11... | collective-permute-start | bytes 786440 | tf_op jit(solution)/shard_map/ppermute | solution.py:38
  70.9 4.2 %collective-permute-done.14.refs_3_ = bf16[512,256]{1,0:T(8,128)(2,1)S(1)} collective-permute-done((bf16[512,256]{1,0:T(8,128)(2,1)S(1)}, bf16[512,256]{1,0:T(8,128)(2,1)S(1)}, u32[]{:S(2)}, u32[]{:S(2)}) %collective-permute-start.14) | collective-permute-done | bytes 262176 | tf_op jit(solution)/shard_map/ppermute | solution.py:229
  75.1 1.1 pad_maximum_fusion.1
  76.2 1.3 collective-permute-start.15
  77.6 4.4 %scale0.1.refs_4_ = bf16[2048,256]{1,0:T(8,128)(2,1)} custom-call(s32[5]{0:T(128)} %stack.51.m, bf16[4,2,4,256,256]{4,3,2,1,0:T(8,128)(2,1)} %bitcast.25, bf16[16,512]{1,0:T(8,128)(2,1)} %bitcast.38), custom_call_target="tpu_custom_call" | custom-call | tf_op jit(solution)/shard_map/scale0/pallas_call | solution.py:72
  82.0 0.9 copy-done
  83.3 1.0 copy-done.2
  84.3 3.7 %partial1.1 = bf16[512,512]{1,0:T(8,128)(2,1)} custom-call(s32[5]{0:T(128)} %stack.51.m, bf16[512,256]{1,0:T(8,128)(2,1)} %copy-done.3, bf16[512,256]{1,0:T(8,128)(2,1)} %copy-done.4, bf16[512,256]{1,0:T(8,128)(2,1)} %copy-done.5, bf16[512,256]{1,0:T(8,128)(2,1)} %copy-done.6, bf16[2048,256]{1,0:T(8,128)(2,1)} %scale0.1.refs_4_, bf16[2048,256]{1,0:T(8,128)(2,1)} %copy-done, ...), custom_call_target="tpu_custom_call" | custom-call | tf_op jit(solution)/shard_map/partial1/pallas_call | solution.py:101
  88.0 1.9 %collective-permute-start.8 = (bf16[512,512]{1,0:T(8,128)(2,1)}, bf16[512,512]{1,0:T(8,128)(2,1)S(1)}, u32[]{:S(2)}, u32[]{:S(2)}) collective-permute-start(bf16[512,512]{1,0:T(8,128)(2,1)} %partial1.1), channel_id=1, source_target_pairs={{0,32},{1,5},{4,36},{5,9},{8,40},{9,13},{12,44},{13,1},{32,64},{33... | collective-permute-start | bytes 1572872 | tf_op jit(solution)/shard_map/ppermute | solution.py:34
  89.9 3.7 %partial2.1 = bf16[512,512]{1,0:T(8,128)(2,1)} custom-call(s32[5]{0:T(128)} %stack.51.m, bf16[512,256]{1,0:T(8,128)(2,1)} %copy-done.3, bf16[512,256]{1,0:T(8,128)(2,1)} %copy-done.4, bf16[512,256]{1,0:T(8,128)(2,1)} %copy-done.5, bf16[512,256]{1,0:T(8,128)(2,1)} %copy-done.6, bf16[2048,256]{1,0:T(8,128)(2,1)} %scale0.1.refs_4_, bf16[2048,256]{1,0:T(8,128)(2,1)} %copy-done, ...), custom_call_target="tpu_custom_call" | custom-call | tf_op jit(solution)/shard_map/partial2/pallas_call | solution.py:101
  93.7 0.7 collective-permute-start.9
  94.4 3.7 %partial3.1 = bf16[512,512]{1,0:T(8,128)(2,1)} custom-call(s32[5]{0:T(128)} %stack.51.m, bf16[512,256]{1,0:T(8,128)(2,1)} %copy-done.3, bf16[512,256]{1,0:T(8,128)(2,1)} %copy-done.4, bf16[512,256]{1,0:T(8,128)(2,1)} %copy-done.5, bf16[512,256]{1,0:T(8,128)(2,1)} %copy-done.6, bf16[2048,256]{1,0:T(8,128)(2,1)} %scale0.1.refs_4_, bf16[2048,256]{1,0:T(8,128)(2,1)} %copy-done, ...), custom_call_target="tpu_custom_call" | custom-call | tf_op jit(solution)/shard_map/partial3/pallas_call | solution.py:101
  98.1 1.7 %collective-permute-start.10 = (bf16[512,512]{1,0:T(8,128)(2,1)}, bf16[512,512]{1,0:T(8,128)(2,1)S(1)}, u32[]{:S(2)}, u32[]{:S(2)}) collective-permute-start(bf16[512,512]{1,0:T(8,128)(2,1)} %partial3.1), channel_id=1, source_target_pairs={{0,96},{1,13},{4,100},{5,1},{8,104},{9,5},{12,108},{13,9},{32,0},{... | collective-permute-start | bytes 1572872 | tf_op jit(solution)/shard_map/ppermute | solution.py:34
  99.8 1.4 maximum_select_fusion.1
  101.2 2.7 %collective-permute-start.17 = (bf16[256,1024]{1,0:T(8,128)(2,1)S(1)}, bf16[256,1024]{1,0:T(8,128)(2,1)S(1)}, u32[]{:S(2)}, u32[]{:S(2)}) collective-permute-start(bf16[256,1024]{1,0:T(8,128)(2,1)S(1)} %maximum_select_fusion.1), channel_id=1, source_target_pairs={{0,2},{2,0},{1,3},{3,1},{4,6},{6,4},{5,7},{7,5},{8,10},{10,8},{9,1... | collective-permute-start | bytes 1572872 | tf_op jit(solution)/shard_map/ppermute | solution.py:38
  103.9 3.9 %partial0.1.a = f32[512,512]{1,0:T(8,128)} custom-call(s32[5]{0:T(128)} %stack.51.m, bf16[512,256]{1,0:T(8,128)(2,1)} %copy-done.3, bf16[512,256]{1,0:T(8,128)(2,1)} %copy-done.4, bf16[512,256]{1,0:T(8,128)(2,1)} %copy-done.5, bf16[512,256]{1,0:T(8,128)(2,1)} %copy-done.6, bf16[2048,256]{1,0:T(8,128)(2,1)} %scale0.1.refs_4_, bf16[2048,256]{1,0:T(8,128)(2,1)} %copy-done, ...), custom_call_target="tpu_custom_call" | custom-call | tf_op jit(solution)/shard_map/partial0/pallas_call | solution.py:101
  107.8 0.8 copy-done.13
  108.8 0.8 copy-done.15
  109.6 2.7 %summed.1 = bf16[8,128,256]{2,1,0:T(8,128)(2,1)} custom-call(f32[512,512]{1,0:T(8,128)} %partial0.1.a, bf16[512,512]{1,0:T(8,128)(2,1)} %copy-done.13, bf16[512,512]{1,0:T(8,128)(2,1)} %copy-done.14, bf16[512,512]{1,0:T(8,128)(2,1)} %copy-done.15), custom_call_target="tpu_custom_call" | custom-call | tf_op jit(solution)/shard_map/summed/pallas_call | solution.py:124
  112.3 6.7 %all-to-all-start = ((bf16[8,128,256]{2,1,0:T(8,128)(2,1)}), bf16[8,128,256]{2,1,0:T(8,128)(2,1)S(1)}, u32[]{:S(2)}, u32[]{:S(2)}) async-start(bf16[8,128,256]{2,1,0:T(8,128)(2,1)} %summed.1), calls=%async_computation | async-start | bytes 1048576 | tf_op jit(solution)/shard_map/all_to_all | solution.py:216
  118.9 1.5 %maximum_select_fusion.refs_5_ = bf16[512,1024]{1,0:T(8,128)(2,1)} fusion(bf16[256,1024]{1,0:T(8,128)(2,1)S(1)} %collective-permute-done.17, bf16[256,1024]{1,0:T(8,128)(2,1)S(1)} %maximum_select_fusion.1, pred[]{:T(512)S(6)} %eq.5), kind=kLoop, calls=%fused_computation.2 | loop fusion | flops 4718592 | bytes 2097153 | tf_op jit(solution)/shard_map/jit(_where)/select_n | solution.py:190
  120.4 7.3 %all-to-all-done.r_ref = bf16[8,128,256]{2,1,0:T(8,128)(2,1)S(1)} async-done(((bf16[8,128,256]{2,1,0:T(8,128)(2,1)}), bf16[8,128,256]{2,1,0:T(8,128)(2,1)S(1)}, u32[]{:S(2)}, u32[]{:S(2)}) %all-to-all-start) | async-done | bytes 524320 | tf_op jit(solution)/shard_map/all_to_all | solution.py:216
  127.7 0.8 copy-done.9
  128.5 2.3 %finish.1 = bf16[128,4,256]{2,1,0:T(4,128)(2,1)} custom-call(bf16[8,128,256]{2,1,0:T(8,128)(2,1)} %copy-done.9), custom_call_target="tpu_custom_call" | custom-call | tf_op jit(solution)/shard_map/finish/pallas_call | solution.py:137
  130.8 11.8 %outer.1 = bf16[2048,4,256]{2,1,0:T(4,128)(2,1)} custom-call(s32[5]{0:T(128)} %stack.51.m, bf16[512,256]{1,0:T(8,128)(2,1)} %copy-done.8, bf16[512,256]{1,0:T(8,128)(2,1)} %copy-done.10, bf16[512,256]{1,0:T(8,128)(2,1)} %copy-done.11, bf16[512,256]{1,0:T(8,128)(2,1)} %copy-done.12, bf16[4,512,256]{2,1,0:T(8,128)(2,1)} %collective-permute-done.15.refs_4_, ...), custom_call_target="tpu_custom_call" | custom-call | tf_op jit(solution)/shard_map/outer/pallas_call | solution.py:172
  (44 shorter events, 2.3 us)
Async XLA Ops:
  0.6 2.6 %collective-permute-start = (bf16[128,256]{1,0:T(8,128)(2,1)}, bf16[128,256]{1,0:T(8,128)(2,1)S(1)}, u32[]{:S(2)}, u32[]{:S(2)}) collective-permute-start(bf16[128,256]{1,0:T(8,128)(2,1)} %param.5), channel_id=1, source_target_pairs={{0,1},{1,0},{2,3},{3,2},{4,5},{5,4},{6,7},{7,6},{8,9},{9,8},{10,11... | collective-permute-start | bytes 196616 | tf_op jit(solution)/shard_map/ppermute | solution.py:38
  4.2 6.4 %collective-permute-start.1 = (bf16[256,256]{1,0:T(8,128)(2,1)S(1)}, bf16[256,256]{1,0:T(8,128)(2,1)S(1)}, u32[]{:S(2)}, u32[]{:S(2)}) collective-permute-start(bf16[256,256]{1,0:T(8,128)(2,1)S(1)} %maximum_select_fusion.4), channel_id=1, source_target_pairs={{0,2},{2,0},{1,3},{3,1},{4,6},{6,4},{5,7},{7,5},{8,10},{10,8},{9,1... | collective-permute-start | bytes 393224 | tf_op jit(solution)/shard_map/ppermute | solution.py:38
  10.7 22.1 %copy-start.3 = (bf16[512,256]{1,0:T(8,128)(2,1)}, bf16[512,256]{1,0:T(8,128)(2,1)S(1)}, u32[]{:S(2)}) copy-start(bf16[512,256]{1,0:T(8,128)(2,1)S(1)} %maximum_select_fusion.2.refs_0_) | copy-start | bytes 786436
  10.7 7.9 %collective-permute-start.2 = (bf16[512,256]{1,0:T(8,128)(2,1)S(1)}, bf16[512,256]{1,0:T(8,128)(2,1)S(1)}, u32[]{:S(2)}, u32[]{:S(2)}) collective-permute-start(bf16[512,256]{1,0:T(8,128)(2,1)S(1)} %maximum_select_fusion.2.refs_0_), channel_id=1, source_target_pairs={{0,4},{1,33},{4,8},{5,37},{8,12},{9,41},{12,0},{13,45},{32,36},{33... | collective-permute-start | bytes 786440 | tf_op jit(solution)/shard_map/ppermute | solution.py:34
  12.4 10.2 %collective-permute-start.3 = (bf16[512,256]{1,0:T(8,128)(2,1)S(1)}, bf16[512,256]{1,0:T(8,128)(2,1)S(1)}, u32[]{:S(2)}, u32[]{:S(2)}) collective-permute-start(bf16[512,256]{1,0:T(8,128)(2,1)S(1)} %maximum_select_fusion.2.refs_0_), channel_id=1, source_target_pairs={{0,8},{1,65},{4,12},{5,69},{8,0},{9,73},{12,4},{13,77},{32,40},{33... | collective-permute-start | bytes 786440 | tf_op jit(solution)/shard_map/ppermute | solution.py:34
  15.7 6.9 %collective-permute-start.4 = (bf16[512,256]{1,0:T(8,128)(2,1)S(1)}, bf16[512,256]{1,0:T(8,128)(2,1)S(1)}, u32[]{:S(2)}, u32[]{:S(2)}) collective-permute-start(bf16[512,256]{1,0:T(8,128)(2,1)S(1)} %maximum_select_fusion.2.refs_0_), channel_id=1, source_target_pairs={{0,12},{1,97},{4,0},{5,101},{8,4},{9,105},{12,8},{13,109},{32,44},... | collective-permute-start | bytes 786440 | tf_op jit(solution)/shard_map/ppermute | solution.py:34
  18.6 9.8 %copy-start.4 = (bf16[512,256]{1,0:T(8,128)(2,1)}, bf16[512,256]{1,0:T(8,128)(2,1)S(1)}, u32[]{:S(2)}) copy-start(bf16[512,256]{1,0:T(8,128)(2,1)S(1)} %collective-permute-done.2.refs_1_) | copy-start | bytes 786436
  22.6 5.8 %copy-start.5 = (bf16[512,256]{1,0:T(8,128)(2,1)}, bf16[512,256]{1,0:T(8,128)(2,1)S(1)}, u32[]{:S(2)}) copy-start(bf16[512,256]{1,0:T(8,128)(2,1)S(1)} %collective-permute-done.3.refs_2_) | copy-start | bytes 786436
  22.6 5.8 %copy-start.6 = (bf16[512,256]{1,0:T(8,128)(2,1)}, bf16[512,256]{1,0:T(8,128)(2,1)S(1)}, u32[]{:S(2)}) copy-start(bf16[512,256]{1,0:T(8,128)(2,1)S(1)} %collective-permute-done.4.refs_3_) | copy-start | bytes 786436
  22.7 1.0 copy-start.7
  24.4 22.9 %collective-permute-start.11 = (bf16[512,256]{1,0:T(8,128)(2,1)}, bf16[512,256]{1,0:T(8,128)(2,1)}, u32[]{:S(2)}, u32[]{:S(2)}) collective-permute-start(bf16[512,256]{1,0:T(8,128)(2,1)} %dynamic-slice_bitcast_fusion), channel_id=1, source_target_pairs={{1,0},{3,2},{5,4},{7,6},{9,8},{11,10},{13,12},{15,14},{17,16},{19,... | collective-permute-start | bytes 786440 | tf_op jit(solution)/shard_map/ppermute | solution.py:226
  32.8 49.2 %collective-permute-start.5 = (bf16[2048,256]{1,0:T(8,128)(2,1)}, bf16[2048,256]{1,0:T(8,128)(2,1)S(1)}, u32[]{:S(2)}, u32[]{:S(2)}) collective-permute-start(bf16[2048,256]{1,0:T(8,128)(2,1)} %scale1.1), channel_id=1, source_target_pairs={{0,4},{1,33},{4,8},{5,37},{8,12},{9,41},{12,0},{13,45},{32,36},{33... | collective-permute-start | bytes 3145736 | tf_op jit(solution)/shard_map/ppermute | solution.py:34
  38.9 43.1 %collective-permute-start.6 = (bf16[2048,256]{1,0:T(8,128)(2,1)}, bf16[2048,256]{1,0:T(8,128)(2,1)S(1)}, u32[]{:S(2)}, u32[]{:S(2)}) collective-permute-start(bf16[2048,256]{1,0:T(8,128)(2,1)} %scale2.1), channel_id=1, source_target_pairs={{0,8},{1,65},{4,12},{5,69},{8,0},{9,73},{12,4},{13,77},{32,40},{33... | collective-permute-start | bytes 3145736 | tf_op jit(solution)/shard_map/ppermute | solution.py:34
  46.6 35.4 %collective-permute-start.7 = (bf16[2048,256]{1,0:T(8,128)(2,1)}, bf16[2048,256]{1,0:T(8,128)(2,1)S(1)}, u32[]{:S(2)}, u32[]{:S(2)}) collective-permute-start(bf16[2048,256]{1,0:T(8,128)(2,1)} %scale3.1), channel_id=1, source_target_pairs={{0,12},{1,97},{4,0},{5,101},{8,4},{9,105},{12,8},{13,109},{32,44},... | collective-permute-start | bytes 3145736 | tf_op jit(solution)/shard_map/ppermute | solution.py:34
  48.3 33.7 %copy-start.8 = (bf16[512,256]{1,0:T(8,128)(2,1)}, bf16[512,256]{1,0:T(8,128)(2,1)S(1)}, u32[]{:S(2)}) copy-start(bf16[512,256]{1,0:T(8,128)(2,1)S(1)} %bitcast_select_fusion.refs_0_) | copy-start | bytes 786436
  48.3 19.3 %collective-permute-start.12 = (bf16[512,256]{1,0:T(8,128)(2,1)S(1)}, bf16[512,256]{1,0:T(8,128)(2,1)S(1)}, u32[]{:S(2)}, u32[]{:S(2)}) collective-permute-start(bf16[512,256]{1,0:T(8,128)(2,1)S(1)} %bitcast_select_fusion.refs_0_), channel_id=1, source_target_pairs={{0,4},{4,8},{8,12},{12,0},{1,5},{5,9},{9,13},{13,1},{2,6},{6,10},{... | collective-permute-start | bytes 786440 | tf_op jit(solution)/shard_map/ppermute | solution.py:229
  50.0 19.4 %collective-permute-start.13 = (bf16[512,256]{1,0:T(8,128)(2,1)S(1)}, bf16[512,256]{1,0:T(8,128)(2,1)S(1)}, u32[]{:S(2)}, u32[]{:S(2)}) collective-permute-start(bf16[512,256]{1,0:T(8,128)(2,1)S(1)} %bitcast_select_fusion.refs_0_), channel_id=1, source_target_pairs={{0,8},{4,12},{8,0},{12,4},{1,9},{5,13},{9,1},{13,5},{2,10},{6,14},... | collective-permute-start | bytes 786440 | tf_op jit(solution)/shard_map/ppermute | solution.py:229
  67.6 7.5 %copy-start.10 = (bf16[512,256]{1,0:T(8,128)(2,1)}, bf16[512,256]{1,0:T(8,128)(2,1)S(1)}, u32[]{:S(2)}) copy-start(bf16[512,256]{1,0:T(8,128)(2,1)S(1)} %collective-permute-done.12.refs_1_) | copy-start | bytes 786436
  67.6 7.5 %collective-permute-start.14 = (bf16[512,256]{1,0:T(8,128)(2,1)S(1)}, bf16[512,256]{1,0:T(8,128)(2,1)S(1)}, u32[]{:S(2)}, u32[]{:S(2)}) collective-permute-start(bf16[512,256]{1,0:T(8,128)(2,1)S(1)} %bitcast_select_fusion.refs_0_), channel_id=1, source_target_pairs={{0,12},{4,0},{8,4},{12,8},{1,13},{5,1},{9,5},{13,9},{2,14},{6,2},{... | collective-permute-start | bytes 786440 | tf_op jit(solution)/shard_map/ppermute | solution.py:229
  69.4 6.8 %copy-start.11 = (bf16[512,256]{1,0:T(8,128)(2,1)}, bf16[512,256]{1,0:T(8,128)(2,1)S(1)}, u32[]{:S(2)}) copy-start(bf16[512,256]{1,0:T(8,128)(2,1)S(1)} %collective-permute-done.13.refs_2_) | copy-start | bytes 786436
  69.4 30.4 %collective-permute-start.16 = (bf16[128,1024]{1,0:T(8,128)(2,1)}, bf16[128,1024]{1,0:T(8,128)(2,1)}, u32[]{:S(2)}, u32[]{:S(2)}) collective-permute-start(bf16[128,1024]{1,0:T(8,128)(2,1)} %bitcast.19), channel_id=1, source_target_pairs={{0,1},{1,0},{2,3},{3,2},{4,5},{5,4},{6,7},{7,6},{8,9},{9,8},{10,11... | collective-permute-start | bytes 786440 | tf_op jit(solution)/shard_map/ppermute | solution.py:38
  75.1 1.1 copy-start.12
  76.2 54.6 %collective-permute-start.15 = (bf16[4,512,256]{2,1,0:T(8,128)(2,1)}, bf16[4,512,256]{2,1,0:T(8,128)(2,1)}, u32[]{:S(2)}, u32[]{:S(2)}) collective-permute-start(bf16[4,512,256]{2,1,0:T(8,128)(2,1)} %pad_maximum_fusion.1), channel_id=1, source_target_pairs={{0,16},{16,0},{1,17},{17,1},{2,18},{18,2},{3,19},{19,3},{4,20},{20... | collective-permute-start | bytes 3145736 | tf_op jit(solution)/shard_map/ppermute | solution.py:38
  82.0 1.0 copy-start
  82.0 1.3 copy-start.1
  83.3 1.0 copy-start.2
  88.0 19.8 %collective-permute-start.8 = (bf16[512,512]{1,0:T(8,128)(2,1)}, bf16[512,512]{1,0:T(8,128)(2,1)S(1)}, u32[]{:S(2)}, u32[]{:S(2)}) collective-permute-start(bf16[512,512]{1,0:T(8,128)(2,1)} %partial1.1), channel_id=1, source_target_pairs={{0,32},{1,5},{4,36},{5,9},{8,40},{9,13},{12,44},{13,1},{32,64},{33... | collective-permute-start | bytes 1572872 | tf_op jit(solution)/shard_map/ppermute | solution.py:34
  93.7 14.1 %collective-permute-start.9 = (bf16[512,512]{1,0:T(8,128)(2,1)}, bf16[512,512]{1,0:T(8,128)(2,1)S(1)}, u32[]{:S(2)}, u32[]{:S(2)}) collective-permute-start(bf16[512,512]{1,0:T(8,128)(2,1)} %partial2.1), channel_id=1, source_target_pairs={{0,64},{1,9},{4,68},{5,13},{8,72},{9,1},{12,76},{13,5},{32,96},{33... | collective-permute-start | bytes 1572872 | tf_op jit(solution)/shard_map/ppermute | solution.py:34
  98.1 9.7 %collective-permute-start.10 = (bf16[512,512]{1,0:T(8,128)(2,1)}, bf16[512,512]{1,0:T(8,128)(2,1)S(1)}, u32[]{:S(2)}, u32[]{:S(2)}) collective-permute-start(bf16[512,512]{1,0:T(8,128)(2,1)} %partial3.1), channel_id=1, source_target_pairs={{0,96},{1,13},{4,100},{5,1},{8,104},{9,5},{12,108},{13,9},{32,0},{... | collective-permute-start | bytes 1572872 | tf_op jit(solution)/shard_map/ppermute | solution.py:34
  101.2 17.7 %collective-permute-start.17 = (bf16[256,1024]{1,0:T(8,128)(2,1)S(1)}, bf16[256,1024]{1,0:T(8,128)(2,1)S(1)}, u32[]{:S(2)}, u32[]{:S(2)}) collective-permute-start(bf16[256,1024]{1,0:T(8,128)(2,1)S(1)} %maximum_select_fusion.1), channel_id=1, source_target_pairs={{0,2},{2,0},{1,3},{3,1},{4,6},{6,4},{5,7},{7,5},{8,10},{10,8},{9,1... | collective-permute-start | bytes 1572872 | tf_op jit(solution)/shard_map/ppermute | solution.py:38
  107.8 0.8 copy-start.13
  107.8 1.0 copy-start.14
  108.8 0.8 copy-start.15
  112.3 15.4 %all-to-all-start = ((bf16[8,128,256]{2,1,0:T(8,128)(2,1)}), bf16[8,128,256]{2,1,0:T(8,128)(2,1)S(1)}, u32[]{:S(2)}, u32[]{:S(2)}) async-start(bf16[8,128,256]{2,1,0:T(8,128)(2,1)} %summed.1), calls=%async_computation | async-start | bytes 1048576 | tf_op jit(solution)/shard_map/all_to_all | solution.py:216
  127.7 0.8 copy-start.9

commit v2 on v0

v2 whole, which is shorter than its diff:
```python
import functools

import jax
import jax.numpy as jnp
from jax import lax
from jax.experimental import pallas as pl
from jax.experimental.pallas import tpu as pltpu
from jax.sharding import Mesh, PartitionSpec as P

BF = jnp.bfloat16
F32 = jnp.float32
VM = pltpu.VMEM


def first_axis_steps(k):
    pairs = []
    for z in range(4):
        for x in range(4):
            pairs.append(((z * 4 + x) * 2, (z * 4 + (x + k) % 4) * 2))
            pairs.append(((z * 4 + x) * 2 + 1, (((z + k) % 4) * 4 + x) * 2 + 1))
    return pairs


def second_axis_steps(k):
    pairs = []
    for z in range(4):
        for x in range(4):
            pairs.append(((z * 4 + x) * 2, (((z + k) % 4) * 4 + x) * 2))
            pairs.append(((z * 4 + x) * 2 + 1, (z * 4 + (x + k) % 4) * 2 + 1))
    return pairs


def shift(value, pairs):
    return lax.ppermute(value, ("z", "x", "c"), pairs)


def swap(value, axis):
    return lax.ppermute(value, axis, [(0, 1), (1, 0)])


LIMIT = pltpu.CompilerParams(vmem_limit_bytes=12 << 20)
IN = pl.BlockSpec(memory_space=VM)
HBM = pl.BlockSpec(memory_space=pltpu.HBM)


def kept(*values):
    return [pltpu.with_memory_space_constraint(v, VM) for v in values]


def roles():
    c, x, z = lax.axis_index("c"), lax.axis_index("x"), lax.axis_index("z")
    return c, jnp.where(c == 0, x, z), jnp.where(c == 0, z, x)


ORDER = (2, 1, 3, 0)


def scale_body(w_ref, s_ref, *refs):
    outs, wide_ref, sems = refs[:4], refs[4], refs[5]
    c, first, _ = roles()
    copies = []
    for k in ORDER:
        p = (first + k) & 3
        for i in range(4):
            z, x = c * p + (1 - c) * i, c * i + (1 - c) * p
            copy = pltpu.make_async_copy(w_ref.at[z, :, x], outs[k].at[i], sems.at[k * 4 + i])
            copy.start()
            copies.append((copy, outs[k].at[i], z, x))
    row = lax.broadcasted_iota(jnp.int32, (16, 256), 0)
    col = lax.broadcasted_iota(jnp.int32, (16, 256), 1)
    spread = jnp.where(col // 16 == row, 1.0, 0.0).astype(BF)
    wide_ref[...] = lax.dot_general(
        s_ref[...], spread, (((0,), (0,)), ((), ())), preferred_element_type=F32
    )
    for copy, o_ref, z, x in copies:
        copy.wait()
        for yl in range(2):
            r = pl.multiple_of((z * 8 + yl * 4 + x) * 16, 16)
            s = wide_ref[pl.ds(r, 16), :]
            w = o_ref[yl].astype(F32).reshape(16, 16, 256)
            o_ref[yl] = (w * s[:, None, :]).reshape(256, 256).astype(BF)


def scaled_rows(w5, scales_t):
    outs = pl.pallas_call(
        scale_body,
        out_shape=[VM((4, 2, 256, 256), BF)] * 4,
        in_specs=[HBM, IN],
        out_specs=[IN] * 4,
        scratch_shapes=[VM((512, 256), F32), pltpu.SemaphoreType.DMA((16,))],
        compiler_params=LIMIT,
        name="scale",
    )(w5, scales_t)
    return [o.reshape(2048, 256) for o in outs]


def partial_body(*refs):
    g, w, outs = refs[:4], refs[4:8], refs[8:12]
    _, _, second = roles()
    for k in ORDER:
        r = pl.multiple_of(((second + k) & 3) * 512, 512)
        total = None
        for a, b in zip(g, w):
            part = lax.dot_general(
                a[...], b[pl.ds(r, 512), :], (((1,), (1,)), ((), ())), preferred_element_type=F32
            )
            total = part if total is None else total + part
        outs[k][...] = total.astype(outs[k].dtype)


def partial_sums(grads, weights):
    return pl.pallas_call(
        partial_body,
        out_shape=[VM((512, 512), F32)] + [VM((512, 512), BF)] * 3,
        in_specs=[IN] * 8,
        out_specs=[IN] * 4,
        compiler_params=LIMIT,
        name="partial",
    )(*kept(*grads, *weights))


def gather_body(a, b, c, d, o_ref):
    total = a[...] + b[...].astype(F32) + c[...].astype(F32) + d[...].astype(F32)
    total = total.astype(BF)
    for yl in range(2):
        for n in range(4):
            t = ((n & 1) * 2 + (n >> 1)) * 128
            o_ref[yl * 4 + n] = total[t : t + 128, yl * 256 : (yl + 1) * 256]


def summed_blocks(parts):
    return pl.pallas_call(
        gather_body,
        out_shape=VM((8, 128, 256), BF),
        in_specs=[IN] * 4,
        out_specs=IN,
        compiler_params=LIMIT,
        name="summed",
    )(*kept(*parts))


def finish_body(r_ref, o_ref):
    r = [(r_ref[n].astype(F32) + r_ref[4 + n].astype(F32)).astype(BF) for n in range(4)]
    o_ref[...] = jnp.concatenate(r, axis=1).reshape(128, 4, 256)


def finished(blocks):
    return pl.pallas_call(
        finish_body,
        out_shape=jax.ShapeDtypeStruct((128, 4, 256), BF),
        in_specs=[IN],
        out_specs=IN,
        compiler_params=LIMIT,
        name="finish",
    )(*kept(blocks))


def outer_body(*refs):
    g, h_ref, o_ref, buf, sems = refs[:8], refs[8], refs[9], refs[10], refs[11]
    yl, x = lax.axis_index("yl"), lax.axis_index("x")
    copies = []
    for i in range(8):
        here = yl if i < 4 else 1 - yl
        r = pl.multiple_of((here * 4 + ((x - i) & 3)) * 256, 256)
        p = lax.dot_general(
            g[i][...], h_ref[...], (((0,), (0,)), ((), ())), preferred_element_type=F32
        )
        buf[i] = p.astype(BF).reshape(256, 4, 256)
        copy = pltpu.make_async_copy(buf.at[i], o_ref.at[pl.ds(r, 256)], sems.at[i])
        copy.start()
        copies.append(copy)
    for copy in copies:
        copy.wait()


def outer_product(blocks, hidden):
    return pl.pallas_call(
        outer_body,
        out_shape=jax.ShapeDtypeStruct((2048, 4, 256), BF),
        in_specs=[IN] * 9,
        out_specs=HBM,
        scratch_shapes=[VM((8, 256, 4, 256), BF), pltpu.SemaphoreType.DMA((8,))],
        compiler_params=LIMIT,
        name="outer",
    )(*kept(*blocks, hidden))


def joined(a, b, first):
    return jnp.where(first, jnp.concatenate([a, b], 0), jnp.concatenate([b, a], 0))


def per_device(hidden, grad_out, weight_base, block_scale):
    z, x = lax.axis_index("z"), lax.axis_index("x")
    yh, c = lax.axis_index("yh"), lax.axis_index("c")

    w5 = weight_base.reshape(4, 2, 4, 256, 256)
    sent = scaled_rows(w5, block_scale.T)
    rows = [sent[0]] + [None] * 3
    for k in (2, 1, 3):
        rows[k] = shift(sent[k], first_axis_steps(k))

    g2 = joined(grad_out, swap(grad_out, "yh"), yh == 0)
    g4 = joined(g2, swap(g2, "c"), c == 0)
    grads = [g4] + [shift(g4, first_axis_steps(k)) for k in (1, 2, 3)]

    sums = partial_sums(grads, rows)
    parts = [sums[0]] + [None] * 3
    for k in (2, 1, 3):
        parts[k] = shift(sums[k], second_axis_steps(k))
    blocks = summed_blocks(parts)
    blocks = lax.all_to_all(blocks, ("yl", "yh", "c"), 0, 0, tiled=True)
    grad_hidden = finished(blocks)

    h = hidden.reshape(128, 1024)
    h2 = joined(h, swap(h, "yh"), yh == 0)
    h4 = joined(h2, swap(h2, "c"), c == 0)

    def of_plane(p):
        k = (z - p) & 3
        return jnp.where(k < 2, jnp.where(k == 0, grads[0], grads[1]), jnp.where(k == 2, grads[2], grads[3]))

    got = lax.ppermute(of_plane(yh * 2), "c", [(1, 0)])
    seed = jnp.where(c == 0, got, of_plane(yh * 2 + 1))
    ring = lambda k: [(i, (i + k) % 4) for i in range(4)]
    mine = [seed] + [lax.ppermute(seed, "x", ring(k)) for k in (1, 2, 3)]
    theirs = [swap(m, "yl") for m in mine]
    grad_weight = outer_product(mine + theirs, h4)
    return grad_hidden, grad_weight


def solution(mesh):
    fine = Mesh(mesh.devices.reshape(4, 2, 4, 2, 2), ("z", "yl", "x", "yh", "c"))
    narrow, wide = ("yh", "c"), ("z", "yl", "x")
    return jax.shard_map(
        per_device,
        mesh=fine,
        in_specs=(
            P(narrow, None, wide),
            P(narrow, wide),
            P(narrow, wide),
            P(narrow, wide),
        ),
        out_specs=(P(narrow, None, wide), P(narrow, None, wide)),
        check_vma=False,
    )
```

time: 284 us -> 122 us (0.43)
  blocking collectives: 84.9 us -> 0 us
  local copies, waits for them, and re-layouts: 71.2 us -> 4.64 us
  matrix products: 25 us -> 0 us
  Pallas kernels: 0 us -> 16.1 us
  between operations: 14.2 us -> 0.71 us
  starting transfers between devices: 27.1 us -> 36 us
  other arithmetic: 0 us -> 5.23 us
  waiting for transfers between devices: 60.2 us -> 56.7 us
    all_to_all x3 -> x1, waiting for transfers between devices: 60.1 us -> 0.01 us  [per_device(): blocks = lax.all_to_all(blocks, ('yl', 'yh', 'c'), 0, 0, tiled=True)]
    ppermute x0 -> x21, waiting for transfers between devices: none -> 56.7 us  [the longest x9 30.3 us: shift(): return lax.ppermute(value, ('z', 'x', 'c'), pairs)]
    all_gather x1 -> x0, blocking collectives: 51.1 us -> none  [per_device(): lax.all_gather(row_scales, 'narrow', axis=0, tiled=True)]
    mul x2 -> x0, local copies, waits for them, and re-layouts: 44.7 us -> none  [apply_scales(): blocked = blocked * widened[:, None, :]]
    all_to_all x1 -> x0, blocking collectives: 33.7 us -> none  [from_everyone(): lax.all_to_all(jnp.broadcast_to(shard[None], (length, *shard.shape)), axi...]
    ppermute x0 -> x21, starting transfers between devices: none -> 31.2 us  [the longest x9 16.1 us: shift(): return lax.ppermute(value, ('z', 'x', 'c'), pairs)]
    dot_general x2 -> x0, matrix products: 25 us -> none  [the longest x1 19.3 us: per_device(): lax.dot_general(incoming, effective, contract_last, preferred_element_typ...]
    all_to_all x3 -> x1, starting transfers between devices: 27 us -> 4.78 us  [per_device(): blocks = lax.all_to_all(blocks, ('yl', 'yh', 'c'), 0, 0, tiled=True)]
  transfers between devices with their start and end apart: 5 -> 22, of which waited for: 2 -> 11; matrix products, arithmetic and copies ran while one was open for 27% -> 5% of each run, Pallas kernels for 0% -> 13%
where the time goes in v2:
time: 122 us; the launch traced here: 119 us
  waiting for transfers between devices  56.7 us (46%)
  starting transfers between devices  36 us (30%)
  Pallas kernels  16.1 us (13%)
  other arithmetic  5.23 us (4%)
  local copies, waits for them, and re-layouts  4.64 us (4%)
    ppermute x9, waiting for transfers between devices, shift(): return lax.ppermute(value, ('z', 'x', 'c'), pairs)  30.3 us
    ppermute x8, waiting for transfers between devices, swap(): return lax.ppermute(value, axis, [(0, 1), (1, 0)])  26 us
    ppermute x9, starting transfers between devices, shift(): return lax.ppermute(value, ('z', 'x', 'c'), pairs)  16.1 us
    ppermute x8, starting transfers between devices, swap(): return lax.ppermute(value, axis, [(0, 1), (1, 0)])  9.37 us
    pallas_call x1, Pallas kernels, outer_product(): pl.pallas_call(outer_body, out_shape=jax.ShapeDtypeStruct((2048, 4, 256),...  5.36 us
    all_to_all x1, starting transfers between devices, per_device(): blocks = lax.all_to_all(blocks, ('yl', 'yh', 'c'), 0, 0, tiled=True)  4.78 us
    unnamed x13, local copies, waits for them, and re-layouts  4.64 us
    pallas_call x1, Pallas kernels, partial_sums(): pl.pallas_call(partial_body, out_shape=[VM((512, 512), F32)] + [VM((512,...  4.42 us
  transfers between devices with their start and end apart: 22, of which 11 were waited for; matrix products, arithmetic and copies ran while one was open for 5% of the time, Pallas kernels for 13%

profile of v2, /device:TPU:1, one launch (start us, length us, event | category | flops | bytes accessed | tf_op | source)
XLA Modules:
  0.0 119.3 jit_solution(6506244765562537893)
XLA Ops:
  0.6 3.8 %collective-permute-start = (bf16[128,256]{1,0:T(8,128)(2,1)}, bf16[128,256]{1,0:T(8,128)(2,1)S(1)}, u32[]{:S(2)}, u32[]{:S(2)}) collective-permute-start(bf16[128,256]{1,0:T(8,128)(2,1)} %param.5), channel_id=1, source_target_pairs={{0,2},{2,0},{1,3},{3,1},{4,6},{6,4},{5,7},{7,5},{8,10},{10,8},{9,1... | collective-permute-start | bytes 196616 | tf_op jit(solution)/shard_map/ppermute | solution.py:38
  4.5 2.2 %copy-done = bf16[8192,256]{1,0:T(8,128)(2,1)S(1)} copy-done((bf16[8192,256]{1,0:T(8,128)(2,1)S(1)}, bf16[8192,256]{1,0:T(8,128)(2,1)}, u32[]{:S(2)}) %copy-start) | copy-done | bytes 4194328
  6.6 0.7 copy-done.3
  7.4 3.4 %scale.1 = (bf16[4,2,256,256]{3,2,1,0:T(8,128)(2,1)S(1)}, bf16[4,2,256,256]{3,2,1,0:T(8,128)(2,1)}, bf16[4,2,256,256]{3,2,1,0:T(8,128)(2,1)}, bf16[4,2,256,256]{3,2,1,0:T(8,128)(2,1)}) custom-call(bf16[4,2,4,256,256]{4,3,2,1,0:T(8,128)(2,1)S(1)} %bitcast.8, bf16[16,512]{1,0:T(8,128)(2,1)S(1)} %bitcast.10), custom_call_target="tpu_custom_call" | custom-call | tf_op jit(solution)/shard_map/scale/pallas_call | solution.py:85
  10.7 1.7 %collective-permute-start.5 = (bf16[2048,256]{1,0:T(8,128)(2,1)}, bf16[2048,256]{1,0:T(8,128)(2,1)S(1)}, u32[]{:S(2)}, u32[]{:S(2)}) collective-permute-start(bf16[2048,256]{1,0:T(8,128)(2,1)} %bitcast.3), channel_id=1, source_target_pairs={{0,4},{1,33},{4,8},{5,37},{8,12},{9,41},{12,0},{13,45},{32,36},{33... | collective-permute-start | bytes 3145736 | tf_op jit(solution)/shard_map/ppermute | solution.py:34
  12.4 3.3 %collective-permute-start.6 = (bf16[2048,256]{1,0:T(8,128)(2,1)}, bf16[2048,256]{1,0:T(8,128)(2,1)}, u32[]{:S(2)}, u32[]{:S(2)}) collective-permute-start(bf16[2048,256]{1,0:T(8,128)(2,1)} %bitcast.4), channel_id=1, source_target_pairs={{0,8},{1,65},{4,12},{5,69},{8,0},{9,73},{12,4},{13,77},{32,40},{33... | collective-permute-start | bytes 3145736 | tf_op jit(solution)/shard_map/ppermute | solution.py:34
  15.7 0.7 collective-permute-start.7
  16.5 0.0 collective-permute-done
  16.5 1.0 collective-permute-start.1
  17.5 1.0 collective-permute-done.1
  18.5 0.1 maximum_select_fusion.2.refs_0_
  18.6 1.7 %collective-permute-start.2 = (bf16[512,256]{1,0:T(8,128)(2,1)S(1)}, bf16[512,256]{1,0:T(8,128)(2,1)S(1)}, u32[]{:S(2)}, u32[]{:S(2)}) collective-permute-start(bf16[512,256]{1,0:T(8,128)(2,1)S(1)} %maximum_select_fusion.2.refs_0_), channel_id=1, source_target_pairs={{0,4},{1,33},{4,8},{5,37},{8,12},{9,41},{12,0},{13,45},{32,36},{33... | collective-permute-start | bytes 786440 | tf_op jit(solution)/shard_map/ppermute | solution.py:34
  20.3 3.3 %collective-permute-start.3 = (bf16[512,256]{1,0:T(8,128)(2,1)S(1)}, bf16[512,256]{1,0:T(8,128)(2,1)S(1)}, u32[]{:S(2)}, u32[]{:S(2)}) collective-permute-start(bf16[512,256]{1,0:T(8,128)(2,1)S(1)} %maximum_select_fusion.2.refs_0_), channel_id=1, source_target_pairs={{0,8},{1,65},{4,12},{5,69},{8,0},{9,73},{12,4},{13,77},{32,40},{33... | collective-permute-start | bytes 786440 | tf_op jit(solution)/shard_map/ppermute | solution.py:34
  23.6 17.7 %collective-permute-done.2.refs_1_ = bf16[512,256]{1,0:T(8,128)(2,1)S(1)} collective-permute-done((bf16[512,256]{1,0:T(8,128)(2,1)S(1)}, bf16[512,256]{1,0:T(8,128)(2,1)S(1)}, u32[]{:S(2)}, u32[]{:S(2)}) %collective-permute-start.2) | collective-permute-done | bytes 262176 | tf_op jit(solution)/shard_map/ppermute | solution.py:34
  41.3 1.6 %collective-permute-start.4 = (bf16[512,256]{1,0:T(8,128)(2,1)S(1)}, bf16[512,256]{1,0:T(8,128)(2,1)S(1)}, u32[]{:S(2)}, u32[]{:S(2)}) collective-permute-start(bf16[512,256]{1,0:T(8,128)(2,1)S(1)} %maximum_select_fusion.2.refs_0_), channel_id=1, source_target_pairs={{0,12},{1,97},{4,0},{5,101},{8,4},{9,105},{12,8},{13,109},{32,44},... | collective-permute-start | bytes 786440 | tf_op jit(solution)/shard_map/ppermute | solution.py:34
  42.9 0.8 copy.6
  43.7 1.7 %collective-permute-done.3.refs_2_ = bf16[512,256]{1,0:T(8,128)(2,1)S(1)} collective-permute-done((bf16[512,256]{1,0:T(8,128)(2,1)S(1)}, bf16[512,256]{1,0:T(8,128)(2,1)S(1)}, u32[]{:S(2)}, u32[]{:S(2)}) %collective-permute-start.3) | collective-permute-done | bytes 262176 | tf_op jit(solution)/shard_map/ppermute | solution.py:34
  45.3 0.1 collective-permute-start.19
  45.4 1.6 %collective-permute-done.4.refs_3_ = bf16[512,256]{1,0:T(8,128)(2,1)S(1)} collective-permute-done((bf16[512,256]{1,0:T(8,128)(2,1)S(1)}, bf16[512,256]{1,0:T(8,128)(2,1)S(1)}, u32[]{:S(2)}, u32[]{:S(2)}) %collective-permute-start.4) | collective-permute-done | bytes 262176 | tf_op jit(solution)/shard_map/ppermute | solution.py:34
  46.9 0.8 select_select_fusion.1
  47.7 4.1 %collective-permute-start.11 = (bf16[512,256]{1,0:T(8,128)(2,1)}, bf16[512,256]{1,0:T(8,128)(2,1)}, u32[]{:S(2)}, u32[]{:S(2)}) collective-permute-start(bf16[512,256]{1,0:T(8,128)(2,1)} %select_select_fusion.1), channel_id=1, source_target_pairs={{1,0},{3,2},{5,4},{7,6},{9,8},{11,10},{13,12},{15,14},{17,16},{19,... | collective-permute-start | bytes 786440 | tf_op jit(solution)/shard_map/ppermute | solution.py:222
  51.8 4.4 %partial.1 = (f32[512,512]{1,0:T(8,128)S(1)}, bf16[512,512]{1,0:T(8,128)(2,1)}, bf16[512,512]{1,0:T(8,128)(2,1)}, bf16[512,512]{1,0:T(8,128)(2,1)}) custom-call(bf16[512,256]{1,0:T(8,128)(2,1)S(1)} %maximum_select_fusion.2.refs_0_, bf16[512,256]{1,0:T(8,128)(2,1)S(1)} %collective-permute-done.2.refs_1_, bf16[512,256]{1,0:T(8,128)(2,1)S(1)} %collective-permute-done.3.refs_2_, ...), custom_call_target="tpu_custom_call" | custom-call | tf_op jit(solution)/shard_map/partial/pallas_call | solution.py:112
  56.2 1.0 copy-done.1
  57.2 0.0 collective-permute-start.8
  57.2 3.7 %collective-permute-start.9 = (bf16[512,512]{1,0:T(8,128)(2,1)}, bf16[512,512]{1,0:T(8,128)(2,1)S(1)}, u32[]{:S(2)}, u32[]{:S(2)}) collective-permute-start(bf16[512,512]{1,0:T(8,128)(2,1)} %get-tuple-element.16), channel_id=1, source_target_pairs={{0,64},{1,9},{4,68},{5,13},{8,72},{9,1},{12,76},{13,5},{32,96},{33... | collective-permute-start | bytes 1572872 | tf_op jit(solution)/shard_map/ppermute | solution.py:34
  60.9 0.0 collective-permute-start.10
  60.9 0.0 collective-permute-done.19
  60.9 2.2 %maximum_select_fusion.1 = bf16[256,1024]{1,0:T(8,128)(2,1)} fusion(bf16[128,1024]{1,0:T(8,128)(2,1)} %collective-permute-done.19, bf16[128,1024]{1,0:T(8,128)(2,1)} %bitcast.7, pred[]{:T(512)S(6)} %eq.22), kind=kLoop, calls=%fused_computation.1 | loop fusion | flops 2359296 | bytes 1048577 | tf_op jit(solution)/shard_map/jit(_where)/select_n | solution.py:189
  63.1 1.5 %collective-permute-start.20 = (bf16[256,1024]{1,0:T(8,128)(2,1)}, bf16[256,1024]{1,0:T(8,128)(2,1)}, u32[]{:S(2)}, u32[]{:S(2)}) collective-permute-start(bf16[256,1024]{1,0:T(8,128)(2,1)} %maximum_select_fusion.1), channel_id=1, source_target_pairs={{0,1},{1,0},{2,3},{3,2},{4,5},{5,4},{6,7},{7,6},{8,9},{9,8},{10,11... | collective-permute-start | bytes 1572872 | tf_op jit(solution)/shard_map/ppermute | solution.py:38
  64.6 0.1 select_select_fusion.refs_0_
  64.7 0.1 collective-permute-start.12
  64.8 2.1 %collective-permute-done.8.b = bf16[512,512]{1,0:T(8,128)(2,1)S(1)} collective-permute-done((bf16[512,512]{1,0:T(8,128)(2,1)}, bf16[512,512]{1,0:T(8,128)(2,1)S(1)}, u32[]{:S(2)}, u32[]{:S(2)}) %collective-permute-start.8) | collective-permute-done | bytes 524320 | tf_op jit(solution)/shard_map/ppermute | solution.py:34
  66.9 1.6 %collective-permute-start.13 = (bf16[512,256]{1,0:T(8,128)(2,1)S(1)}, bf16[512,256]{1,0:T(8,128)(2,1)S(1)}, u32[]{:S(2)}, u32[]{:S(2)}) collective-permute-start(bf16[512,256]{1,0:T(8,128)(2,1)S(1)} %select_select_fusion.refs_0_), channel_id=1, source_target_pairs={{0,8},{4,12},{8,0},{12,4},{1,9},{5,13},{9,1},{13,5},{2,10},{6,14},... | collective-permute-start | bytes 786440 | tf_op jit(solution)/shard_map/ppermute | solution.py:225
  68.5 7.3 %collective-permute-done.9.c = bf16[512,512]{1,0:T(8,128)(2,1)S(1)} collective-permute-done((bf16[512,512]{1,0:T(8,128)(2,1)}, bf16[512,512]{1,0:T(8,128)(2,1)S(1)}, u32[]{:S(2)}, u32[]{:S(2)}) %collective-permute-start.9) | collective-permute-done | bytes 524320 | tf_op jit(solution)/shard_map/ppermute | solution.py:34
  75.8 2.1 %summed.1 = bf16[8,128,256]{2,1,0:T(8,128)(2,1)} custom-call(f32[512,512]{1,0:T(8,128)S(1)} %copy-done.2, bf16[512,512]{1,0:T(8,128)(2,1)S(1)} %collective-permute-done.8.b, bf16[512,512]{1,0:T(8,128)(2,1)S(1)} %collective-permute-done.9.c, bf16[512,512]{1,0:T(8,128)(2,1)} %collective-permute-done.10.d), custom_call_target="tpu_custom_call" | custom-call | tf_op jit(solution)/shard_map/summed/pallas_call | solution.py:132
  77.8 4.8 %all-to-all-start = ((bf16[8,128,256]{2,1,0:T(8,128)(2,1)}), bf16[8,128,256]{2,1,0:T(8,128)(2,1)S(1)}, u32[]{:S(2)}, u32[]{:S(2)}) async-start(bf16[8,128,256]{2,1,0:T(8,128)(2,1)} %summed.1), calls=%async_computation | async-start | bytes 1048576 | tf_op jit(solution)/shard_map/all_to_all | solution.py:211
  82.6 1.4 %collective-permute-start.15 = (bf16[512,256]{1,0:T(8,128)(2,1)S(1)}, bf16[512,256]{1,0:T(8,128)(2,1)S(1)}, u32[]{:S(2)}, u32[]{:S(2)}) collective-permute-start(bf16[512,256]{1,0:T(8,128)(2,1)S(1)} %select_select_fusion.refs_0_), channel_id=1, source_target_pairs={{0,16},{16,0},{1,17},{17,1},{2,18},{18,2},{3,19},{19,3},{4,20},{20... | collective-permute-start | bytes 786440 | tf_op jit(solution)/shard_map/ppermute | solution.py:38
  84.0 0.1 collective-permute-start.16
  84.1 0.5 collective-permute-done.13.refs_2_
  84.5 0.9 collective-permute-start.17
  85.5 0.6 collective-permute-start.18
  86.0 2.0 %maximum_select_fusion.refs_8_ = bf16[512,1024]{1,0:T(8,128)(2,1)S(1)} fusion(bf16[256,1024]{1,0:T(8,128)(2,1)} %collective-permute-done.20, bf16[256,1024]{1,0:T(8,128)(2,1)} %maximum_select_fusion.1, pred[]{:T(512)S(6)} %eq.21), kind=kLoop, calls=%fused_computation | loop fusion | flops 4718592 | bytes 2097153 | tf_op jit(solution)/shard_map/jit(_where)/select_n | solution.py:189
  88.1 8.1 %collective-permute-done.15.refs_4_ = bf16[512,256]{1,0:T(8,128)(2,1)S(1)} collective-permute-done((bf16[512,256]{1,0:T(8,128)(2,1)S(1)}, bf16[512,256]{1,0:T(8,128)(2,1)S(1)}, u32[]{:S(2)}, u32[]{:S(2)}) %collective-permute-start.15) | collective-permute-done | bytes 262176 | tf_op jit(solution)/shard_map/ppermute | solution.py:38
  96.2 5.6 %collective-permute-done.16.refs_5_ = bf16[512,256]{1,0:T(8,128)(2,1)S(1)} collective-permute-done((bf16[512,256]{1,0:T(8,128)(2,1)S(1)}, bf16[512,256]{1,0:T(8,128)(2,1)S(1)}, u32[]{:S(2)}, u32[]{:S(2)}) %collective-permute-start.16) | collective-permute-done | bytes 262176 | tf_op jit(solution)/shard_map/ppermute | solution.py:38
  101.8 5.6 %collective-permute-done.17.refs_6_ = bf16[512,256]{1,0:T(8,128)(2,1)S(1)} collective-permute-done((bf16[512,256]{1,0:T(8,128)(2,1)S(1)}, bf16[512,256]{1,0:T(8,128)(2,1)S(1)}, u32[]{:S(2)}, u32[]{:S(2)}) %collective-permute-start.17) | collective-permute-done | bytes 262176 | tf_op jit(solution)/shard_map/ppermute | solution.py:38
  107.5 5.6 %collective-permute-done.18.refs_7_ = bf16[512,256]{1,0:T(8,128)(2,1)S(1)} collective-permute-done((bf16[512,256]{1,0:T(8,128)(2,1)}, bf16[512,256]{1,0:T(8,128)(2,1)S(1)}, u32[]{:S(2)}, u32[]{:S(2)}) %collective-permute-start.18) | collective-permute-done | bytes 262176 | tf_op jit(solution)/shard_map/ppermute | solution.py:38
  113.1 5.4 %outer.1 = bf16[2048,4,256]{2,1,0:T(4,128)(2,1)} custom-call(bf16[512,256]{1,0:T(8,128)(2,1)S(1)} %select_select_fusion.refs_0_, bf16[512,256]{1,0:T(8,128)(2,1)S(1)} %collective-permute-done.12.refs_1_, bf16[512,256]{1,0:T(8,128)(2,1)S(1)} %collective-permute-done.13.refs_2_, bf16[512,256]{1,0:T(8,128)(2,1)} %collective-permute-done.14.refs_3_, ...), custom_call_target="tpu_custom_call" | custom-call | tf_op jit(solution)/shard_map/outer/pallas_call | solution.py:177
  118.5 0.9 finish.1
  (20 shorter events, 0.1 us)
Async XLA Ops:
  0.6 15.8 %collective-permute-start = (bf16[128,256]{1,0:T(8,128)(2,1)}, bf16[128,256]{1,0:T(8,128)(2,1)S(1)}, u32[]{:S(2)}, u32[]{:S(2)}) collective-permute-start(bf16[128,256]{1,0:T(8,128)(2,1)} %param.5), channel_id=1, source_target_pairs={{0,2},{2,0},{1,3},{3,1},{4,6},{6,4},{5,7},{7,5},{8,10},{10,8},{9,1... | collective-permute-start | bytes 196616 | tf_op jit(solution)/shard_map/ppermute | solution.py:38
  4.5 2.2 %copy-start = (bf16[8192,256]{1,0:T(8,128)(2,1)S(1)}, bf16[8192,256]{1,0:T(8,128)(2,1)}, u32[]{:S(2)}) copy-start(bf16[8192,256]{1,0:T(8,128)(2,1)} %param.6) | copy-start | bytes 12582916
  6.6 0.7 copy-start.3
  7.4 9.1 %copy-start.5 = (bf16[128,256]{1,0:T(8,128)(2,1)S(1)}, bf16[128,256]{1,0:T(8,128)(2,1)}, u32[]{:S(2)}) copy-start(bf16[128,256]{1,0:T(8,128)(2,1)} %param.5) | copy-start | bytes 196612
  7.4 35.5 %copy-start.4 = (bf16[128,4,256]{2,1,0:T(4,128)(2,1)S(1)}, bf16[128,4,256]{2,1,0:T(4,128)(2,1)}, u32[]{:S(2)}) copy-start(bf16[128,4,256]{2,1,0:T(4,128)(2,1)} %param.4) | copy-start | bytes 786436
  10.7 41.0 %collective-permute-start.5 = (bf16[2048,256]{1,0:T(8,128)(2,1)}, bf16[2048,256]{1,0:T(8,128)(2,1)S(1)}, u32[]{:S(2)}, u32[]{:S(2)}) collective-permute-start(bf16[2048,256]{1,0:T(8,128)(2,1)} %bitcast.3), channel_id=1, source_target_pairs={{0,4},{1,33},{4,8},{5,37},{8,12},{9,41},{12,0},{13,45},{32,36},{33... | collective-permute-start | bytes 3145736 | tf_op jit(solution)/shard_map/ppermute | solution.py:34
  12.4 39.3 %collective-permute-start.6 = (bf16[2048,256]{1,0:T(8,128)(2,1)}, bf16[2048,256]{1,0:T(8,128)(2,1)}, u32[]{:S(2)}, u32[]{:S(2)}) collective-permute-start(bf16[2048,256]{1,0:T(8,128)(2,1)} %bitcast.4), channel_id=1, source_target_pairs={{0,8},{1,65},{4,12},{5,69},{8,0},{9,73},{12,4},{13,77},{32,40},{33... | collective-permute-start | bytes 3145736 | tf_op jit(solution)/shard_map/ppermute | solution.py:34
  15.7 36.0 %collective-permute-start.7 = (bf16[2048,256]{1,0:T(8,128)(2,1)}, bf16[2048,256]{1,0:T(8,128)(2,1)}, u32[]{:S(2)}, u32[]{:S(2)}) collective-permute-start(bf16[2048,256]{1,0:T(8,128)(2,1)} %bitcast.5), channel_id=1, source_target_pairs={{0,12},{1,97},{4,0},{5,101},{8,4},{9,105},{12,8},{13,109},{32,44},... | collective-permute-start | bytes 3145736 | tf_op jit(solution)/shard_map/ppermute | solution.py:34
  16.5 2.0 %collective-permute-start.1 = (bf16[256,256]{1,0:T(8,128)(2,1)S(1)}, bf16[256,256]{1,0:T(8,128)(2,1)S(1)}, u32[]{:S(2)}, u32[]{:S(2)}) collective-permute-start(bf16[256,256]{1,0:T(8,128)(2,1)S(1)} %maximum_select_fusion.3), channel_id=1, source_target_pairs={{0,1},{1,0},{2,3},{3,2},{4,5},{5,4},{6,7},{7,6},{8,9},{9,8},{10,11... | collective-permute-start | bytes 393224 | tf_op jit(solution)/shard_map/ppermute | solution.py:38
  18.6 22.7 %collective-permute-start.2 = (bf16[512,256]{1,0:T(8,128)(2,1)S(1)}, bf16[512,256]{1,0:T(8,128)(2,1)S(1)}, u32[]{:S(2)}, u32[]{:S(2)}) collective-permute-start(bf16[512,256]{1,0:T(8,128)(2,1)S(1)} %maximum_select_fusion.2.refs_0_), channel_id=1, source_target_pairs={{0,4},{1,33},{4,8},{5,37},{8,12},{9,41},{12,0},{13,45},{32,36},{33... | collective-permute-start | bytes 786440 | tf_op jit(solution)/shard_map/ppermute | solution.py:34
  20.3 25.0 %collective-permute-start.3 = (bf16[512,256]{1,0:T(8,128)(2,1)S(1)}, bf16[512,256]{1,0:T(8,128)(2,1)S(1)}, u32[]{:S(2)}, u32[]{:S(2)}) collective-permute-start(bf16[512,256]{1,0:T(8,128)(2,1)S(1)} %maximum_select_fusion.2.refs_0_), channel_id=1, source_target_pairs={{0,8},{1,65},{4,12},{5,69},{8,0},{9,73},{12,4},{13,77},{32,40},{33... | collective-permute-start | bytes 786440 | tf_op jit(solution)/shard_map/ppermute | solution.py:34
  41.3 5.6 %collective-permute-start.4 = (bf16[512,256]{1,0:T(8,128)(2,1)S(1)}, bf16[512,256]{1,0:T(8,128)(2,1)S(1)}, u32[]{:S(2)}, u32[]{:S(2)}) collective-permute-start(bf16[512,256]{1,0:T(8,128)(2,1)S(1)} %maximum_select_fusion.2.refs_0_), channel_id=1, source_target_pairs={{0,12},{1,97},{4,0},{5,101},{8,4},{9,105},{12,8},{13,109},{32,44},... | collective-permute-start | bytes 786440 | tf_op jit(solution)/shard_map/ppermute | solution.py:34
  45.3 15.6 %collective-permute-start.19 = (bf16[128,1024]{1,0:T(8,128)(2,1)}, bf16[128,1024]{1,0:T(8,128)(2,1)}, u32[]{:S(2)}, u32[]{:S(2)}) collective-permute-start(bf16[128,1024]{1,0:T(8,128)(2,1)} %bitcast.7), channel_id=1, source_target_pairs={{0,2},{2,0},{1,3},{3,1},{4,6},{6,4},{5,7},{7,5},{8,10},{10,8},{9,1... | collective-permute-start | bytes 786440 | tf_op jit(solution)/shard_map/ppermute | solution.py:38
  47.7 16.9 %collective-permute-start.11 = (bf16[512,256]{1,0:T(8,128)(2,1)}, bf16[512,256]{1,0:T(8,128)(2,1)}, u32[]{:S(2)}, u32[]{:S(2)}) collective-permute-start(bf16[512,256]{1,0:T(8,128)(2,1)} %select_select_fusion.1), channel_id=1, source_target_pairs={{1,0},{3,2},{5,4},{7,6},{9,8},{11,10},{13,12},{15,14},{17,16},{19,... | collective-permute-start | bytes 786440 | tf_op jit(solution)/shard_map/ppermute | solution.py:222
  56.2 1.0 copy-start.1
  57.2 18.6 %copy-start.2 = (f32[512,512]{1,0:T(8,128)S(1)}, f32[512,512]{1,0:T(8,128)}, u32[]{:S(2)}) copy-start(f32[512,512]{1,0:T(8,128)} %copy-done.1) | copy-start | bytes 3145732
  57.2 9.7 %collective-permute-start.8 = (bf16[512,512]{1,0:T(8,128)(2,1)}, bf16[512,512]{1,0:T(8,128)(2,1)S(1)}, u32[]{:S(2)}, u32[]{:S(2)}) collective-permute-start(bf16[512,512]{1,0:T(8,128)(2,1)} %get-tuple-element.15), channel_id=1, source_target_pairs={{0,32},{1,5},{4,36},{5,9},{8,40},{9,13},{12,44},{13,1},{32,64},{33... | collective-permute-start | bytes 1572872 | tf_op jit(solution)/shard_map/ppermute | solution.py:34
  57.2 18.5 %collective-permute-start.9 = (bf16[512,512]{1,0:T(8,128)(2,1)}, bf16[512,512]{1,0:T(8,128)(2,1)S(1)}, u32[]{:S(2)}, u32[]{:S(2)}) collective-permute-start(bf16[512,512]{1,0:T(8,128)(2,1)} %get-tuple-element.16), channel_id=1, source_target_pairs={{0,64},{1,9},{4,68},{5,13},{8,72},{9,1},{12,76},{13,5},{32,96},{33... | collective-permute-start | bytes 1572872 | tf_op jit(solution)/shard_map/ppermute | solution.py:34
  60.9 14.9 %collective-permute-start.10 = (bf16[512,512]{1,0:T(8,128)(2,1)}, bf16[512,512]{1,0:T(8,128)(2,1)}, u32[]{:S(2)}, u32[]{:S(2)}) collective-permute-start(bf16[512,512]{1,0:T(8,128)(2,1)} %get-tuple-element.17), channel_id=1, source_target_pairs={{0,96},{1,13},{4,100},{5,1},{8,104},{9,5},{12,108},{13,9},{32,0},{... | collective-permute-start | bytes 1572872 | tf_op jit(solution)/shard_map/ppermute | solution.py:34
  63.1 22.9 %collective-permute-start.20 = (bf16[256,1024]{1,0:T(8,128)(2,1)}, bf16[256,1024]{1,0:T(8,128)(2,1)}, u32[]{:S(2)}, u32[]{:S(2)}) collective-permute-start(bf16[256,1024]{1,0:T(8,128)(2,1)} %maximum_select_fusion.1), channel_id=1, source_target_pairs={{0,1},{1,0},{2,3},{3,2},{4,5},{5,4},{6,7},{7,6},{8,9},{9,8},{10,11... | collective-permute-start | bytes 1572872 | tf_op jit(solution)/shard_map/ppermute | solution.py:38
  64.7 19.3 %collective-permute-start.12 = (bf16[512,256]{1,0:T(8,128)(2,1)S(1)}, bf16[512,256]{1,0:T(8,128)(2,1)S(1)}, u32[]{:S(2)}, u32[]{:S(2)}) collective-permute-start(bf16[512,256]{1,0:T(8,128)(2,1)S(1)} %select_select_fusion.refs_0_), channel_id=1, source_target_pairs={{0,4},{4,8},{8,12},{12,0},{1,5},{5,9},{9,13},{13,1},{2,6},{6,10},{... | collective-permute-start | bytes 786440 | tf_op jit(solution)/shard_map/ppermute | solution.py:225
  66.9 17.7 %collective-permute-start.13 = (bf16[512,256]{1,0:T(8,128)(2,1)S(1)}, bf16[512,256]{1,0:T(8,128)(2,1)S(1)}, u32[]{:S(2)}, u32[]{:S(2)}) collective-permute-start(bf16[512,256]{1,0:T(8,128)(2,1)S(1)} %select_select_fusion.refs_0_), channel_id=1, source_target_pairs={{0,8},{4,12},{8,0},{12,4},{1,9},{5,13},{9,1},{13,5},{2,10},{6,14},... | collective-permute-start | bytes 786440 | tf_op jit(solution)/shard_map/ppermute | solution.py:225
  75.8 9.7 %collective-permute-start.14 = (bf16[512,256]{1,0:T(8,128)(2,1)S(1)}, bf16[512,256]{1,0:T(8,128)(2,1)}, u32[]{:S(2)}, u32[]{:S(2)}) collective-permute-start(bf16[512,256]{1,0:T(8,128)(2,1)S(1)} %select_select_fusion.refs_0_), channel_id=1, source_target_pairs={{0,12},{4,0},{8,4},{12,8},{1,13},{5,1},{9,5},{13,9},{2,14},{6,2},{... | collective-permute-start | bytes 786440 | tf_op jit(solution)/shard_map/ppermute | solution.py:225
  77.8 40.6 %all-to-all-start = ((bf16[8,128,256]{2,1,0:T(8,128)(2,1)}), bf16[8,128,256]{2,1,0:T(8,128)(2,1)S(1)}, u32[]{:S(2)}, u32[]{:S(2)}) async-start(bf16[8,128,256]{2,1,0:T(8,128)(2,1)} %summed.1), calls=%async_computation | async-start | bytes 1048576 | tf_op jit(solution)/shard_map/all_to_all | solution.py:211
  82.6 13.6 %collective-permute-start.15 = (bf16[512,256]{1,0:T(8,128)(2,1)S(1)}, bf16[512,256]{1,0:T(8,128)(2,1)S(1)}, u32[]{:S(2)}, u32[]{:S(2)}) collective-permute-start(bf16[512,256]{1,0:T(8,128)(2,1)S(1)} %select_select_fusion.refs_0_), channel_id=1, source_target_pairs={{0,16},{16,0},{1,17},{17,1},{2,18},{18,2},{3,19},{19,3},{4,20},{20... | collective-permute-start | bytes 786440 | tf_op jit(solution)/shard_map/ppermute | solution.py:38
  84.0 17.8 %collective-permute-start.16 = (bf16[512,256]{1,0:T(8,128)(2,1)S(1)}, bf16[512,256]{1,0:T(8,128)(2,1)S(1)}, u32[]{:S(2)}, u32[]{:S(2)}) collective-permute-start(bf16[512,256]{1,0:T(8,128)(2,1)S(1)} %collective-permute-done.12.refs_1_), channel_id=1, source_target_pairs={{0,16},{16,0},{1,17},{17,1},{2,18},{18,2},{3,19},{19,3},{4,20},{20... | collective-permute-start | bytes 786440 | tf_op jit(solution)/shard_map/ppermute | solution.py:38
  84.5 22.9 %collective-permute-start.17 = (bf16[512,256]{1,0:T(8,128)(2,1)S(1)}, bf16[512,256]{1,0:T(8,128)(2,1)S(1)}, u32[]{:S(2)}, u32[]{:S(2)}) collective-permute-start(bf16[512,256]{1,0:T(8,128)(2,1)S(1)} %collective-permute-done.13.refs_2_), channel_id=1, source_target_pairs={{0,16},{16,0},{1,17},{17,1},{2,18},{18,2},{3,19},{19,3},{4,20},{20... | collective-permute-start | bytes 786440 | tf_op jit(solution)/shard_map/ppermute | solution.py:38
  85.5 27.6 %collective-permute-start.18 = (bf16[512,256]{1,0:T(8,128)(2,1)}, bf16[512,256]{1,0:T(8,128)(2,1)S(1)}, u32[]{:S(2)}, u32[]{:S(2)}) collective-permute-start(bf16[512,256]{1,0:T(8,128)(2,1)} %collective-permute-done.14.refs_3_), channel_id=1, source_target_pairs={{0,16},{16,0},{1,17},{17,1},{2,18},{18,2},{3,19},{19,3},{4,20},{20... | collective-permute-start | bytes 786440 | tf_op jit(solution)/shard_map/ppermute | solution.py:38

commit v3 on v2

v3 whole, which is shorter than its diff:
```python
import functools

import jax
import jax.numpy as jnp
from jax import lax
from jax.experimental import pallas as pl
from jax.experimental.pallas import tpu as pltpu
from jax.sharding import Mesh, PartitionSpec as P

BF = jnp.bfloat16
F32 = jnp.float32
VM = pltpu.VMEM


def first_axis_steps(k):
    pairs = []
    for z in range(4):
        for x in range(4):
            pairs.append(((z * 4 + x) * 2, (z * 4 + (x + k) % 4) * 2))
            pairs.append(((z * 4 + x) * 2 + 1, (((z + k) % 4) * 4 + x) * 2 + 1))
    return pairs


def second_axis_steps(k):
    pairs = []
    for z in range(4):
        for x in range(4):
            pairs.append(((z * 4 + x) * 2, (((z + k) % 4) * 4 + x) * 2))
            pairs.append(((z * 4 + x) * 2 + 1, (z * 4 + (x + k) % 4) * 2 + 1))
    return pairs


def shift(value, pairs):
    return lax.ppermute(value, ("z", "x", "c"), pairs)


def swap(value, axis):
    return lax.ppermute(value, axis, [(0, 1), (1, 0)])


LIMIT = pltpu.CompilerParams(vmem_limit_bytes=12 << 20)
EARLY = int(2e9)
NEAR = int(20e9)
IN = pl.BlockSpec(memory_space=VM)
HBM = pl.BlockSpec(memory_space=pltpu.HBM)


def kept(*values):
    return [pltpu.with_memory_space_constraint(v, VM) for v in values]


def roles():
    c, x, z = lax.axis_index("c"), lax.axis_index("x"), lax.axis_index("z")
    return c, jnp.where(c == 0, x, z), jnp.where(c == 0, z, x)


def spread_scales(s_ref, wide_ref):
    row = lax.broadcasted_iota(jnp.int32, (16, 256), 0)
    col = lax.broadcasted_iota(jnp.int32, (16, 256), 1)
    spread = jnp.where(col // 16 == row, 1.0, 0.0).astype(BF)
    wide_ref[...] = lax.dot_general(
        s_ref[...], spread, (((0,), (0,)), ((), ())), preferred_element_type=F32
    )


def scale_into(outs, w_ref, s_ref, wide_ref, sems, between=None):
    c, first, _ = roles()
    copies = []
    for j, (k, o_ref) in enumerate(outs):
        p = (first + k) & 3
        for i in range(4):
            z, x = c * p + (1 - c) * i, c * i + (1 - c) * p
            copy = pltpu.make_async_copy(
                w_ref.at[z, :, x], o_ref.at[pl.ds(2 * i, 2)], sems.at[j * 4 + i]
            )
            copy.start()
            copies.append((copy, o_ref, i, z, x))
    spread_scales(s_ref, wide_ref)
    if between is not None:
        between()
    for copy, o_ref, i, z, x in copies:
        copy.wait()
        for yl in range(2):
            r = pl.multiple_of((z * 8 + yl * 4 + x) * 16, 16)
            s = wide_ref[pl.ds(r, 16), :]
            w = o_ref[2 * i + yl].astype(F32).reshape(16, 16, 256)
            o_ref[2 * i + yl] = (w * s[:, None, :]).reshape(256, 256).astype(BF)


def far_body(w_ref, s_ref, o_ref, wide_ref, sems):
    scale_into([(2, o_ref)], w_ref, s_ref, wide_ref, sems)


def far_rows(w5, scales_t):
    return pl.pallas_call(
        far_body,
        out_shape=VM((8, 256, 256), BF),
        in_specs=[HBM, IN],
        out_specs=IN,
        scratch_shapes=[VM((512, 256), F32), pltpu.SemaphoreType.DMA((4,))],
        compiler_params=LIMIT,
        name="far",
    )(w5, scales_t)


def near_body(w_ref, s_ref, g0, g1, g2, g3, o1, o3, o0, og, wide_ref, sems):
    n = lax.axis_index("yh") * 2 + lax.axis_index("c")

    def tokens():
        for r, g in enumerate((g0, g1, g2, g3)):
            t = n ^ r
            og[t >> 1, pl.ds(pl.multiple_of((t & 1) * 128, 128), 128), :] = g[...]
        o1[8:10] = og[...]
        o3[8:10] = og[...]

    scale_into([(1, o1), (3, o3), (0, o0)], w_ref, s_ref, wide_ref, sems, tokens)


def near_rows(w5, scales_t, pieces):
    return pl.pallas_call(
        near_body,
        out_shape=[VM((10, 256, 256), BF)] * 2 + [VM((8, 256, 256), BF), VM((2, 256, 256), BF)],
        in_specs=[HBM] + [IN] * 5,
        out_specs=[IN] * 4,
        scratch_shapes=[VM((512, 256), F32), pltpu.SemaphoreType.DMA((12,))],
        compiler_params=LIMIT,
        cost_estimate=pl.CostEstimate(flops=NEAR, bytes_accessed=8 << 20, transcendentals=0),
        name="near",
    )(w5, scales_t, *pieces)


def block_product(g, w, q):
    return lax.dot_general(
        g[...].reshape(512, 256),
        w[pl.ds(q, 2)].reshape(512, 256),
        (((1,), (1,)), ((), ())),
        preferred_element_type=F32,
    )


def early_body(r0, r2, g0, g2, acc):
    for q in range(4):
        acc[q] = block_product(g0, r0, 2 * q) + block_product(g2, r2, 2 * q)


def early_sums(*operands):
    return pl.pallas_call(
        early_body,
        out_shape=VM((4, 512, 512), F32),
        in_specs=[IN] * 4,
        out_specs=IN,
        compiler_params=LIMIT,
        cost_estimate=pl.CostEstimate(flops=EARLY, bytes_accessed=6 << 20, transcendentals=0),
        name="early",
    )(*kept(*operands))


def partial_body(acc, r1, r3, g0, g2, *outs):
    keep, give = outs[4:]
    _, _, second = roles()
    z, yh = lax.axis_index("z"), lax.axis_index("yh")
    g = (g0, r1.at[8:10], g2, r3.at[8:10])
    for k in range(4):

        @pl.when(((z - 2 * yh) & 3) == k)
        def _():
            give[...] = g[k][...]

        @pl.when(((z - 2 * yh - 1) & 3) == k)
        def _():
            keep[...] = g[k][...]

    for k in (2, 1, 3, 0):
        q = (second + k) & 3
        total = acc[q] + block_product(g[1], r1, 2 * q) + block_product(g[3], r3, 2 * q)
        outs[k][...] = total.astype(outs[k].dtype)


def partial_sums(*operands):
    return pl.pallas_call(
        partial_body,
        out_shape=[VM((512, 512), F32)]
        + [VM((512, 512), BF)] * 3
        + [VM((2, 256, 256), BF)] * 2,
        in_specs=[IN] * 5,
        out_specs=[IN] * 6,
        compiler_params=LIMIT,
        name="partial",
    )(*kept(*operands))


def gather_body(a, b, c, d, o_ref):
    total = a[...] + b[...].astype(F32) + c[...].astype(F32) + d[...].astype(F32)
    total = total.astype(BF)
    for yl in range(2):
        for n in range(4):
            t = n * 128
            o_ref[yl * 4 + n] = total[t : t + 128, yl * 256 : (yl + 1) * 256]


def summed_blocks(parts):
    return pl.pallas_call(
        gather_body,
        out_shape=VM((8, 128, 256), BF),
        in_specs=[IN] * 4,
        out_specs=IN,
        compiler_params=LIMIT,
        name="summed",
    )(parts[0], *kept(*parts[1:]))


def finish_body(r_ref, o_ref):
    r = [(r_ref[n].astype(F32) + r_ref[4 + n].astype(F32)).astype(BF) for n in range(4)]
    o_ref[...] = jnp.concatenate(r, axis=1).reshape(128, 4, 256)


def finished(blocks):
    return pl.pallas_call(
        finish_body,
        out_shape=jax.ShapeDtypeStruct((128, 4, 256), BF),
        in_specs=[IN],
        out_specs=IN,
        compiler_params=LIMIT,
        name="finish",
    )(*kept(blocks))


def picked_body(a_ref, b_ref, o_ref):
    @pl.when(lax.axis_index("c") == 0)
    def _():
        o_ref[...] = a_ref[...]

    @pl.when(lax.axis_index("c") == 1)
    def _():
        o_ref[...] = b_ref[...]


def picked(for_core_0, for_core_1):
    return pl.pallas_call(
        picked_body,
        out_shape=VM((2, 256, 256), BF),
        in_specs=[IN] * 2,
        out_specs=IN,
        compiler_params=LIMIT,
        name="picked",
    )(for_core_0, for_core_1)


def outer_body(*refs):
    g, pieces, o_ref, h_ref, buf, sems = refs[:8], refs[8:12], *refs[12:]
    yl, x = lax.axis_index("yl"), lax.axis_index("x")
    n = lax.axis_index("yh") * 2 + lax.axis_index("c")
    for r, piece in enumerate(pieces):
        h_ref[pl.ds(pl.multiple_of((n ^ r) * 128, 128), 128), :] = piece[...]
    copies = []
    for i in range(8):
        here = yl if i < 4 else 1 - yl
        r = pl.multiple_of((here * 4 + ((x - i) & 3)) * 256, 256)
        p = lax.dot_general(
            g[i][...].reshape(512, 256),
            h_ref[...],
            (((0,), (0,)), ((), ())),
            preferred_element_type=F32,
        )
        buf[i] = p.astype(BF).reshape(256, 4, 256)
        copy = pltpu.make_async_copy(buf.at[i], o_ref.at[pl.ds(r, 256)], sems.at[i])
        copy.start()
        copies.append(copy)
    for copy in copies:
        copy.wait()


def outer_product(blocks, pieces):
    return pl.pallas_call(
        outer_body,
        out_shape=jax.ShapeDtypeStruct((2048, 4, 256), BF),
        in_specs=[IN] * 12,
        out_specs=HBM,
        scratch_shapes=[
            VM((512, 1024), BF),
            VM((8, 256, 4, 256), BF),
            pltpu.SemaphoreType.DMA((8,)),
        ],
        compiler_params=LIMIT,
        name="outer",
    )(*kept(*blocks, *pieces))


def token_pieces(own):
    far = swap(own, "yh")
    return [own, swap(own, "c"), far, swap(far, "c")]


def per_device(hidden, grad_out, weight_base, block_scale):
    w5 = pltpu.with_memory_space_constraint(weight_base.reshape(4, 2, 4, 256, 256), pltpu.HBM)
    scales_t = block_scale.T

    tokens = token_pieces(grad_out)
    sent2 = far_rows(w5, scales_t)
    r2 = shift(sent2, first_axis_steps(2))
    tokens, _ = lax.optimization_barrier((tokens, sent2))
    sent1, sent3, r0, g0 = near_rows(w5, scales_t, tokens)
    r1 = shift(sent1, first_axis_steps(1))
    r3 = shift(sent3, first_axis_steps(3))
    g2 = shift(g0, first_axis_steps(2))

    acc = early_sums(r0, r2, g0, g2)
    h, acc = lax.optimization_barrier((hidden, acc))
    pieces = token_pieces(h.reshape(128, 1024))
    acc, pieces = lax.optimization_barrier((acc, pieces))
    *sums, keep, give = partial_sums(acc, r1, r3, g0, g2)
    parts = [sums[0]] + [None] * 3
    for k in (2, 1, 3):
        parts[k] = shift(sums[k], second_axis_steps(k))
    blocks = summed_blocks(parts)
    blocks = lax.all_to_all(blocks, ("yl", "yh", "c"), 0, 0, tiled=True)
    grad_hidden = finished(blocks)

    seed = picked(lax.ppermute(give, "c", [(1, 0)]), keep)
    ring = lambda k: [(i, (i + k) % 4) for i in range(4)]
    mine = [seed] + [lax.ppermute(seed, "x", ring(k)) for k in (1, 2, 3)]
    theirs = [swap(m, "yl") for m in mine]
    grad_weight = outer_product(mine + theirs, pieces)
    return grad_hidden, grad_weight


def solution(mesh):
    fine = Mesh(mesh.devices.reshape(4, 2, 4, 2, 2), ("z", "yl", "x", "yh", "c"))
    narrow, wide = ("yh", "c"), ("z", "yl", "x")
    return jax.shard_map(
        per_device,
        mesh=fine,
        in_specs=(
            P(narrow, None, wide),
            P(narrow, wide),
            P(narrow, wide),
            P(narrow, wide),
        ),
        out_specs=(P(narrow, None, wide), P(narrow, None, wide)),
        check_vma=False,
    )
```

time: 122 us -> 119 us (0.975)
  waiting for transfers between devices: 56.7 us -> 64.3 us
  other arithmetic: 5.23 us -> 0 us
  local copies, waits for them, and re-layouts: 4.64 us -> 0.76 us
  Pallas kernels: 16.1 us -> 12.4 us
  starting transfers between devices: 36 us -> 38.9 us
    ppermute x8 -> x10, waiting for transfers between devices: 26 us -> 33.2 us  [swap(): return lax.ppermute(value, axis, [(0, 1), (1, 0)])]
    ppermute x8 -> x10, starting transfers between devices: 9.37 us -> 15.7 us  [swap(): return lax.ppermute(value, axis, [(0, 1), (1, 0)])]
    select_n x6 -> x0, other arithmetic: 5.23 us -> none  [the longest x4 4.41 us: joined(): jnp.where(first, jnp.concatenate([a, b], 0), jnp.concatenate([b, a], 0))]
    ppermute x9 -> x7, starting transfers between devices: 16.1 us -> 11.3 us  [shift(): return lax.ppermute(value, ('z', 'x', 'c'), pairs)]
    unnamed x13 -> x7, local copies, waits for them, and re-layouts: 4.64 us -> 0.76 us
    pallas_call x1, Pallas kernels: 4.42 us -> 1.35 us  [partial_sums(): pl.pallas_call(partial_body, out_shape=[VM((512, 512), F32)] + [VM((512,...]
    ppermute x3, starting transfers between devices: 1.7 us -> 3.67 us  [per_device(): mine = [seed] + [lax.ppermute(seed, 'x', ring(k)) for k in (1, 2, 3)]]
    pallas_call x1 -> x4, Pallas kernels: 3.35 us -> 4.76 us  [the longest x1 2.13 us: near_rows(): pl.pallas_call(near_body, out_shape=[VM((10, 256, 256), BF)] * 2 + [VM((8...]
  transfers between devices with their start and end apart: 22 -> 22, of which waited for: 11 -> 12; matrix products, arithmetic and copies ran while one was open for 5% -> 0% of each run, Pallas kernels for 13% -> 9%
where the time goes in v3:
time: 119 us; the launch traced here: 117 us
  waiting for transfers between devices  64.3 us (54%)
  starting transfers between devices  38.9 us (33%)
  Pallas kernels  12.4 us (10%)
    ppermute x10, waiting for transfers between devices, swap(): return lax.ppermute(value, axis, [(0, 1), (1, 0)])  33.2 us
    ppermute x7, waiting for transfers between devices, shift(): return lax.ppermute(value, ('z', 'x', 'c'), pairs)  29.4 us
    ppermute x10, starting transfers between devices, swap(): return lax.ppermute(value, axis, [(0, 1), (1, 0)])  15.7 us
    ppermute x7, starting transfers between devices, shift(): return lax.ppermute(value, ('z', 'x', 'c'), pairs)  11.3 us
    all_to_all x1, starting transfers between devices, per_device(): blocks = lax.all_to_all(blocks, ('yl', 'yh', 'c'), 0, 0, tiled=True)  4.64 us
    pallas_call x1, Pallas kernels, outer_product(): pl.pallas_call(outer_body, out_shape=jax.ShapeDtypeStruct((2048, 4, 256),...  4.35 us
    ppermute x3, starting transfers between devices, per_device(): mine = [seed] + [lax.ppermute(seed, 'x', ring(k)) for k in (1, 2, 3)]  3.67 us
    ppermute x1, starting transfers between devices, per_device(): seed = picked(lax.ppermute(give, 'c', [(1, 0)]), keep)  3.62 us
  transfers between devices with their start and end apart: 22, of which 12 were waited for; matrix products, arithmetic and copies ran while one was open for 0% of the time, Pallas kernels for 9%

profile of v3, /device:TPU:1, one launch (start us, length us, event | category | flops | bytes accessed | tf_op | source)
XLA Modules:
  0.0 117.0 jit_solution(2744946525214844716)
XLA Ops:
  0.6 3.8 %collective-permute-start.1 = (bf16[128,256]{1,0:T(8,128)(2,1)}, bf16[128,256]{1,0:T(8,128)(2,1)S(1)}, u32[]{:S(2)}, u32[]{:S(2)}) collective-permute-start(bf16[128,256]{1,0:T(8,128)(2,1)} %g0), channel_id=1, source_target_pairs={{0,2},{2,0},{1,3},{3,1},{4,6},{6,4},{5,7},{7,5},{8,10},{10,8},{9,1... | collective-permute-start | bytes 196616 | tf_op jit(solution)/shard_map/ppermute | solution.py:38
  4.5 1.0 collective-permute-start
  5.4 0.9 collective-permute-done.1.g2
  6.3 1.8 %collective-permute-start.2 = (bf16[128,256]{1,0:T(8,128)(2,1)S(1)}, bf16[128,256]{1,0:T(8,128)(2,1)S(1)}, u32[]{:S(2)}, u32[]{:S(2)}) collective-permute-start(bf16[128,256]{1,0:T(8,128)(2,1)S(1)} %collective-permute-done.1.g2), channel_id=1, source_target_pairs={{0,1},{1,0},{2,3},{3,2},{4,5},{5,4},{6,7},{7,6},{8,9},{9,8},{10,11... | collective-permute-start | bytes 196616 | tf_op jit(solution)/shard_map/ppermute | solution.py:38
  8.1 0.7 copy-done
  8.8 1.3 %far.1 = bf16[8,256,256]{2,1,0:T(8,128)(2,1)S(1)} custom-call(bf16[4,2,4,256,256]{4,3,2,1,0:T(8,128)(2,1)} %bitcast.9, bf16[16,512]{1,0:T(8,128)(2,1)S(1)} %bitcast.7), custom_call_target="tpu_custom_call" | custom-call | tf_op jit(solution)/shard_map/far/pallas_call | solution.py:95
  10.2 3.8 %collective-permute-start.3 = (bf16[8,256,256]{2,1,0:T(8,128)(2,1)S(1)}, bf16[8,256,256]{2,1,0:T(8,128)(2,1)S(1)}, u32[]{:S(2)}, u32[]{:S(2)}) collective-permute-start(bf16[8,256,256]{2,1,0:T(8,128)(2,1)S(1)} %far.1), channel_id=1, source_target_pairs={{0,8},{1,65},{4,12},{5,69},{8,0},{9,73},{12,4},{13,77},{32,40},{33... | collective-permute-start | bytes 3145736 | tf_op jit(solution)/shard_map/ppermute | solution.py:34
  13.9 0.0 collective-permute-done.g1
  13.9 0.0 collective-permute-done.2.g3
  13.9 2.1 %near.1 = (bf16[10,256,256]{2,1,0:T(8,128)(2,1)S(1)}, bf16[10,256,256]{2,1,0:T(8,128)(2,1)S(1)}, bf16[8,256,256]{2,1,0:T(8,128)(2,1)S(1)}, bf16[2,256,256]{2,1,0:T(8,128)(2,1)S(1)}) custom-call(bf16[4,2,4,256,256]{4,3,2,1,0:T(8,128)(2,1)} %bitcast.10, bf16[16,512]{1,0:T(8,128)(2,1)S(1)} %bitcast.8, bf16[128,256]{1,0:T(8,128)(2,1)S(1)} %copy-done.1, ...), custom_call_target="tpu_custom_call" | custom-call | flops 20000000000 | bytes 8388608 | tf_op jit(solution)/shard_map/near/pallas_call | solution.py:120
  16.1 0.8 collective-permute-start.8
  16.9 1.9 %collective-permute-start.9 = (bf16[10,256,256]{2,1,0:T(8,128)(2,1)S(1)}, bf16[10,256,256]{2,1,0:T(8,128)(2,1)S(1)}, u32[]{:S(2)}, u32[]{:S(2)}) collective-permute-start(bf16[10,256,256]{2,1,0:T(8,128)(2,1)S(1)} %get-tuple-element.33), channel_id=1, source_target_pairs={{0,12},{1,97},{4,0},{5,101},{8,4},{9,105},{12,8},{13,109},{32,44},... | collective-permute-start | bytes 3932168 | tf_op jit(solution)/shard_map/ppermute | solution.py:34
  18.8 0.0 collective-permute-start.4
  18.8 24.2 %collective-permute-done.4.g2 = bf16[2,256,256]{2,1,0:T(8,128)(2,1)S(1)} collective-permute-done((bf16[2,256,256]{2,1,0:T(8,128)(2,1)S(1)}, bf16[2,256,256]{2,1,0:T(8,128)(2,1)S(1)}, u32[]{:S(2)}, u32[]{:S(2)}) %collective-permute-start.4) | collective-permute-done | bytes 262176 | tf_op jit(solution)/shard_map/ppermute | solution.py:34
  43.1 0.0 collective-permute-done.3.r2
  43.1 1.3 %early.1.acc = f32[4,512,512]{2,1,0:T(8,128)S(1)} custom-call(bf16[8,256,256]{2,1,0:T(8,128)(2,1)S(1)} %get-tuple-element.27.r0, bf16[8,256,256]{2,1,0:T(8,128)(2,1)S(1)} %collective-permute-done.3.r2, bf16[2,256,256]{2,1,0:T(8,128)(2,1)S(1)} %get-tuple-element.28.g0, bf16[2,256,256]{2,1,0:T(8,128)(2,1)S(1)} %collective-permute-done.4.g2), custom_call_target="tpu_custom_call" | custom-call | flops 2000000000 | bytes 6291456 | tf_op jit(solution)/shard_map/early/pallas_call | solution.py:147
  44.4 3.1 %collective-permute-start.6 = (bf16[128,1024]{1,0:T(8,128)(2,1)S(1)}, bf16[128,1024]{1,0:T(8,128)(2,1)S(1)}, u32[]{:S(2)}, u32[]{:S(2)}) collective-permute-start(bf16[128,1024]{1,0:T(8,128)(2,1)S(1)} %bitcast.4), channel_id=1, source_target_pairs={{0,2},{2,0},{1,3},{3,1},{4,6},{6,4},{5,7},{7,5},{8,10},{10,8},{9,1... | collective-permute-start | bytes 786440 | tf_op jit(solution)/shard_map/ppermute | solution.py:38
  47.5 0.7 collective-permute-start.5
  48.2 5.4 %collective-permute-done.6.refs_10_ = bf16[128,1024]{1,0:T(8,128)(2,1)S(1)} collective-permute-done((bf16[128,1024]{1,0:T(8,128)(2,1)S(1)}, bf16[128,1024]{1,0:T(8,128)(2,1)S(1)}, u32[]{:S(2)}, u32[]{:S(2)}) %collective-permute-start.6) | collective-permute-done | bytes 262176 | tf_op jit(solution)/shard_map/ppermute | solution.py:38
  53.5 1.2 %collective-permute-start.7 = (bf16[128,1024]{1,0:T(8,128)(2,1)S(1)}, bf16[128,1024]{1,0:T(8,128)(2,1)S(1)}, u32[]{:S(2)}, u32[]{:S(2)}) collective-permute-start(bf16[128,1024]{1,0:T(8,128)(2,1)S(1)} %collective-permute-done.6.refs_10_), channel_id=1, source_target_pairs={{0,1},{1,0},{2,3},{3,2},{4,5},{5,4},{6,7},{7,6},{8,9},{9,8},{10,11... | collective-permute-start | bytes 786440 | tf_op jit(solution)/shard_map/ppermute | solution.py:38
  54.7 0.0 collective-permute-done.5.refs_9_
  54.7 1.2 collective-permute-done.7.refs_11_
  55.9 0.0 collective-permute-done.8.r1
  55.9 1.3 %partial.1 = (f32[512,512]{1,0:T(8,128)S(1)}, bf16[512,512]{1,0:T(8,128)(2,1)S(1)}, bf16[512,512]{1,0:T(8,128)(2,1)S(1)}, bf16[512,512]{1,0:T(8,128)(2,1)S(1)}, ...) custom-call(f32[4,512,512]{2,1,0:T(8,128)S(1)} %early.1.acc, ...), custom_call_target="tpu_custom_call" | custom-call | tf_op jit(solution)/shard_map/partial/pallas_call | solution.py:180
  57.3 1.2 %collective-permute-start.10 = (bf16[512,512]{1,0:T(8,128)(2,1)S(1)}, bf16[512,512]{1,0:T(8,128)(2,1)S(1)}, u32[]{:S(2)}, u32[]{:S(2)}) collective-permute-start(bf16[512,512]{1,0:T(8,128)(2,1)S(1)} %get-tuple-element.35), channel_id=1, source_target_pairs={{0,32},{1,5},{4,36},{5,9},{8,40},{9,13},{12,44},{13,1},{32,64},{33... | collective-permute-start | bytes 1572872 | tf_op jit(solution)/shard_map/ppermute | solution.py:34
  58.5 2.6 %collective-permute-start.11 = (bf16[512,512]{1,0:T(8,128)(2,1)S(1)}, bf16[512,512]{1,0:T(8,128)(2,1)S(1)}, u32[]{:S(2)}, u32[]{:S(2)}) collective-permute-start(bf16[512,512]{1,0:T(8,128)(2,1)S(1)} %get-tuple-element.36), channel_id=1, source_target_pairs={{0,64},{1,9},{4,68},{5,13},{8,72},{9,1},{12,76},{13,5},{32,96},{33... | collective-permute-start | bytes 1572872 | tf_op jit(solution)/shard_map/ppermute | solution.py:34
  61.0 1.0 collective-permute-start.12
  62.1 3.6 %collective-permute-start.13 = (bf16[2,256,256]{2,1,0:T(8,128)(2,1)S(1)}, bf16[2,256,256]{2,1,0:T(8,128)(2,1)S(1)}, u32[]{:S(2)}, u32[]{:S(2)}) collective-permute-start(bf16[2,256,256]{2,1,0:T(8,128)(2,1)S(1)} %get-tuple-element.38), channel_id=1, source_target_pairs={{1,0},{3,2},{5,4},{7,6},{9,8},{11,10},{13,12},{15,14},{17,16},{19,... | collective-permute-start | bytes 786440 | tf_op jit(solution)/shard_map/ppermute | solution.py:319
  65.7 1.1 collective-permute-done.13.a_ref
  66.9 2.5 %collective-permute-start.16 = (bf16[2,256,256]{2,1,0:T(8,128)(2,1)S(1)}, bf16[2,256,256]{2,1,0:T(8,128)(2,1)S(1)}, u32[]{:S(2)}, u32[]{:S(2)}) collective-permute-start(bf16[2,256,256]{2,1,0:T(8,128)(2,1)S(1)} %picked.1.refs_0_), channel_id=1, source_target_pairs={{0,12},{4,0},{8,4},{12,8},{1,13},{5,1},{9,5},{13,9},{2,14},{6,2},{... | collective-permute-start | bytes 786440 | tf_op jit(solution)/shard_map/ppermute | solution.py:321
  69.4 0.5 collective-permute-start.15
  69.9 0.0 collective-permute-done.10.b
  69.9 0.6 collective-permute-start.14
  70.5 3.0 %collective-permute-done.11.c = bf16[512,512]{1,0:T(8,128)(2,1)S(1)} collective-permute-done((bf16[512,512]{1,0:T(8,128)(2,1)S(1)}, bf16[512,512]{1,0:T(8,128)(2,1)S(1)}, u32[]{:S(2)}, u32[]{:S(2)}) %collective-permute-start.11) | collective-permute-done | bytes 524320 | tf_op jit(solution)/shard_map/ppermute | solution.py:34
  73.5 2.2 %collective-permute-done.12.d = bf16[512,512]{1,0:T(8,128)(2,1)S(1)} collective-permute-done((bf16[512,512]{1,0:T(8,128)(2,1)S(1)}, bf16[512,512]{1,0:T(8,128)(2,1)S(1)}, u32[]{:S(2)}, u32[]{:S(2)}) %collective-permute-start.12) | collective-permute-done | bytes 524320 | tf_op jit(solution)/shard_map/ppermute | solution.py:34
  75.7 1.0 summed.1
  76.7 4.6 %all-to-all-start = ((bf16[8,128,256]{2,1,0:T(8,128)(2,1)}), bf16[8,128,256]{2,1,0:T(8,128)(2,1)S(1)}, u32[]{:S(2)}, u32[]{:S(2)}) async-start(bf16[8,128,256]{2,1,0:T(8,128)(2,1)} %summed.1), calls=%async_computation | async-start | bytes 1048576 | tf_op jit(solution)/shard_map/all_to_all | solution.py:316
  81.3 1.4 %collective-permute-start.17 = (bf16[2,256,256]{2,1,0:T(8,128)(2,1)S(1)}, bf16[2,256,256]{2,1,0:T(8,128)(2,1)S(1)}, u32[]{:S(2)}, u32[]{:S(2)}) collective-permute-start(bf16[2,256,256]{2,1,0:T(8,128)(2,1)S(1)} %picked.1.refs_0_), channel_id=1, source_target_pairs={{0,16},{16,0},{1,17},{17,1},{2,18},{18,2},{3,19},{19,3},{4,20},{20... | collective-permute-start | bytes 786440 | tf_op jit(solution)/shard_map/ppermute | solution.py:38
  82.7 0.1 collective-permute-start.20
  82.8 1.4 %collective-permute-start.19 = (bf16[2,256,256]{2,1,0:T(8,128)(2,1)S(1)}, bf16[2,256,256]{2,1,0:T(8,128)(2,1)S(1)}, u32[]{:S(2)}, u32[]{:S(2)}) collective-permute-start(bf16[2,256,256]{2,1,0:T(8,128)(2,1)S(1)} %collective-permute-done.15.refs_2_), channel_id=1, source_target_pairs={{0,16},{16,0},{1,17},{17,1},{2,18},{18,2},{3,19},{19,3},{4,20},{20... | collective-permute-start | bytes 786440 | tf_op jit(solution)/shard_map/ppermute | solution.py:38
  84.2 0.5 collective-permute-done.14.refs_1_
  84.8 1.3 %collective-permute-start.18 = (bf16[2,256,256]{2,1,0:T(8,128)(2,1)S(1)}, bf16[2,256,256]{2,1,0:T(8,128)(2,1)S(1)}, u32[]{:S(2)}, u32[]{:S(2)}) collective-permute-start(bf16[2,256,256]{2,1,0:T(8,128)(2,1)S(1)} %collective-permute-done.14.refs_1_), channel_id=1, source_target_pairs={{0,16},{16,0},{1,17},{17,1},{2,18},{18,2},{3,19},{19,3},{4,20},{20... | collective-permute-start | bytes 786440 | tf_op jit(solution)/shard_map/ppermute | solution.py:38
  86.1 8.9 %collective-permute-done.17.refs_4_ = bf16[2,256,256]{2,1,0:T(8,128)(2,1)S(1)} collective-permute-done((bf16[2,256,256]{2,1,0:T(8,128)(2,1)S(1)}, bf16[2,256,256]{2,1,0:T(8,128)(2,1)S(1)}, u32[]{:S(2)}, u32[]{:S(2)}) %collective-permute-start.17) | collective-permute-done | bytes 262176 | tf_op jit(solution)/shard_map/ppermute | solution.py:38
  94.9 5.6 %collective-permute-done.20.refs_7_ = bf16[2,256,256]{2,1,0:T(8,128)(2,1)S(1)} collective-permute-done((bf16[2,256,256]{2,1,0:T(8,128)(2,1)S(1)}, bf16[2,256,256]{2,1,0:T(8,128)(2,1)S(1)}, u32[]{:S(2)}, u32[]{:S(2)}) %collective-permute-start.20) | collective-permute-done | bytes 262176 | tf_op jit(solution)/shard_map/ppermute | solution.py:38
  100.6 5.6 %collective-permute-done.19.refs_6_ = bf16[2,256,256]{2,1,0:T(8,128)(2,1)S(1)} collective-permute-done((bf16[2,256,256]{2,1,0:T(8,128)(2,1)S(1)}, bf16[2,256,256]{2,1,0:T(8,128)(2,1)S(1)}, u32[]{:S(2)}, u32[]{:S(2)}) %collective-permute-start.19) | collective-permute-done | bytes 262176 | tf_op jit(solution)/shard_map/ppermute | solution.py:38
  106.2 5.6 %collective-permute-done.18.refs_5_ = bf16[2,256,256]{2,1,0:T(8,128)(2,1)S(1)} collective-permute-done((bf16[2,256,256]{2,1,0:T(8,128)(2,1)S(1)}, bf16[2,256,256]{2,1,0:T(8,128)(2,1)S(1)}, u32[]{:S(2)}, u32[]{:S(2)}) %collective-permute-start.18) | collective-permute-done | bytes 262176 | tf_op jit(solution)/shard_map/ppermute | solution.py:38
  111.8 4.3 %outer.1 = bf16[2048,4,256]{2,1,0:T(4,128)(2,1)} custom-call(bf16[2,256,256]{2,1,0:T(8,128)(2,1)S(1)} %picked.1.refs_0_, bf16[2,256,256]{2,1,0:T(8,128)(2,1)S(1)} %collective-permute-done.14.refs_1_, bf16[2,256,256]{2,1,0:T(8,128)(2,1)S(1)} %collective-permute-done.15.refs_2_, bf16[2,256,256]{2,1,0:T(8,128)(2,1)S(1)} %collective-permute-done.16.refs_3_, ...), custom_call_target="tpu_custom_call" | custom-call | tf_op jit(solution)/shard_map/outer/pallas_call | solution.py:274
  116.2 0.9 finish.1
  (11 shorter events, 0.1 us)
Async XLA Ops:
  0.6 5.7 %collective-permute-start.1 = (bf16[128,256]{1,0:T(8,128)(2,1)}, bf16[128,256]{1,0:T(8,128)(2,1)S(1)}, u32[]{:S(2)}, u32[]{:S(2)}) collective-permute-start(bf16[128,256]{1,0:T(8,128)(2,1)} %g0), channel_id=1, source_target_pairs={{0,2},{2,0},{1,3},{3,1},{4,6},{6,4},{5,7},{7,5},{8,10},{10,8},{9,1... | collective-permute-start | bytes 196616 | tf_op jit(solution)/shard_map/ppermute | solution.py:38
  4.5 9.5 %collective-permute-start = (bf16[128,256]{1,0:T(8,128)(2,1)}, bf16[128,256]{1,0:T(8,128)(2,1)S(1)}, u32[]{:S(2)}, u32[]{:S(2)}) collective-permute-start(bf16[128,256]{1,0:T(8,128)(2,1)} %g0), channel_id=1, source_target_pairs={{0,1},{1,0},{2,3},{3,2},{4,5},{5,4},{6,7},{7,6},{8,9},{9,8},{10,11... | collective-permute-start | bytes 196616 | tf_op jit(solution)/shard_map/ppermute | solution.py:38
  6.3 7.6 %collective-permute-start.2 = (bf16[128,256]{1,0:T(8,128)(2,1)S(1)}, bf16[128,256]{1,0:T(8,128)(2,1)S(1)}, u32[]{:S(2)}, u32[]{:S(2)}) collective-permute-start(bf16[128,256]{1,0:T(8,128)(2,1)S(1)} %collective-permute-done.1.g2), channel_id=1, source_target_pairs={{0,1},{1,0},{2,3},{3,2},{4,5},{5,4},{6,7},{7,6},{8,9},{9,8},{10,11... | collective-permute-start | bytes 196616 | tf_op jit(solution)/shard_map/ppermute | solution.py:38
  8.1 0.7 copy-start
  8.8 5.1 %copy-start.1 = (bf16[128,256]{1,0:T(8,128)(2,1)S(1)}, bf16[128,256]{1,0:T(8,128)(2,1)}, u32[]{:S(2)}) copy-start(bf16[128,256]{1,0:T(8,128)(2,1)} %g0) | copy-start | bytes 196612
  10.2 32.9 %collective-permute-start.3 = (bf16[8,256,256]{2,1,0:T(8,128)(2,1)S(1)}, bf16[8,256,256]{2,1,0:T(8,128)(2,1)S(1)}, u32[]{:S(2)}, u32[]{:S(2)}) collective-permute-start(bf16[8,256,256]{2,1,0:T(8,128)(2,1)S(1)} %far.1), channel_id=1, source_target_pairs={{0,8},{1,65},{4,12},{5,69},{8,0},{9,73},{12,4},{13,77},{32,40},{33... | collective-permute-start | bytes 3145736 | tf_op jit(solution)/shard_map/ppermute | solution.py:34
  16.1 39.8 %collective-permute-start.8 = (bf16[10,256,256]{2,1,0:T(8,128)(2,1)S(1)}, bf16[10,256,256]{2,1,0:T(8,128)(2,1)S(1)}, u32[]{:S(2)}, u32[]{:S(2)}) collective-permute-start(bf16[10,256,256]{2,1,0:T(8,128)(2,1)S(1)} %get-tuple-element.32), channel_id=1, source_target_pairs={{0,4},{1,33},{4,8},{5,37},{8,12},{9,41},{12,0},{13,45},{32,36},{33... | collective-permute-start | bytes 3932168 | tf_op jit(solution)/shard_map/ppermute | solution.py:34
  16.9 39.0 %collective-permute-start.9 = (bf16[10,256,256]{2,1,0:T(8,128)(2,1)S(1)}, bf16[10,256,256]{2,1,0:T(8,128)(2,1)S(1)}, u32[]{:S(2)}, u32[]{:S(2)}) collective-permute-start(bf16[10,256,256]{2,1,0:T(8,128)(2,1)S(1)} %get-tuple-element.33), channel_id=1, source_target_pairs={{0,12},{1,97},{4,0},{5,101},{8,4},{9,105},{12,8},{13,109},{32,44},... | collective-permute-start | bytes 3932168 | tf_op jit(solution)/shard_map/ppermute | solution.py:34
  18.8 24.2 %collective-permute-start.4 = (bf16[2,256,256]{2,1,0:T(8,128)(2,1)S(1)}, bf16[2,256,256]{2,1,0:T(8,128)(2,1)S(1)}, u32[]{:S(2)}, u32[]{:S(2)}) collective-permute-start(bf16[2,256,256]{2,1,0:T(8,128)(2,1)S(1)} %get-tuple-element.28.g0), channel_id=1, source_target_pairs={{0,8},{1,65},{4,12},{5,69},{8,0},{9,73},{12,4},{13,77},{32,40},{33... | collective-permute-start | bytes 786440 | tf_op jit(solution)/shard_map/ppermute | solution.py:34
  43.1 1.3 %copy-start.2 = (bf16[128,4,256]{2,1,0:T(4,128)(2,1)S(1)}, bf16[128,4,256]{2,1,0:T(4,128)(2,1)}, u32[]{:S(2)}) copy-start(bf16[128,4,256]{2,1,0:T(4,128)(2,1)} %param.4) | copy-start | bytes 786436
  44.4 9.1 %collective-permute-start.6 = (bf16[128,1024]{1,0:T(8,128)(2,1)S(1)}, bf16[128,1024]{1,0:T(8,128)(2,1)S(1)}, u32[]{:S(2)}, u32[]{:S(2)}) collective-permute-start(bf16[128,1024]{1,0:T(8,128)(2,1)S(1)} %bitcast.4), channel_id=1, source_target_pairs={{0,2},{2,0},{1,3},{3,1},{4,6},{6,4},{5,7},{7,5},{8,10},{10,8},{9,1... | collective-permute-start | bytes 786440 | tf_op jit(solution)/shard_map/ppermute | solution.py:38
  47.5 7.3 %collective-permute-start.5 = (bf16[128,1024]{1,0:T(8,128)(2,1)S(1)}, bf16[128,1024]{1,0:T(8,128)(2,1)S(1)}, u32[]{:S(2)}, u32[]{:S(2)}) collective-permute-start(bf16[128,1024]{1,0:T(8,128)(2,1)S(1)} %bitcast.5), channel_id=1, source_target_pairs={{0,1},{1,0},{2,3},{3,2},{4,5},{5,4},{6,7},{7,6},{8,9},{9,8},{10,11... | collective-permute-start | bytes 786440 | tf_op jit(solution)/shard_map/ppermute | solution.py:38
  53.5 2.4 %collective-permute-start.7 = (bf16[128,1024]{1,0:T(8,128)(2,1)S(1)}, bf16[128,1024]{1,0:T(8,128)(2,1)S(1)}, u32[]{:S(2)}, u32[]{:S(2)}) collective-permute-start(bf16[128,1024]{1,0:T(8,128)(2,1)S(1)} %collective-permute-done.6.refs_10_), channel_id=1, source_target_pairs={{0,1},{1,0},{2,3},{3,2},{4,5},{5,4},{6,7},{7,6},{8,9},{9,8},{10,11... | collective-permute-start | bytes 786440 | tf_op jit(solution)/shard_map/ppermute | solution.py:38
  57.3 12.7 %collective-permute-start.10 = (bf16[512,512]{1,0:T(8,128)(2,1)S(1)}, bf16[512,512]{1,0:T(8,128)(2,1)S(1)}, u32[]{:S(2)}, u32[]{:S(2)}) collective-permute-start(bf16[512,512]{1,0:T(8,128)(2,1)S(1)} %get-tuple-element.35), channel_id=1, source_target_pairs={{0,32},{1,5},{4,36},{5,9},{8,40},{9,13},{12,44},{13,1},{32,64},{33... | collective-permute-start | bytes 1572872 | tf_op jit(solution)/shard_map/ppermute | solution.py:34
  58.5 15.1 %collective-permute-start.11 = (bf16[512,512]{1,0:T(8,128)(2,1)S(1)}, bf16[512,512]{1,0:T(8,128)(2,1)S(1)}, u32[]{:S(2)}, u32[]{:S(2)}) collective-permute-start(bf16[512,512]{1,0:T(8,128)(2,1)S(1)} %get-tuple-element.36), channel_id=1, source_target_pairs={{0,64},{1,9},{4,68},{5,13},{8,72},{9,1},{12,76},{13,5},{32,96},{33... | collective-permute-start | bytes 1572872 | tf_op jit(solution)/shard_map/ppermute | solution.py:34
  61.0 14.6 %collective-permute-start.12 = (bf16[512,512]{1,0:T(8,128)(2,1)S(1)}, bf16[512,512]{1,0:T(8,128)(2,1)S(1)}, u32[]{:S(2)}, u32[]{:S(2)}) collective-permute-start(bf16[512,512]{1,0:T(8,128)(2,1)S(1)} %get-tuple-element.37), channel_id=1, source_target_pairs={{0,96},{1,13},{4,100},{5,1},{8,104},{9,5},{12,108},{13,9},{32,0},{... | collective-permute-start | bytes 1572872 | tf_op jit(solution)/shard_map/ppermute | solution.py:34
  62.1 4.8 %collective-permute-start.13 = (bf16[2,256,256]{2,1,0:T(8,128)(2,1)S(1)}, bf16[2,256,256]{2,1,0:T(8,128)(2,1)S(1)}, u32[]{:S(2)}, u32[]{:S(2)}) collective-permute-start(bf16[2,256,256]{2,1,0:T(8,128)(2,1)S(1)} %get-tuple-element.38), channel_id=1, source_target_pairs={{1,0},{3,2},{5,4},{7,6},{9,8},{11,10},{13,12},{15,14},{17,16},{19,... | collective-permute-start | bytes 786440 | tf_op jit(solution)/shard_map/ppermute | solution.py:319
  66.9 15.9 %collective-permute-start.16 = (bf16[2,256,256]{2,1,0:T(8,128)(2,1)S(1)}, bf16[2,256,256]{2,1,0:T(8,128)(2,1)S(1)}, u32[]{:S(2)}, u32[]{:S(2)}) collective-permute-start(bf16[2,256,256]{2,1,0:T(8,128)(2,1)S(1)} %picked.1.refs_0_), channel_id=1, source_target_pairs={{0,12},{4,0},{8,4},{12,8},{1,13},{5,1},{9,5},{13,9},{2,14},{6,2},{... | collective-permute-start | bytes 786440 | tf_op jit(solution)/shard_map/ppermute | solution.py:321
  69.4 13.4 %collective-permute-start.15 = (bf16[2,256,256]{2,1,0:T(8,128)(2,1)S(1)}, bf16[2,256,256]{2,1,0:T(8,128)(2,1)S(1)}, u32[]{:S(2)}, u32[]{:S(2)}) collective-permute-start(bf16[2,256,256]{2,1,0:T(8,128)(2,1)S(1)} %picked.1.refs_0_), channel_id=1, source_target_pairs={{0,8},{4,12},{8,0},{12,4},{1,9},{5,13},{9,1},{13,5},{2,10},{6,14},... | collective-permute-start | bytes 786440 | tf_op jit(solution)/shard_map/ppermute | solution.py:321
  69.9 14.8 %collective-permute-start.14 = (bf16[2,256,256]{2,1,0:T(8,128)(2,1)S(1)}, bf16[2,256,256]{2,1,0:T(8,128)(2,1)S(1)}, u32[]{:S(2)}, u32[]{:S(2)}) collective-permute-start(bf16[2,256,256]{2,1,0:T(8,128)(2,1)S(1)} %picked.1.refs_0_), channel_id=1, source_target_pairs={{0,4},{4,8},{8,12},{12,0},{1,5},{5,9},{9,13},{13,1},{2,6},{6,10},{... | collective-permute-start | bytes 786440 | tf_op jit(solution)/shard_map/ppermute | solution.py:321
  76.7 39.4 %all-to-all-start = ((bf16[8,128,256]{2,1,0:T(8,128)(2,1)}), bf16[8,128,256]{2,1,0:T(8,128)(2,1)S(1)}, u32[]{:S(2)}, u32[]{:S(2)}) async-start(bf16[8,128,256]{2,1,0:T(8,128)(2,1)} %summed.1), calls=%async_computation | async-start | bytes 1048576 | tf_op jit(solution)/shard_map/all_to_all | solution.py:316
  81.3 13.6 %collective-permute-start.17 = (bf16[2,256,256]{2,1,0:T(8,128)(2,1)S(1)}, bf16[2,256,256]{2,1,0:T(8,128)(2,1)S(1)}, u32[]{:S(2)}, u32[]{:S(2)}) collective-permute-start(bf16[2,256,256]{2,1,0:T(8,128)(2,1)S(1)} %picked.1.refs_0_), channel_id=1, source_target_pairs={{0,16},{16,0},{1,17},{17,1},{2,18},{18,2},{3,19},{19,3},{4,20},{20... | collective-permute-start | bytes 786440 | tf_op jit(solution)/shard_map/ppermute | solution.py:38
  82.7 17.8 %collective-permute-start.20 = (bf16[2,256,256]{2,1,0:T(8,128)(2,1)S(1)}, bf16[2,256,256]{2,1,0:T(8,128)(2,1)S(1)}, u32[]{:S(2)}, u32[]{:S(2)}) collective-permute-start(bf16[2,256,256]{2,1,0:T(8,128)(2,1)S(1)} %collective-permute-done.16.refs_3_), channel_id=1, source_target_pairs={{0,16},{16,0},{1,17},{17,1},{2,18},{18,2},{3,19},{19,3},{4,20},{20... | collective-permute-start | bytes 786440 | tf_op jit(solution)/shard_map/ppermute | solution.py:38
  82.8 23.4 %collective-permute-start.19 = (bf16[2,256,256]{2,1,0:T(8,128)(2,1)S(1)}, bf16[2,256,256]{2,1,0:T(8,128)(2,1)S(1)}, u32[]{:S(2)}, u32[]{:S(2)}) collective-permute-start(bf16[2,256,256]{2,1,0:T(8,128)(2,1)S(1)} %collective-permute-done.15.refs_2_), channel_id=1, source_target_pairs={{0,16},{16,0},{1,17},{17,1},{2,18},{18,2},{3,19},{19,3},{4,20},{20... | collective-permute-start | bytes 786440 | tf_op jit(solution)/shard_map/ppermute | solution.py:38
  84.8 27.0 %collective-permute-start.18 = (bf16[2,256,256]{2,1,0:T(8,128)(2,1)S(1)}, bf16[2,256,256]{2,1,0:T(8,128)(2,1)S(1)}, u32[]{:S(2)}, u32[]{:S(2)}) collective-permute-start(bf16[2,256,256]{2,1,0:T(8,128)(2,1)S(1)} %collective-permute-done.14.refs_1_), channel_id=1, source_target_pairs={{0,16},{16,0},{1,17},{17,1},{2,18},{18,2},{3,19},{19,3},{4,20},{20... | collective-permute-start | bytes 786440 | tf_op jit(solution)/shard_map/ppermute | solution.py:38

commit v4 on v3

--- a/solution.py
+++ b/solution.py
@@ -40,7 +40,6 @@
 
 LIMIT = pltpu.CompilerParams(vmem_limit_bytes=12 << 20)
 EARLY = int(2e9)
-NEAR = int(20e9)
 IN = pl.BlockSpec(memory_space=VM)
 HBM = pl.BlockSpec(memory_space=pltpu.HBM)
 
@@ -63,7 +62,7 @@
     )
 
 
-def scale_into(outs, w_ref, s_ref, wide_ref, sems, between=None):
+def scale_into(outs, w_ref, s_ref, wide_ref, sems):
     c, first, _ = roles()
     copies = []
     for j, (k, o_ref) in enumerate(outs):
@@ -76,8 +75,6 @@
             copy.start()
             copies.append((copy, o_ref, i, z, x))
     spread_scales(s_ref, wide_ref)
-    if between is not None:
-        between()
     for copy, o_ref, i, z, x in copies:
         copy.wait()
         for yl in range(2):
@@ -87,46 +84,62 @@
             o_ref[2 * i + yl] = (w * s[:, None, :]).reshape(256, 256).astype(BF)
 
 
-def far_body(w_ref, s_ref, o_ref, wide_ref, sems):
-    scale_into([(2, o_ref)], w_ref, s_ref, wide_ref, sems)
-
-
-def far_rows(w5, scales_t):
-    return pl.pallas_call(
-        far_body,
-        out_shape=VM((8, 256, 256), BF),
+def scale_body(w_ref, s_ref, *refs):
+    outs, wide_ref, sems = refs[:4], refs[4], refs[5]
+    scale_into([(k, outs[k]) for k in (2, 1, 3, 0)], w_ref, s_ref, wide_ref, sems)
+
+
+def scaled_rows(w5, scales_t):
+    return pl.pallas_call(
+        scale_body,
+        out_shape=[VM((8, 256, 256), BF)] * 4,
         in_specs=[HBM, IN],
-        out_specs=IN,
-        scratch_shapes=[VM((512, 256), F32), pltpu.SemaphoreType.DMA((4,))],
-        compiler_params=LIMIT,
-        name="far",
+        out_specs=[IN] * 4,
+        scratch_shapes=[VM((512, 256), F32), pltpu.SemaphoreType.DMA((16,))],
+        compiler_params=LIMIT,
+        name="scale",
     )(w5, scales_t)
 
 
-def near_body(w_ref, s_ref, g0, g1, g2, g3, o1, o3, o0, og, wide_ref, sems):
+def packed_body(g_ref, h_ref, o_ref):
+    o_ref[0] = g_ref[...]
+    h = h_ref[...].reshape(128, 1024)
+    for n in range(4):
+        o_ref[1 + n] = h[:, n * 256 : (n + 1) * 256]
+
+
+def packed(grad_out, hidden):
+    return pl.pallas_call(
+        packed_body,
+        out_shape=VM((5, 128, 256), BF),
+        in_specs=[IN] * 2,
+        out_specs=IN,
+        compiler_params=LIMIT,
+        name="packed",
+    )(grad_out, hidden)
+
+
+def tokens_body(p0, p1, p2, p3, g_ref, h_ref):
     n = lax.axis_index("yh") * 2 + lax.axis_index("c")
-
-    def tokens():
-        for r, g in enumerate((g0, g1, g2, g3)):
-            t = n ^ r
-            og[t >> 1, pl.ds(pl.multiple_of((t & 1) * 128, 128), 128), :] = g[...]
-        o1[8:10] = og[...]
-        o3[8:10] = og[...]
-
-    scale_into([(1, o1), (3, o3), (0, o0)], w_ref, s_ref, wide_ref, sems, tokens)
-
-
-def near_rows(w5, scales_t, pieces):
-    return pl.pallas_call(
-        near_body,
-        out_shape=[VM((10, 256, 256), BF)] * 2 + [VM((8, 256, 256), BF), VM((2, 256, 256), BF)],
-        in_specs=[HBM] + [IN] * 5,
-        out_specs=[IN] * 4,
-        scratch_shapes=[VM((512, 256), F32), pltpu.SemaphoreType.DMA((12,))],
-        compiler_params=LIMIT,
-        cost_estimate=pl.CostEstimate(flops=NEAR, bytes_accessed=8 << 20, transcendentals=0),
-        name="near",
-    )(w5, scales_t, *pieces)
+    for r, p in enumerate((p0, p1, p2, p3)):
+        t = n ^ r
+        g_ref[t >> 1, pl.ds(pl.multiple_of((t & 1) * 128, 128), 128), :] = p[0]
+        rows = pl.ds(pl.multiple_of(t * 128, 128), 128)
+        for m in range(4):
+            h_ref[rows, m * 256 : (m + 1) * 256] = p[1 + m]
+
+
+def all_tokens(own):
+    far = swap(own, "yh")
+    pieces = [own, swap(own, "c"), far, swap(far, "c")]
+    return pl.pallas_call(
+        tokens_body,
+        out_shape=[VM((2, 256, 256), BF), VM((512, 1024), BF)],
+        in_specs=[IN] * 4,
+        out_specs=[IN] * 2,
+        compiler_params=LIMIT,
+        name="tokens",
+    )(*kept(*pieces))
 
 
 def block_product(g, w, q):
@@ -155,11 +168,11 @@
     )(*kept(*operands))
 
 
-def partial_body(acc, r1, r3, g0, g2, *outs):
+def partial_body(acc, r1, r3, g0, g1, g2, g3, *outs):
     keep, give = outs[4:]
     _, _, second = roles()
     z, yh = lax.axis_index("z"), lax.axis_index("yh")
-    g = (g0, r1.at[8:10], g2, r3.at[8:10])
+    g = (g0, g1, g2, g3)
     for k in range(4):
 
         @pl.when(((z - 2 * yh) & 3) == k)
@@ -182,7 +195,7 @@
         out_shape=[VM((512, 512), F32)]
         + [VM((512, 512), BF)] * 3
         + [VM((2, 256, 256), BF)] * 2,
-        in_specs=[IN] * 5,
+        in_specs=[IN] * 7,
         out_specs=[IN] * 6,
         compiler_params=LIMIT,
         name="partial",
@@ -247,11 +260,8 @@
 
 
 def outer_body(*refs):
-    g, pieces, o_ref, h_ref, buf, sems = refs[:8], refs[8:12], *refs[12:]
+    g, (h_ref, o_ref, buf, sems) = refs[:8], refs[8:]
     yl, x = lax.axis_index("yl"), lax.axis_index("x")
-    n = lax.axis_index("yh") * 2 + lax.axis_index("c")
-    for r, piece in enumerate(pieces):
-        h_ref[pl.ds(pl.multiple_of((n ^ r) * 128, 128), 128), :] = piece[...]
     copies = []
     for i in range(8):
         here = yl if i < 4 else 1 - yl
@@ -270,45 +280,35 @@
         copy.wait()
 
 
-def outer_product(blocks, pieces):
+def outer_product(blocks, hidden):
     return pl.pallas_call(
         outer_body,
         out_shape=jax.ShapeDtypeStruct((2048, 4, 256), BF),
-        in_specs=[IN] * 12,
+        in_specs=[IN] * 9,
         out_specs=HBM,
         scratch_shapes=[
-            VM((512, 1024), BF),
             VM((8, 256, 4, 256), BF),
             pltpu.SemaphoreType.DMA((8,)),
         ],
         compiler_params=LIMIT,
         name="outer",
-    )(*kept(*blocks, *pieces))
-
-
-def token_pieces(own):
-    far = swap(own, "yh")
-    return [own, swap(own, "c"), far, swap(far, "c")]
+    )(*kept(*blocks, hidden))
 
 
 def per_device(hidden, grad_out, weight_base, block_scale):
     w5 = pltpu.with_memory_space_constraint(weight_base.reshape(4, 2, 4, 256, 256), pltpu.HBM)
     scales_t = block_scale.T
 
-    tokens = token_pieces(grad_out)
-    sent2 = far_rows(w5, scales_t)
-    r2 = shift(sent2, first_axis_steps(2))
-    tokens, _ = lax.optimization_barrier((tokens, sent2))
-    sent1, sent3, r0, g0 = near_rows(w5, scales_t, tokens)
-    r1 = shift(sent1, first_axis_steps(1))
-    r3 = shift(sent3, first_axis_steps(3))
-    g2 = shift(g0, first_axis_steps(2))
+    sent = scaled_rows(w5, scales_t)
+    r0 = sent[0]
+    r1, r2, r3 = [shift(sent[k], first_axis_steps(k)) for k in (1, 2, 3)]
+
+    grad_out, hidden, _ = lax.optimization_barrier((grad_out, hidden, r0))
+    g0, h = all_tokens(packed(grad_out, hidden))
+    g1, g2, g3 = [shift(g0, first_axis_steps(k)) for k in (1, 2, 3)]
 
     acc = early_sums(r0, r2, g0, g2)
-    h, acc = lax.optimization_barrier((hidden, acc))
-    pieces = token_pieces(h.reshape(128, 1024))
-    acc, pieces = lax.optimization_barrier((acc, pieces))
-    *sums, keep, give = partial_sums(acc, r1, r3, g0, g2)
+    *sums, keep, give = partial_sums(acc, r1, r3, g0, g1, g2, g3)
     parts = [sums[0]] + [None] * 3
     for k in (2, 1, 3):
         parts[k] = shift(sums[k], second_axis_steps(k))
@@ -320,7 +320,7 @@
     ring = lambda k: [(i, (i + k) % 4) for i in range(4)]
     mine = [seed] + [lax.ppermute(seed, "x", ring(k)) for k in (1, 2, 3)]
     theirs = [swap(m, "yl") for m in mine]
-    grad_weight = outer_product(mine + theirs, pieces)
+    grad_weight = outer_product(mine + theirs, h)
     return grad_hidden, grad_weight
 
 

time: 119 us -> 104 us (0.87); the launches traced: 117 us -> 104 us
  waiting for transfers between devices: 64.3 us -> 52 us
    ppermute x7 -> x9, waiting for transfers between devices: 29.4 us -> 18.8 us  [shift(): return lax.ppermute(value, ('z', 'x', 'c'), pairs)]
    ppermute x10 -> x7, starting transfers between devices: 15.7 us -> 8.67 us  [swap(): return lax.ppermute(value, axis, [(0, 1), (1, 0)])]
    ppermute x7 -> x9, starting transfers between devices: 11.3 us -> 15.8 us  [shift(): return lax.ppermute(value, ('z', 'x', 'c'), pairs)]
    all_to_all x1, starting transfers between devices: 4.64 us -> 6.95 us  [per_device(): blocks = lax.all_to_all(blocks, ('yl', 'yh', 'c'), 0, 0, tiled=True)]
    ppermute x1, starting transfers between devices: 3.62 us -> 5.37 us  [per_device(): seed = picked(lax.ppermute(give, 'c', [(1, 0)]), keep)]
    ppermute x3, starting transfers between devices: 3.67 us -> 2.46 us  [per_device(): mine = [seed] + [lax.ppermute(seed, 'x', ring(k)) for k in (1, 2, 3)]]
    ppermute x10 -> x7, waiting for transfers between devices: 33.2 us -> 32.1 us  [swap(): return lax.ppermute(value, axis, [(0, 1), (1, 0)])]
    pallas_call x2 -> x3, Pallas kernels: 3.46 us -> 2.56 us  [the longest x1 2.36 us: scaled_rows(): pl.pallas_call(scale_body, out_shape=[VM((8, 256, 256), BF)] * 4, in_spec...]
  transfers between devices with their start and end apart: 22 -> 21, of which waited for: 12 -> 12; matrix products, arithmetic and copies ran while one was open for 0% -> 0% of each run, Pallas kernels for 9% -> 7%
where the time goes in v4:
time: 104 us
  waiting for transfers between devices  52 us (50%)
  starting transfers between devices  39.2 us (38%)
  Pallas kernels  11.4 us (11%)
    ppermute x7, waiting for transfers between devices, swap(): return lax.ppermute(value, axis, [(0, 1), (1, 0)])  32.1 us
    ppermute x9, waiting for transfers between devices, shift(): return lax.ppermute(value, ('z', 'x', 'c'), pairs)  18.8 us
    ppermute x9, starting transfers between devices, shift(): return lax.ppermute(value, ('z', 'x', 'c'), pairs)  15.8 us
    ppermute x7, starting transfers between devices, swap(): return lax.ppermute(value, axis, [(0, 1), (1, 0)])  8.67 us
    all_to_all x1, starting transfers between devices, per_device(): blocks = lax.all_to_all(blocks, ('yl', 'yh', 'c'), 0, 0, tiled=True)  6.95 us
    ppermute x1, starting transfers between devices, per_device(): seed = picked(lax.ppermute(give, 'c', [(1, 0)]), keep)  5.37 us
    pallas_call x1, Pallas kernels, outer_product(): pl.pallas_call(outer_body, out_shape=jax.ShapeDtypeStruct((2048, 4, 256),...  4.29 us
    ppermute x3, starting transfers between devices, per_device(): mine = [seed] + [lax.ppermute(seed, 'x', ring(k)) for k in (1, 2, 3)]  2.46 us
  transfers between devices with their start and end apart: 21, of which 12 were waited for; matrix products, arithmetic and copies ran while one was open for 0% of the time, Pallas kernels for 7%

profile of v4, /device:TPU:1, one launch (start us, length us, event | category | flops | bytes accessed | tf_op | source)
XLA Modules:
  0.0 104.2 jit_solution(6087628067849756601)
XLA Ops:
  0.7 0.8 copy-done.2
  1.4 2.4 %scale.1 = (bf16[8,256,256]{2,1,0:T(8,128)(2,1)S(1)}, bf16[8,256,256]{2,1,0:T(8,128)(2,1)S(1)}, bf16[8,256,256]{2,1,0:T(8,128)(2,1)S(1)}, bf16[8,256,256]{2,1,0:T(8,128)(2,1)S(1)}) custom-call(bf16[4,2,4,256,256]{4,3,2,1,0:T(8,128)(2,1)} %bitcast.3, bf16[16,512]{1,0:T(8,128)(2,1)S(1)} %bitcast.2), custom_call_target="tpu_custom_call" | custom-call | tf_op jit(solution)/shard_map/scale/pallas_call | solution.py:93
  3.8 4.5 %collective-permute-start = (bf16[8,256,256]{2,1,0:T(8,128)(2,1)S(1)}, bf16[8,256,256]{2,1,0:T(8,128)(2,1)S(1)}, u32[]{:S(2)}, u32[]{:S(2)}) collective-permute-start(bf16[8,256,256]{2,1,0:T(8,128)(2,1)S(1)} %get-tuple-element.17), channel_id=1, source_target_pairs={{0,8},{1,65},{4,12},{5,69},{8,0},{9,73},{12,4},{13,77},{32,40},{33... | collective-permute-start | bytes 3145736 | tf_op jit(solution)/shard_map/ppermute | solution.py:34
  8.3 0.1 packed.1.p0
  8.4 3.0 %collective-permute-start.2 = (bf16[5,128,256]{2,1,0:T(8,128)(2,1)S(1)}, bf16[5,128,256]{2,1,0:T(8,128)(2,1)S(1)}, u32[]{:S(2)}, u32[]{:S(2)}) collective-permute-start(bf16[5,128,256]{2,1,0:T(8,128)(2,1)S(1)} %packed.1.p0), channel_id=1, source_target_pairs={{0,2},{2,0},{1,3},{3,1},{4,6},{6,4},{5,7},{7,5},{8,10},{10,8},{9,1... | collective-permute-start | bytes 983048 | tf_op jit(solution)/shard_map/ppermute | solution.py:38
  11.4 0.7 collective-permute-start.5
  12.1 2.0 %collective-permute-start.6 = (bf16[8,256,256]{2,1,0:T(8,128)(2,1)S(1)}, bf16[8,256,256]{2,1,0:T(8,128)(2,1)S(1)}, u32[]{:S(2)}, u32[]{:S(2)}) collective-permute-start(bf16[8,256,256]{2,1,0:T(8,128)(2,1)S(1)} %get-tuple-element.22), channel_id=1, source_target_pairs={{0,12},{1,97},{4,0},{5,101},{8,4},{9,105},{12,8},{13,109},{32,44},... | collective-permute-start | bytes 3145736 | tf_op jit(solution)/shard_map/ppermute | solution.py:34
  14.1 0.9 collective-permute-start.1
  15.0 4.2 %collective-permute-done.2.p2 = bf16[5,128,256]{2,1,0:T(8,128)(2,1)S(1)} collective-permute-done((bf16[5,128,256]{2,1,0:T(8,128)(2,1)S(1)}, bf16[5,128,256]{2,1,0:T(8,128)(2,1)S(1)}, u32[]{:S(2)}, u32[]{:S(2)}) %collective-permute-start.2) | collective-permute-done | bytes 327712 | tf_op jit(solution)/shard_map/ppermute | solution.py:38
  19.2 0.9 collective-permute-start.3
  20.1 0.0 collective-permute-done.1.p1
  20.1 1.3 %collective-permute-done.3.p3 = bf16[5,128,256]{2,1,0:T(8,128)(2,1)S(1)} collective-permute-done((bf16[5,128,256]{2,1,0:T(8,128)(2,1)S(1)}, bf16[5,128,256]{2,1,0:T(8,128)(2,1)S(1)}, u32[]{:S(2)}, u32[]{:S(2)}) %collective-permute-start.3) | collective-permute-done | bytes 327712 | tf_op jit(solution)/shard_map/ppermute | solution.py:38
  21.4 0.1 tokens.1
  21.5 0.7 collective-permute-start.4
  22.2 2.5 %collective-permute-start.8 = (bf16[2,256,256]{2,1,0:T(8,128)(2,1)S(1)}, bf16[2,256,256]{2,1,0:T(8,128)(2,1)S(1)}, u32[]{:S(2)}, u32[]{:S(2)}) collective-permute-start(bf16[2,256,256]{2,1,0:T(8,128)(2,1)S(1)} %get-tuple-element.20.g0), channel_id=1, source_target_pairs={{0,12},{1,97},{4,0},{5,101},{8,4},{9,105},{12,8},{13,109},{32,44},... | collective-permute-start | bytes 786440 | tf_op jit(solution)/shard_map/ppermute | solution.py:34
  24.7 10.2 %collective-permute-done.4.g2 = bf16[2,256,256]{2,1,0:T(8,128)(2,1)S(1)} collective-permute-done((bf16[2,256,256]{2,1,0:T(8,128)(2,1)S(1)}, bf16[2,256,256]{2,1,0:T(8,128)(2,1)S(1)}, u32[]{:S(2)}, u32[]{:S(2)}) %collective-permute-start.4) | collective-permute-done | bytes 262176 | tf_op jit(solution)/shard_map/ppermute | solution.py:34
  34.9 1.0 %collective-permute-start.7 = (bf16[2,256,256]{2,1,0:T(8,128)(2,1)S(1)}, bf16[2,256,256]{2,1,0:T(8,128)(2,1)S(1)}, u32[]{:S(2)}, u32[]{:S(2)}) collective-permute-start(bf16[2,256,256]{2,1,0:T(8,128)(2,1)S(1)} %get-tuple-element.20.g0), channel_id=1, source_target_pairs={{0,4},{1,33},{4,8},{5,37},{8,12},{9,41},{12,0},{13,45},{32,36},{33... | collective-permute-start | bytes 786440 | tf_op jit(solution)/shard_map/ppermute | solution.py:34
  35.9 0.0 collective-permute-done.r2
  35.9 1.3 %early.1.acc = f32[4,512,512]{2,1,0:T(8,128)S(1)} custom-call(bf16[8,256,256]{2,1,0:T(8,128)(2,1)S(1)} %get-tuple-element.16.r0, bf16[8,256,256]{2,1,0:T(8,128)(2,1)S(1)} %collective-permute-done.r2, bf16[2,256,256]{2,1,0:T(8,128)(2,1)S(1)} %get-tuple-element.20.g0, bf16[2,256,256]{2,1,0:T(8,128)(2,1)S(1)} %collective-permute-done.4.g2), custom_call_target="tpu_custom_call" | custom-call | flops 2000000000 | bytes 6291456 | tf_op jit(solution)/shard_map/early/pallas_call | solution.py:160
  37.2 1.1 %collective-permute-done.8.g3 = bf16[2,256,256]{2,1,0:T(8,128)(2,1)S(1)} collective-permute-done((bf16[2,256,256]{2,1,0:T(8,128)(2,1)S(1)}, bf16[2,256,256]{2,1,0:T(8,128)(2,1)S(1)}, u32[]{:S(2)}, u32[]{:S(2)}) %collective-permute-start.8) | collective-permute-done | bytes 262176 | tf_op jit(solution)/shard_map/ppermute | solution.py:34
  38.3 3.8 %collective-permute-done.7.g1 = bf16[2,256,256]{2,1,0:T(8,128)(2,1)S(1)} collective-permute-done((bf16[2,256,256]{2,1,0:T(8,128)(2,1)S(1)}, bf16[2,256,256]{2,1,0:T(8,128)(2,1)S(1)}, u32[]{:S(2)}, u32[]{:S(2)}) %collective-permute-start.7) | collective-permute-done | bytes 262176 | tf_op jit(solution)/shard_map/ppermute | solution.py:34
  42.1 0.0 collective-permute-done.5.r1
  42.1 1.3 %partial.1 = (f32[512,512]{1,0:T(8,128)S(1)}, bf16[512,512]{1,0:T(8,128)(2,1)S(1)}, bf16[512,512]{1,0:T(8,128)(2,1)S(1)}, bf16[512,512]{1,0:T(8,128)(2,1)S(1)}, ...) custom-call(f32[4,512,512]{2,1,0:T(8,128)S(1)} %early.1.acc, ...), custom_call_target="tpu_custom_call" | custom-call | tf_op jit(solution)/shard_map/partial/pallas_call | solution.py:193
  43.4 0.8 collective-permute-start.9
  44.2 2.7 %collective-permute-start.10 = (bf16[512,512]{1,0:T(8,128)(2,1)S(1)}, bf16[512,512]{1,0:T(8,128)(2,1)S(1)}, u32[]{:S(2)}, u32[]{:S(2)}) collective-permute-start(bf16[512,512]{1,0:T(8,128)(2,1)S(1)} %get-tuple-element.25), channel_id=1, source_target_pairs={{0,64},{1,9},{4,68},{5,13},{8,72},{9,1},{12,76},{13,5},{32,96},{33... | collective-permute-start | bytes 1572872 | tf_op jit(solution)/shard_map/ppermute | solution.py:34
  46.9 0.9 collective-permute-start.11
  47.8 5.4 %collective-permute-start.12 = (bf16[2,256,256]{2,1,0:T(8,128)(2,1)S(1)}, bf16[2,256,256]{2,1,0:T(8,128)(2,1)S(1)}, u32[]{:S(2)}, u32[]{:S(2)}) collective-permute-start(bf16[2,256,256]{2,1,0:T(8,128)(2,1)S(1)} %get-tuple-element.27), channel_id=1, source_target_pairs={{1,0},{3,2},{5,4},{7,6},{9,8},{11,10},{13,12},{15,14},{17,16},{19,... | collective-permute-start | bytes 786440 | tf_op jit(solution)/shard_map/ppermute | solution.py:319
  53.2 1.1 %collective-permute-done.12.a_ref = bf16[2,256,256]{2,1,0:T(8,128)(2,1)S(1)} collective-permute-done((bf16[2,256,256]{2,1,0:T(8,128)(2,1)S(1)}, bf16[2,256,256]{2,1,0:T(8,128)(2,1)S(1)}, u32[]{:S(2)}, u32[]{:S(2)}) %collective-permute-start.12) | collective-permute-done | bytes 262176 | tf_op jit(solution)/shard_map/ppermute | solution.py:319
  54.3 1.4 %collective-permute-start.15 = (bf16[2,256,256]{2,1,0:T(8,128)(2,1)S(1)}, bf16[2,256,256]{2,1,0:T(8,128)(2,1)S(1)}, u32[]{:S(2)}, u32[]{:S(2)}) collective-permute-start(bf16[2,256,256]{2,1,0:T(8,128)(2,1)S(1)} %picked.1.refs_0_), channel_id=1, source_target_pairs={{0,12},{4,0},{8,4},{12,8},{1,13},{5,1},{9,5},{13,9},{2,14},{6,2},{... | collective-permute-start | bytes 786440 | tf_op jit(solution)/shard_map/ppermute | solution.py:321
  55.8 0.5 collective-permute-start.14
  56.3 0.0 collective-permute-done.9.b
  56.3 0.5 collective-permute-start.13
  56.8 2.6 %collective-permute-done.10.c = bf16[512,512]{1,0:T(8,128)(2,1)S(1)} collective-permute-done((bf16[512,512]{1,0:T(8,128)(2,1)S(1)}, bf16[512,512]{1,0:T(8,128)(2,1)S(1)}, u32[]{:S(2)}, u32[]{:S(2)}) %collective-permute-start.10) | collective-permute-done | bytes 524320 | tf_op jit(solution)/shard_map/ppermute | solution.py:34
  59.4 1.2 %collective-permute-done.11.d = bf16[512,512]{1,0:T(8,128)(2,1)S(1)} collective-permute-done((bf16[512,512]{1,0:T(8,128)(2,1)S(1)}, bf16[512,512]{1,0:T(8,128)(2,1)S(1)}, u32[]{:S(2)}, u32[]{:S(2)}) %collective-permute-start.11) | collective-permute-done | bytes 524320 | tf_op jit(solution)/shard_map/ppermute | solution.py:34
  60.6 1.0 summed.1
  61.6 6.9 %all-to-all-start = ((bf16[8,128,256]{2,1,0:T(8,128)(2,1)}), bf16[8,128,256]{2,1,0:T(8,128)(2,1)S(1)}, u32[]{:S(2)}, u32[]{:S(2)}) async-start(bf16[8,128,256]{2,1,0:T(8,128)(2,1)} %summed.1), calls=%async_computation | async-start | bytes 1048576 | tf_op jit(solution)/shard_map/all_to_all | solution.py:316
  68.5 1.4 %collective-permute-start.16 = (bf16[2,256,256]{2,1,0:T(8,128)(2,1)S(1)}, bf16[2,256,256]{2,1,0:T(8,128)(2,1)S(1)}, u32[]{:S(2)}, u32[]{:S(2)}) collective-permute-start(bf16[2,256,256]{2,1,0:T(8,128)(2,1)S(1)} %picked.1.refs_0_), channel_id=1, source_target_pairs={{0,16},{16,0},{1,17},{17,1},{2,18},{18,2},{3,19},{19,3},{4,20},{20... | collective-permute-start | bytes 786440 | tf_op jit(solution)/shard_map/ppermute | solution.py:38
  69.9 0.0 collective-permute-done.15.refs_3_
  69.9 0.1 collective-permute-start.19
  70.0 0.0 collective-permute-done.14.refs_2_
  70.0 1.4 %collective-permute-start.18 = (bf16[2,256,256]{2,1,0:T(8,128)(2,1)S(1)}, bf16[2,256,256]{2,1,0:T(8,128)(2,1)S(1)}, u32[]{:S(2)}, u32[]{:S(2)}) collective-permute-start(bf16[2,256,256]{2,1,0:T(8,128)(2,1)S(1)} %collective-permute-done.14.refs_2_), channel_id=1, source_target_pairs={{0,16},{16,0},{1,17},{17,1},{2,18},{18,2},{3,19},{19,3},{4,20},{20... | collective-permute-start | bytes 786440 | tf_op jit(solution)/shard_map/ppermute | solution.py:38
  71.4 1.0 collective-permute-start.17
  72.4 9.7 %collective-permute-done.16.refs_4_ = bf16[2,256,256]{2,1,0:T(8,128)(2,1)S(1)} collective-permute-done((bf16[2,256,256]{2,1,0:T(8,128)(2,1)S(1)}, bf16[2,256,256]{2,1,0:T(8,128)(2,1)S(1)}, u32[]{:S(2)}, u32[]{:S(2)}) %collective-permute-start.16) | collective-permute-done | bytes 262176 | tf_op jit(solution)/shard_map/ppermute | solution.py:38
  82.1 5.6 %collective-permute-done.19.refs_7_ = bf16[2,256,256]{2,1,0:T(8,128)(2,1)S(1)} collective-permute-done((bf16[2,256,256]{2,1,0:T(8,128)(2,1)S(1)}, bf16[2,256,256]{2,1,0:T(8,128)(2,1)S(1)}, u32[]{:S(2)}, u32[]{:S(2)}) %collective-permute-start.19) | collective-permute-done | bytes 262176 | tf_op jit(solution)/shard_map/ppermute | solution.py:38
  87.8 5.6 %collective-permute-done.18.refs_6_ = bf16[2,256,256]{2,1,0:T(8,128)(2,1)S(1)} collective-permute-done((bf16[2,256,256]{2,1,0:T(8,128)(2,1)S(1)}, bf16[2,256,256]{2,1,0:T(8,128)(2,1)S(1)}, u32[]{:S(2)}, u32[]{:S(2)}) %collective-permute-start.18) | collective-permute-done | bytes 262176 | tf_op jit(solution)/shard_map/ppermute | solution.py:38
  93.4 5.6 %collective-permute-done.17.refs_5_ = bf16[2,256,256]{2,1,0:T(8,128)(2,1)S(1)} collective-permute-done((bf16[2,256,256]{2,1,0:T(8,128)(2,1)S(1)}, bf16[2,256,256]{2,1,0:T(8,128)(2,1)S(1)}, u32[]{:S(2)}, u32[]{:S(2)}) %collective-permute-start.17) | collective-permute-done | bytes 262176 | tf_op jit(solution)/shard_map/ppermute | solution.py:38
  99.0 4.3 %outer.1 = bf16[2048,4,256]{2,1,0:T(4,128)(2,1)} custom-call(bf16[2,256,256]{2,1,0:T(8,128)(2,1)S(1)} %picked.1.refs_0_, bf16[2,256,256]{2,1,0:T(8,128)(2,1)S(1)} %collective-permute-done.13.refs_1_, bf16[2,256,256]{2,1,0:T(8,128)(2,1)S(1)} %collective-permute-done.14.refs_2_, bf16[2,256,256]{2,1,0:T(8,128)(2,1)S(1)} %collective-permute-done.15.refs_3_, ...), custom_call_target="tpu_custom_call" | custom-call | tf_op jit(solution)/shard_map/outer/pallas_call | solution.py:284
  103.3 0.9 finish.1
  (9 shorter events, 0.0 us)
Async XLA Ops:
  0.6 7.7 %copy-start.1 = (bf16[128,256]{1,0:T(8,128)(2,1)S(1)}, bf16[128,256]{1,0:T(8,128)(2,1)}, u32[]{:S(2)}) copy-start(bf16[128,256]{1,0:T(8,128)(2,1)} %g_ref) | copy-start | bytes 196612
  0.6 7.7 %copy-start = (bf16[128,4,256]{2,1,0:T(4,128)(2,1)S(1)}, bf16[128,4,256]{2,1,0:T(4,128)(2,1)}, u32[]{:S(2)}) copy-start(bf16[128,4,256]{2,1,0:T(4,128)(2,1)} %h_ref) | copy-start | bytes 786436
  0.7 0.8 copy-start.2
  3.8 32.1 %collective-permute-start = (bf16[8,256,256]{2,1,0:T(8,128)(2,1)S(1)}, bf16[8,256,256]{2,1,0:T(8,128)(2,1)S(1)}, u32[]{:S(2)}, u32[]{:S(2)}) collective-permute-start(bf16[8,256,256]{2,1,0:T(8,128)(2,1)S(1)} %get-tuple-element.17), channel_id=1, source_target_pairs={{0,8},{1,65},{4,12},{5,69},{8,0},{9,73},{12,4},{13,77},{32,40},{33... | collective-permute-start | bytes 3145736 | tf_op jit(solution)/shard_map/ppermute | solution.py:34
  8.4 10.9 %collective-permute-start.2 = (bf16[5,128,256]{2,1,0:T(8,128)(2,1)S(1)}, bf16[5,128,256]{2,1,0:T(8,128)(2,1)S(1)}, u32[]{:S(2)}, u32[]{:S(2)}) collective-permute-start(bf16[5,128,256]{2,1,0:T(8,128)(2,1)S(1)} %packed.1.p0), channel_id=1, source_target_pairs={{0,2},{2,0},{1,3},{3,1},{4,6},{6,4},{5,7},{7,5},{8,10},{10,8},{9,1... | collective-permute-start | bytes 983048 | tf_op jit(solution)/shard_map/ppermute | solution.py:38
  11.4 30.7 %collective-permute-start.5 = (bf16[8,256,256]{2,1,0:T(8,128)(2,1)S(1)}, bf16[8,256,256]{2,1,0:T(8,128)(2,1)S(1)}, u32[]{:S(2)}, u32[]{:S(2)}) collective-permute-start(bf16[8,256,256]{2,1,0:T(8,128)(2,1)S(1)} %get-tuple-element.21), channel_id=1, source_target_pairs={{0,4},{1,33},{4,8},{5,37},{8,12},{9,41},{12,0},{13,45},{32,36},{33... | collective-permute-start | bytes 3145736 | tf_op jit(solution)/shard_map/ppermute | solution.py:34
  12.1 30.0 %collective-permute-start.6 = (bf16[8,256,256]{2,1,0:T(8,128)(2,1)S(1)}, bf16[8,256,256]{2,1,0:T(8,128)(2,1)S(1)}, u32[]{:S(2)}, u32[]{:S(2)}) collective-permute-start(bf16[8,256,256]{2,1,0:T(8,128)(2,1)S(1)} %get-tuple-element.22), channel_id=1, source_target_pairs={{0,12},{1,97},{4,0},{5,101},{8,4},{9,105},{12,8},{13,109},{32,44},... | collective-permute-start | bytes 3145736 | tf_op jit(solution)/shard_map/ppermute | solution.py:34
  14.1 6.0 %collective-permute-start.1 = (bf16[5,128,256]{2,1,0:T(8,128)(2,1)S(1)}, bf16[5,128,256]{2,1,0:T(8,128)(2,1)S(1)}, u32[]{:S(2)}, u32[]{:S(2)}) collective-permute-start(bf16[5,128,256]{2,1,0:T(8,128)(2,1)S(1)} %packed.1.p0), channel_id=1, source_target_pairs={{0,1},{1,0},{2,3},{3,2},{4,5},{5,4},{6,7},{7,6},{8,9},{9,8},{10,11... | collective-permute-start | bytes 983048 | tf_op jit(solution)/shard_map/ppermute | solution.py:38
  19.2 2.1 %collective-permute-start.3 = (bf16[5,128,256]{2,1,0:T(8,128)(2,1)S(1)}, bf16[5,128,256]{2,1,0:T(8,128)(2,1)S(1)}, u32[]{:S(2)}, u32[]{:S(2)}) collective-permute-start(bf16[5,128,256]{2,1,0:T(8,128)(2,1)S(1)} %collective-permute-done.2.p2), channel_id=1, source_target_pairs={{0,1},{1,0},{2,3},{3,2},{4,5},{5,4},{6,7},{7,6},{8,9},{9,8},{10,11... | collective-permute-start | bytes 983048 | tf_op jit(solution)/shard_map/ppermute | solution.py:38
  21.5 13.4 %collective-permute-start.4 = (bf16[2,256,256]{2,1,0:T(8,128)(2,1)S(1)}, bf16[2,256,256]{2,1,0:T(8,128)(2,1)S(1)}, u32[]{:S(2)}, u32[]{:S(2)}) collective-permute-start(bf16[2,256,256]{2,1,0:T(8,128)(2,1)S(1)} %get-tuple-element.20.g0), channel_id=1, source_target_pairs={{0,8},{1,65},{4,12},{5,69},{8,0},{9,73},{12,4},{13,77},{32,40},{33... | collective-permute-start | bytes 786440 | tf_op jit(solution)/shard_map/ppermute | solution.py:34
  22.2 16.1 %collective-permute-start.8 = (bf16[2,256,256]{2,1,0:T(8,128)(2,1)S(1)}, bf16[2,256,256]{2,1,0:T(8,128)(2,1)S(1)}, u32[]{:S(2)}, u32[]{:S(2)}) collective-permute-start(bf16[2,256,256]{2,1,0:T(8,128)(2,1)S(1)} %get-tuple-element.20.g0), channel_id=1, source_target_pairs={{0,12},{1,97},{4,0},{5,101},{8,4},{9,105},{12,8},{13,109},{32,44},... | collective-permute-start | bytes 786440 | tf_op jit(solution)/shard_map/ppermute | solution.py:34
  34.9 7.2 %collective-permute-start.7 = (bf16[2,256,256]{2,1,0:T(8,128)(2,1)S(1)}, bf16[2,256,256]{2,1,0:T(8,128)(2,1)S(1)}, u32[]{:S(2)}, u32[]{:S(2)}) collective-permute-start(bf16[2,256,256]{2,1,0:T(8,128)(2,1)S(1)} %get-tuple-element.20.g0), channel_id=1, source_target_pairs={{0,4},{1,33},{4,8},{5,37},{8,12},{9,41},{12,0},{13,45},{32,36},{33... | collective-permute-start | bytes 786440 | tf_op jit(solution)/shard_map/ppermute | solution.py:34
  43.4 12.9 %collective-permute-start.9 = (bf16[512,512]{1,0:T(8,128)(2,1)S(1)}, bf16[512,512]{1,0:T(8,128)(2,1)S(1)}, u32[]{:S(2)}, u32[]{:S(2)}) collective-permute-start(bf16[512,512]{1,0:T(8,128)(2,1)S(1)} %get-tuple-element.24), channel_id=1, source_target_pairs={{0,32},{1,5},{4,36},{5,9},{8,40},{9,13},{12,44},{13,1},{32,64},{33... | collective-permute-start | bytes 1572872 | tf_op jit(solution)/shard_map/ppermute | solution.py:34
  44.2 15.2 %collective-permute-start.10 = (bf16[512,512]{1,0:T(8,128)(2,1)S(1)}, bf16[512,512]{1,0:T(8,128)(2,1)S(1)}, u32[]{:S(2)}, u32[]{:S(2)}) collective-permute-start(bf16[512,512]{1,0:T(8,128)(2,1)S(1)} %get-tuple-element.25), channel_id=1, source_target_pairs={{0,64},{1,9},{4,68},{5,13},{8,72},{9,1},{12,76},{13,5},{32,96},{33... | collective-permute-start | bytes 1572872 | tf_op jit(solution)/shard_map/ppermute | solution.py:34
  46.9 13.7 %collective-permute-start.11 = (bf16[512,512]{1,0:T(8,128)(2,1)S(1)}, bf16[512,512]{1,0:T(8,128)(2,1)S(1)}, u32[]{:S(2)}, u32[]{:S(2)}) collective-permute-start(bf16[512,512]{1,0:T(8,128)(2,1)S(1)} %get-tuple-element.26), channel_id=1, source_target_pairs={{0,96},{1,13},{4,100},{5,1},{8,104},{9,5},{12,108},{13,9},{32,0},{... | collective-permute-start | bytes 1572872 | tf_op jit(solution)/shard_map/ppermute | solution.py:34
  47.8 6.5 %collective-permute-start.12 = (bf16[2,256,256]{2,1,0:T(8,128)(2,1)S(1)}, bf16[2,256,256]{2,1,0:T(8,128)(2,1)S(1)}, u32[]{:S(2)}, u32[]{:S(2)}) collective-permute-start(bf16[2,256,256]{2,1,0:T(8,128)(2,1)S(1)} %get-tuple-element.27), channel_id=1, source_target_pairs={{1,0},{3,2},{5,4},{7,6},{9,8},{11,10},{13,12},{15,14},{17,16},{19,... | collective-permute-start | bytes 786440 | tf_op jit(solution)/shard_map/ppermute | solution.py:319
  54.3 15.6 %collective-permute-start.15 = (bf16[2,256,256]{2,1,0:T(8,128)(2,1)S(1)}, bf16[2,256,256]{2,1,0:T(8,128)(2,1)S(1)}, u32[]{:S(2)}, u32[]{:S(2)}) collective-permute-start(bf16[2,256,256]{2,1,0:T(8,128)(2,1)S(1)} %picked.1.refs_0_), channel_id=1, source_target_pairs={{0,12},{4,0},{8,4},{12,8},{1,13},{5,1},{9,5},{13,9},{2,14},{6,2},{... | collective-permute-start | bytes 786440 | tf_op jit(solution)/shard_map/ppermute | solution.py:321
  55.8 14.2 %collective-permute-start.14 = (bf16[2,256,256]{2,1,0:T(8,128)(2,1)S(1)}, bf16[2,256,256]{2,1,0:T(8,128)(2,1)S(1)}, u32[]{:S(2)}, u32[]{:S(2)}) collective-permute-start(bf16[2,256,256]{2,1,0:T(8,128)(2,1)S(1)} %picked.1.refs_0_), channel_id=1, source_target_pairs={{0,8},{4,12},{8,0},{12,4},{1,9},{5,13},{9,1},{13,5},{2,10},{6,14},... | collective-permute-start | bytes 786440 | tf_op jit(solution)/shard_map/ppermute | solution.py:321
  56.3 15.1 %collective-permute-start.13 = (bf16[2,256,256]{2,1,0:T(8,128)(2,1)S(1)}, bf16[2,256,256]{2,1,0:T(8,128)(2,1)S(1)}, u32[]{:S(2)}, u32[]{:S(2)}) collective-permute-start(bf16[2,256,256]{2,1,0:T(8,128)(2,1)S(1)} %picked.1.refs_0_), channel_id=1, source_target_pairs={{0,4},{4,8},{8,12},{12,0},{1,5},{5,9},{9,13},{13,1},{2,6},{6,10},{... | collective-permute-start | bytes 786440 | tf_op jit(solution)/shard_map/ppermute | solution.py:321
  61.6 41.7 %all-to-all-start = ((bf16[8,128,256]{2,1,0:T(8,128)(2,1)}), bf16[8,128,256]{2,1,0:T(8,128)(2,1)S(1)}, u32[]{:S(2)}, u32[]{:S(2)}) async-start(bf16[8,128,256]{2,1,0:T(8,128)(2,1)} %summed.1), calls=%async_computation | async-start | bytes 1048576 | tf_op jit(solution)/shard_map/all_to_all | solution.py:316
  68.5 13.6 %collective-permute-start.16 = (bf16[2,256,256]{2,1,0:T(8,128)(2,1)S(1)}, bf16[2,256,256]{2,1,0:T(8,128)(2,1)S(1)}, u32[]{:S(2)}, u32[]{:S(2)}) collective-permute-start(bf16[2,256,256]{2,1,0:T(8,128)(2,1)S(1)} %picked.1.refs_0_), channel_id=1, source_target_pairs={{0,16},{16,0},{1,17},{17,1},{2,18},{18,2},{3,19},{19,3},{4,20},{20... | collective-permute-start | bytes 786440 | tf_op jit(solution)/shard_map/ppermute | solution.py:38
  69.9 17.8 %collective-permute-start.19 = (bf16[2,256,256]{2,1,0:T(8,128)(2,1)S(1)}, bf16[2,256,256]{2,1,0:T(8,128)(2,1)S(1)}, u32[]{:S(2)}, u32[]{:S(2)}) collective-permute-start(bf16[2,256,256]{2,1,0:T(8,128)(2,1)S(1)} %collective-permute-done.15.refs_3_), channel_id=1, source_target_pairs={{0,16},{16,0},{1,17},{17,1},{2,18},{18,2},{3,19},{19,3},{4,20},{20... | collective-permute-start | bytes 786440 | tf_op jit(solution)/shard_map/ppermute | solution.py:38
  70.0 23.4 %collective-permute-start.18 = (bf16[2,256,256]{2,1,0:T(8,128)(2,1)S(1)}, bf16[2,256,256]{2,1,0:T(8,128)(2,1)S(1)}, u32[]{:S(2)}, u32[]{:S(2)}) collective-permute-start(bf16[2,256,256]{2,1,0:T(8,128)(2,1)S(1)} %collective-permute-done.14.refs_2_), channel_id=1, source_target_pairs={{0,16},{16,0},{1,17},{17,1},{2,18},{18,2},{3,19},{19,3},{4,20},{20... | collective-permute-start | bytes 786440 | tf_op jit(solution)/shard_map/ppermute | solution.py:38
  71.4 27.6 %collective-permute-start.17 = (bf16[2,256,256]{2,1,0:T(8,128)(2,1)S(1)}, bf16[2,256,256]{2,1,0:T(8,128)(2,1)S(1)}, u32[]{:S(2)}, u32[]{:S(2)}) collective-permute-start(bf16[2,256,256]{2,1,0:T(8,128)(2,1)S(1)} %collective-permute-done.13.refs_1_), channel_id=1, source_target_pairs={{0,16},{16,0},{1,17},{17,1},{2,18},{18,2},{3,19},{19,3},{4,20},{20... | collective-permute-start | bytes 786440 | tf_op jit(solution)/shard_map/ppermute | solution.py:38

commit v5 on v4

--- a/solution.py
+++ b/solution.py
@@ -259,15 +259,33 @@
     )(for_core_0, for_core_1)
 
 
-def outer_body(*refs):
-    g, (h_ref, o_ref, buf, sems) = refs[:8], refs[8:]
+def paired_body(a_ref, b_ref, o_ref):
+    o_ref[0:2] = a_ref[...]
+    o_ref[2:4] = b_ref[...]
+
+
+def paired(a, b):
+    return pl.pallas_call(
+        paired_body,
+        out_shape=VM((4, 256, 256), BF),
+        in_specs=[IN] * 2,
+        out_specs=IN,
+        compiler_params=LIMIT,
+        name="paired",
+    )(*kept(a, b))
+
+
+def outer_body(h_ref, far_ref, *refs):
+    near, (o_ref, buf, sems) = refs[:6], refs[6:]
     yl, x = lax.axis_index("yl"), lax.axis_index("x")
+    blocks = [(yl, k, r) for k, r in zip((0, 1, 3), near[:3])]
+    blocks += [(1 - yl, k, r) for k, r in zip((0, 1, 3), near[3:])]
+    blocks += [(yl, 2, far_ref.at[0:2]), (1 - yl, 2, far_ref.at[2:4])]
     copies = []
-    for i in range(8):
-        here = yl if i < 4 else 1 - yl
-        r = pl.multiple_of((here * 4 + ((x - i) & 3)) * 256, 256)
+    for i, (here, k, g) in enumerate(blocks):
+        r = pl.multiple_of((here * 4 + ((x - k) & 3)) * 256, 256)
         p = lax.dot_general(
-            g[i][...].reshape(512, 256),
+            g[...].reshape(512, 256),
             h_ref[...],
             (((0,), (0,)), ((), ())),
             preferred_element_type=F32,
@@ -280,11 +298,11 @@
         copy.wait()
 
 
-def outer_product(blocks, hidden):
+def outer_product(*operands):
     return pl.pallas_call(
         outer_body,
         out_shape=jax.ShapeDtypeStruct((2048, 4, 256), BF),
-        in_specs=[IN] * 9,
+        in_specs=[IN] * 8,
         out_specs=HBM,
         scratch_shapes=[
             VM((8, 256, 4, 256), BF),
@@ -292,7 +310,7 @@
         ],
         compiler_params=LIMIT,
         name="outer",
-    )(*kept(*blocks, hidden))
+    )(*kept(*operands))
 
 
 def per_device(hidden, grad_out, weight_base, block_scale):
@@ -305,7 +323,9 @@
 
     grad_out, hidden, _ = lax.optimization_barrier((grad_out, hidden, r0))
     g0, h = all_tokens(packed(grad_out, hidden))
-    g1, g2, g3 = [shift(g0, first_axis_steps(k)) for k in (1, 2, 3)]
+    g2, g3 = [shift(g0, first_axis_steps(k)) for k in (2, 3)]
+    later, r2 = lax.optimization_barrier((g0, r2))
+    g1 = shift(later, first_axis_steps(1))
 
     acc = early_sums(r0, r2, g0, g2)
     *sums, keep, give = partial_sums(acc, r1, r3, g0, g1, g2, g3)
@@ -318,9 +338,10 @@
 
     seed = picked(lax.ppermute(give, "c", [(1, 0)]), keep)
     ring = lambda k: [(i, (i + k) % 4) for i in range(4)]
-    mine = [seed] + [lax.ppermute(seed, "x", ring(k)) for k in (1, 2, 3)]
-    theirs = [swap(m, "yl") for m in mine]
-    grad_weight = outer_product(mine + theirs, h)
+    other = swap(seed, "yl")
+    x1, x3 = [lax.ppermute(seed, "x", ring(k)) for k in (1, 3)]
+    x2 = lax.ppermute(paired(seed, other), "x", ring(2))
+    grad_weight = outer_product(h, x2, seed, x1, x3, other, swap(x1, "yl"), swap(x3, "yl"))
     return grad_hidden, grad_weight
 
 

time: 104 us -> 93.7 us (0.901)
  the two profiles are of different devices: /device:TPU:1 before, /device:TPU:96 now
where the time goes in v5:
time: 93.7 us; the launch traced here: 93.5 us
  starting transfers between devices  41.5 us (44%)
  waiting for transfers between devices  37.7 us (40%)
  Pallas kernels  12.6 us (13%)
    ppermute x6, waiting for transfers between devices, swap(): return lax.ppermute(value, axis, [(0, 1), (1, 0)])  15.7 us
    ppermute x9, waiting for transfers between devices, shift(): return lax.ppermute(value, ('z', 'x', 'c'), pairs)  14.3 us
    ppermute x9, starting transfers between devices, shift(): return lax.ppermute(value, ('z', 'x', 'c'), pairs)  13.6 us
    all_to_all x1, starting transfers between devices, per_device(): blocks = lax.all_to_all(blocks, ('yl', 'yh', 'c'), 0, 0, tiled=True)  10.3 us
    all_to_all x1, waiting for transfers between devices, per_device(): blocks = lax.all_to_all(blocks, ('yl', 'yh', 'c'), 0, 0, tiled=True)  7.75 us
    ppermute x6, starting transfers between devices, swap(): return lax.ppermute(value, axis, [(0, 1), (1, 0)])  7.23 us
    pallas_call x1, Pallas kernels, outer_product(): pl.pallas_call(outer_body, out_shape=jax.ShapeDtypeStruct((2048, 4, 256),...  5.42 us
    ppermute x2, starting transfers between devices, per_device(): x1, x3 = [lax.ppermute(seed, 'x', ring(k)) for k in (1, 3)]  4.69 us
  transfers between devices with their start and end apart: 20, of which 9 were waited for; matrix products, arithmetic and copies ran while one was open for 0% of the time, Pallas kernels for 4%

profile of v5, /device:TPU:96, one launch (start us, length us, event | category | flops | bytes accessed | tf_op | source)
XLA Modules:
  0.0 93.5 jit_solution(4105721553839603367)
XLA Ops:
  0.7 0.8 copy-done.2
  1.4 2.4 %scale.1 = (bf16[8,256,256]{2,1,0:T(8,128)(2,1)S(1)}, bf16[8,256,256]{2,1,0:T(8,128)(2,1)S(1)}, bf16[8,256,256]{2,1,0:T(8,128)(2,1)S(1)}, bf16[8,256,256]{2,1,0:T(8,128)(2,1)S(1)}) custom-call(bf16[4,2,4,256,256]{4,3,2,1,0:T(8,128)(2,1)} %bitcast.3, bf16[16,512]{1,0:T(8,128)(2,1)S(1)} %bitcast.2), custom_call_target="tpu_custom_call" | custom-call | tf_op jit(solution)/shard_map/scale/pallas_call | solution.py:93
  3.8 3.1 %collective-permute-start.3 = (bf16[8,256,256]{2,1,0:T(8,128)(2,1)S(1)}, bf16[8,256,256]{2,1,0:T(8,128)(2,1)S(1)}, u32[]{:S(2)}, u32[]{:S(2)}) collective-permute-start(bf16[8,256,256]{2,1,0:T(8,128)(2,1)S(1)} %get-tuple-element.22), channel_id=1, source_target_pairs={{0,8},{1,65},{4,12},{5,69},{8,0},{9,73},{12,4},{13,77},{32,40},{33... | collective-permute-start | bytes 3145736 | tf_op jit(solution)/shard_map/ppermute | solution.py:34
  6.9 0.1 packed.1.p0
  7.0 3.3 %collective-permute-start.1 = (bf16[5,128,256]{2,1,0:T(8,128)(2,1)S(1)}, bf16[5,128,256]{2,1,0:T(8,128)(2,1)S(1)}, u32[]{:S(2)}, u32[]{:S(2)}) collective-permute-start(bf16[5,128,256]{2,1,0:T(8,128)(2,1)S(1)} %packed.1.p0), channel_id=1, source_target_pairs={{0,2},{2,0},{1,3},{3,1},{4,6},{6,4},{5,7},{7,5},{8,10},{10,8},{9,1... | collective-permute-start | bytes 983048 | tf_op jit(solution)/shard_map/ppermute | solution.py:38
  10.2 0.6 collective-permute-start.5
  10.8 2.6 %collective-permute-start.6 = (bf16[8,256,256]{2,1,0:T(8,128)(2,1)S(1)}, bf16[8,256,256]{2,1,0:T(8,128)(2,1)S(1)}, u32[]{:S(2)}, u32[]{:S(2)}) collective-permute-start(bf16[8,256,256]{2,1,0:T(8,128)(2,1)S(1)} %get-tuple-element.25), channel_id=1, source_target_pairs={{0,12},{1,97},{4,0},{5,101},{8,4},{9,105},{12,8},{13,109},{32,44},... | collective-permute-start | bytes 3145736 | tf_op jit(solution)/shard_map/ppermute | solution.py:34
  13.5 0.0 collective-permute-start
  13.5 2.1 %collective-permute-done.1.p2 = bf16[5,128,256]{2,1,0:T(8,128)(2,1)S(1)} collective-permute-done((bf16[5,128,256]{2,1,0:T(8,128)(2,1)S(1)}, bf16[5,128,256]{2,1,0:T(8,128)(2,1)S(1)}, u32[]{:S(2)}, u32[]{:S(2)}) %collective-permute-start.1) | collective-permute-done | bytes 327712 | tf_op jit(solution)/shard_map/ppermute | solution.py:38
  15.6 0.0 collective-permute-start.2
  15.6 0.0 collective-permute-done.p1
  15.6 1.6 %collective-permute-done.2.p3 = bf16[5,128,256]{2,1,0:T(8,128)(2,1)S(1)} collective-permute-done((bf16[5,128,256]{2,1,0:T(8,128)(2,1)S(1)}, bf16[5,128,256]{2,1,0:T(8,128)(2,1)S(1)}, u32[]{:S(2)}, u32[]{:S(2)}) %collective-permute-start.2) | collective-permute-done | bytes 327712 | tf_op jit(solution)/shard_map/ppermute | solution.py:38
  17.3 0.1 tokens.1
  17.4 2.7 %collective-permute-start.4 = (bf16[2,256,256]{2,1,0:T(8,128)(2,1)S(1)}, bf16[2,256,256]{2,1,0:T(8,128)(2,1)S(1)}, u32[]{:S(2)}, u32[]{:S(2)}) collective-permute-start(bf16[2,256,256]{2,1,0:T(8,128)(2,1)S(1)} %get-tuple-element.26.g0), channel_id=1, source_target_pairs={{0,8},{1,65},{4,12},{5,69},{8,0},{9,73},{12,4},{13,77},{32,40},{33... | collective-permute-start | bytes 786440 | tf_op jit(solution)/shard_map/ppermute | solution.py:34
  20.1 1.1 %collective-permute-start.8 = (bf16[2,256,256]{2,1,0:T(8,128)(2,1)S(1)}, bf16[2,256,256]{2,1,0:T(8,128)(2,1)S(1)}, u32[]{:S(2)}, u32[]{:S(2)}) collective-permute-start(bf16[2,256,256]{2,1,0:T(8,128)(2,1)S(1)} %get-tuple-element.26.g0), channel_id=1, source_target_pairs={{0,12},{1,97},{4,0},{5,101},{8,4},{9,105},{12,8},{13,109},{32,44},... | collective-permute-start | bytes 786440 | tf_op jit(solution)/shard_map/ppermute | solution.py:34
  21.3 0.0 collective-permute-done.3.r2
  21.3 0.9 collective-permute-start.7
  22.2 12.2 %collective-permute-done.4.g2 = bf16[2,256,256]{2,1,0:T(8,128)(2,1)S(1)} collective-permute-done((bf16[2,256,256]{2,1,0:T(8,128)(2,1)S(1)}, bf16[2,256,256]{2,1,0:T(8,128)(2,1)S(1)}, u32[]{:S(2)}, u32[]{:S(2)}) %collective-permute-start.4) | collective-permute-done | bytes 262176 | tf_op jit(solution)/shard_map/ppermute | solution.py:34
  34.4 1.3 %early.1.acc = f32[4,512,512]{2,1,0:T(8,128)S(1)} custom-call(bf16[8,256,256]{2,1,0:T(8,128)(2,1)S(1)} %get-tuple-element.18.r0, bf16[8,256,256]{2,1,0:T(8,128)(2,1)S(1)} %collective-permute-done.3.r2, bf16[2,256,256]{2,1,0:T(8,128)(2,1)S(1)} %get-tuple-element.26.g0, bf16[2,256,256]{2,1,0:T(8,128)(2,1)S(1)} %collective-permute-done.4.g2), custom_call_target="tpu_custom_call" | custom-call | flops 2000000000 | bytes 6291456 | tf_op jit(solution)/shard_map/early/pallas_call | solution.py:160
  35.6 1.5 %collective-permute-done.8.g3 = bf16[2,256,256]{2,1,0:T(8,128)(2,1)S(1)} collective-permute-done((bf16[2,256,256]{2,1,0:T(8,128)(2,1)S(1)}, bf16[2,256,256]{2,1,0:T(8,128)(2,1)S(1)}, u32[]{:S(2)}, u32[]{:S(2)}) %collective-permute-start.8) | collective-permute-done | bytes 262176 | tf_op jit(solution)/shard_map/ppermute | solution.py:34
  37.2 0.0 collective-permute-done.5.r1
  37.2 0.0 collective-permute-done.6.r3
  37.2 0.0 collective-permute-done.7.g1
  37.2 1.4 %partial.1 = (f32[512,512]{1,0:T(8,128)S(1)}, bf16[512,512]{1,0:T(8,128)(2,1)S(1)}, bf16[512,512]{1,0:T(8,128)(2,1)S(1)}, bf16[512,512]{1,0:T(8,128)(2,1)S(1)}, ...) custom-call(f32[4,512,512]{2,1,0:T(8,128)S(1)} %early.1.acc, ...), custom_call_target="tpu_custom_call" | custom-call | tf_op jit(solution)/shard_map/partial/pallas_call | solution.py:193
  38.6 1.3 %collective-permute-start.12 = (bf16[2,256,256]{2,1,0:T(8,128)(2,1)S(1)}, bf16[2,256,256]{2,1,0:T(8,128)(2,1)S(1)}, u32[]{:S(2)}, u32[]{:S(2)}) collective-permute-start(bf16[2,256,256]{2,1,0:T(8,128)(2,1)S(1)} %get-tuple-element.32), channel_id=1, source_target_pairs={{1,0},{3,2},{5,4},{7,6},{9,8},{11,10},{13,12},{15,14},{17,16},{19,... | collective-permute-start | bytes 786440 | tf_op jit(solution)/shard_map/ppermute | solution.py:339
  39.9 0.1 collective-permute-start.9
  40.0 2.5 %collective-permute-start.10 = (bf16[512,512]{1,0:T(8,128)(2,1)S(1)}, bf16[512,512]{1,0:T(8,128)(2,1)S(1)}, u32[]{:S(2)}, u32[]{:S(2)}) collective-permute-start(bf16[512,512]{1,0:T(8,128)(2,1)S(1)} %get-tuple-element.29), channel_id=1, source_target_pairs={{0,64},{1,9},{4,68},{5,13},{8,72},{9,1},{12,76},{13,5},{32,96},{33... | collective-permute-start | bytes 1572872 | tf_op jit(solution)/shard_map/ppermute | solution.py:34
  42.4 0.0 collective-permute-start.11
  42.4 0.0 collective-permute-done.12.a_ref
  42.5 1.7 %collective-permute-start.13 = (bf16[2,256,256]{2,1,0:T(8,128)(2,1)S(1)}, bf16[2,256,256]{2,1,0:T(8,128)(2,1)S(1)}, u32[]{:S(2)}, u32[]{:S(2)}) collective-permute-start(bf16[2,256,256]{2,1,0:T(8,128)(2,1)S(1)} %picked.1.a_ref.refs_0_), channel_id=1, source_target_pairs={{0,16},{16,0},{1,17},{17,1},{2,18},{18,2},{3,19},{19,3},{4,20},{20... | collective-permute-start | bytes 786440 | tf_op jit(solution)/shard_map/ppermute | solution.py:38
  44.1 2.6 %collective-permute-start.16 = (bf16[2,256,256]{2,1,0:T(8,128)(2,1)S(1)}, bf16[2,256,256]{2,1,0:T(8,128)(2,1)S(1)}, u32[]{:S(2)}, u32[]{:S(2)}) collective-permute-start(bf16[2,256,256]{2,1,0:T(8,128)(2,1)S(1)} %picked.1.a_ref.refs_0_), channel_id=1, source_target_pairs={{0,12},{4,0},{8,4},{12,8},{1,13},{5,1},{9,5},{13,9},{2,14},{6,2},{... | collective-permute-start | bytes 786440 | tf_op jit(solution)/shard_map/ppermute | solution.py:342
  46.7 2.7 %collective-permute-done.13.b_ref.refs_3_ = bf16[2,256,256]{2,1,0:T(8,128)(2,1)S(1)} collective-permute-done((bf16[2,256,256]{2,1,0:T(8,128)(2,1)S(1)}, bf16[2,256,256]{2,1,0:T(8,128)(2,1)S(1)}, u32[]{:S(2)}, u32[]{:S(2)}) %collective-permute-start.13) | collective-permute-done | bytes 262176 | tf_op jit(solution)/shard_map/ppermute | solution.py:38
  49.4 2.1 %collective-permute-start.15 = (bf16[2,256,256]{2,1,0:T(8,128)(2,1)S(1)}, bf16[2,256,256]{2,1,0:T(8,128)(2,1)}, u32[]{:S(2)}, u32[]{:S(2)}) collective-permute-start(bf16[2,256,256]{2,1,0:T(8,128)(2,1)S(1)} %picked.1.a_ref.refs_0_), channel_id=1, source_target_pairs={{0,4},{4,8},{8,12},{12,0},{1,5},{5,9},{9,13},{13,1},{2,6},{6,10},{... | collective-permute-start | bytes 786440 | tf_op jit(solution)/shard_map/ppermute | solution.py:342
  51.5 0.0 collective-permute-done.9.b
  51.5 4.3 %collective-permute-start.14 = (bf16[4,256,256]{2,1,0:T(8,128)(2,1)S(1)}, bf16[4,256,256]{2,1,0:T(8,128)(2,1)S(1)}, u32[]{:S(2)}, u32[]{:S(2)}) collective-permute-start(bf16[4,256,256]{2,1,0:T(8,128)(2,1)S(1)} %paired.1), channel_id=1, source_target_pairs={{0,8},{4,12},{8,0},{12,4},{1,9},{5,13},{9,1},{13,5},{2,10},{6,14},... | collective-permute-start | bytes 1572872 | tf_op jit(solution)/shard_map/ppermute | solution.py:343
  55.9 0.0 collective-permute-done.10.c
  55.9 0.5 collective-permute-done.11.d
  56.4 1.0 %summed.1 = bf16[8,128,256]{2,1,0:T(8,128)(2,1)} custom-call(f32[512,512]{1,0:T(8,128)S(1)} %get-tuple-element.27.a, bf16[512,512]{1,0:T(8,128)(2,1)S(1)} %collective-permute-done.9.b, bf16[512,512]{1,0:T(8,128)(2,1)S(1)} %collective-permute-done.10.c, bf16[512,512]{1,0:T(8,128)(2,1)S(1)} %collective-permute-done.11.d), custom_call_target="tpu_custom_call" | custom-call | tf_op jit(solution)/shard_map/summed/pallas_call | solution.py:215
  57.4 10.3 %all-to-all-start = ((bf16[8,128,256]{2,1,0:T(8,128)(2,1)}), bf16[8,128,256]{2,1,0:T(8,128)(2,1)S(1)}, u32[]{:S(2)}, u32[]{:S(2)}) async-start(bf16[8,128,256]{2,1,0:T(8,128)(2,1)} %summed.1), calls=%async_computation | async-start | bytes 1048576 | tf_op jit(solution)/shard_map/all_to_all | solution.py:336
  67.7 0.0 collective-permute-done.16.refs_2_
  67.7 2.0 %collective-permute-start.18 = (bf16[2,256,256]{2,1,0:T(8,128)(2,1)S(1)}, bf16[2,256,256]{2,1,0:T(8,128)(2,1)}, u32[]{:S(2)}, u32[]{:S(2)}) collective-permute-start(bf16[2,256,256]{2,1,0:T(8,128)(2,1)S(1)} %collective-permute-done.16.refs_2_), channel_id=1, source_target_pairs={{0,16},{16,0},{1,17},{17,1},{2,18},{18,2},{3,19},{19,3},{4,20},{20... | collective-permute-start | bytes 786440 | tf_op jit(solution)/shard_map/ppermute | solution.py:38
  69.7 0.0 collective-permute-done.15.refs_1_
  69.7 0.3 collective-permute-start.17
  70.0 7.8 %all-to-all-done.r_ref = bf16[8,128,256]{2,1,0:T(8,128)(2,1)S(1)} async-done(((bf16[8,128,256]{2,1,0:T(8,128)(2,1)}), bf16[8,128,256]{2,1,0:T(8,128)(2,1)S(1)}, u32[]{:S(2)}, u32[]{:S(2)}) %all-to-all-start) | async-done | bytes 524320 | tf_op jit(solution)/shard_map/all_to_all | solution.py:336
  77.7 0.9 finish.1
  78.6 4.1 %collective-permute-done.18.refs_5_ = bf16[2,256,256]{2,1,0:T(8,128)(2,1)} collective-permute-done((bf16[2,256,256]{2,1,0:T(8,128)(2,1)S(1)}, bf16[2,256,256]{2,1,0:T(8,128)(2,1)}, u32[]{:S(2)}, u32[]{:S(2)}) %collective-permute-start.18) | collective-permute-done | bytes 262176 | tf_op jit(solution)/shard_map/ppermute | solution.py:38
  82.7 5.1 %collective-permute-done.17.refs_4_ = bf16[2,256,256]{2,1,0:T(8,128)(2,1)} collective-permute-done((bf16[2,256,256]{2,1,0:T(8,128)(2,1)}, bf16[2,256,256]{2,1,0:T(8,128)(2,1)}, u32[]{:S(2)}, u32[]{:S(2)}) %collective-permute-start.17) | collective-permute-done | bytes 262176 | tf_op jit(solution)/shard_map/ppermute | solution.py:38
  87.9 5.4 %outer.1 = bf16[2048,4,256]{2,1,0:T(4,128)(2,1)} custom-call(bf16[512,1024]{1,0:T(8,128)(2,1)S(1)} %get-tuple-element.31.h_ref, bf16[4,256,256]{2,1,0:T(8,128)(2,1)S(1)} %collective-permute-done.14.far_ref, bf16[2,256,256]{2,1,0:T(8,128)(2,1)S(1)} %picked.1.a_ref.refs_0_, bf16[2,256,256]{2,1,0:T(8,128)(2,1)} %collective-permute-done.15.refs_1_, ...), custom_call_target="tpu_custom_call" | custom-call | tf_op jit(solution)/shard_map/outer/pallas_call | solution.py:302
  (8 shorter events, 0.1 us)
Async XLA Ops:
  0.6 6.3 %copy-start.1 = (bf16[128,256]{1,0:T(8,128)(2,1)S(1)}, bf16[128,256]{1,0:T(8,128)(2,1)}, u32[]{:S(2)}) copy-start(bf16[128,256]{1,0:T(8,128)(2,1)} %g_ref) | copy-start | bytes 196612
  0.6 6.3 %copy-start = (bf16[128,4,256]{2,1,0:T(4,128)(2,1)S(1)}, bf16[128,4,256]{2,1,0:T(4,128)(2,1)}, u32[]{:S(2)}) copy-start(bf16[128,4,256]{2,1,0:T(4,128)(2,1)} %h_ref) | copy-start | bytes 786436
  0.7 0.8 copy-start.2
  3.8 17.5 %collective-permute-start.3 = (bf16[8,256,256]{2,1,0:T(8,128)(2,1)S(1)}, bf16[8,256,256]{2,1,0:T(8,128)(2,1)S(1)}, u32[]{:S(2)}, u32[]{:S(2)}) collective-permute-start(bf16[8,256,256]{2,1,0:T(8,128)(2,1)S(1)} %get-tuple-element.22), channel_id=1, source_target_pairs={{0,8},{1,65},{4,12},{5,69},{8,0},{9,73},{12,4},{13,77},{32,40},{33... | collective-permute-start | bytes 3145736 | tf_op jit(solution)/shard_map/ppermute | solution.py:34
  7.0 8.7 %collective-permute-start.1 = (bf16[5,128,256]{2,1,0:T(8,128)(2,1)S(1)}, bf16[5,128,256]{2,1,0:T(8,128)(2,1)S(1)}, u32[]{:S(2)}, u32[]{:S(2)}) collective-permute-start(bf16[5,128,256]{2,1,0:T(8,128)(2,1)S(1)} %packed.1.p0), channel_id=1, source_target_pairs={{0,2},{2,0},{1,3},{3,1},{4,6},{6,4},{5,7},{7,5},{8,10},{10,8},{9,1... | collective-permute-start | bytes 983048 | tf_op jit(solution)/shard_map/ppermute | solution.py:38
  10.2 27.0 %collective-permute-start.5 = (bf16[8,256,256]{2,1,0:T(8,128)(2,1)S(1)}, bf16[8,256,256]{2,1,0:T(8,128)(2,1)S(1)}, u32[]{:S(2)}, u32[]{:S(2)}) collective-permute-start(bf16[8,256,256]{2,1,0:T(8,128)(2,1)S(1)} %get-tuple-element.24), channel_id=1, source_target_pairs={{0,4},{1,33},{4,8},{5,37},{8,12},{9,41},{12,0},{13,45},{32,36},{33... | collective-permute-start | bytes 3145736 | tf_op jit(solution)/shard_map/ppermute | solution.py:34
  10.8 26.4 %collective-permute-start.6 = (bf16[8,256,256]{2,1,0:T(8,128)(2,1)S(1)}, bf16[8,256,256]{2,1,0:T(8,128)(2,1)S(1)}, u32[]{:S(2)}, u32[]{:S(2)}) collective-permute-start(bf16[8,256,256]{2,1,0:T(8,128)(2,1)S(1)} %get-tuple-element.25), channel_id=1, source_target_pairs={{0,12},{1,97},{4,0},{5,101},{8,4},{9,105},{12,8},{13,109},{32,44},... | collective-permute-start | bytes 3145736 | tf_op jit(solution)/shard_map/ppermute | solution.py:34
  13.5 2.2 %collective-permute-start = (bf16[5,128,256]{2,1,0:T(8,128)(2,1)S(1)}, bf16[5,128,256]{2,1,0:T(8,128)(2,1)S(1)}, u32[]{:S(2)}, u32[]{:S(2)}) collective-permute-start(bf16[5,128,256]{2,1,0:T(8,128)(2,1)S(1)} %packed.1.p0), channel_id=1, source_target_pairs={{0,1},{1,0},{2,3},{3,2},{4,5},{5,4},{6,7},{7,6},{8,9},{9,8},{10,11... | collective-permute-start | bytes 983048 | tf_op jit(solution)/shard_map/ppermute | solution.py:38
  15.6 1.6 %collective-permute-start.2 = (bf16[5,128,256]{2,1,0:T(8,128)(2,1)S(1)}, bf16[5,128,256]{2,1,0:T(8,128)(2,1)S(1)}, u32[]{:S(2)}, u32[]{:S(2)}) collective-permute-start(bf16[5,128,256]{2,1,0:T(8,128)(2,1)S(1)} %collective-permute-done.1.p2), channel_id=1, source_target_pairs={{0,1},{1,0},{2,3},{3,2},{4,5},{5,4},{6,7},{7,6},{8,9},{9,8},{10,11... | collective-permute-start | bytes 983048 | tf_op jit(solution)/shard_map/ppermute | solution.py:38
  17.4 17.0 %collective-permute-start.4 = (bf16[2,256,256]{2,1,0:T(8,128)(2,1)S(1)}, bf16[2,256,256]{2,1,0:T(8,128)(2,1)S(1)}, u32[]{:S(2)}, u32[]{:S(2)}) collective-permute-start(bf16[2,256,256]{2,1,0:T(8,128)(2,1)S(1)} %get-tuple-element.26.g0), channel_id=1, source_target_pairs={{0,8},{1,65},{4,12},{5,69},{8,0},{9,73},{12,4},{13,77},{32,40},{33... | collective-permute-start | bytes 786440 | tf_op jit(solution)/shard_map/ppermute | solution.py:34
  20.1 17.1 %collective-permute-start.8 = (bf16[2,256,256]{2,1,0:T(8,128)(2,1)S(1)}, bf16[2,256,256]{2,1,0:T(8,128)(2,1)S(1)}, u32[]{:S(2)}, u32[]{:S(2)}) collective-permute-start(bf16[2,256,256]{2,1,0:T(8,128)(2,1)S(1)} %get-tuple-element.26.g0), channel_id=1, source_target_pairs={{0,12},{1,97},{4,0},{5,101},{8,4},{9,105},{12,8},{13,109},{32,44},... | collective-permute-start | bytes 786440 | tf_op jit(solution)/shard_map/ppermute | solution.py:34
  21.3 15.9 %collective-permute-start.7 = (bf16[2,256,256]{2,1,0:T(8,128)(2,1)S(1)}, bf16[2,256,256]{2,1,0:T(8,128)(2,1)S(1)}, u32[]{:S(2)}, u32[]{:S(2)}) collective-permute-start(bf16[2,256,256]{2,1,0:T(8,128)(2,1)S(1)} %get-tuple-element.26.g0), channel_id=1, source_target_pairs={{0,4},{1,33},{4,8},{5,37},{8,12},{9,41},{12,0},{13,45},{32,36},{33... | collective-permute-start | bytes 786440 | tf_op jit(solution)/shard_map/ppermute | solution.py:34
  38.6 3.8 %collective-permute-start.12 = (bf16[2,256,256]{2,1,0:T(8,128)(2,1)S(1)}, bf16[2,256,256]{2,1,0:T(8,128)(2,1)S(1)}, u32[]{:S(2)}, u32[]{:S(2)}) collective-permute-start(bf16[2,256,256]{2,1,0:T(8,128)(2,1)S(1)} %get-tuple-element.32), channel_id=1, source_target_pairs={{1,0},{3,2},{5,4},{7,6},{9,8},{11,10},{13,12},{15,14},{17,16},{19,... | collective-permute-start | bytes 786440 | tf_op jit(solution)/shard_map/ppermute | solution.py:339
  39.9 11.6 %collective-permute-start.9 = (bf16[512,512]{1,0:T(8,128)(2,1)S(1)}, bf16[512,512]{1,0:T(8,128)(2,1)S(1)}, u32[]{:S(2)}, u32[]{:S(2)}) collective-permute-start(bf16[512,512]{1,0:T(8,128)(2,1)S(1)} %get-tuple-element.28), channel_id=1, source_target_pairs={{0,32},{1,5},{4,36},{5,9},{8,40},{9,13},{12,44},{13,1},{32,64},{33... | collective-permute-start | bytes 1572872 | tf_op jit(solution)/shard_map/ppermute | solution.py:34
  40.0 15.9 %collective-permute-start.10 = (bf16[512,512]{1,0:T(8,128)(2,1)S(1)}, bf16[512,512]{1,0:T(8,128)(2,1)S(1)}, u32[]{:S(2)}, u32[]{:S(2)}) collective-permute-start(bf16[512,512]{1,0:T(8,128)(2,1)S(1)} %get-tuple-element.29), channel_id=1, source_target_pairs={{0,64},{1,9},{4,68},{5,13},{8,72},{9,1},{12,76},{13,5},{32,96},{33... | collective-permute-start | bytes 1572872 | tf_op jit(solution)/shard_map/ppermute | solution.py:34
  42.4 13.9 %collective-permute-start.11 = (bf16[512,512]{1,0:T(8,128)(2,1)S(1)}, bf16[512,512]{1,0:T(8,128)(2,1)S(1)}, u32[]{:S(2)}, u32[]{:S(2)}) collective-permute-start(bf16[512,512]{1,0:T(8,128)(2,1)S(1)} %get-tuple-element.30), channel_id=1, source_target_pairs={{0,96},{1,13},{4,100},{5,1},{8,104},{9,5},{12,108},{13,9},{32,0},{... | collective-permute-start | bytes 1572872 | tf_op jit(solution)/shard_map/ppermute | solution.py:34
  42.5 6.9 %collective-permute-start.13 = (bf16[2,256,256]{2,1,0:T(8,128)(2,1)S(1)}, bf16[2,256,256]{2,1,0:T(8,128)(2,1)S(1)}, u32[]{:S(2)}, u32[]{:S(2)}) collective-permute-start(bf16[2,256,256]{2,1,0:T(8,128)(2,1)S(1)} %picked.1.a_ref.refs_0_), channel_id=1, source_target_pairs={{0,16},{16,0},{1,17},{17,1},{2,18},{18,2},{3,19},{19,3},{4,20},{20... | collective-permute-start | bytes 786440 | tf_op jit(solution)/shard_map/ppermute | solution.py:38
  44.1 23.6 %collective-permute-start.16 = (bf16[2,256,256]{2,1,0:T(8,128)(2,1)S(1)}, bf16[2,256,256]{2,1,0:T(8,128)(2,1)S(1)}, u32[]{:S(2)}, u32[]{:S(2)}) collective-permute-start(bf16[2,256,256]{2,1,0:T(8,128)(2,1)S(1)} %picked.1.a_ref.refs_0_), channel_id=1, source_target_pairs={{0,12},{4,0},{8,4},{12,8},{1,13},{5,1},{9,5},{13,9},{2,14},{6,2},{... | collective-permute-start | bytes 786440 | tf_op jit(solution)/shard_map/ppermute | solution.py:342
  49.4 20.3 %collective-permute-start.15 = (bf16[2,256,256]{2,1,0:T(8,128)(2,1)S(1)}, bf16[2,256,256]{2,1,0:T(8,128)(2,1)}, u32[]{:S(2)}, u32[]{:S(2)}) collective-permute-start(bf16[2,256,256]{2,1,0:T(8,128)(2,1)S(1)} %picked.1.a_ref.refs_0_), channel_id=1, source_target_pairs={{0,4},{4,8},{8,12},{12,0},{1,5},{5,9},{9,13},{13,1},{2,6},{6,10},{... | collective-permute-start | bytes 786440 | tf_op jit(solution)/shard_map/ppermute | solution.py:342
  51.5 36.3 %collective-permute-start.14 = (bf16[4,256,256]{2,1,0:T(8,128)(2,1)S(1)}, bf16[4,256,256]{2,1,0:T(8,128)(2,1)S(1)}, u32[]{:S(2)}, u32[]{:S(2)}) collective-permute-start(bf16[4,256,256]{2,1,0:T(8,128)(2,1)S(1)} %paired.1), channel_id=1, source_target_pairs={{0,8},{4,12},{8,0},{12,4},{1,9},{5,13},{9,1},{13,5},{2,10},{6,14},... | collective-permute-start | bytes 1572872 | tf_op jit(solution)/shard_map/ppermute | solution.py:343
  57.4 20.4 %all-to-all-start = ((bf16[8,128,256]{2,1,0:T(8,128)(2,1)}), bf16[8,128,256]{2,1,0:T(8,128)(2,1)S(1)}, u32[]{:S(2)}, u32[]{:S(2)}) async-start(bf16[8,128,256]{2,1,0:T(8,128)(2,1)} %summed.1), calls=%async_computation | async-start | bytes 1048576 | tf_op jit(solution)/shard_map/all_to_all | solution.py:336
  67.7 15.0 %collective-permute-start.18 = (bf16[2,256,256]{2,1,0:T(8,128)(2,1)S(1)}, bf16[2,256,256]{2,1,0:T(8,128)(2,1)}, u32[]{:S(2)}, u32[]{:S(2)}) collective-permute-start(bf16[2,256,256]{2,1,0:T(8,128)(2,1)S(1)} %collective-permute-done.16.refs_2_), channel_id=1, source_target_pairs={{0,16},{16,0},{1,17},{17,1},{2,18},{18,2},{3,19},{19,3},{4,20},{20... | collective-permute-start | bytes 786440 | tf_op jit(solution)/shard_map/ppermute | solution.py:38
  69.7 18.2 %collective-permute-start.17 = (bf16[2,256,256]{2,1,0:T(8,128)(2,1)}, bf16[2,256,256]{2,1,0:T(8,128)(2,1)}, u32[]{:S(2)}, u32[]{:S(2)}) collective-permute-start(bf16[2,256,256]{2,1,0:T(8,128)(2,1)} %collective-permute-done.15.refs_1_), channel_id=1, source_target_pairs={{0,16},{16,0},{1,17},{17,1},{2,18},{18,2},{3,19},{19,3},{4,20},{20... | collective-permute-start | bytes 786440 | tf_op jit(solution)/shard_map/ppermute | solution.py:38

commit v6 on v5

--- a/solution.py
+++ b/solution.py
@@ -62,8 +62,10 @@
     )
 
 
-def scale_into(outs, w_ref, s_ref, wide_ref, sems):
+def scale_into(outs, w_ref, s_ref, narrow_ref, wide_ref, sems):
     c, first, _ = roles()
+    scales = pltpu.make_async_copy(s_ref, narrow_ref, sems.at[16])
+    scales.start()
     copies = []
     for j, (k, o_ref) in enumerate(outs):
         p = (first + k) & 3
@@ -74,7 +76,8 @@
             )
             copy.start()
             copies.append((copy, o_ref, i, z, x))
-    spread_scales(s_ref, wide_ref)
+    scales.wait()
+    spread_scales(narrow_ref, wide_ref)
     for copy, o_ref, i, z, x in copies:
         copy.wait()
         for yl in range(2):
@@ -85,17 +88,17 @@
 
 
 def scale_body(w_ref, s_ref, *refs):
-    outs, wide_ref, sems = refs[:4], refs[4], refs[5]
-    scale_into([(k, outs[k]) for k in (2, 1, 3, 0)], w_ref, s_ref, wide_ref, sems)
+    outs, scratch = refs[:4], refs[4:]
+    scale_into([(k, outs[k]) for k in (1, 3, 2, 0)], w_ref, s_ref, *scratch)
 
 
 def scaled_rows(w5, scales_t):
     return pl.pallas_call(
         scale_body,
         out_shape=[VM((8, 256, 256), BF)] * 4,
-        in_specs=[HBM, IN],
+        in_specs=[HBM, HBM],
         out_specs=[IN] * 4,
-        scratch_shapes=[VM((512, 256), F32), pltpu.SemaphoreType.DMA((16,))],
+        scratch_shapes=[VM((16, 512), BF), VM((512, 256), F32), pltpu.SemaphoreType.DMA((17,))],
         compiler_params=LIMIT,
         name="scale",
     )(w5, scales_t)
@@ -151,9 +154,9 @@
     )
 
 
-def early_body(r0, r2, g0, g2, acc):
+def early_body(r0, r3, g0, g3, acc):
     for q in range(4):
-        acc[q] = block_product(g0, r0, 2 * q) + block_product(g2, r2, 2 * q)
+        acc[q] = block_product(g0, r0, 2 * q) + block_product(g3, r3, 2 * q)
 
 
 def early_sums(*operands):
@@ -168,7 +171,7 @@
     )(*kept(*operands))
 
 
-def partial_body(acc, r1, r3, g0, g1, g2, g3, *outs):
+def partial_body(acc, r1, r2, g0, g1, g2, g3, *outs):
     keep, give = outs[4:]
     _, _, second = roles()
     z, yh = lax.axis_index("z"), lax.axis_index("yh")
@@ -185,7 +188,7 @@
 
     for k in (2, 1, 3, 0):
         q = (second + k) & 3
-        total = acc[q] + block_product(g[1], r1, 2 * q) + block_product(g[3], r3, 2 * q)
+        total = acc[q] + block_product(g[1], r1, 2 * q) + block_product(g[2], r2, 2 * q)
         outs[k][...] = total.astype(outs[k].dtype)
 
 
@@ -275,15 +278,11 @@
     )(*kept(a, b))
 
 
-def outer_body(h_ref, far_ref, *refs):
-    near, (o_ref, buf, sems) = refs[:6], refs[6:]
-    yl, x = lax.axis_index("yl"), lax.axis_index("x")
-    blocks = [(yl, k, r) for k, r in zip((0, 1, 3), near[:3])]
-    blocks += [(1 - yl, k, r) for k, r in zip((0, 1, 3), near[3:])]
-    blocks += [(yl, 2, far_ref.at[0:2]), (1 - yl, 2, far_ref.at[2:4])]
+def outer_into(blocks, h_ref, o_ref, buf, sems):
+    x = lax.axis_index("x")
     copies = []
-    for i, (here, k, g) in enumerate(blocks):
-        r = pl.multiple_of((here * 4 + ((x - k) & 3)) * 256, 256)
+    for i, (yl, k, g) in enumerate(blocks):
+        r = pl.multiple_of((yl * 4 + ((x - k) & 3)) * 256, 256)
         p = lax.dot_general(
             g[...].reshape(512, 256),
             h_ref[...],
@@ -298,24 +297,48 @@
         copy.wait()
 
 
-def outer_product(*operands):
-    return pl.pallas_call(
-        outer_body,
+def first_half_body(h_ref, seed, other, back, back_other, *refs):
+    yl, c = lax.axis_index("yl"), lax.axis_index("c")
+    k = 3 - 2 * c
+    blocks = [(yl, 0, seed), (1 - yl, 0, other), (yl, k, back), (1 - yl, k, back_other)]
+    outer_into(blocks, h_ref, *refs)
+
+
+def second_half_body(o_in, h_ref, ahead, far, *refs):
+    yl, c = lax.axis_index("yl"), lax.axis_index("c")
+    blocks = []
+    for k, ref in ((1 + 2 * c, ahead), (2, far)):
+        blocks += [(yl, k, ref.at[0:2]), (1 - yl, k, ref.at[2:4])]
+    outer_into(blocks, h_ref, *refs)
+
+
+def outer_half(body, name, operands, so_far=None):
+    aliased = so_far is not None
+    return pl.pallas_call(
+        body,
         out_shape=jax.ShapeDtypeStruct((2048, 4, 256), BF),
-        in_specs=[IN] * 8,
+        in_specs=[HBM] * aliased + [IN] * len(operands),
         out_specs=HBM,
-        scratch_shapes=[
-            VM((8, 256, 4, 256), BF),
-            pltpu.SemaphoreType.DMA((8,)),
-        ],
-        compiler_params=LIMIT,
-        name="outer",
-    )(*kept(*operands))
+        scratch_shapes=[VM((4, 256, 4, 256), BF), pltpu.SemaphoreType.DMA((4,))],
+        input_output_aliases={0: 0} if aliased else {},
+        compiler_params=LIMIT,
+        cost_estimate=pl.CostEstimate(flops=int(2e9), bytes_accessed=5 << 20, transcendentals=0),
+        name=name,
+    )(*([so_far] if aliased else []), *kept(*operands))
+
+
+def along_x(value, forward_core):
+    pairs = []
+    for x in range(4):
+        for c in range(2):
+            k = 1 if c == forward_core else 3
+            pairs.append((x * 2 + c, (x + k) % 4 * 2 + c))
+    return lax.ppermute(value, ("x", "c"), pairs)
 
 
 def per_device(hidden, grad_out, weight_base, block_scale):
     w5 = pltpu.with_memory_space_constraint(weight_base.reshape(4, 2, 4, 256, 256), pltpu.HBM)
-    scales_t = block_scale.T
+    scales_t = pltpu.with_memory_space_constraint(block_scale.T, pltpu.HBM)
 
     sent = scaled_rows(w5, scales_t)
     r0 = sent[0]
@@ -324,11 +347,11 @@
     grad_out, hidden, _ = lax.optimization_barrier((grad_out, hidden, r0))
     g0, h = all_tokens(packed(grad_out, hidden))
     g2, g3 = [shift(g0, first_axis_steps(k)) for k in (2, 3)]
-    later, r2 = lax.optimization_barrier((g0, r2))
+    later, r1 = lax.optimization_barrier((g0, r1))
     g1 = shift(later, first_axis_steps(1))
 
-    acc = early_sums(r0, r2, g0, g2)
-    *sums, keep, give = partial_sums(acc, r1, r3, g0, g1, g2, g3)
+    acc = early_sums(r0, r3, g0, g3)
+    *sums, keep, give = partial_sums(acc, r1, r2, g0, g1, g2, g3)
     parts = [sums[0]] + [None] * 3
     for k in (2, 1, 3):
         parts[k] = shift(sums[k], second_axis_steps(k))
@@ -337,11 +360,13 @@
     grad_hidden = finished(blocks)
 
     seed = picked(lax.ppermute(give, "c", [(1, 0)]), keep)
-    ring = lambda k: [(i, (i + k) % 4) for i in range(4)]
     other = swap(seed, "yl")
-    x1, x3 = [lax.ppermute(seed, "x", ring(k)) for k in (1, 3)]
-    x2 = lax.ppermute(paired(seed, other), "x", ring(2))
-    grad_weight = outer_product(h, x2, seed, x1, x3, other, swap(x1, "yl"), swap(x3, "yl"))
+    back = along_x(seed, 1)
+    both = paired(seed, other)
+    ahead = along_x(both, 0)
+    far = lax.ppermute(both, "x", [(i, (i + 2) % 4) for i in range(4)])
+    half = outer_half(first_half_body, "first_half", (h, seed, other, back, swap(back, "yl")))
+    grad_weight = outer_half(second_half_body, "second_half", (h, ahead, far), half)
     return grad_hidden, grad_weight
 
 

time: 93.7 us -> 98.1 us (1.047)
  the two profiles are of different devices: /device:TPU:96 before, /device:TPU:103 now
where the time goes in v6:
time: 98.1 us; the launch traced here: 97.8 us
  waiting for transfers between devices  46.1 us (47%)
  starting transfers between devices  36.5 us (37%)
  Pallas kernels  13.4 us (14%)
    ppermute x9, waiting for transfers between devices, shift(): return lax.ppermute(value, ('z', 'x', 'c'), pairs)  25 us
    ppermute x5, waiting for transfers between devices, swap(): return lax.ppermute(value, axis, [(0, 1), (1, 0)])  21 us
    ppermute x5, starting transfers between devices, swap(): return lax.ppermute(value, axis, [(0, 1), (1, 0)])  11 us
    all_to_all x1, starting transfers between devices, per_device(): blocks = lax.all_to_all(blocks, ('yl', 'yh', 'c'), 0, 0, tiled=True)  10.9 us
    ppermute x9, starting transfers between devices, shift(): return lax.ppermute(value, ('z', 'x', 'c'), pairs)  6.26 us
    pallas_call x2, Pallas kernels, outer_half(): pl.pallas_call(body, out_shape=jax.ShapeDtypeStruct((2048, 4, 256), BF),...  6.19 us
    ppermute x1, starting transfers between devices, per_device(): seed = picked(lax.ppermute(give, 'c', [(1, 0)]), keep)  3.85 us
    pallas_call x1, Pallas kernels, scaled_rows(): pl.pallas_call(scale_body, out_shape=[VM((8, 256, 256), BF)] * 4, in_spec...  2.41 us
  transfers between devices with their start and end apart: 19, of which 7 were waited for; matrix products, arithmetic and copies ran while one was open for 0% of the time, Pallas kernels for 7%

profile of v6, /device:TPU:103, one launch (start us, length us, event | category | flops | bytes accessed | tf_op | source)
XLA Modules:
  0.0 97.8 jit_solution(729189368514933204)
XLA Ops:
  0.7 2.4 %scale.1 = (bf16[8,256,256]{2,1,0:T(8,128)(2,1)S(1)}, bf16[8,256,256]{2,1,0:T(8,128)(2,1)S(1)}, bf16[8,256,256]{2,1,0:T(8,128)(2,1)S(1)}, bf16[8,256,256]{2,1,0:T(8,128)(2,1)S(1)}) custom-call(bf16[4,2,4,256,256]{4,3,2,1,0:T(8,128)(2,1)} %bitcast.2, bf16[16,512]{1,0:T(8,128)(2,1)} %bitcast.3), custom_call_target="tpu_custom_call" | custom-call | tf_op jit(solution)/shard_map/scale/pallas_call | solution.py:96
  3.1 0.1 collective-permute-start.5
  3.2 1.5 %collective-permute-start = (bf16[8,256,256]{2,1,0:T(8,128)(2,1)S(1)}, bf16[8,256,256]{2,1,0:T(8,128)(2,1)S(1)}, u32[]{:S(2)}, u32[]{:S(2)}) collective-permute-start(bf16[8,256,256]{2,1,0:T(8,128)(2,1)S(1)} %get-tuple-element.19), channel_id=1, source_target_pairs={{0,12},{1,97},{4,0},{5,101},{8,4},{9,105},{12,8},{13,109},{32,44},... | collective-permute-start | bytes 3145736 | tf_op jit(solution)/shard_map/ppermute | solution.py:34
  4.6 0.1 packed.1.p0
  4.7 3.0 %collective-permute-start.2 = (bf16[5,128,256]{2,1,0:T(8,128)(2,1)S(1)}, bf16[5,128,256]{2,1,0:T(8,128)(2,1)S(1)}, u32[]{:S(2)}, u32[]{:S(2)}) collective-permute-start(bf16[5,128,256]{2,1,0:T(8,128)(2,1)S(1)} %packed.1.p0), channel_id=1, source_target_pairs={{0,2},{2,0},{1,3},{3,1},{4,6},{6,4},{5,7},{7,5},{8,10},{10,8},{9,1... | collective-permute-start | bytes 983048 | tf_op jit(solution)/shard_map/ppermute | solution.py:38
  7.7 0.5 collective-permute-start.6
  8.1 2.5 %collective-permute-start.1 = (bf16[5,128,256]{2,1,0:T(8,128)(2,1)S(1)}, bf16[5,128,256]{2,1,0:T(8,128)(2,1)S(1)}, u32[]{:S(2)}, u32[]{:S(2)}) collective-permute-start(bf16[5,128,256]{2,1,0:T(8,128)(2,1)S(1)} %packed.1.p0), channel_id=1, source_target_pairs={{0,1},{1,0},{2,3},{3,2},{4,5},{5,4},{6,7},{7,6},{8,9},{9,8},{10,11... | collective-permute-start | bytes 983048 | tf_op jit(solution)/shard_map/ppermute | solution.py:38
  10.6 3.6 %collective-permute-done.2.p2 = bf16[5,128,256]{2,1,0:T(8,128)(2,1)S(1)} collective-permute-done((bf16[5,128,256]{2,1,0:T(8,128)(2,1)S(1)}, bf16[5,128,256]{2,1,0:T(8,128)(2,1)S(1)}, u32[]{:S(2)}, u32[]{:S(2)}) %collective-permute-start.2) | collective-permute-done | bytes 327712 | tf_op jit(solution)/shard_map/ppermute | solution.py:38
  14.2 2.2 %collective-permute-start.3 = (bf16[5,128,256]{2,1,0:T(8,128)(2,1)S(1)}, bf16[5,128,256]{2,1,0:T(8,128)(2,1)S(1)}, u32[]{:S(2)}, u32[]{:S(2)}) collective-permute-start(bf16[5,128,256]{2,1,0:T(8,128)(2,1)S(1)} %collective-permute-done.2.p2), channel_id=1, source_target_pairs={{0,1},{1,0},{2,3},{3,2},{4,5},{5,4},{6,7},{7,6},{8,9},{9,8},{10,11... | collective-permute-start | bytes 983048 | tf_op jit(solution)/shard_map/ppermute | solution.py:38
  16.4 0.0 collective-permute-done.1.p1
  16.4 1.3 %collective-permute-done.3.p3 = bf16[5,128,256]{2,1,0:T(8,128)(2,1)S(1)} collective-permute-done((bf16[5,128,256]{2,1,0:T(8,128)(2,1)S(1)}, bf16[5,128,256]{2,1,0:T(8,128)(2,1)S(1)}, u32[]{:S(2)}, u32[]{:S(2)}) %collective-permute-start.3) | collective-permute-done | bytes 327712 | tf_op jit(solution)/shard_map/ppermute | solution.py:38
  17.7 0.1 tokens.1
  17.8 0.2 collective-permute-start.4
  18.0 1.4 %collective-permute-start.8 = (bf16[2,256,256]{2,1,0:T(8,128)(2,1)S(1)}, bf16[2,256,256]{2,1,0:T(8,128)(2,1)S(1)}, u32[]{:S(2)}, u32[]{:S(2)}) collective-permute-start(bf16[2,256,256]{2,1,0:T(8,128)(2,1)S(1)} %get-tuple-element.26.g0), channel_id=1, source_target_pairs={{0,8},{1,65},{4,12},{5,69},{8,0},{9,73},{12,4},{13,77},{32,40},{33... | collective-permute-start | bytes 786440 | tf_op jit(solution)/shard_map/ppermute | solution.py:34
  19.3 0.0 collective-permute-done.5.r1
  19.3 1.2 %collective-permute-start.7 = (bf16[2,256,256]{2,1,0:T(8,128)(2,1)S(1)}, bf16[2,256,256]{2,1,0:T(8,128)(2,1)S(1)}, u32[]{:S(2)}, u32[]{:S(2)}) collective-permute-start(bf16[2,256,256]{2,1,0:T(8,128)(2,1)S(1)} %get-tuple-element.26.g0), channel_id=1, source_target_pairs={{0,4},{1,33},{4,8},{5,37},{8,12},{9,41},{12,0},{13,45},{32,36},{33... | collective-permute-start | bytes 786440 | tf_op jit(solution)/shard_map/ppermute | solution.py:34
  20.5 14.7 %collective-permute-done.4.g3 = bf16[2,256,256]{2,1,0:T(8,128)(2,1)S(1)} collective-permute-done((bf16[2,256,256]{2,1,0:T(8,128)(2,1)S(1)}, bf16[2,256,256]{2,1,0:T(8,128)(2,1)S(1)}, u32[]{:S(2)}, u32[]{:S(2)}) %collective-permute-start.4) | collective-permute-done | bytes 262176 | tf_op jit(solution)/shard_map/ppermute | solution.py:34
  35.2 0.0 collective-permute-done.r3
  35.2 1.3 %early.1.acc = f32[4,512,512]{2,1,0:T(8,128)S(1)} custom-call(bf16[8,256,256]{2,1,0:T(8,128)(2,1)S(1)} %get-tuple-element.18.r0, bf16[8,256,256]{2,1,0:T(8,128)(2,1)S(1)} %collective-permute-done.r3, bf16[2,256,256]{2,1,0:T(8,128)(2,1)S(1)} %get-tuple-element.26.g0, bf16[2,256,256]{2,1,0:T(8,128)(2,1)S(1)} %collective-permute-done.4.g3), custom_call_target="tpu_custom_call" | custom-call | flops 2000000000 | bytes 6291456 | tf_op jit(solution)/shard_map/early/pallas_call | solution.py:163
  36.5 0.0 collective-permute-done.8.g2
  36.5 0.0 collective-permute-done.6.r2
  36.5 0.0 collective-permute-done.7.g1
  36.6 1.4 %partial.1 = (f32[512,512]{1,0:T(8,128)S(1)}, bf16[512,512]{1,0:T(8,128)(2,1)S(1)}, bf16[512,512]{1,0:T(8,128)(2,1)S(1)}, bf16[512,512]{1,0:T(8,128)(2,1)S(1)}, ...) custom-call(f32[4,512,512]{2,1,0:T(8,128)S(1)} %early.1.acc, ...), custom_call_target="tpu_custom_call" | custom-call | tf_op jit(solution)/shard_map/partial/pallas_call | solution.py:196
  37.9 3.9 %collective-permute-start.12 = (bf16[2,256,256]{2,1,0:T(8,128)(2,1)S(1)}, bf16[2,256,256]{2,1,0:T(8,128)(2,1)S(1)}, u32[]{:S(2)}, u32[]{:S(2)}) collective-permute-start(bf16[2,256,256]{2,1,0:T(8,128)(2,1)S(1)} %get-tuple-element.32), channel_id=1, source_target_pairs={{1,0},{3,2},{5,4},{7,6},{9,8},{11,10},{13,12},{15,14},{17,16},{19,... | collective-permute-start | bytes 786440 | tf_op jit(solution)/shard_map/ppermute | solution.py:362
  41.8 0.1 collective-permute-start.9
  41.9 0.3 collective-permute-start.10
  42.2 1.1 %collective-permute-start.11 = (bf16[512,512]{1,0:T(8,128)(2,1)S(1)}, bf16[512,512]{1,0:T(8,128)(2,1)S(1)}, u32[]{:S(2)}, u32[]{:S(2)}) collective-permute-start(bf16[512,512]{1,0:T(8,128)(2,1)S(1)} %get-tuple-element.30), channel_id=1, source_target_pairs={{0,96},{1,13},{4,100},{5,1},{8,104},{9,5},{12,108},{13,9},{32,0},{... | collective-permute-start | bytes 1572872 | tf_op jit(solution)/shard_map/ppermute | solution.py:34
  43.3 0.0 collective-permute-done.12.a_ref
  43.4 1.4 %collective-permute-start.13 = (bf16[2,256,256]{2,1,0:T(8,128)(2,1)S(1)}, bf16[2,256,256]{2,1,0:T(8,128)(2,1)S(1)}, u32[]{:S(2)}, u32[]{:S(2)}) collective-permute-start(bf16[2,256,256]{2,1,0:T(8,128)(2,1)S(1)} %picked.1.seed.a_ref), channel_id=1, source_target_pairs={{0,16},{16,0},{1,17},{17,1},{2,18},{18,2},{3,19},{19,3},{4,20},{20... | collective-permute-start | bytes 786440 | tf_op jit(solution)/shard_map/ppermute | solution.py:38
  44.7 2.4 %collective-permute-start.14 = (bf16[2,256,256]{2,1,0:T(8,128)(2,1)S(1)}, bf16[2,256,256]{2,1,0:T(8,128)(2,1)}, u32[]{:S(2)}, u32[]{:S(2)}) collective-permute-start(bf16[2,256,256]{2,1,0:T(8,128)(2,1)S(1)} %picked.1.seed.a_ref), channel_id=1, source_target_pairs={{0,12},{1,5},{4,0},{5,9},{8,4},{9,13},{12,8},{13,1},{2,14},{3,7},{... | collective-permute-start | bytes 786440 | tf_op jit(solution)/shard_map/ppermute | solution.py:336
  47.1 3.9 %collective-permute-done.13.other.b_ref = bf16[2,256,256]{2,1,0:T(8,128)(2,1)S(1)} collective-permute-done((bf16[2,256,256]{2,1,0:T(8,128)(2,1)S(1)}, bf16[2,256,256]{2,1,0:T(8,128)(2,1)S(1)}, u32[]{:S(2)}, u32[]{:S(2)}) %collective-permute-start.13) | collective-permute-done | bytes 262176 | tf_op jit(solution)/shard_map/ppermute | solution.py:38
  51.1 2.0 %collective-permute-start.17 = (bf16[4,256,256]{2,1,0:T(8,128)(2,1)S(1)}, bf16[4,256,256]{2,1,0:T(8,128)(2,1)S(1)}, u32[]{:S(2)}, u32[]{:S(2)}) collective-permute-start(bf16[4,256,256]{2,1,0:T(8,128)(2,1)S(1)} %paired.1), channel_id=1, source_target_pairs={{0,8},{4,12},{8,0},{12,4},{1,9},{5,13},{9,1},{13,5},{2,10},{6,14},... | collective-permute-start | bytes 1572872 | tf_op jit(solution)/shard_map/ppermute | solution.py:367
  53.1 0.0 collective-permute-done.9.b
  53.1 0.0 collective-permute-start.16
  53.1 1.3 %collective-permute-done.10.c = bf16[512,512]{1,0:T(8,128)(2,1)S(1)} collective-permute-done((bf16[512,512]{1,0:T(8,128)(2,1)S(1)}, bf16[512,512]{1,0:T(8,128)(2,1)S(1)}, u32[]{:S(2)}, u32[]{:S(2)}) %collective-permute-start.10) | collective-permute-done | bytes 524320 | tf_op jit(solution)/shard_map/ppermute | solution.py:34
  54.4 9.0 %collective-permute-done.11.d = bf16[512,512]{1,0:T(8,128)(2,1)S(1)} collective-permute-done((bf16[512,512]{1,0:T(8,128)(2,1)S(1)}, bf16[512,512]{1,0:T(8,128)(2,1)S(1)}, u32[]{:S(2)}, u32[]{:S(2)}) %collective-permute-start.11) | collective-permute-done | bytes 524320 | tf_op jit(solution)/shard_map/ppermute | solution.py:34
  63.4 1.0 %summed.1 = bf16[8,128,256]{2,1,0:T(8,128)(2,1)} custom-call(f32[512,512]{1,0:T(8,128)S(1)} %get-tuple-element.27.a, bf16[512,512]{1,0:T(8,128)(2,1)S(1)} %collective-permute-done.9.b, bf16[512,512]{1,0:T(8,128)(2,1)S(1)} %collective-permute-done.10.c, bf16[512,512]{1,0:T(8,128)(2,1)S(1)} %collective-permute-done.11.d), custom_call_target="tpu_custom_call" | custom-call | tf_op jit(solution)/shard_map/summed/pallas_call | solution.py:218
  64.4 10.9 %all-to-all-start = ((bf16[8,128,256]{2,1,0:T(8,128)(2,1)}), bf16[8,128,256]{2,1,0:T(8,128)(2,1)S(1)}, u32[]{:S(2)}, u32[]{:S(2)}) async-start(bf16[8,128,256]{2,1,0:T(8,128)(2,1)} %summed.1), calls=%async_computation | async-start | bytes 1048576 | tf_op jit(solution)/shard_map/all_to_all | solution.py:359
  75.4 0.0 collective-permute-done.14.back
  75.4 2.1 %collective-permute-start.15 = (bf16[2,256,256]{2,1,0:T(8,128)(2,1)}, bf16[2,256,256]{2,1,0:T(8,128)(2,1)S(1)}, u32[]{:S(2)}, u32[]{:S(2)}) collective-permute-start(bf16[2,256,256]{2,1,0:T(8,128)(2,1)} %collective-permute-done.14.back), channel_id=1, source_target_pairs={{0,16},{16,0},{1,17},{17,1},{2,18},{18,2},{3,19},{19,3},{4,20},{20... | collective-permute-start | bytes 786440 | tf_op jit(solution)/shard_map/ppermute | solution.py:38
  77.4 12.2 %collective-permute-done.15.back_other = bf16[2,256,256]{2,1,0:T(8,128)(2,1)S(1)} collective-permute-done((bf16[2,256,256]{2,1,0:T(8,128)(2,1)}, bf16[2,256,256]{2,1,0:T(8,128)(2,1)S(1)}, u32[]{:S(2)}, u32[]{:S(2)}) %collective-permute-start.15) | collective-permute-done | bytes 262176 | tf_op jit(solution)/shard_map/ppermute | solution.py:38
  89.6 0.9 copy-done.2
  90.6 3.6 %first_half.1.o_in = bf16[2048,4,256]{2,1,0:T(4,128)(2,1)} custom-call(bf16[512,1024]{1,0:T(8,128)(2,1)S(1)} %get-tuple-element.31.h_ref, bf16[2,256,256]{2,1,0:T(8,128)(2,1)S(1)} %picked.1.seed.a_ref, bf16[2,256,256]{2,1,0:T(8,128)(2,1)S(1)} %copy-done.2, bf16[2,256,256]{2,1,0:T(8,128)(2,1)} %collective-permute-done.14.back, ...), custom_call_target="tpu_custom_call" | custom-call | flops 2000000000 | bytes 5242880 | tf_op jit(solution)/shard_map/first_half/pallas_call | solution.py:317
  94.2 0.0 all-to-all-done.r_ref
  94.2 0.9 finish.1
  95.0 0.0 collective-permute-done.17.far
  95.0 0.0 collective-permute-done.16.ahead
  95.1 2.6 %second_half.1 = bf16[2048,4,256]{2,1,0:T(4,128)(2,1)} custom-call(bf16[2048,4,256]{2,1,0:T(4,128)(2,1)} %first_half.1.o_in, bf16[512,1024]{1,0:T(8,128)(2,1)S(1)} %get-tuple-element.31.h_ref, bf16[4,256,256]{2,1,0:T(8,128)(2,1)S(1)} %collective-permute-done.16.ahead, ...), custom_call_target="tpu_custom_call", output_to_operand_aliasing={{}: (0, {})} | custom-call | flops 2000000000 | bytes 5242880 | tf_op jit(solution)/shard_map/second_half/pallas_call | solution.py:317
  (9 shorter events, 0.1 us)
Async XLA Ops:
  0.6 4.0 %copy-start.3 = (bf16[128,256]{1,0:T(8,128)(2,1)S(1)}, bf16[128,256]{1,0:T(8,128)(2,1)}, u32[]{:S(2)}) copy-start(bf16[128,256]{1,0:T(8,128)(2,1)} %g_ref) | copy-start | bytes 196612
  0.6 4.0 %copy-start = (bf16[128,4,256]{2,1,0:T(4,128)(2,1)S(1)}, bf16[128,4,256]{2,1,0:T(4,128)(2,1)}, u32[]{:S(2)}) copy-start(bf16[128,4,256]{2,1,0:T(4,128)(2,1)} %h_ref) | copy-start | bytes 786436
  3.1 16.3 %collective-permute-start.5 = (bf16[8,256,256]{2,1,0:T(8,128)(2,1)S(1)}, bf16[8,256,256]{2,1,0:T(8,128)(2,1)S(1)}, u32[]{:S(2)}, u32[]{:S(2)}) collective-permute-start(bf16[8,256,256]{2,1,0:T(8,128)(2,1)S(1)} %get-tuple-element.23), channel_id=1, source_target_pairs={{0,4},{1,33},{4,8},{5,37},{8,12},{9,41},{12,0},{13,45},{32,36},{33... | collective-permute-start | bytes 3145736 | tf_op jit(solution)/shard_map/ppermute | solution.py:34
  3.2 32.1 %collective-permute-start = (bf16[8,256,256]{2,1,0:T(8,128)(2,1)S(1)}, bf16[8,256,256]{2,1,0:T(8,128)(2,1)S(1)}, u32[]{:S(2)}, u32[]{:S(2)}) collective-permute-start(bf16[8,256,256]{2,1,0:T(8,128)(2,1)S(1)} %get-tuple-element.19), channel_id=1, source_target_pairs={{0,12},{1,97},{4,0},{5,101},{8,4},{9,105},{12,8},{13,109},{32,44},... | collective-permute-start | bytes 3145736 | tf_op jit(solution)/shard_map/ppermute | solution.py:34
  4.7 9.5 %collective-permute-start.2 = (bf16[5,128,256]{2,1,0:T(8,128)(2,1)S(1)}, bf16[5,128,256]{2,1,0:T(8,128)(2,1)S(1)}, u32[]{:S(2)}, u32[]{:S(2)}) collective-permute-start(bf16[5,128,256]{2,1,0:T(8,128)(2,1)S(1)} %packed.1.p0), channel_id=1, source_target_pairs={{0,2},{2,0},{1,3},{3,1},{4,6},{6,4},{5,7},{7,5},{8,10},{10,8},{9,1... | collective-permute-start | bytes 983048 | tf_op jit(solution)/shard_map/ppermute | solution.py:38
  7.7 28.9 %collective-permute-start.6 = (bf16[8,256,256]{2,1,0:T(8,128)(2,1)S(1)}, bf16[8,256,256]{2,1,0:T(8,128)(2,1)S(1)}, u32[]{:S(2)}, u32[]{:S(2)}) collective-permute-start(bf16[8,256,256]{2,1,0:T(8,128)(2,1)S(1)} %get-tuple-element.25), channel_id=1, source_target_pairs={{0,8},{1,65},{4,12},{5,69},{8,0},{9,73},{12,4},{13,77},{32,40},{33... | collective-permute-start | bytes 3145736 | tf_op jit(solution)/shard_map/ppermute | solution.py:34
  8.1 8.3 %collective-permute-start.1 = (bf16[5,128,256]{2,1,0:T(8,128)(2,1)S(1)}, bf16[5,128,256]{2,1,0:T(8,128)(2,1)S(1)}, u32[]{:S(2)}, u32[]{:S(2)}) collective-permute-start(bf16[5,128,256]{2,1,0:T(8,128)(2,1)S(1)} %packed.1.p0), channel_id=1, source_target_pairs={{0,1},{1,0},{2,3},{3,2},{4,5},{5,4},{6,7},{7,6},{8,9},{9,8},{10,11... | collective-permute-start | bytes 983048 | tf_op jit(solution)/shard_map/ppermute | solution.py:38
  14.2 3.4 %collective-permute-start.3 = (bf16[5,128,256]{2,1,0:T(8,128)(2,1)S(1)}, bf16[5,128,256]{2,1,0:T(8,128)(2,1)S(1)}, u32[]{:S(2)}, u32[]{:S(2)}) collective-permute-start(bf16[5,128,256]{2,1,0:T(8,128)(2,1)S(1)} %collective-permute-done.2.p2), channel_id=1, source_target_pairs={{0,1},{1,0},{2,3},{3,2},{4,5},{5,4},{6,7},{7,6},{8,9},{9,8},{10,11... | collective-permute-start | bytes 983048 | tf_op jit(solution)/shard_map/ppermute | solution.py:38
  17.8 17.4 %collective-permute-start.4 = (bf16[2,256,256]{2,1,0:T(8,128)(2,1)S(1)}, bf16[2,256,256]{2,1,0:T(8,128)(2,1)S(1)}, u32[]{:S(2)}, u32[]{:S(2)}) collective-permute-start(bf16[2,256,256]{2,1,0:T(8,128)(2,1)S(1)} %get-tuple-element.26.g0), channel_id=1, source_target_pairs={{0,12},{1,97},{4,0},{5,101},{8,4},{9,105},{12,8},{13,109},{32,44},... | collective-permute-start | bytes 786440 | tf_op jit(solution)/shard_map/ppermute | solution.py:34
  18.0 18.5 %collective-permute-start.8 = (bf16[2,256,256]{2,1,0:T(8,128)(2,1)S(1)}, bf16[2,256,256]{2,1,0:T(8,128)(2,1)S(1)}, u32[]{:S(2)}, u32[]{:S(2)}) collective-permute-start(bf16[2,256,256]{2,1,0:T(8,128)(2,1)S(1)} %get-tuple-element.26.g0), channel_id=1, source_target_pairs={{0,8},{1,65},{4,12},{5,69},{8,0},{9,73},{12,4},{13,77},{32,40},{33... | collective-permute-start | bytes 786440 | tf_op jit(solution)/shard_map/ppermute | solution.py:34
  19.3 17.2 %collective-permute-start.7 = (bf16[2,256,256]{2,1,0:T(8,128)(2,1)S(1)}, bf16[2,256,256]{2,1,0:T(8,128)(2,1)S(1)}, u32[]{:S(2)}, u32[]{:S(2)}) collective-permute-start(bf16[2,256,256]{2,1,0:T(8,128)(2,1)S(1)} %get-tuple-element.26.g0), channel_id=1, source_target_pairs={{0,4},{1,33},{4,8},{5,37},{8,12},{9,41},{12,0},{13,45},{32,36},{33... | collective-permute-start | bytes 786440 | tf_op jit(solution)/shard_map/ppermute | solution.py:34
  37.9 5.4 %collective-permute-start.12 = (bf16[2,256,256]{2,1,0:T(8,128)(2,1)S(1)}, bf16[2,256,256]{2,1,0:T(8,128)(2,1)S(1)}, u32[]{:S(2)}, u32[]{:S(2)}) collective-permute-start(bf16[2,256,256]{2,1,0:T(8,128)(2,1)S(1)} %get-tuple-element.32), channel_id=1, source_target_pairs={{1,0},{3,2},{5,4},{7,6},{9,8},{11,10},{13,12},{15,14},{17,16},{19,... | collective-permute-start | bytes 786440 | tf_op jit(solution)/shard_map/ppermute | solution.py:362
  41.8 11.3 %collective-permute-start.9 = (bf16[512,512]{1,0:T(8,128)(2,1)S(1)}, bf16[512,512]{1,0:T(8,128)(2,1)S(1)}, u32[]{:S(2)}, u32[]{:S(2)}) collective-permute-start(bf16[512,512]{1,0:T(8,128)(2,1)S(1)} %get-tuple-element.28), channel_id=1, source_target_pairs={{0,32},{1,5},{4,36},{5,9},{8,40},{9,13},{12,44},{13,1},{32,64},{33... | collective-permute-start | bytes 1572872 | tf_op jit(solution)/shard_map/ppermute | solution.py:34
  41.9 12.5 %collective-permute-start.10 = (bf16[512,512]{1,0:T(8,128)(2,1)S(1)}, bf16[512,512]{1,0:T(8,128)(2,1)S(1)}, u32[]{:S(2)}, u32[]{:S(2)}) collective-permute-start(bf16[512,512]{1,0:T(8,128)(2,1)S(1)} %get-tuple-element.29), channel_id=1, source_target_pairs={{0,64},{1,9},{4,68},{5,13},{8,72},{9,1},{12,76},{13,5},{32,96},{33... | collective-permute-start | bytes 1572872 | tf_op jit(solution)/shard_map/ppermute | solution.py:34
  42.2 21.2 %collective-permute-start.11 = (bf16[512,512]{1,0:T(8,128)(2,1)S(1)}, bf16[512,512]{1,0:T(8,128)(2,1)S(1)}, u32[]{:S(2)}, u32[]{:S(2)}) collective-permute-start(bf16[512,512]{1,0:T(8,128)(2,1)S(1)} %get-tuple-element.30), channel_id=1, source_target_pairs={{0,96},{1,13},{4,100},{5,1},{8,104},{9,5},{12,108},{13,9},{32,0},{... | collective-permute-start | bytes 1572872 | tf_op jit(solution)/shard_map/ppermute | solution.py:34
  43.4 7.7 %collective-permute-start.13 = (bf16[2,256,256]{2,1,0:T(8,128)(2,1)S(1)}, bf16[2,256,256]{2,1,0:T(8,128)(2,1)S(1)}, u32[]{:S(2)}, u32[]{:S(2)}) collective-permute-start(bf16[2,256,256]{2,1,0:T(8,128)(2,1)S(1)} %picked.1.seed.a_ref), channel_id=1, source_target_pairs={{0,16},{16,0},{1,17},{17,1},{2,18},{18,2},{3,19},{19,3},{4,20},{20... | collective-permute-start | bytes 786440 | tf_op jit(solution)/shard_map/ppermute | solution.py:38
  44.7 30.6 %collective-permute-start.14 = (bf16[2,256,256]{2,1,0:T(8,128)(2,1)S(1)}, bf16[2,256,256]{2,1,0:T(8,128)(2,1)}, u32[]{:S(2)}, u32[]{:S(2)}) collective-permute-start(bf16[2,256,256]{2,1,0:T(8,128)(2,1)S(1)} %picked.1.seed.a_ref), channel_id=1, source_target_pairs={{0,12},{1,5},{4,0},{5,9},{8,4},{9,13},{12,8},{13,1},{2,14},{3,7},{... | collective-permute-start | bytes 786440 | tf_op jit(solution)/shard_map/ppermute | solution.py:336
  51.0 12.4 %copy-start.1 = (bf16[2,256,256]{2,1,0:T(8,128)(2,1)}, bf16[2,256,256]{2,1,0:T(8,128)(2,1)S(1)}, u32[]{:S(2)}) copy-start(bf16[2,256,256]{2,1,0:T(8,128)(2,1)S(1)} %collective-permute-done.13.other.b_ref) | copy-start | bytes 786436
  51.1 44.0 %collective-permute-start.17 = (bf16[4,256,256]{2,1,0:T(8,128)(2,1)S(1)}, bf16[4,256,256]{2,1,0:T(8,128)(2,1)S(1)}, u32[]{:S(2)}, u32[]{:S(2)}) collective-permute-start(bf16[4,256,256]{2,1,0:T(8,128)(2,1)S(1)} %paired.1), channel_id=1, source_target_pairs={{0,8},{4,12},{8,0},{12,4},{1,9},{5,13},{9,1},{13,5},{2,10},{6,14},... | collective-permute-start | bytes 1572872 | tf_op jit(solution)/shard_map/ppermute | solution.py:367
  53.1 42.0 %collective-permute-start.16 = (bf16[4,256,256]{2,1,0:T(8,128)(2,1)S(1)}, bf16[4,256,256]{2,1,0:T(8,128)(2,1)S(1)}, u32[]{:S(2)}, u32[]{:S(2)}) collective-permute-start(bf16[4,256,256]{2,1,0:T(8,128)(2,1)S(1)} %paired.1), channel_id=1, source_target_pairs={{0,4},{1,13},{4,8},{5,1},{8,12},{9,5},{12,0},{13,9},{2,6},{3,15},{... | collective-permute-start | bytes 1572872 | tf_op jit(solution)/shard_map/ppermute | solution.py:336
  64.4 29.8 %all-to-all-start = ((bf16[8,128,256]{2,1,0:T(8,128)(2,1)}), bf16[8,128,256]{2,1,0:T(8,128)(2,1)S(1)}, u32[]{:S(2)}, u32[]{:S(2)}) async-start(bf16[8,128,256]{2,1,0:T(8,128)(2,1)} %summed.1), calls=%async_computation | async-start | bytes 1048576 | tf_op jit(solution)/shard_map/all_to_all | solution.py:359
  75.4 14.3 %collective-permute-start.15 = (bf16[2,256,256]{2,1,0:T(8,128)(2,1)}, bf16[2,256,256]{2,1,0:T(8,128)(2,1)S(1)}, u32[]{:S(2)}, u32[]{:S(2)}) collective-permute-start(bf16[2,256,256]{2,1,0:T(8,128)(2,1)} %collective-permute-done.14.back), channel_id=1, source_target_pairs={{0,16},{16,0},{1,17},{17,1},{2,18},{18,2},{3,19},{19,3},{4,20},{20... | collective-permute-start | bytes 786440 | tf_op jit(solution)/shard_map/ppermute | solution.py:38
  89.6 1.0 copy-start.2

commit v7 on v6

--- a/solution.py
+++ b/solution.py
@@ -104,45 +104,42 @@
     )(w5, scales_t)
 
 
-def packed_body(g_ref, h_ref, o_ref):
-    o_ref[0] = g_ref[...]
-    h = h_ref[...].reshape(128, 1024)
-    for n in range(4):
-        o_ref[1 + n] = h[:, n * 256 : (n + 1) * 256]
-
-
-def packed(grad_out, hidden):
-    return pl.pallas_call(
-        packed_body,
-        out_shape=VM((5, 128, 256), BF),
-        in_specs=[IN] * 2,
-        out_specs=IN,
-        compiler_params=LIMIT,
-        name="packed",
-    )(grad_out, hidden)
-
-
-def tokens_body(p0, p1, p2, p3, g_ref, h_ref):
+def swapped(own):
+    far = swap(own, "yh")
+    return [own, swap(own, "c"), far, swap(far, "c")]
+
+
+def tokens_body(p0, p1, p2, p3, g_ref):
     n = lax.axis_index("yh") * 2 + lax.axis_index("c")
     for r, p in enumerate((p0, p1, p2, p3)):
         t = n ^ r
-        g_ref[t >> 1, pl.ds(pl.multiple_of((t & 1) * 128, 128), 128), :] = p[0]
-        rows = pl.ds(pl.multiple_of(t * 128, 128), 128)
-        for m in range(4):
-            h_ref[rows, m * 256 : (m + 1) * 256] = p[1 + m]
+        g_ref[t >> 1, pl.ds(pl.multiple_of((t & 1) * 128, 128), 128), :] = p[...]
 
 
 def all_tokens(own):
-    far = swap(own, "yh")
-    pieces = [own, swap(own, "c"), far, swap(far, "c")]
     return pl.pallas_call(
         tokens_body,
-        out_shape=[VM((2, 256, 256), BF), VM((512, 1024), BF)],
+        out_shape=VM((2, 256, 256), BF),
         in_specs=[IN] * 4,
-        out_specs=[IN] * 2,
+        out_specs=IN,
         compiler_params=LIMIT,
         name="tokens",
-    )(*kept(*pieces))
+    )(*kept(*swapped(own)))
+
+
+def flat_body(h_ref, o_ref):
+    o_ref[...] = h_ref[...].reshape(128, 1024)
+
+
+def flat(hidden):
+    return pl.pallas_call(
+        flat_body,
+        out_shape=VM((128, 1024), BF),
+        in_specs=[IN],
+        out_specs=IN,
+        compiler_params=LIMIT,
+        name="flat",
+    )(hidden)
 
 
 def block_product(g, w, q):
@@ -154,16 +151,20 @@
     )
 
 
-def early_body(r0, r3, g0, g3, acc):
+def early_body(r0, r1, r3, g0, g1, g3, acc):
     for q in range(4):
-        acc[q] = block_product(g0, r0, 2 * q) + block_product(g3, r3, 2 * q)
+        acc[q] = (
+            block_product(g0, r0, 2 * q)
+            + block_product(g1, r1, 2 * q)
+            + block_product(g3, r3, 2 * q)
+        )
 
 
 def early_sums(*operands):
     return pl.pallas_call(
         early_body,
         out_shape=VM((4, 512, 512), F32),
-        in_specs=[IN] * 4,
+        in_specs=[IN] * 6,
         out_specs=IN,
         compiler_params=LIMIT,
         cost_estimate=pl.CostEstimate(flops=EARLY, bytes_accessed=6 << 20, transcendentals=0),
@@ -171,9 +172,7 @@
     )(*kept(*operands))
 
 
-def partial_body(acc, r1, r2, g0, g1, g2, g3, *outs):
-    keep, give = outs[4:]
-    _, _, second = roles()
+def plane_body(g0, g1, g2, g3, keep, give):
     z, yh = lax.axis_index("z"), lax.axis_index("yh")
     g = (g0, g1, g2, g3)
     for k in range(4):
@@ -186,9 +185,23 @@
         def _():
             keep[...] = g[k][...]
 
+
+def plane_blocks(*grads):
+    return pl.pallas_call(
+        plane_body,
+        out_shape=[VM((2, 256, 256), BF)] * 2,
+        in_specs=[IN] * 4,
+        out_specs=[IN] * 2,
+        compiler_params=LIMIT,
+        name="plane",
+    )(*kept(*grads))
+
+
+def partial_body(acc, r2, g2, *outs):
+    _, _, second = roles()
     for k in (2, 1, 3, 0):
         q = (second + k) & 3
-        total = acc[q] + block_product(g[1], r1, 2 * q) + block_product(g[2], r2, 2 * q)
+        total = acc[q] + block_product(g2, r2, 2 * q)
         outs[k][...] = total.astype(outs[k].dtype)
 
 
@@ -196,10 +209,9 @@
     return pl.pallas_call(
         partial_body,
         out_shape=[VM((512, 512), F32)]
-        + [VM((512, 512), BF)] * 3
-        + [VM((2, 256, 256), BF)] * 2,
-        in_specs=[IN] * 7,
-        out_specs=[IN] * 6,
+        + [VM((512, 512), BF)] * 3,
+        in_specs=[IN] * 3,
+        out_specs=[IN] * 4,
         compiler_params=LIMIT,
         name="partial",
     )(*kept(*operands))
@@ -297,11 +309,14 @@
         copy.wait()
 
 
-def first_half_body(h_ref, seed, other, back, back_other, *refs):
+def first_half_body(p0, p1, p2, p3, seed, other, back, back_other, o_ref, h_ref, *refs):
     yl, c = lax.axis_index("yl"), lax.axis_index("c")
+    n = lax.axis_index("yh") * 2 + c
+    for r, p in enumerate((p0, p1, p2, p3)):
+        h_ref[pl.ds(pl.multiple_of((n ^ r) * 128, 128), 128), :] = p[...]
     k = 3 - 2 * c
     blocks = [(yl, 0, seed), (1 - yl, 0, other), (yl, k, back), (1 - yl, k, back_other)]
-    outer_into(blocks, h_ref, *refs)
+    outer_into(blocks, h_ref, o_ref, *refs)
 
 
 def second_half_body(o_in, h_ref, ahead, far, *refs):
@@ -314,11 +329,12 @@
 
 def outer_half(body, name, operands, so_far=None):
     aliased = so_far is not None
+    out = jax.ShapeDtypeStruct((2048, 4, 256), BF)
     return pl.pallas_call(
         body,
-        out_shape=jax.ShapeDtypeStruct((2048, 4, 256), BF),
+        out_shape=[out] if aliased else [out, VM((512, 1024), BF)],
         in_specs=[HBM] * aliased + [IN] * len(operands),
-        out_specs=HBM,
+        out_specs=[HBM] if aliased else [HBM, IN],
         scratch_shapes=[VM((4, 256, 4, 256), BF), pltpu.SemaphoreType.DMA((4,))],
         input_output_aliases={0: 0} if aliased else {},
         compiler_params=LIMIT,
@@ -342,31 +358,40 @@
 
     sent = scaled_rows(w5, scales_t)
     r0 = sent[0]
-    r1, r2, r3 = [shift(sent[k], first_axis_steps(k)) for k in (1, 2, 3)]
-
+    r1, r3 = [shift(sent[k], first_axis_steps(k)) for k in (1, 3)]
     grad_out, hidden, _ = lax.optimization_barrier((grad_out, hidden, r0))
-    g0, h = all_tokens(packed(grad_out, hidden))
-    g2, g3 = [shift(g0, first_axis_steps(k)) for k in (2, 3)]
-    later, r1 = lax.optimization_barrier((g0, r1))
-    g1 = shift(later, first_axis_steps(1))
-
-    acc = early_sums(r0, r3, g0, g3)
-    *sums, keep, give = partial_sums(acc, r1, r2, g0, g1, g2, g3)
+    g0 = all_tokens(grad_out)
+    g1, g3 = [shift(g0, first_axis_steps(k)) for k in (1, 3)]
+    sent2, _ = lax.optimization_barrier((sent[2], g0))
+    r2, g2 = shift(sent2, first_axis_steps(2)), shift(g0, first_axis_steps(2))
+
+    acc = early_sums(r0, r1, r3, g0, g1, g3)
+    plane, acc, hidden = lax.optimization_barrier(((g0, g1, g2, g3), acc, hidden))
+    keep, give = plane_blocks(*plane)
+    seed = picked(lax.ppermute(give, "c", [(1, 0)]), keep)
+    other = swap(seed, "yl")
+    both = paired(seed, other)
+    pieces = swapped(flat(hidden))
+    acc, both, seed, pieces = lax.optimization_barrier((acc, both, seed, pieces))
+
+    sums = partial_sums(acc, r2, g2)
     parts = [sums[0]] + [None] * 3
-    for k in (2, 1, 3):
+    for k in (1, 3, 2):
         parts[k] = shift(sums[k], second_axis_steps(k))
+    seed, both, _ = lax.optimization_barrier((seed, both, sums[0]))
+    back = along_x(seed, 1)
+    ahead = along_x(both, 0)
+    far = lax.ppermute(both, "x", [(i, (i + 2) % 4) for i in range(4)])
+    back, parts[0] = lax.optimization_barrier((back, parts[0]))
+    back_other = swap(back, "yl")
+
     blocks = summed_blocks(parts)
     blocks = lax.all_to_all(blocks, ("yl", "yh", "c"), 0, 0, tiled=True)
     grad_hidden = finished(blocks)
-
-    seed = picked(lax.ppermute(give, "c", [(1, 0)]), keep)
-    other = swap(seed, "yl")
-    back = along_x(seed, 1)
-    both = paired(seed, other)
-    ahead = along_x(both, 0)
-    far = lax.ppermute(both, "x", [(i, (i + 2) % 4) for i in range(4)])
-    half = outer_half(first_half_body, "first_half", (h, seed, other, back, swap(back, "yl")))
-    grad_weight = outer_half(second_half_body, "second_half", (h, ahead, far), half)
+    half, h = outer_half(
+        first_half_body, "first_half", (*pieces, seed, other, back, back_other)
+    )
+    grad_weight = outer_half(second_half_body, "second_half", (h, ahead, far), half)[0]
     return grad_hidden, grad_weight
 
 

time: 98.1 us -> 102 us (1.040)
  the two profiles are of different devices: /device:TPU:103 before, /device:TPU:1 now
where the time goes in v7:
time: 102 us; the launch traced here: 101 us
  waiting for transfers between devices  51.3 us (50%)
  starting transfers between devices  33.9 us (33%)
  Pallas kernels  13.4 us (13%)
  local copies, waits for them, and re-layouts  1.65 us (2%)
    ppermute x9, waiting for transfers between devices, shift(): return lax.ppermute(value, ('z', 'x', 'c'), pairs)  19.4 us
    ppermute x2, waiting for transfers between devices, along_x(): return lax.ppermute(value, ('x', 'c'), pairs)  16.6 us
    ppermute x8, waiting for transfers between devices, swap(): return lax.ppermute(value, axis, [(0, 1), (1, 0)])  14.9 us
    ppermute x9, starting transfers between devices, shift(): return lax.ppermute(value, ('z', 'x', 'c'), pairs)  13.7 us
    ppermute x8, starting transfers between devices, swap(): return lax.ppermute(value, axis, [(0, 1), (1, 0)])  11 us
    pallas_call x2, Pallas kernels, outer_half(): pl.pallas_call(body, out_shape=[out] if aliased else [out, VM((512, 1024)...  6.35 us
    ppermute x2, starting transfers between devices, along_x(): return lax.ppermute(value, ('x', 'c'), pairs)  4.19 us
    all_to_all x1, starting transfers between devices, per_device(): blocks = lax.all_to_all(blocks, ('yl', 'yh', 'c'), 0, 0, tiled=True)  3.62 us
  transfers between devices with their start and end apart: 22, of which 10 were waited for; matrix products, arithmetic and copies ran while one was open for 0% of the time, Pallas kernels for 9%

profile of v7, /device:TPU:1, one launch (start us, length us, event | category | flops | bytes accessed | tf_op | source)
XLA Modules:
  0.0 101.1 jit_solution(12456841726809470510)
XLA Ops:
  0.6 2.4 %scale.1 = (bf16[8,256,256]{2,1,0:T(8,128)(2,1)S(1)}, bf16[8,256,256]{2,1,0:T(8,128)(2,1)S(1)}, bf16[8,256,256]{2,1,0:T(8,128)(2,1)S(1)}, bf16[8,256,256]{2,1,0:T(8,128)(2,1)S(1)}) custom-call(bf16[4,2,4,256,256]{4,3,2,1,0:T(8,128)(2,1)} %bitcast.2, bf16[16,512]{1,0:T(8,128)(2,1)} %bitcast.3), custom_call_target="tpu_custom_call" | custom-call | tf_op jit(solution)/shard_map/scale/pallas_call | solution.py:96
  3.0 2.5 %collective-permute-start.6 = (bf16[8,256,256]{2,1,0:T(8,128)(2,1)S(1)}, bf16[8,256,256]{2,1,0:T(8,128)(2,1)S(1)}, u32[]{:S(2)}, u32[]{:S(2)}) collective-permute-start(bf16[8,256,256]{2,1,0:T(8,128)(2,1)S(1)} %get-tuple-element.36), channel_id=1, source_target_pairs={{0,4},{1,33},{4,8},{5,37},{8,12},{9,41},{12,0},{13,45},{32,36},{33... | collective-permute-start | bytes 3145736 | tf_op jit(solution)/shard_map/ppermute | solution.py:34
  5.6 2.2 %collective-permute-start.7 = (bf16[8,256,256]{2,1,0:T(8,128)(2,1)S(1)}, bf16[8,256,256]{2,1,0:T(8,128)(2,1)S(1)}, u32[]{:S(2)}, u32[]{:S(2)}) collective-permute-start(bf16[8,256,256]{2,1,0:T(8,128)(2,1)S(1)} %get-tuple-element.37), channel_id=1, source_target_pairs={{0,12},{1,97},{4,0},{5,101},{8,4},{9,105},{12,8},{13,109},{32,44},... | collective-permute-start | bytes 3145736 | tf_op jit(solution)/shard_map/ppermute | solution.py:34
  7.8 2.9 %collective-permute-start.1 = (bf16[128,256]{1,0:T(8,128)(2,1)S(1)}, bf16[128,256]{1,0:T(8,128)(2,1)S(1)}, u32[]{:S(2)}, u32[]{:S(2)}) collective-permute-start(bf16[128,256]{1,0:T(8,128)(2,1)S(1)} %copy-done.1), channel_id=1, source_target_pairs={{0,2},{2,0},{1,3},{3,1},{4,6},{6,4},{5,7},{7,5},{8,10},{10,8},{9,1... | collective-permute-start | bytes 196616 | tf_op jit(solution)/shard_map/ppermute | solution.py:38
  10.7 0.4 collective-permute-start
  11.1 2.0 %collective-permute-done.1.p2 = bf16[128,256]{1,0:T(8,128)(2,1)S(1)} collective-permute-done((bf16[128,256]{1,0:T(8,128)(2,1)S(1)}, bf16[128,256]{1,0:T(8,128)(2,1)S(1)}, u32[]{:S(2)}, u32[]{:S(2)}) %collective-permute-start.1) | collective-permute-done | bytes 65568 | tf_op jit(solution)/shard_map/ppermute | solution.py:38
  13.0 0.8 collective-permute-start.2
  13.8 0.9 collective-permute-done.2.p3
  14.7 3.7 %collective-permute-start.5 = (bf16[2,256,256]{2,1,0:T(8,128)(2,1)S(1)}, bf16[2,256,256]{2,1,0:T(8,128)(2,1)S(1)}, u32[]{:S(2)}, u32[]{:S(2)}) collective-permute-start(bf16[2,256,256]{2,1,0:T(8,128)(2,1)S(1)} %tokens.1.g0), channel_id=1, source_target_pairs={{0,12},{1,97},{4,0},{5,101},{8,4},{9,105},{12,8},{13,109},{32,44},... | collective-permute-start | bytes 786440 | tf_op jit(solution)/shard_map/ppermute | solution.py:34
  18.4 0.0 collective-permute-start.13
  18.4 0.7 collective-permute-start.3
  19.1 14.5 %collective-permute-done.5.g3 = bf16[2,256,256]{2,1,0:T(8,128)(2,1)S(1)} collective-permute-done((bf16[2,256,256]{2,1,0:T(8,128)(2,1)S(1)}, bf16[2,256,256]{2,1,0:T(8,128)(2,1)S(1)}, u32[]{:S(2)}, u32[]{:S(2)}) %collective-permute-start.5) | collective-permute-done | bytes 262176 | tf_op jit(solution)/shard_map/ppermute | solution.py:34
  33.6 0.0 collective-permute-start.4
  33.6 2.8 %collective-permute-done.3.g1 = bf16[2,256,256]{2,1,0:T(8,128)(2,1)S(1)} collective-permute-done((bf16[2,256,256]{2,1,0:T(8,128)(2,1)S(1)}, bf16[2,256,256]{2,1,0:T(8,128)(2,1)S(1)}, u32[]{:S(2)}, u32[]{:S(2)}) %collective-permute-start.3) | collective-permute-done | bytes 262176 | tf_op jit(solution)/shard_map/ppermute | solution.py:34
  36.4 0.0 collective-permute-done.6.r1
  36.4 0.0 collective-permute-done.7.r3
  36.4 1.8 %early.1.acc = f32[4,512,512]{2,1,0:T(8,128)S(1)} custom-call(bf16[8,256,256]{2,1,0:T(8,128)(2,1)S(1)} %get-tuple-element.34.r0, bf16[8,256,256]{2,1,0:T(8,128)(2,1)S(1)} %collective-permute-done.6.r1, bf16[8,256,256]{2,1,0:T(8,128)(2,1)S(1)} %collective-permute-done.7.r3, bf16[2,256,256]{2,1,0:T(8,128)(2,1)S(1)} %tokens.1.g0, ...), custom_call_target="tpu_custom_call" | custom-call | flops 2000000000 | bytes 6291456 | tf_op jit(solution)/shard_map/early/pallas_call | solution.py:164
  38.2 2.1 %collective-permute-done.4.g2 = bf16[2,256,256]{2,1,0:T(8,128)(2,1)S(1)} collective-permute-done((bf16[2,256,256]{2,1,0:T(8,128)(2,1)S(1)}, bf16[2,256,256]{2,1,0:T(8,128)(2,1)S(1)}, u32[]{:S(2)}, u32[]{:S(2)}) %collective-permute-start.4) | collective-permute-done | bytes 262176 | tf_op jit(solution)/shard_map/ppermute | solution.py:34
  40.3 0.1 plane.1
  40.4 1.3 %collective-permute-start.8 = (bf16[2,256,256]{2,1,0:T(8,128)(2,1)S(1)}, bf16[2,256,256]{2,1,0:T(8,128)(2,1)S(1)}, u32[]{:S(2)}, u32[]{:S(2)}) collective-permute-start(bf16[2,256,256]{2,1,0:T(8,128)(2,1)S(1)} %get-tuple-element.44), channel_id=1, source_target_pairs={{1,0},{3,2},{5,4},{7,6},{9,8},{11,10},{13,12},{15,14},{17,16},{19,... | collective-permute-start | bytes 786440 | tf_op jit(solution)/shard_map/ppermute | solution.py:371
  41.7 0.1 flat.1.p0
  41.8 5.4 %collective-permute-start.11 = (bf16[128,1024]{1,0:T(8,128)(2,1)S(1)}, bf16[128,1024]{1,0:T(8,128)(2,1)S(1)}, u32[]{:S(2)}, u32[]{:S(2)}) collective-permute-start(bf16[128,1024]{1,0:T(8,128)(2,1)S(1)} %flat.1.p0), channel_id=1, source_target_pairs={{0,2},{2,0},{1,3},{3,1},{4,6},{6,4},{5,7},{7,5},{8,10},{10,8},{9,1... | collective-permute-start | bytes 786440 | tf_op jit(solution)/shard_map/ppermute | solution.py:38
  47.2 0.5 collective-permute-start.9
  47.7 6.0 %collective-permute-done.11.p2 = bf16[128,1024]{1,0:T(8,128)(2,1)S(1)} collective-permute-done((bf16[128,1024]{1,0:T(8,128)(2,1)S(1)}, bf16[128,1024]{1,0:T(8,128)(2,1)S(1)}, u32[]{:S(2)}, u32[]{:S(2)}) %collective-permute-start.11) | collective-permute-done | bytes 262176 | tf_op jit(solution)/shard_map/ppermute | solution.py:38
  53.7 0.0 collective-permute-start.12
  53.7 6.0 %collective-permute-done.9.b_ref.other = bf16[2,256,256]{2,1,0:T(8,128)(2,1)S(1)} collective-permute-done((bf16[2,256,256]{2,1,0:T(8,128)(2,1)S(1)}, bf16[2,256,256]{2,1,0:T(8,128)(2,1)S(1)}, u32[]{:S(2)}, u32[]{:S(2)}) %collective-permute-start.9) | collective-permute-done | bytes 262176 | tf_op jit(solution)/shard_map/ppermute | solution.py:38
  59.8 0.0 collective-permute-done.12.p3
  59.8 0.0 copy-start.2
  59.8 0.7 copy-done.2
  60.5 0.7 partial.1
  61.2 0.8 collective-permute-start.15
  62.0 3.8 %collective-permute-start.16 = (bf16[512,512]{1,0:T(8,128)(2,1)S(1)}, bf16[512,512]{1,0:T(8,128)(2,1)S(1)}, u32[]{:S(2)}, u32[]{:S(2)}) collective-permute-start(bf16[512,512]{1,0:T(8,128)(2,1)S(1)} %get-tuple-element.56), channel_id=1, source_target_pairs={{0,64},{1,9},{4,68},{5,13},{8,72},{9,1},{12,76},{13,5},{32,96},{33... | collective-permute-start | bytes 1572872 | tf_op jit(solution)/shard_map/ppermute | solution.py:34
  65.9 0.0 collective-permute-start.17
  65.9 1.5 %collective-permute-start.14 = (bf16[2,256,256]{2,1,0:T(8,128)(2,1)S(1)}, bf16[2,256,256]{2,1,0:T(8,128)(2,1)}, u32[]{:S(2)}, u32[]{:S(2)}) collective-permute-start(bf16[2,256,256]{2,1,0:T(8,128)(2,1)S(1)} %picked.1.a_ref.seed), channel_id=1, source_target_pairs={{0,12},{1,5},{4,0},{5,9},{8,4},{9,13},{12,8},{13,1},{2,14},{3,7},{... | collective-permute-start | bytes 786440 | tf_op jit(solution)/shard_map/ppermute | solution.py:352
  67.3 0.0 collective-permute-start.20
  67.3 16.0 %collective-permute-done.14.back = bf16[2,256,256]{2,1,0:T(8,128)(2,1)} collective-permute-done((bf16[2,256,256]{2,1,0:T(8,128)(2,1)S(1)}, bf16[2,256,256]{2,1,0:T(8,128)(2,1)}, u32[]{:S(2)}, u32[]{:S(2)}) %collective-permute-start.14) | collective-permute-done | bytes 262176 | tf_op jit(solution)/shard_map/ppermute | solution.py:352
  83.3 2.7 %collective-permute-start.19 = (bf16[4,256,256]{2,1,0:T(8,128)(2,1)S(1)}, bf16[4,256,256]{2,1,0:T(8,128)(2,1)S(1)}, u32[]{:S(2)}, u32[]{:S(2)}) collective-permute-start(bf16[4,256,256]{2,1,0:T(8,128)(2,1)S(1)} %paired.1), channel_id=1, source_target_pairs={{0,4},{1,13},{4,8},{5,1},{8,12},{9,5},{12,0},{13,9},{2,6},{3,15},{... | collective-permute-start | bytes 1572872 | tf_op jit(solution)/shard_map/ppermute | solution.py:352
  86.1 1.1 %collective-permute-start.18 = (bf16[2,256,256]{2,1,0:T(8,128)(2,1)}, bf16[2,256,256]{2,1,0:T(8,128)(2,1)}, u32[]{:S(2)}, u32[]{:S(2)}) collective-permute-start(bf16[2,256,256]{2,1,0:T(8,128)(2,1)} %collective-permute-done.14.back), channel_id=1, source_target_pairs={{0,16},{16,0},{1,17},{17,1},{2,18},{18,2},{3,19},{19,3},{4,20},{20... | collective-permute-start | bytes 786440 | tf_op jit(solution)/shard_map/ppermute | solution.py:38
  87.1 0.0 collective-permute-done.16.c
  87.1 1.0 %summed.1 = bf16[8,128,256]{2,1,0:T(8,128)(2,1)} custom-call(f32[512,512]{1,0:T(8,128)S(1)} %get-tuple-element.54.a, bf16[512,512]{1,0:T(8,128)(2,1)S(1)} %collective-permute-done.15.b, bf16[512,512]{1,0:T(8,128)(2,1)S(1)} %collective-permute-done.16.c, bf16[512,512]{1,0:T(8,128)(2,1)S(1)} %collective-permute-done.17.d), custom_call_target="tpu_custom_call" | custom-call | tf_op jit(solution)/shard_map/summed/pallas_call | solution.py:230
  88.2 3.6 %all-to-all-start = ((bf16[8,128,256]{2,1,0:T(8,128)(2,1)}), bf16[8,128,256]{2,1,0:T(8,128)(2,1)S(1)}, u32[]{:S(2)}, u32[]{:S(2)}) async-start(bf16[8,128,256]{2,1,0:T(8,128)(2,1)} %summed.1), calls=%async_computation | async-start | bytes 1048576 | tf_op jit(solution)/shard_map/all_to_all | solution.py:389
  91.8 0.0 copy-start.3
  91.8 0.9 copy-done.3
  92.8 3.7 %first_half.1 = (bf16[2048,4,256]{2,1,0:T(4,128)(2,1)}, bf16[512,1024]{1,0:T(8,128)(2,1)S(1)}) custom-call(bf16[128,1024]{1,0:T(8,128)(2,1)S(1)} %flat.1.p0, bf16[128,1024]{1,0:T(8,128)(2,1)S(1)} %collective-permute-done.10.p1, bf16[128,1024]{1,0:T(8,128)(2,1)S(1)} %collective-permute-done.11.p2, bf16[128,1024]{1,0:T(8,128)(2,1)S(1)} %copy-done.3, ...), custom_call_target="tpu_custom_call" | custom-call | flops 2000000000 | bytes 5242880 | tf_op jit(solution)/shard_map/first_half/pallas_call | solution.py:333
  96.5 0.5 collective-permute-done.20.far
  97.0 0.6 collective-permute-done.19.ahead
  97.6 2.6 %second_half.1 = bf16[2048,4,256]{2,1,0:T(4,128)(2,1)} custom-call(bf16[2048,4,256]{2,1,0:T(4,128)(2,1)} %get-tuple-element.63.o_in, bf16[512,1024]{1,0:T(8,128)(2,1)S(1)} %get-tuple-element.64.h_ref, bf16[4,256,256]{2,1,0:T(8,128)(2,1)S(1)} %collective-permute-done.19.ahead, ...), custom_call_target="tpu_custom_call", output_to_operand_aliasing={{}: (0, {})} | custom-call | flops 2000000000 | bytes 5242880 | tf_op jit(solution)/shard_map/second_half/pallas_call | solution.py:333
  100.2 0.9 finish.1
  (16 shorter events, 0.1 us)
Async XLA Ops:
  0.6 7.2 %copy-start.1 = (bf16[128,256]{1,0:T(8,128)(2,1)S(1)}, bf16[128,256]{1,0:T(8,128)(2,1)}, u32[]{:S(2)}) copy-start(bf16[128,256]{1,0:T(8,128)(2,1)} %p0) | copy-start | bytes 196612
  3.0 33.3 %collective-permute-start.6 = (bf16[8,256,256]{2,1,0:T(8,128)(2,1)S(1)}, bf16[8,256,256]{2,1,0:T(8,128)(2,1)S(1)}, u32[]{:S(2)}, u32[]{:S(2)}) collective-permute-start(bf16[8,256,256]{2,1,0:T(8,128)(2,1)S(1)} %get-tuple-element.36), channel_id=1, source_target_pairs={{0,4},{1,33},{4,8},{5,37},{8,12},{9,41},{12,0},{13,45},{32,36},{33... | collective-permute-start | bytes 3145736 | tf_op jit(solution)/shard_map/ppermute | solution.py:34
  5.6 30.8 %collective-permute-start.7 = (bf16[8,256,256]{2,1,0:T(8,128)(2,1)S(1)}, bf16[8,256,256]{2,1,0:T(8,128)(2,1)S(1)}, u32[]{:S(2)}, u32[]{:S(2)}) collective-permute-start(bf16[8,256,256]{2,1,0:T(8,128)(2,1)S(1)} %get-tuple-element.37), channel_id=1, source_target_pairs={{0,12},{1,97},{4,0},{5,101},{8,4},{9,105},{12,8},{13,109},{32,44},... | collective-permute-start | bytes 3145736 | tf_op jit(solution)/shard_map/ppermute | solution.py:34
  7.8 5.2 %collective-permute-start.1 = (bf16[128,256]{1,0:T(8,128)(2,1)S(1)}, bf16[128,256]{1,0:T(8,128)(2,1)S(1)}, u32[]{:S(2)}, u32[]{:S(2)}) collective-permute-start(bf16[128,256]{1,0:T(8,128)(2,1)S(1)} %copy-done.1), channel_id=1, source_target_pairs={{0,2},{2,0},{1,3},{3,1},{4,6},{6,4},{5,7},{7,5},{8,10},{10,8},{9,1... | collective-permute-start | bytes 196616 | tf_op jit(solution)/shard_map/ppermute | solution.py:38
  10.7 3.1 %collective-permute-start = (bf16[128,256]{1,0:T(8,128)(2,1)S(1)}, bf16[128,256]{1,0:T(8,128)(2,1)S(1)}, u32[]{:S(2)}, u32[]{:S(2)}) collective-permute-start(bf16[128,256]{1,0:T(8,128)(2,1)S(1)} %copy-done.1), channel_id=1, source_target_pairs={{0,1},{1,0},{2,3},{3,2},{4,5},{5,4},{6,7},{7,6},{8,9},{9,8},{10,11... | collective-permute-start | bytes 196616 | tf_op jit(solution)/shard_map/ppermute | solution.py:38
  13.0 1.7 %collective-permute-start.2 = (bf16[128,256]{1,0:T(8,128)(2,1)S(1)}, bf16[128,256]{1,0:T(8,128)(2,1)S(1)}, u32[]{:S(2)}, u32[]{:S(2)}) collective-permute-start(bf16[128,256]{1,0:T(8,128)(2,1)S(1)} %collective-permute-done.1.p2), channel_id=1, source_target_pairs={{0,1},{1,0},{2,3},{3,2},{4,5},{5,4},{6,7},{7,6},{8,9},{9,8},{10,11... | collective-permute-start | bytes 196616 | tf_op jit(solution)/shard_map/ppermute | solution.py:38
  14.7 18.8 %collective-permute-start.5 = (bf16[2,256,256]{2,1,0:T(8,128)(2,1)S(1)}, bf16[2,256,256]{2,1,0:T(8,128)(2,1)S(1)}, u32[]{:S(2)}, u32[]{:S(2)}) collective-permute-start(bf16[2,256,256]{2,1,0:T(8,128)(2,1)S(1)} %tokens.1.g0), channel_id=1, source_target_pairs={{0,12},{1,97},{4,0},{5,101},{8,4},{9,105},{12,8},{13,109},{32,44},... | collective-permute-start | bytes 786440 | tf_op jit(solution)/shard_map/ppermute | solution.py:34
  18.4 23.3 %copy-start = (bf16[128,4,256]{2,1,0:T(4,128)(2,1)S(1)}, bf16[128,4,256]{2,1,0:T(4,128)(2,1)}, u32[]{:S(2)}) copy-start(bf16[128,4,256]{2,1,0:T(4,128)(2,1)} %h_ref) | copy-start | bytes 786436
  18.4 42.1 %collective-permute-start.13 = (bf16[8,256,256]{2,1,0:T(8,128)(2,1)S(1)}, bf16[8,256,256]{2,1,0:T(8,128)(2,1)S(1)}, u32[]{:S(2)}, u32[]{:S(2)}) collective-permute-start(bf16[8,256,256]{2,1,0:T(8,128)(2,1)S(1)} %get-tuple-element.51), channel_id=1, source_target_pairs={{0,8},{1,65},{4,12},{5,69},{8,0},{9,73},{12,4},{13,77},{32,40},{33... | collective-permute-start | bytes 3145736 | tf_op jit(solution)/shard_map/ppermute | solution.py:34
  18.4 18.0 %collective-permute-start.3 = (bf16[2,256,256]{2,1,0:T(8,128)(2,1)S(1)}, bf16[2,256,256]{2,1,0:T(8,128)(2,1)S(1)}, u32[]{:S(2)}, u32[]{:S(2)}) collective-permute-start(bf16[2,256,256]{2,1,0:T(8,128)(2,1)S(1)} %tokens.1.g0), channel_id=1, source_target_pairs={{0,4},{1,33},{4,8},{5,37},{8,12},{9,41},{12,0},{13,45},{32,36},{33... | collective-permute-start | bytes 786440 | tf_op jit(solution)/shard_map/ppermute | solution.py:34
  33.6 6.7 %collective-permute-start.4 = (bf16[2,256,256]{2,1,0:T(8,128)(2,1)S(1)}, bf16[2,256,256]{2,1,0:T(8,128)(2,1)S(1)}, u32[]{:S(2)}, u32[]{:S(2)}) collective-permute-start(bf16[2,256,256]{2,1,0:T(8,128)(2,1)S(1)} %tokens.1.g0), channel_id=1, source_target_pairs={{0,8},{1,65},{4,12},{5,69},{8,0},{9,73},{12,4},{13,77},{32,40},{33... | collective-permute-start | bytes 786440 | tf_op jit(solution)/shard_map/ppermute | solution.py:34
  40.4 6.8 %collective-permute-start.8 = (bf16[2,256,256]{2,1,0:T(8,128)(2,1)S(1)}, bf16[2,256,256]{2,1,0:T(8,128)(2,1)S(1)}, u32[]{:S(2)}, u32[]{:S(2)}) collective-permute-start(bf16[2,256,256]{2,1,0:T(8,128)(2,1)S(1)} %get-tuple-element.44), channel_id=1, source_target_pairs={{1,0},{3,2},{5,4},{7,6},{9,8},{11,10},{13,12},{15,14},{17,16},{19,... | collective-permute-start | bytes 786440 | tf_op jit(solution)/shard_map/ppermute | solution.py:371
  41.8 11.9 %collective-permute-start.11 = (bf16[128,1024]{1,0:T(8,128)(2,1)S(1)}, bf16[128,1024]{1,0:T(8,128)(2,1)S(1)}, u32[]{:S(2)}, u32[]{:S(2)}) collective-permute-start(bf16[128,1024]{1,0:T(8,128)(2,1)S(1)} %flat.1.p0), channel_id=1, source_target_pairs={{0,2},{2,0},{1,3},{3,1},{4,6},{6,4},{5,7},{7,5},{8,10},{10,8},{9,1... | collective-permute-start | bytes 786440 | tf_op jit(solution)/shard_map/ppermute | solution.py:38
  47.2 12.5 %collective-permute-start.9 = (bf16[2,256,256]{2,1,0:T(8,128)(2,1)S(1)}, bf16[2,256,256]{2,1,0:T(8,128)(2,1)S(1)}, u32[]{:S(2)}, u32[]{:S(2)}) collective-permute-start(bf16[2,256,256]{2,1,0:T(8,128)(2,1)S(1)} %picked.1.a_ref.seed), channel_id=1, source_target_pairs={{0,16},{16,0},{1,17},{17,1},{2,18},{18,2},{3,19},{19,3},{4,20},{20... | collective-permute-start | bytes 786440 | tf_op jit(solution)/shard_map/ppermute | solution.py:38
  47.7 12.1 %collective-permute-start.10 = (bf16[128,1024]{1,0:T(8,128)(2,1)S(1)}, bf16[128,1024]{1,0:T(8,128)(2,1)S(1)}, u32[]{:S(2)}, u32[]{:S(2)}) collective-permute-start(bf16[128,1024]{1,0:T(8,128)(2,1)S(1)} %flat.1.p0), channel_id=1, source_target_pairs={{0,1},{1,0},{2,3},{3,2},{4,5},{5,4},{6,7},{7,6},{8,9},{9,8},{10,11... | collective-permute-start | bytes 786440 | tf_op jit(solution)/shard_map/ppermute | solution.py:38
  53.7 6.1 %collective-permute-start.12 = (bf16[128,1024]{1,0:T(8,128)(2,1)S(1)}, bf16[128,1024]{1,0:T(8,128)(2,1)S(1)}, u32[]{:S(2)}, u32[]{:S(2)}) collective-permute-start(bf16[128,1024]{1,0:T(8,128)(2,1)S(1)} %collective-permute-done.11.p2), channel_id=1, source_target_pairs={{0,1},{1,0},{2,3},{3,2},{4,5},{5,4},{6,7},{7,6},{8,9},{9,8},{10,11... | collective-permute-start | bytes 786440 | tf_op jit(solution)/shard_map/ppermute | solution.py:38
  59.8 0.7 copy-start.2
  61.2 24.8 %collective-permute-start.15 = (bf16[512,512]{1,0:T(8,128)(2,1)S(1)}, bf16[512,512]{1,0:T(8,128)(2,1)S(1)}, u32[]{:S(2)}, u32[]{:S(2)}) collective-permute-start(bf16[512,512]{1,0:T(8,128)(2,1)S(1)} %get-tuple-element.55), channel_id=1, source_target_pairs={{0,32},{1,5},{4,36},{5,9},{8,40},{9,13},{12,44},{13,1},{32,64},{33... | collective-permute-start | bytes 1572872 | tf_op jit(solution)/shard_map/ppermute | solution.py:34
  62.0 25.1 %collective-permute-start.16 = (bf16[512,512]{1,0:T(8,128)(2,1)S(1)}, bf16[512,512]{1,0:T(8,128)(2,1)S(1)}, u32[]{:S(2)}, u32[]{:S(2)}) collective-permute-start(bf16[512,512]{1,0:T(8,128)(2,1)S(1)} %get-tuple-element.56), channel_id=1, source_target_pairs={{0,64},{1,9},{4,68},{5,13},{8,72},{9,1},{12,76},{13,5},{32,96},{33... | collective-permute-start | bytes 1572872 | tf_op jit(solution)/shard_map/ppermute | solution.py:34
  65.9 21.3 %collective-permute-start.17 = (bf16[512,512]{1,0:T(8,128)(2,1)S(1)}, bf16[512,512]{1,0:T(8,128)(2,1)S(1)}, u32[]{:S(2)}, u32[]{:S(2)}) collective-permute-start(bf16[512,512]{1,0:T(8,128)(2,1)S(1)} %get-tuple-element.57), channel_id=1, source_target_pairs={{0,96},{1,13},{4,100},{5,1},{8,104},{9,5},{12,108},{13,9},{32,0},{... | collective-permute-start | bytes 1572872 | tf_op jit(solution)/shard_map/ppermute | solution.py:34
  65.9 17.5 %collective-permute-start.14 = (bf16[2,256,256]{2,1,0:T(8,128)(2,1)S(1)}, bf16[2,256,256]{2,1,0:T(8,128)(2,1)}, u32[]{:S(2)}, u32[]{:S(2)}) collective-permute-start(bf16[2,256,256]{2,1,0:T(8,128)(2,1)S(1)} %picked.1.a_ref.seed), channel_id=1, source_target_pairs={{0,12},{1,5},{4,0},{5,9},{8,4},{9,13},{12,8},{13,1},{2,14},{3,7},{... | collective-permute-start | bytes 786440 | tf_op jit(solution)/shard_map/ppermute | solution.py:352
  67.3 29.7 %collective-permute-start.20 = (bf16[4,256,256]{2,1,0:T(8,128)(2,1)S(1)}, bf16[4,256,256]{2,1,0:T(8,128)(2,1)S(1)}, u32[]{:S(2)}, u32[]{:S(2)}) collective-permute-start(bf16[4,256,256]{2,1,0:T(8,128)(2,1)S(1)} %paired.1), channel_id=1, source_target_pairs={{0,8},{4,12},{8,0},{12,4},{1,9},{5,13},{9,1},{13,5},{2,10},{6,14},... | collective-permute-start | bytes 1572872 | tf_op jit(solution)/shard_map/ppermute | solution.py:384
  83.3 14.3 %collective-permute-start.19 = (bf16[4,256,256]{2,1,0:T(8,128)(2,1)S(1)}, bf16[4,256,256]{2,1,0:T(8,128)(2,1)S(1)}, u32[]{:S(2)}, u32[]{:S(2)}) collective-permute-start(bf16[4,256,256]{2,1,0:T(8,128)(2,1)S(1)} %paired.1), channel_id=1, source_target_pairs={{0,4},{1,13},{4,8},{5,1},{8,12},{9,5},{12,0},{13,9},{2,6},{3,15},{... | collective-permute-start | bytes 1572872 | tf_op jit(solution)/shard_map/ppermute | solution.py:352
  86.1 5.8 %collective-permute-start.18 = (bf16[2,256,256]{2,1,0:T(8,128)(2,1)}, bf16[2,256,256]{2,1,0:T(8,128)(2,1)}, u32[]{:S(2)}, u32[]{:S(2)}) collective-permute-start(bf16[2,256,256]{2,1,0:T(8,128)(2,1)} %collective-permute-done.14.back), channel_id=1, source_target_pairs={{0,16},{16,0},{1,17},{17,1},{2,18},{18,2},{3,19},{19,3},{4,20},{20... | collective-permute-start | bytes 786440 | tf_op jit(solution)/shard_map/ppermute | solution.py:38
  88.2 12.0 %all-to-all-start = ((bf16[8,128,256]{2,1,0:T(8,128)(2,1)}), bf16[8,128,256]{2,1,0:T(8,128)(2,1)S(1)}, u32[]{:S(2)}, u32[]{:S(2)}) async-start(bf16[8,128,256]{2,1,0:T(8,128)(2,1)} %summed.1), calls=%async_computation | async-start | bytes 1048576 | tf_op jit(solution)/shard_map/all_to_all | solution.py:389
  91.8 1.0 copy-start.3

commit v8 on v6

--- a/solution.py
+++ b/solution.py
@@ -171,9 +171,7 @@
     )(*kept(*operands))
 
 
-def partial_body(acc, r1, r2, g0, g1, g2, g3, *outs):
-    keep, give = outs[4:]
-    _, _, second = roles()
+def plane_body(g0, g1, g2, g3, keep, give):
     z, yh = lax.axis_index("z"), lax.axis_index("yh")
     g = (g0, g1, g2, g3)
     for k in range(4):
@@ -186,9 +184,23 @@
         def _():
             keep[...] = g[k][...]
 
+
+def plane_blocks(*grads):
+    return pl.pallas_call(
+        plane_body,
+        out_shape=[VM((2, 256, 256), BF)] * 2,
+        in_specs=[IN] * 4,
+        out_specs=[IN] * 2,
+        compiler_params=LIMIT,
+        name="plane",
+    )(*kept(*grads))
+
+
+def partial_body(acc, r1, r2, g1, g2, *outs):
+    _, _, second = roles()
     for k in (2, 1, 3, 0):
         q = (second + k) & 3
-        total = acc[q] + block_product(g[1], r1, 2 * q) + block_product(g[2], r2, 2 * q)
+        total = acc[q] + block_product(g1, r1, 2 * q) + block_product(g2, r2, 2 * q)
         outs[k][...] = total.astype(outs[k].dtype)
 
 
@@ -196,10 +208,9 @@
     return pl.pallas_call(
         partial_body,
         out_shape=[VM((512, 512), F32)]
-        + [VM((512, 512), BF)] * 3
-        + [VM((2, 256, 256), BF)] * 2,
-        in_specs=[IN] * 7,
-        out_specs=[IN] * 6,
+        + [VM((512, 512), BF)] * 3,
+        in_specs=[IN] * 5,
+        out_specs=[IN] * 4,
         compiler_params=LIMIT,
         name="partial",
     )(*kept(*operands))
@@ -343,7 +354,6 @@
     sent = scaled_rows(w5, scales_t)
     r0 = sent[0]
     r1, r2, r3 = [shift(sent[k], first_axis_steps(k)) for k in (1, 2, 3)]
-
     grad_out, hidden, _ = lax.optimization_barrier((grad_out, hidden, r0))
     g0, h = all_tokens(packed(grad_out, hidden))
     g2, g3 = [shift(g0, first_axis_steps(k)) for k in (2, 3)]
@@ -351,21 +361,26 @@
     g1 = shift(later, first_axis_steps(1))
 
     acc = early_sums(r0, r3, g0, g3)
-    *sums, keep, give = partial_sums(acc, r1, r2, g0, g1, g2, g3)
+    plane, acc = lax.optimization_barrier(((g0, g1, g2, g3), acc))
+    keep, give = plane_blocks(*plane)
+    acc, keep, give = lax.optimization_barrier((acc, keep, give))
+    sums = partial_sums(acc, r1, r2, g1, g2)
     parts = [sums[0]] + [None] * 3
-    for k in (2, 1, 3):
+    for k in (1, 3, 2):
         parts[k] = shift(sums[k], second_axis_steps(k))
+    seed = picked(lax.ppermute(give, "c", [(1, 0)]), keep)
+    other = swap(seed, "yl")
+    both = paired(seed, other)
+    back = along_x(seed, 1)
+    ahead = along_x(both, 0)
+    far = lax.ppermute(both, "x", [(i, (i + 2) % 4) for i in range(4)])
+    back, parts[0] = lax.optimization_barrier((back, parts[0]))
+    back_other = swap(back, "yl")
+
     blocks = summed_blocks(parts)
     blocks = lax.all_to_all(blocks, ("yl", "yh", "c"), 0, 0, tiled=True)
     grad_hidden = finished(blocks)
-
-    seed = picked(lax.ppermute(give, "c", [(1, 0)]), keep)
-    other = swap(seed, "yl")
-    back = along_x(seed, 1)
-    both = paired(seed, other)
-    ahead = along_x(both, 0)
-    far = lax.ppermute(both, "x", [(i, (i + 2) % 4) for i in range(4)])
-    half = outer_half(first_half_body, "first_half", (h, seed, other, back, swap(back, "yl")))
+    half = outer_half(first_half_body, "first_half", (h, seed, other, back, back_other))
     grad_weight = outer_half(second_half_body, "second_half", (h, ahead, far), half)
     return grad_hidden, grad_weight
 

time: 98.1 us -> 98.2 us (level)
  starting transfers between devices: 36.5 us -> 34.6 us
  local copies, waits for them, and re-layouts: 0.96 us -> 2.5 us
  waiting for transfers between devices: 46.1 us -> 47.4 us
    ppermute x2, waiting for transfers between devices: 0.01 us -> 11.8 us  [along_x(): return lax.ppermute(value, ('x', 'c'), pairs)]
    ppermute x9, waiting for transfers between devices: 25 us -> 14.7 us  [shift(): return lax.ppermute(value, ('z', 'x', 'c'), pairs)]
    all_to_all x1, starting transfers between devices: 10.9 us -> 8.92 us  [per_device(): blocks = lax.all_to_all(blocks, ('yl', 'yh', 'c'), 0, 0, tiled=True)]
    unnamed x8 -> x12, local copies, waits for them, and re-layouts: 0.96 us -> 2.5 us
  transfers between devices with their start and end apart: 19 -> 19, of which waited for: 7 -> 6; matrix products, arithmetic and copies ran while one was open for 0% -> 0% of each run, Pallas kernels for 7% -> 8%
where the time goes in v8:
time: 98.2 us; the launch traced here: 97.9 us
  waiting for transfers between devices  47.4 us (48%)
  starting transfers between devices  34.6 us (35%)
  Pallas kernels  12.5 us (13%)
  local copies, waits for them, and re-layouts  2.5 us (3%)
    ppermute x5, waiting for transfers between devices, swap(): return lax.ppermute(value, axis, [(0, 1), (1, 0)])  20.9 us
    ppermute x9, waiting for transfers between devices, shift(): return lax.ppermute(value, ('z', 'x', 'c'), pairs)  14.7 us
    ppermute x2, waiting for transfers between devices, along_x(): return lax.ppermute(value, ('x', 'c'), pairs)  11.8 us
    ppermute x5, starting transfers between devices, swap(): return lax.ppermute(value, axis, [(0, 1), (1, 0)])  11 us
    all_to_all x1, starting transfers between devices, per_device(): blocks = lax.all_to_all(blocks, ('yl', 'yh', 'c'), 0, 0, tiled=True)  8.92 us
    ppermute x9, starting transfers between devices, shift(): return lax.ppermute(value, ('z', 'x', 'c'), pairs)  6.26 us
    pallas_call x2, Pallas kernels, outer_half(): pl.pallas_call(body, out_shape=jax.ShapeDtypeStruct((2048, 4, 256), BF),...  5.25 us
    ppermute x1, starting transfers between devices, per_device(): seed = picked(lax.ppermute(give, 'c', [(1, 0)]), keep)  3.85 us
  transfers between devices with their start and end apart: 19, of which 6 were waited for; matrix products, arithmetic and copies ran while one was open for 0% of the time, Pallas kernels for 8%

profile of v8, /device:TPU:103, one launch (start us, length us, event | category | flops | bytes accessed | tf_op | source)
XLA Modules:
  0.0 97.9 jit_solution(5313023539564115976)
XLA Ops:
  0.7 2.4 %scale.1 = (bf16[8,256,256]{2,1,0:T(8,128)(2,1)S(1)}, bf16[8,256,256]{2,1,0:T(8,128)(2,1)S(1)}, bf16[8,256,256]{2,1,0:T(8,128)(2,1)S(1)}, bf16[8,256,256]{2,1,0:T(8,128)(2,1)S(1)}) custom-call(bf16[4,2,4,256,256]{4,3,2,1,0:T(8,128)(2,1)} %bitcast.2, bf16[16,512]{1,0:T(8,128)(2,1)} %bitcast.3), custom_call_target="tpu_custom_call" | custom-call | tf_op jit(solution)/shard_map/scale/pallas_call | solution.py:96
  3.1 0.1 collective-permute-start.3
  3.2 1.5 %collective-permute-start.7 = (bf16[8,256,256]{2,1,0:T(8,128)(2,1)S(1)}, bf16[8,256,256]{2,1,0:T(8,128)(2,1)S(1)}, u32[]{:S(2)}, u32[]{:S(2)}) collective-permute-start(bf16[8,256,256]{2,1,0:T(8,128)(2,1)S(1)} %get-tuple-element.34), channel_id=1, source_target_pairs={{0,12},{1,97},{4,0},{5,101},{8,4},{9,105},{12,8},{13,109},{32,44},... | collective-permute-start | bytes 3145736 | tf_op jit(solution)/shard_map/ppermute | solution.py:34
  4.6 0.1 packed.1.p0
  4.7 3.0 %collective-permute-start.1 = (bf16[5,128,256]{2,1,0:T(8,128)(2,1)S(1)}, bf16[5,128,256]{2,1,0:T(8,128)(2,1)S(1)}, u32[]{:S(2)}, u32[]{:S(2)}) collective-permute-start(bf16[5,128,256]{2,1,0:T(8,128)(2,1)S(1)} %packed.1.p0), channel_id=1, source_target_pairs={{0,2},{2,0},{1,3},{3,1},{4,6},{6,4},{5,7},{7,5},{8,10},{10,8},{9,1... | collective-permute-start | bytes 983048 | tf_op jit(solution)/shard_map/ppermute | solution.py:38
  7.7 0.5 collective-permute-start.10
  8.1 2.5 %collective-permute-start = (bf16[5,128,256]{2,1,0:T(8,128)(2,1)S(1)}, bf16[5,128,256]{2,1,0:T(8,128)(2,1)S(1)}, u32[]{:S(2)}, u32[]{:S(2)}) collective-permute-start(bf16[5,128,256]{2,1,0:T(8,128)(2,1)S(1)} %packed.1.p0), channel_id=1, source_target_pairs={{0,1},{1,0},{2,3},{3,2},{4,5},{5,4},{6,7},{7,6},{8,9},{9,8},{10,11... | collective-permute-start | bytes 983048 | tf_op jit(solution)/shard_map/ppermute | solution.py:38
  10.6 3.6 %collective-permute-done.1.p2 = bf16[5,128,256]{2,1,0:T(8,128)(2,1)S(1)} collective-permute-done((bf16[5,128,256]{2,1,0:T(8,128)(2,1)S(1)}, bf16[5,128,256]{2,1,0:T(8,128)(2,1)S(1)}, u32[]{:S(2)}, u32[]{:S(2)}) %collective-permute-start.1) | collective-permute-done | bytes 327712 | tf_op jit(solution)/shard_map/ppermute | solution.py:38
  14.2 2.2 %collective-permute-start.2 = (bf16[5,128,256]{2,1,0:T(8,128)(2,1)S(1)}, bf16[5,128,256]{2,1,0:T(8,128)(2,1)S(1)}, u32[]{:S(2)}, u32[]{:S(2)}) collective-permute-start(bf16[5,128,256]{2,1,0:T(8,128)(2,1)S(1)} %collective-permute-done.1.p2), channel_id=1, source_target_pairs={{0,1},{1,0},{2,3},{3,2},{4,5},{5,4},{6,7},{7,6},{8,9},{9,8},{10,11... | collective-permute-start | bytes 983048 | tf_op jit(solution)/shard_map/ppermute | solution.py:38
  16.4 0.0 collective-permute-done.p1
  16.4 1.3 %collective-permute-done.2.p3 = bf16[5,128,256]{2,1,0:T(8,128)(2,1)S(1)} collective-permute-done((bf16[5,128,256]{2,1,0:T(8,128)(2,1)S(1)}, bf16[5,128,256]{2,1,0:T(8,128)(2,1)S(1)}, u32[]{:S(2)}, u32[]{:S(2)}) %collective-permute-start.2) | collective-permute-done | bytes 327712 | tf_op jit(solution)/shard_map/ppermute | solution.py:38
  17.7 0.1 tokens.1
  17.8 0.2 collective-permute-start.6
  18.0 1.4 %collective-permute-start.5 = (bf16[2,256,256]{2,1,0:T(8,128)(2,1)S(1)}, bf16[2,256,256]{2,1,0:T(8,128)(2,1)S(1)}, u32[]{:S(2)}, u32[]{:S(2)}) collective-permute-start(bf16[2,256,256]{2,1,0:T(8,128)(2,1)S(1)} %get-tuple-element.36.g0), channel_id=1, source_target_pairs={{0,8},{1,65},{4,12},{5,69},{8,0},{9,73},{12,4},{13,77},{32,40},{33... | collective-permute-start | bytes 786440 | tf_op jit(solution)/shard_map/ppermute | solution.py:34
  19.3 0.0 collective-permute-done.3.r1
  19.3 1.2 %collective-permute-start.4 = (bf16[2,256,256]{2,1,0:T(8,128)(2,1)S(1)}, bf16[2,256,256]{2,1,0:T(8,128)(2,1)S(1)}, u32[]{:S(2)}, u32[]{:S(2)}) collective-permute-start(bf16[2,256,256]{2,1,0:T(8,128)(2,1)S(1)} %get-tuple-element.36.g0), channel_id=1, source_target_pairs={{0,4},{1,33},{4,8},{5,37},{8,12},{9,41},{12,0},{13,45},{32,36},{33... | collective-permute-start | bytes 786440 | tf_op jit(solution)/shard_map/ppermute | solution.py:34
  20.5 14.7 %collective-permute-done.6.g3 = bf16[2,256,256]{2,1,0:T(8,128)(2,1)S(1)} collective-permute-done((bf16[2,256,256]{2,1,0:T(8,128)(2,1)S(1)}, bf16[2,256,256]{2,1,0:T(8,128)(2,1)S(1)}, u32[]{:S(2)}, u32[]{:S(2)}) %collective-permute-start.6) | collective-permute-done | bytes 262176 | tf_op jit(solution)/shard_map/ppermute | solution.py:34
  35.2 0.0 collective-permute-done.7.r3
  35.2 1.3 %early.1.acc = f32[4,512,512]{2,1,0:T(8,128)S(1)} custom-call(bf16[8,256,256]{2,1,0:T(8,128)(2,1)S(1)} %get-tuple-element.28.r0, bf16[8,256,256]{2,1,0:T(8,128)(2,1)S(1)} %collective-permute-done.7.r3, bf16[2,256,256]{2,1,0:T(8,128)(2,1)S(1)} %get-tuple-element.36.g0, bf16[2,256,256]{2,1,0:T(8,128)(2,1)S(1)} %collective-permute-done.6.g3), custom_call_target="tpu_custom_call" | custom-call | flops 2000000000 | bytes 6291456 | tf_op jit(solution)/shard_map/early/pallas_call | solution.py:163
  36.5 0.0 collective-permute-done.5.g2
  36.5 0.0 collective-permute-done.4.g1
  36.5 0.1 plane.1
  36.6 3.8 %collective-permute-start.8 = (bf16[2,256,256]{2,1,0:T(8,128)(2,1)S(1)}, bf16[2,256,256]{2,1,0:T(8,128)(2,1)S(1)}, u32[]{:S(2)}, u32[]{:S(2)}) collective-permute-start(bf16[2,256,256]{2,1,0:T(8,128)(2,1)S(1)} %get-tuple-element.42), channel_id=1, source_target_pairs={{1,0},{3,2},{5,4},{7,6},{9,8},{11,10},{13,12},{15,14},{17,16},{19,... | collective-permute-start | bytes 786440 | tf_op jit(solution)/shard_map/ppermute | solution.py:371
  40.5 0.0 collective-permute-done.10.r2
  40.5 1.3 %partial.1 = (f32[512,512]{1,0:T(8,128)S(1)}, bf16[512,512]{1,0:T(8,128)(2,1)S(1)}, bf16[512,512]{1,0:T(8,128)(2,1)S(1)}, bf16[512,512]{1,0:T(8,128)(2,1)S(1)}) custom-call(f32[4,512,512]{2,1,0:T(8,128)S(1)} %early.1.acc, bf16[8,256,256]{2,1,0:T(8,128)(2,1)S(1)} %collective-permute-done.3.r1, bf16[8,256,256]{2,1,0:T(8,128)(2,1)S(1)} %collective-permute-done.10.r2, ...), custom_call_target="tpu_custom_call" | custom-call | tf_op jit(solution)/shard_map/partial/pallas_call | solution.py:208
  41.8 0.1 collective-permute-start.11
  41.9 0.3 collective-permute-start.12
  42.2 1.1 %collective-permute-start.13 = (bf16[512,512]{1,0:T(8,128)(2,1)S(1)}, bf16[512,512]{1,0:T(8,128)(2,1)S(1)}, u32[]{:S(2)}, u32[]{:S(2)}) collective-permute-start(bf16[512,512]{1,0:T(8,128)(2,1)S(1)} %get-tuple-element.51), channel_id=1, source_target_pairs={{0,96},{1,13},{4,100},{5,1},{8,104},{9,5},{12,108},{13,9},{32,0},{... | collective-permute-start | bytes 1572872 | tf_op jit(solution)/shard_map/ppermute | solution.py:34
  43.3 0.0 collective-permute-done.8.a_ref
  43.4 1.4 %collective-permute-start.14 = (bf16[2,256,256]{2,1,0:T(8,128)(2,1)S(1)}, bf16[2,256,256]{2,1,0:T(8,128)(2,1)S(1)}, u32[]{:S(2)}, u32[]{:S(2)}) collective-permute-start(bf16[2,256,256]{2,1,0:T(8,128)(2,1)S(1)} %picked.1.seed.a_ref), channel_id=1, source_target_pairs={{0,16},{16,0},{1,17},{17,1},{2,18},{18,2},{3,19},{19,3},{4,20},{20... | collective-permute-start | bytes 786440 | tf_op jit(solution)/shard_map/ppermute | solution.py:38
  44.7 2.4 %collective-permute-start.9 = (bf16[2,256,256]{2,1,0:T(8,128)(2,1)S(1)}, bf16[2,256,256]{2,1,0:T(8,128)(2,1)S(1)}, u32[]{:S(2)}, u32[]{:S(2)}) collective-permute-start(bf16[2,256,256]{2,1,0:T(8,128)(2,1)S(1)} %picked.1.seed.a_ref), channel_id=1, source_target_pairs={{0,12},{1,5},{4,0},{5,9},{8,4},{9,13},{12,8},{13,1},{2,14},{3,7},{... | collective-permute-start | bytes 786440 | tf_op jit(solution)/shard_map/ppermute | solution.py:347
  47.1 3.8 %collective-permute-done.14.other.b_ref = bf16[2,256,256]{2,1,0:T(8,128)(2,1)S(1)} collective-permute-done((bf16[2,256,256]{2,1,0:T(8,128)(2,1)S(1)}, bf16[2,256,256]{2,1,0:T(8,128)(2,1)S(1)}, u32[]{:S(2)}, u32[]{:S(2)}) %collective-permute-start.14) | collective-permute-done | bytes 262176 | tf_op jit(solution)/shard_map/ppermute | solution.py:38
  51.0 2.0 %collective-permute-start.17 = (bf16[4,256,256]{2,1,0:T(8,128)(2,1)S(1)}, bf16[4,256,256]{2,1,0:T(8,128)(2,1)S(1)}, u32[]{:S(2)}, u32[]{:S(2)}) collective-permute-start(bf16[4,256,256]{2,1,0:T(8,128)(2,1)S(1)} %paired.1), channel_id=1, source_target_pairs={{0,8},{4,12},{8,0},{12,4},{1,9},{5,13},{9,1},{13,5},{2,10},{6,14},... | collective-permute-start | bytes 1572872 | tf_op jit(solution)/shard_map/ppermute | solution.py:376
  53.0 11.8 %collective-permute-done.9.back = bf16[2,256,256]{2,1,0:T(8,128)(2,1)S(1)} collective-permute-done((bf16[2,256,256]{2,1,0:T(8,128)(2,1)S(1)}, bf16[2,256,256]{2,1,0:T(8,128)(2,1)S(1)}, u32[]{:S(2)}, u32[]{:S(2)}) %collective-permute-start.9) | collective-permute-done | bytes 262176 | tf_op jit(solution)/shard_map/ppermute | solution.py:347
  64.8 0.1 collective-permute-start.16
  64.9 0.0 collective-permute-done.11.b
  64.9 0.0 collective-permute-done.12.c
  64.9 0.6 copy-done.4
  65.5 1.0 %summed.1 = bf16[8,128,256]{2,1,0:T(8,128)(2,1)} custom-call(f32[512,512]{1,0:T(8,128)S(1)} %get-tuple-element.48.a, bf16[512,512]{1,0:T(8,128)(2,1)S(1)} %collective-permute-done.11.b, bf16[512,512]{1,0:T(8,128)(2,1)S(1)} %collective-permute-done.12.c, bf16[512,512]{1,0:T(8,128)(2,1)S(1)} %collective-permute-done.13.d), custom_call_target="tpu_custom_call" | custom-call | tf_op jit(solution)/shard_map/summed/pallas_call | solution.py:229
  66.5 8.9 %all-to-all-start = ((bf16[8,128,256]{2,1,0:T(8,128)(2,1)}), bf16[8,128,256]{2,1,0:T(8,128)(2,1)S(1)}, u32[]{:S(2)}, u32[]{:S(2)}) async-start(bf16[8,128,256]{2,1,0:T(8,128)(2,1)} %summed.1), calls=%async_computation | async-start | bytes 1048576 | tf_op jit(solution)/shard_map/all_to_all | solution.py:381
  75.4 2.0 %collective-permute-start.15 = (bf16[2,256,256]{2,1,0:T(8,128)(2,1)}, bf16[2,256,256]{2,1,0:T(8,128)(2,1)S(1)}, u32[]{:S(2)}, u32[]{:S(2)}) collective-permute-start(bf16[2,256,256]{2,1,0:T(8,128)(2,1)} %copy-done.4), channel_id=1, source_target_pairs={{0,16},{16,0},{1,17},{17,1},{2,18},{18,2},{3,19},{19,3},{4,20},{20... | collective-permute-start | bytes 786440 | tf_op jit(solution)/shard_map/ppermute | solution.py:38
  77.5 12.2 %collective-permute-done.15.back_other = bf16[2,256,256]{2,1,0:T(8,128)(2,1)S(1)} collective-permute-done((bf16[2,256,256]{2,1,0:T(8,128)(2,1)}, bf16[2,256,256]{2,1,0:T(8,128)(2,1)S(1)}, u32[]{:S(2)}, u32[]{:S(2)}) %collective-permute-start.15) | collective-permute-done | bytes 262176 | tf_op jit(solution)/shard_map/ppermute | solution.py:38
  89.7 0.9 copy-done.2
  90.7 0.9 copy-done.5
  91.6 2.6 %first_half.1.o_in = bf16[2048,4,256]{2,1,0:T(4,128)(2,1)} custom-call(bf16[512,1024]{1,0:T(8,128)(2,1)S(1)} %get-tuple-element.52.h_ref, bf16[2,256,256]{2,1,0:T(8,128)(2,1)S(1)} %picked.1.seed.a_ref, bf16[2,256,256]{2,1,0:T(8,128)(2,1)S(1)} %copy-done.2, bf16[2,256,256]{2,1,0:T(8,128)(2,1)S(1)} %copy-done.5, ...), custom_call_target="tpu_custom_call" | custom-call | flops 2000000000 | bytes 5242880 | tf_op jit(solution)/shard_map/first_half/pallas_call | solution.py:328
  94.2 0.0 all-to-all-done.r_ref
  94.3 0.9 finish.1
  95.1 2.6 %second_half.1 = bf16[2048,4,256]{2,1,0:T(4,128)(2,1)} custom-call(bf16[2048,4,256]{2,1,0:T(4,128)(2,1)} %first_half.1.o_in, bf16[512,1024]{1,0:T(8,128)(2,1)S(1)} %get-tuple-element.52.h_ref, bf16[4,256,256]{2,1,0:T(8,128)(2,1)S(1)} %collective-permute-done.16.ahead, ...), custom_call_target="tpu_custom_call", output_to_operand_aliasing={{}: (0, {})} | custom-call | flops 2000000000 | bytes 5242880 | tf_op jit(solution)/shard_map/second_half/pallas_call | solution.py:328
  (14 shorter events, 0.1 us)
Async XLA Ops:
  0.6 4.0 %copy-start.3 = (bf16[128,256]{1,0:T(8,128)(2,1)S(1)}, bf16[128,256]{1,0:T(8,128)(2,1)}, u32[]{:S(2)}) copy-start(bf16[128,256]{1,0:T(8,128)(2,1)} %g_ref) | copy-start | bytes 196612
  0.6 4.0 %copy-start = (bf16[128,4,256]{2,1,0:T(4,128)(2,1)S(1)}, bf16[128,4,256]{2,1,0:T(4,128)(2,1)}, u32[]{:S(2)}) copy-start(bf16[128,4,256]{2,1,0:T(4,128)(2,1)} %h_ref) | copy-start | bytes 786436
  3.1 16.3 %collective-permute-start.3 = (bf16[8,256,256]{2,1,0:T(8,128)(2,1)S(1)}, bf16[8,256,256]{2,1,0:T(8,128)(2,1)S(1)}, u32[]{:S(2)}, u32[]{:S(2)}) collective-permute-start(bf16[8,256,256]{2,1,0:T(8,128)(2,1)S(1)} %get-tuple-element.32), channel_id=1, source_target_pairs={{0,4},{1,33},{4,8},{5,37},{8,12},{9,41},{12,0},{13,45},{32,36},{33... | collective-permute-start | bytes 3145736 | tf_op jit(solution)/shard_map/ppermute | solution.py:34
  3.2 32.1 %collective-permute-start.7 = (bf16[8,256,256]{2,1,0:T(8,128)(2,1)S(1)}, bf16[8,256,256]{2,1,0:T(8,128)(2,1)S(1)}, u32[]{:S(2)}, u32[]{:S(2)}) collective-permute-start(bf16[8,256,256]{2,1,0:T(8,128)(2,1)S(1)} %get-tuple-element.34), channel_id=1, source_target_pairs={{0,12},{1,97},{4,0},{5,101},{8,4},{9,105},{12,8},{13,109},{32,44},... | collective-permute-start | bytes 3145736 | tf_op jit(solution)/shard_map/ppermute | solution.py:34
  4.7 9.5 %collective-permute-start.1 = (bf16[5,128,256]{2,1,0:T(8,128)(2,1)S(1)}, bf16[5,128,256]{2,1,0:T(8,128)(2,1)S(1)}, u32[]{:S(2)}, u32[]{:S(2)}) collective-permute-start(bf16[5,128,256]{2,1,0:T(8,128)(2,1)S(1)} %packed.1.p0), channel_id=1, source_target_pairs={{0,2},{2,0},{1,3},{3,1},{4,6},{6,4},{5,7},{7,5},{8,10},{10,8},{9,1... | collective-permute-start | bytes 983048 | tf_op jit(solution)/shard_map/ppermute | solution.py:38
  7.7 32.8 %collective-permute-start.10 = (bf16[8,256,256]{2,1,0:T(8,128)(2,1)S(1)}, bf16[8,256,256]{2,1,0:T(8,128)(2,1)S(1)}, u32[]{:S(2)}, u32[]{:S(2)}) collective-permute-start(bf16[8,256,256]{2,1,0:T(8,128)(2,1)S(1)} %get-tuple-element.46), channel_id=1, source_target_pairs={{0,8},{1,65},{4,12},{5,69},{8,0},{9,73},{12,4},{13,77},{32,40},{33... | collective-permute-start | bytes 3145736 | tf_op jit(solution)/shard_map/ppermute | solution.py:34
  8.1 8.3 %collective-permute-start = (bf16[5,128,256]{2,1,0:T(8,128)(2,1)S(1)}, bf16[5,128,256]{2,1,0:T(8,128)(2,1)S(1)}, u32[]{:S(2)}, u32[]{:S(2)}) collective-permute-start(bf16[5,128,256]{2,1,0:T(8,128)(2,1)S(1)} %packed.1.p0), channel_id=1, source_target_pairs={{0,1},{1,0},{2,3},{3,2},{4,5},{5,4},{6,7},{7,6},{8,9},{9,8},{10,11... | collective-permute-start | bytes 983048 | tf_op jit(solution)/shard_map/ppermute | solution.py:38
  14.2 3.4 %collective-permute-start.2 = (bf16[5,128,256]{2,1,0:T(8,128)(2,1)S(1)}, bf16[5,128,256]{2,1,0:T(8,128)(2,1)S(1)}, u32[]{:S(2)}, u32[]{:S(2)}) collective-permute-start(bf16[5,128,256]{2,1,0:T(8,128)(2,1)S(1)} %collective-permute-done.1.p2), channel_id=1, source_target_pairs={{0,1},{1,0},{2,3},{3,2},{4,5},{5,4},{6,7},{7,6},{8,9},{9,8},{10,11... | collective-permute-start | bytes 983048 | tf_op jit(solution)/shard_map/ppermute | solution.py:38
  17.8 17.4 %collective-permute-start.6 = (bf16[2,256,256]{2,1,0:T(8,128)(2,1)S(1)}, bf16[2,256,256]{2,1,0:T(8,128)(2,1)S(1)}, u32[]{:S(2)}, u32[]{:S(2)}) collective-permute-start(bf16[2,256,256]{2,1,0:T(8,128)(2,1)S(1)} %get-tuple-element.36.g0), channel_id=1, source_target_pairs={{0,12},{1,97},{4,0},{5,101},{8,4},{9,105},{12,8},{13,109},{32,44},... | collective-permute-start | bytes 786440 | tf_op jit(solution)/shard_map/ppermute | solution.py:34
  18.0 18.5 %collective-permute-start.5 = (bf16[2,256,256]{2,1,0:T(8,128)(2,1)S(1)}, bf16[2,256,256]{2,1,0:T(8,128)(2,1)S(1)}, u32[]{:S(2)}, u32[]{:S(2)}) collective-permute-start(bf16[2,256,256]{2,1,0:T(8,128)(2,1)S(1)} %get-tuple-element.36.g0), channel_id=1, source_target_pairs={{0,8},{1,65},{4,12},{5,69},{8,0},{9,73},{12,4},{13,77},{32,40},{33... | collective-permute-start | bytes 786440 | tf_op jit(solution)/shard_map/ppermute | solution.py:34
  19.3 17.2 %collective-permute-start.4 = (bf16[2,256,256]{2,1,0:T(8,128)(2,1)S(1)}, bf16[2,256,256]{2,1,0:T(8,128)(2,1)S(1)}, u32[]{:S(2)}, u32[]{:S(2)}) collective-permute-start(bf16[2,256,256]{2,1,0:T(8,128)(2,1)S(1)} %get-tuple-element.36.g0), channel_id=1, source_target_pairs={{0,4},{1,33},{4,8},{5,37},{8,12},{9,41},{12,0},{13,45},{32,36},{33... | collective-permute-start | bytes 786440 | tf_op jit(solution)/shard_map/ppermute | solution.py:34
  36.6 6.7 %collective-permute-start.8 = (bf16[2,256,256]{2,1,0:T(8,128)(2,1)S(1)}, bf16[2,256,256]{2,1,0:T(8,128)(2,1)S(1)}, u32[]{:S(2)}, u32[]{:S(2)}) collective-permute-start(bf16[2,256,256]{2,1,0:T(8,128)(2,1)S(1)} %get-tuple-element.42), channel_id=1, source_target_pairs={{1,0},{3,2},{5,4},{7,6},{9,8},{11,10},{13,12},{15,14},{17,16},{19,... | collective-permute-start | bytes 786440 | tf_op jit(solution)/shard_map/ppermute | solution.py:371
  41.8 23.1 %collective-permute-start.11 = (bf16[512,512]{1,0:T(8,128)(2,1)S(1)}, bf16[512,512]{1,0:T(8,128)(2,1)S(1)}, u32[]{:S(2)}, u32[]{:S(2)}) collective-permute-start(bf16[512,512]{1,0:T(8,128)(2,1)S(1)} %get-tuple-element.49), channel_id=1, source_target_pairs={{0,32},{1,5},{4,36},{5,9},{8,40},{9,13},{12,44},{13,1},{32,64},{33... | collective-permute-start | bytes 1572872 | tf_op jit(solution)/shard_map/ppermute | solution.py:34
  41.9 23.0 %collective-permute-start.12 = (bf16[512,512]{1,0:T(8,128)(2,1)S(1)}, bf16[512,512]{1,0:T(8,128)(2,1)S(1)}, u32[]{:S(2)}, u32[]{:S(2)}) collective-permute-start(bf16[512,512]{1,0:T(8,128)(2,1)S(1)} %get-tuple-element.50), channel_id=1, source_target_pairs={{0,64},{1,9},{4,68},{5,13},{8,72},{9,1},{12,76},{13,5},{32,96},{33... | collective-permute-start | bytes 1572872 | tf_op jit(solution)/shard_map/ppermute | solution.py:34
  42.2 22.7 %collective-permute-start.13 = (bf16[512,512]{1,0:T(8,128)(2,1)S(1)}, bf16[512,512]{1,0:T(8,128)(2,1)S(1)}, u32[]{:S(2)}, u32[]{:S(2)}) collective-permute-start(bf16[512,512]{1,0:T(8,128)(2,1)S(1)} %get-tuple-element.51), channel_id=1, source_target_pairs={{0,96},{1,13},{4,100},{5,1},{8,104},{9,5},{12,108},{13,9},{32,0},{... | collective-permute-start | bytes 1572872 | tf_op jit(solution)/shard_map/ppermute | solution.py:34
  43.4 7.6 %collective-permute-start.14 = (bf16[2,256,256]{2,1,0:T(8,128)(2,1)S(1)}, bf16[2,256,256]{2,1,0:T(8,128)(2,1)S(1)}, u32[]{:S(2)}, u32[]{:S(2)}) collective-permute-start(bf16[2,256,256]{2,1,0:T(8,128)(2,1)S(1)} %picked.1.seed.a_ref), channel_id=1, source_target_pairs={{0,16},{16,0},{1,17},{17,1},{2,18},{18,2},{3,19},{19,3},{4,20},{20... | collective-permute-start | bytes 786440 | tf_op jit(solution)/shard_map/ppermute | solution.py:38
  44.7 20.0 %collective-permute-start.9 = (bf16[2,256,256]{2,1,0:T(8,128)(2,1)S(1)}, bf16[2,256,256]{2,1,0:T(8,128)(2,1)S(1)}, u32[]{:S(2)}, u32[]{:S(2)}) collective-permute-start(bf16[2,256,256]{2,1,0:T(8,128)(2,1)S(1)} %picked.1.seed.a_ref), channel_id=1, source_target_pairs={{0,12},{1,5},{4,0},{5,9},{8,4},{9,13},{12,8},{13,1},{2,14},{3,7},{... | collective-permute-start | bytes 786440 | tf_op jit(solution)/shard_map/ppermute | solution.py:347
  51.0 13.9 %copy-start.1 = (bf16[2,256,256]{2,1,0:T(8,128)(2,1)}, bf16[2,256,256]{2,1,0:T(8,128)(2,1)S(1)}, u32[]{:S(2)}) copy-start(bf16[2,256,256]{2,1,0:T(8,128)(2,1)S(1)} %collective-permute-done.14.other.b_ref) | copy-start | bytes 786436
  51.0 44.1 %collective-permute-start.17 = (bf16[4,256,256]{2,1,0:T(8,128)(2,1)S(1)}, bf16[4,256,256]{2,1,0:T(8,128)(2,1)S(1)}, u32[]{:S(2)}, u32[]{:S(2)}) collective-permute-start(bf16[4,256,256]{2,1,0:T(8,128)(2,1)S(1)} %paired.1), channel_id=1, source_target_pairs={{0,8},{4,12},{8,0},{12,4},{1,9},{5,13},{9,1},{13,5},{2,10},{6,14},... | collective-permute-start | bytes 1572872 | tf_op jit(solution)/shard_map/ppermute | solution.py:376
  64.8 0.7 copy-start.4
  64.8 30.4 %collective-permute-start.16 = (bf16[4,256,256]{2,1,0:T(8,128)(2,1)S(1)}, bf16[4,256,256]{2,1,0:T(8,128)(2,1)S(1)}, u32[]{:S(2)}, u32[]{:S(2)}) collective-permute-start(bf16[4,256,256]{2,1,0:T(8,128)(2,1)S(1)} %paired.1), channel_id=1, source_target_pairs={{0,4},{1,13},{4,8},{5,1},{8,12},{9,5},{12,0},{13,9},{2,6},{3,15},{... | collective-permute-start | bytes 1572872 | tf_op jit(solution)/shard_map/ppermute | solution.py:347
  66.5 27.7 %all-to-all-start = ((bf16[8,128,256]{2,1,0:T(8,128)(2,1)}), bf16[8,128,256]{2,1,0:T(8,128)(2,1)S(1)}, u32[]{:S(2)}, u32[]{:S(2)}) async-start(bf16[8,128,256]{2,1,0:T(8,128)(2,1)} %summed.1), calls=%async_computation | async-start | bytes 1048576 | tf_op jit(solution)/shard_map/all_to_all | solution.py:381
  75.4 14.3 %collective-permute-start.15 = (bf16[2,256,256]{2,1,0:T(8,128)(2,1)}, bf16[2,256,256]{2,1,0:T(8,128)(2,1)S(1)}, u32[]{:S(2)}, u32[]{:S(2)}) collective-permute-start(bf16[2,256,256]{2,1,0:T(8,128)(2,1)} %copy-done.4), channel_id=1, source_target_pairs={{0,16},{16,0},{1,17},{17,1},{2,18},{18,2},{3,19},{19,3},{4,20},{20... | collective-permute-start | bytes 786440 | tf_op jit(solution)/shard_map/ppermute | solution.py:38
  89.7 1.0 copy-start.2
  90.7 0.9 copy-start.5

commit v9 on v8

--- a/solution.py
+++ b/solution.py
@@ -308,17 +308,16 @@
         copy.wait()
 
 
-def first_half_body(h_ref, seed, other, back, back_other, *refs):
-    yl, c = lax.axis_index("yl"), lax.axis_index("c")
-    k = 3 - 2 * c
-    blocks = [(yl, 0, seed), (1 - yl, 0, other), (yl, k, back), (1 - yl, k, back_other)]
+def first_half_body(h_ref, seed, other, up, *refs):
+    yl = lax.axis_index("yl")
+    blocks = [(yl, 0, seed), (1 - yl, 0, other), (yl, 1, up.at[0:2]), (1 - yl, 1, up.at[2:4])]
     outer_into(blocks, h_ref, *refs)
 
 
-def second_half_body(o_in, h_ref, ahead, far, *refs):
-    yl, c = lax.axis_index("yl"), lax.axis_index("c")
+def second_half_body(o_in, h_ref, far, down, *refs):
+    yl = lax.axis_index("yl")
     blocks = []
-    for k, ref in ((1 + 2 * c, ahead), (2, far)):
+    for k, ref in ((3, down), (2, far)):
         blocks += [(yl, k, ref.at[0:2]), (1 - yl, k, ref.at[2:4])]
     outer_into(blocks, h_ref, *refs)
 
@@ -333,18 +332,9 @@
         scratch_shapes=[VM((4, 256, 4, 256), BF), pltpu.SemaphoreType.DMA((4,))],
         input_output_aliases={0: 0} if aliased else {},
         compiler_params=LIMIT,
-        cost_estimate=pl.CostEstimate(flops=int(2e9), bytes_accessed=5 << 20, transcendentals=0),
+        cost_estimate=pl.CostEstimate(flops=int(1e6), bytes_accessed=1 << 10, transcendentals=0),
         name=name,
     )(*([so_far] if aliased else []), *kept(*operands))
-
-
-def along_x(value, forward_core):
-    pairs = []
-    for x in range(4):
-        for c in range(2):
-            k = 1 if c == forward_core else 3
-            pairs.append((x * 2 + c, (x + k) % 4 * 2 + c))
-    return lax.ppermute(value, ("x", "c"), pairs)
 
 
 def per_device(hidden, grad_out, weight_base, block_scale):
@@ -371,18 +361,16 @@
     seed = picked(lax.ppermute(give, "c", [(1, 0)]), keep)
     other = swap(seed, "yl")
     both = paired(seed, other)
-    back = along_x(seed, 1)
-    ahead = along_x(both, 0)
-    far = lax.ppermute(both, "x", [(i, (i + 2) % 4) for i in range(4)])
-    back, parts[0] = lax.optimization_barrier((back, parts[0]))
-    back_other = swap(back, "yl")
+    up, far, down = [
+        lax.ppermute(both, "x", [(i, (i + k) % 4) for i in range(4)]) for k in (1, 2, 3)
+    ]
 
     blocks = summed_blocks(parts)
     blocks = lax.all_to_all(blocks, ("yl", "yh", "c"), 0, 0, tiled=True)
-    grad_hidden = finished(blocks)
-    half = outer_half(first_half_body, "first_half", (h, seed, other, back, back_other))
-    grad_weight = outer_half(second_half_body, "second_half", (h, ahead, far), half)
-    return grad_hidden, grad_weight
+    half = outer_half(first_half_body, "first_half", (h, seed, other, up))
+    grad_weight = outer_half(second_half_body, "second_half", (h, far, down), half)
+    blocks, grad_weight = lax.optimization_barrier((blocks, grad_weight))
+    return finished(blocks), grad_weight
 
 
 def solution(mesh):

time: 98.2 us -> 85.6 us (0.87)
  the two profiles are of different devices: /device:TPU:103 before, /device:TPU:46 now
where the time goes in v9:
time: 85.6 us; the launch traced here: 85.4 us
  waiting for transfers between devices  42.8 us (50%)
  starting transfers between devices  27.4 us (32%)
  Pallas kernels  14.3 us (17%)
    ppermute x9, waiting for transfers between devices, shift(): return lax.ppermute(value, ('z', 'x', 'c'), pairs)  14.9 us
    ppermute x4, waiting for transfers between devices, swap(): return lax.ppermute(value, axis, [(0, 1), (1, 0)])  14.1 us
    ppermute x3, waiting for transfers between devices, per_device(): lax.ppermute(both, 'x', [(i, (i + k) % 4) for i in range(4)])  13.8 us
    ppermute x9, starting transfers between devices, shift(): return lax.ppermute(value, ('z', 'x', 'c'), pairs)  13.3 us
    pallas_call x2, Pallas kernels, outer_half(): pl.pallas_call(body, out_shape=jax.ShapeDtypeStruct((2048, 4, 256), BF),...  6.29 us
    all_to_all x1, starting transfers between devices, per_device(): blocks = lax.all_to_all(blocks, ('yl', 'yh', 'c'), 0, 0, tiled=True)  4.92 us
    ppermute x3, starting transfers between devices, per_device(): lax.ppermute(both, 'x', [(i, (i + k) % 4) for i in range(4)])  4.72 us
    ppermute x4, starting transfers between devices, swap(): return lax.ppermute(value, axis, [(0, 1), (1, 0)])  3.19 us
  transfers between devices with their start and end apart: 18, of which 7 were waited for; matrix products, arithmetic and copies ran while one was open for 0% of the time, Pallas kernels for 13%

profile of v9, /device:TPU:46, one launch (start us, length us, event | category | flops | bytes accessed | tf_op | source)
XLA Modules:
  0.0 85.4 jit_solution(7767185812907403085)
XLA Ops:
  0.6 0.0 copy-start.1
  0.7 2.4 %scale.1 = (bf16[8,256,256]{2,1,0:T(8,128)(2,1)S(1)}, bf16[8,256,256]{2,1,0:T(8,128)(2,1)S(1)}, bf16[8,256,256]{2,1,0:T(8,128)(2,1)S(1)}, bf16[8,256,256]{2,1,0:T(8,128)(2,1)S(1)}) custom-call(bf16[4,2,4,256,256]{4,3,2,1,0:T(8,128)(2,1)} %bitcast.2, bf16[16,512]{1,0:T(8,128)(2,1)} %bitcast.3), custom_call_target="tpu_custom_call" | custom-call | tf_op jit(solution)/shard_map/scale/pallas_call | solution.py:96
  3.1 0.5 collective-permute-start.3
  3.6 1.5 %collective-permute-start.7 = (bf16[8,256,256]{2,1,0:T(8,128)(2,1)S(1)}, bf16[8,256,256]{2,1,0:T(8,128)(2,1)S(1)}, u32[]{:S(2)}, u32[]{:S(2)}) collective-permute-start(bf16[8,256,256]{2,1,0:T(8,128)(2,1)S(1)} %get-tuple-element.34), channel_id=1, source_target_pairs={{0,12},{1,97},{4,0},{5,101},{8,4},{9,105},{12,8},{13,109},{32,44},... | collective-permute-start | bytes 3145736 | tf_op jit(solution)/shard_map/ppermute | solution.py:34
  5.2 0.1 packed.1.p0
  5.2 2.4 %collective-permute-start.1 = (bf16[5,128,256]{2,1,0:T(8,128)(2,1)S(1)}, bf16[5,128,256]{2,1,0:T(8,128)(2,1)S(1)}, u32[]{:S(2)}, u32[]{:S(2)}) collective-permute-start(bf16[5,128,256]{2,1,0:T(8,128)(2,1)S(1)} %packed.1.p0), channel_id=1, source_target_pairs={{0,2},{2,0},{1,3},{3,1},{4,6},{6,4},{5,7},{7,5},{8,10},{10,8},{9,1... | collective-permute-start | bytes 983048 | tf_op jit(solution)/shard_map/ppermute | solution.py:38
  7.6 1.4 %collective-permute-start.8 = (bf16[8,256,256]{2,1,0:T(8,128)(2,1)S(1)}, bf16[8,256,256]{2,1,0:T(8,128)(2,1)S(1)}, u32[]{:S(2)}, u32[]{:S(2)}) collective-permute-start(bf16[8,256,256]{2,1,0:T(8,128)(2,1)S(1)} %get-tuple-element.44), channel_id=1, source_target_pairs={{0,8},{1,65},{4,12},{5,69},{8,0},{9,73},{12,4},{13,77},{32,40},{33... | collective-permute-start | bytes 3145736 | tf_op jit(solution)/shard_map/ppermute | solution.py:34
  9.0 0.3 collective-permute-start
  9.3 6.6 %collective-permute-done.1.p2 = bf16[5,128,256]{2,1,0:T(8,128)(2,1)S(1)} collective-permute-done((bf16[5,128,256]{2,1,0:T(8,128)(2,1)S(1)}, bf16[5,128,256]{2,1,0:T(8,128)(2,1)S(1)}, u32[]{:S(2)}, u32[]{:S(2)}) %collective-permute-start.1) | collective-permute-done | bytes 327712 | tf_op jit(solution)/shard_map/ppermute | solution.py:38
  15.9 0.0 collective-permute-start.2
  15.9 0.0 collective-permute-done.p1
  15.9 1.6 %collective-permute-done.2.p3 = bf16[5,128,256]{2,1,0:T(8,128)(2,1)S(1)} collective-permute-done((bf16[5,128,256]{2,1,0:T(8,128)(2,1)S(1)}, bf16[5,128,256]{2,1,0:T(8,128)(2,1)S(1)}, u32[]{:S(2)}, u32[]{:S(2)}) %collective-permute-start.2) | collective-permute-done | bytes 327712 | tf_op jit(solution)/shard_map/ppermute | solution.py:38
  17.5 0.1 tokens.1
  17.7 0.9 %collective-permute-start.6 = (bf16[2,256,256]{2,1,0:T(8,128)(2,1)S(1)}, bf16[2,256,256]{2,1,0:T(8,128)(2,1)S(1)}, u32[]{:S(2)}, u32[]{:S(2)}) collective-permute-start(bf16[2,256,256]{2,1,0:T(8,128)(2,1)S(1)} %get-tuple-element.36.g0), channel_id=1, source_target_pairs={{0,12},{1,97},{4,0},{5,101},{8,4},{9,105},{12,8},{13,109},{32,44},... | collective-permute-start | bytes 786440 | tf_op jit(solution)/shard_map/ppermute | solution.py:34
  18.6 1.1 %collective-permute-start.5 = (bf16[2,256,256]{2,1,0:T(8,128)(2,1)S(1)}, bf16[2,256,256]{2,1,0:T(8,128)(2,1)S(1)}, u32[]{:S(2)}, u32[]{:S(2)}) collective-permute-start(bf16[2,256,256]{2,1,0:T(8,128)(2,1)S(1)} %get-tuple-element.36.g0), channel_id=1, source_target_pairs={{0,8},{1,65},{4,12},{5,69},{8,0},{9,73},{12,4},{13,77},{32,40},{33... | collective-permute-start | bytes 786440 | tf_op jit(solution)/shard_map/ppermute | solution.py:34
  19.7 0.0 collective-permute-done.3.r1
  19.7 2.1 %collective-permute-start.4 = (bf16[2,256,256]{2,1,0:T(8,128)(2,1)S(1)}, bf16[2,256,256]{2,1,0:T(8,128)(2,1)S(1)}, u32[]{:S(2)}, u32[]{:S(2)}) collective-permute-start(bf16[2,256,256]{2,1,0:T(8,128)(2,1)S(1)} %get-tuple-element.36.g0), channel_id=1, source_target_pairs={{0,4},{1,33},{4,8},{5,37},{8,12},{9,41},{12,0},{13,45},{32,36},{33... | collective-permute-start | bytes 786440 | tf_op jit(solution)/shard_map/ppermute | solution.py:34
  21.8 14.7 %collective-permute-done.6.g3 = bf16[2,256,256]{2,1,0:T(8,128)(2,1)S(1)} collective-permute-done((bf16[2,256,256]{2,1,0:T(8,128)(2,1)S(1)}, bf16[2,256,256]{2,1,0:T(8,128)(2,1)S(1)}, u32[]{:S(2)}, u32[]{:S(2)}) %collective-permute-start.6) | collective-permute-done | bytes 262176 | tf_op jit(solution)/shard_map/ppermute | solution.py:34
  36.5 0.0 collective-permute-done.7.r3
  36.5 1.3 %early.1.acc = f32[4,512,512]{2,1,0:T(8,128)S(1)} custom-call(bf16[8,256,256]{2,1,0:T(8,128)(2,1)S(1)} %get-tuple-element.28.r0, bf16[8,256,256]{2,1,0:T(8,128)(2,1)S(1)} %collective-permute-done.7.r3, bf16[2,256,256]{2,1,0:T(8,128)(2,1)S(1)} %get-tuple-element.36.g0, bf16[2,256,256]{2,1,0:T(8,128)(2,1)S(1)} %collective-permute-done.6.g3), custom_call_target="tpu_custom_call" | custom-call | flops 2000000000 | bytes 6291456 | tf_op jit(solution)/shard_map/early/pallas_call | solution.py:163
  37.8 0.0 collective-permute-done.5.g2
  37.8 0.0 collective-permute-done.4.g1
  37.8 0.1 plane.1
  37.9 1.3 %collective-permute-start.12 = (bf16[2,256,256]{2,1,0:T(8,128)(2,1)S(1)}, bf16[2,256,256]{2,1,0:T(8,128)(2,1)S(1)}, u32[]{:S(2)}, u32[]{:S(2)}) collective-permute-start(bf16[2,256,256]{2,1,0:T(8,128)(2,1)S(1)} %get-tuple-element.50), channel_id=1, source_target_pairs={{1,0},{3,2},{5,4},{7,6},{9,8},{11,10},{13,12},{15,14},{17,16},{19,... | collective-permute-start | bytes 786440 | tf_op jit(solution)/shard_map/ppermute | solution.py:361
  39.2 0.0 collective-permute-done.8.r2
  39.2 1.3 %partial.1 = (f32[512,512]{1,0:T(8,128)S(1)}, bf16[512,512]{1,0:T(8,128)(2,1)S(1)}, bf16[512,512]{1,0:T(8,128)(2,1)S(1)}, bf16[512,512]{1,0:T(8,128)(2,1)S(1)}) custom-call(f32[4,512,512]{2,1,0:T(8,128)S(1)} %early.1.acc, bf16[8,256,256]{2,1,0:T(8,128)(2,1)S(1)} %collective-permute-done.3.r1, bf16[8,256,256]{2,1,0:T(8,128)(2,1)S(1)} %collective-permute-done.8.r2, ...), custom_call_target="tpu_custom_call" | custom-call | tf_op jit(solution)/shard_map/partial/pallas_call | solution.py:208
  40.5 2.0 %collective-permute-start.9 = (bf16[512,512]{1,0:T(8,128)(2,1)S(1)}, bf16[512,512]{1,0:T(8,128)(2,1)S(1)}, u32[]{:S(2)}, u32[]{:S(2)}) collective-permute-start(bf16[512,512]{1,0:T(8,128)(2,1)S(1)} %get-tuple-element.46), channel_id=1, source_target_pairs={{0,32},{1,5},{4,36},{5,9},{8,40},{9,13},{12,44},{13,1},{32,64},{33... | collective-permute-start | bytes 1572872 | tf_op jit(solution)/shard_map/ppermute | solution.py:34
  42.5 1.1 %collective-permute-start.10 = (bf16[512,512]{1,0:T(8,128)(2,1)S(1)}, bf16[512,512]{1,0:T(8,128)(2,1)S(1)}, u32[]{:S(2)}, u32[]{:S(2)}) collective-permute-start(bf16[512,512]{1,0:T(8,128)(2,1)S(1)} %get-tuple-element.47), channel_id=1, source_target_pairs={{0,64},{1,9},{4,68},{5,13},{8,72},{9,1},{12,76},{13,5},{32,96},{33... | collective-permute-start | bytes 1572872 | tf_op jit(solution)/shard_map/ppermute | solution.py:34
  43.6 2.5 %collective-permute-start.11 = (bf16[512,512]{1,0:T(8,128)(2,1)S(1)}, bf16[512,512]{1,0:T(8,128)(2,1)S(1)}, u32[]{:S(2)}, u32[]{:S(2)}) collective-permute-start(bf16[512,512]{1,0:T(8,128)(2,1)S(1)} %get-tuple-element.48), channel_id=1, source_target_pairs={{0,96},{1,13},{4,100},{5,1},{8,104},{9,5},{12,108},{13,9},{32,0},{... | collective-permute-start | bytes 1572872 | tf_op jit(solution)/shard_map/ppermute | solution.py:34
  46.2 0.0 collective-permute-done.12.a_ref
  46.2 0.5 collective-permute-start.13
  46.7 5.9 %collective-permute-done.13.b_ref.other = bf16[2,256,256]{2,1,0:T(8,128)(2,1)S(1)} collective-permute-done((bf16[2,256,256]{2,1,0:T(8,128)(2,1)S(1)}, bf16[2,256,256]{2,1,0:T(8,128)(2,1)S(1)}, u32[]{:S(2)}, u32[]{:S(2)}) %collective-permute-start.13) | collective-permute-done | bytes 262176 | tf_op jit(solution)/shard_map/ppermute | solution.py:38
  52.7 0.8 paired.1
  53.5 1.5 %collective-permute-start.14 = (bf16[4,256,256]{2,1,0:T(8,128)(2,1)}, bf16[4,256,256]{2,1,0:T(8,128)(2,1)S(1)}, u32[]{:S(2)}, u32[]{:S(2)}) collective-permute-start(bf16[4,256,256]{2,1,0:T(8,128)(2,1)} %paired.1), channel_id=1, source_target_pairs={{0,4},{4,8},{8,12},{12,0},{1,5},{5,9},{9,13},{13,1},{2,6},{6,10},{... | collective-permute-start | bytes 1572872 | tf_op jit(solution)/shard_map/ppermute | solution.py:365
  55.0 0.5 collective-permute-start.16
  55.5 0.0 collective-permute-done.9.b
  55.5 2.7 %collective-permute-start.15 = (bf16[4,256,256]{2,1,0:T(8,128)(2,1)}, bf16[4,256,256]{2,1,0:T(8,128)(2,1)}, u32[]{:S(2)}, u32[]{:S(2)}) collective-permute-start(bf16[4,256,256]{2,1,0:T(8,128)(2,1)} %paired.1), channel_id=1, source_target_pairs={{0,8},{4,12},{8,0},{12,4},{1,9},{5,13},{9,1},{13,5},{2,10},{6,14},... | collective-permute-start | bytes 1572872 | tf_op jit(solution)/shard_map/ppermute | solution.py:365
  58.2 0.0 collective-permute-done.10.c
  58.2 0.2 collective-permute-done.11.d
  58.4 1.0 %summed.1 = bf16[8,128,256]{2,1,0:T(8,128)(2,1)} custom-call(f32[512,512]{1,0:T(8,128)S(1)} %get-tuple-element.45.a, bf16[512,512]{1,0:T(8,128)(2,1)S(1)} %collective-permute-done.9.b, bf16[512,512]{1,0:T(8,128)(2,1)S(1)} %collective-permute-done.10.c, bf16[512,512]{1,0:T(8,128)(2,1)S(1)} %collective-permute-done.11.d), custom_call_target="tpu_custom_call" | custom-call | tf_op jit(solution)/shard_map/summed/pallas_call | solution.py:229
  59.5 4.9 %all-to-all-start = ((bf16[8,128,256]{2,1,0:T(8,128)(2,1)}), bf16[8,128,256]{2,1,0:T(8,128)(2,1)S(1)}, u32[]{:S(2)}, u32[]{:S(2)}) async-start(bf16[8,128,256]{2,1,0:T(8,128)(2,1)} %summed.1), calls=%async_computation | async-start | bytes 1048576 | tf_op jit(solution)/shard_map/all_to_all | solution.py:369
  64.4 4.2 %collective-permute-done.14.up = bf16[4,256,256]{2,1,0:T(8,128)(2,1)S(1)} collective-permute-done((bf16[4,256,256]{2,1,0:T(8,128)(2,1)}, bf16[4,256,256]{2,1,0:T(8,128)(2,1)S(1)}, u32[]{:S(2)}, u32[]{:S(2)}) %collective-permute-start.14) | collective-permute-done | bytes 524320 | tf_op jit(solution)/shard_map/ppermute | solution.py:365
  68.6 2.6 %first_half.1.o_in = bf16[2048,4,256]{2,1,0:T(4,128)(2,1)} custom-call(bf16[512,1024]{1,0:T(8,128)(2,1)S(1)} %get-tuple-element.49.h_ref, bf16[2,256,256]{2,1,0:T(8,128)(2,1)S(1)} %picked.1.a_ref.seed, bf16[2,256,256]{2,1,0:T(8,128)(2,1)S(1)} %collective-permute-done.13.b_ref.other, bf16[4,256,256]{2,1,0:T(8,128)(2,1)S(1)} %collective-permute-done.14.up), custom_call_target="tpu_custom_call" | custom-call | flops 1000000 | bytes 1024 | tf_op jit(solution)/shard_map/first_half/pallas_call | solution.py:327
  71.2 0.0 collective-permute-done.16.down
  71.2 9.6 %collective-permute-done.15.far = bf16[4,256,256]{2,1,0:T(8,128)(2,1)} collective-permute-done((bf16[4,256,256]{2,1,0:T(8,128)(2,1)}, bf16[4,256,256]{2,1,0:T(8,128)(2,1)}, u32[]{:S(2)}, u32[]{:S(2)}) %collective-permute-start.15) | collective-permute-done | bytes 524320 | tf_op jit(solution)/shard_map/ppermute | solution.py:365
  80.8 3.7 %second_half.1 = bf16[2048,4,256]{2,1,0:T(4,128)(2,1)} custom-call(bf16[2048,4,256]{2,1,0:T(4,128)(2,1)} %first_half.1.o_in, bf16[512,1024]{1,0:T(8,128)(2,1)S(1)} %get-tuple-element.49.h_ref, bf16[4,256,256]{2,1,0:T(8,128)(2,1)} %collective-permute-done.15.far, bf16[4,256,256]{2,1,0:T(8,128)(2,1)S(1)} %collective-permute-done.16.down), custom_call_target="tpu_custom_call", output_to_operand_aliasing={{}: (0, {})} | custom-call | flops 1000000 | bytes 1024 | tf_op jit(solution)/shard_map/second_half/pallas_call | solution.py:327
  84.5 0.0 all-to-all-done.r_ref
  84.5 0.9 %finish.1 = bf16[128,4,256]{2,1,0:T(4,128)(2,1)} custom-call(bf16[8,128,256]{2,1,0:T(8,128)(2,1)S(1)} %all-to-all-done.r_ref), custom_call_target="tpu_custom_call" | custom-call | tf_op jit(solution)/shard_map/finish/pallas_call | solution.py:245
  (4 shorter events, 0.0 us)
Async XLA Ops:
  0.6 4.5 %copy-start.1 = (bf16[128,256]{1,0:T(8,128)(2,1)S(1)}, bf16[128,256]{1,0:T(8,128)(2,1)}, u32[]{:S(2)}) copy-start(bf16[128,256]{1,0:T(8,128)(2,1)} %g_ref) | copy-start | bytes 196612
  0.6 4.5 %copy-start = (bf16[128,4,256]{2,1,0:T(4,128)(2,1)S(1)}, bf16[128,4,256]{2,1,0:T(4,128)(2,1)}, u32[]{:S(2)}) copy-start(bf16[128,4,256]{2,1,0:T(4,128)(2,1)} %h_ref) | copy-start | bytes 786436
  3.1 16.6 %collective-permute-start.3 = (bf16[8,256,256]{2,1,0:T(8,128)(2,1)S(1)}, bf16[8,256,256]{2,1,0:T(8,128)(2,1)S(1)}, u32[]{:S(2)}, u32[]{:S(2)}) collective-permute-start(bf16[8,256,256]{2,1,0:T(8,128)(2,1)S(1)} %get-tuple-element.32), channel_id=1, source_target_pairs={{0,4},{1,33},{4,8},{5,37},{8,12},{9,41},{12,0},{13,45},{32,36},{33... | collective-permute-start | bytes 3145736 | tf_op jit(solution)/shard_map/ppermute | solution.py:34
  3.6 32.9 %collective-permute-start.7 = (bf16[8,256,256]{2,1,0:T(8,128)(2,1)S(1)}, bf16[8,256,256]{2,1,0:T(8,128)(2,1)S(1)}, u32[]{:S(2)}, u32[]{:S(2)}) collective-permute-start(bf16[8,256,256]{2,1,0:T(8,128)(2,1)S(1)} %get-tuple-element.34), channel_id=1, source_target_pairs={{0,12},{1,97},{4,0},{5,101},{8,4},{9,105},{12,8},{13,109},{32,44},... | collective-permute-start | bytes 3145736 | tf_op jit(solution)/shard_map/ppermute | solution.py:34
  5.2 10.7 %collective-permute-start.1 = (bf16[5,128,256]{2,1,0:T(8,128)(2,1)S(1)}, bf16[5,128,256]{2,1,0:T(8,128)(2,1)S(1)}, u32[]{:S(2)}, u32[]{:S(2)}) collective-permute-start(bf16[5,128,256]{2,1,0:T(8,128)(2,1)S(1)} %packed.1.p0), channel_id=1, source_target_pairs={{0,2},{2,0},{1,3},{3,1},{4,6},{6,4},{5,7},{7,5},{8,10},{10,8},{9,1... | collective-permute-start | bytes 983048 | tf_op jit(solution)/shard_map/ppermute | solution.py:38
  7.6 31.6 %collective-permute-start.8 = (bf16[8,256,256]{2,1,0:T(8,128)(2,1)S(1)}, bf16[8,256,256]{2,1,0:T(8,128)(2,1)S(1)}, u32[]{:S(2)}, u32[]{:S(2)}) collective-permute-start(bf16[8,256,256]{2,1,0:T(8,128)(2,1)S(1)} %get-tuple-element.44), channel_id=1, source_target_pairs={{0,8},{1,65},{4,12},{5,69},{8,0},{9,73},{12,4},{13,77},{32,40},{33... | collective-permute-start | bytes 3145736 | tf_op jit(solution)/shard_map/ppermute | solution.py:34
  9.0 6.9 %collective-permute-start = (bf16[5,128,256]{2,1,0:T(8,128)(2,1)S(1)}, bf16[5,128,256]{2,1,0:T(8,128)(2,1)S(1)}, u32[]{:S(2)}, u32[]{:S(2)}) collective-permute-start(bf16[5,128,256]{2,1,0:T(8,128)(2,1)S(1)} %packed.1.p0), channel_id=1, source_target_pairs={{0,1},{1,0},{2,3},{3,2},{4,5},{5,4},{6,7},{7,6},{8,9},{9,8},{10,11... | collective-permute-start | bytes 983048 | tf_op jit(solution)/shard_map/ppermute | solution.py:38
  15.9 1.6 %collective-permute-start.2 = (bf16[5,128,256]{2,1,0:T(8,128)(2,1)S(1)}, bf16[5,128,256]{2,1,0:T(8,128)(2,1)S(1)}, u32[]{:S(2)}, u32[]{:S(2)}) collective-permute-start(bf16[5,128,256]{2,1,0:T(8,128)(2,1)S(1)} %collective-permute-done.1.p2), channel_id=1, source_target_pairs={{0,1},{1,0},{2,3},{3,2},{4,5},{5,4},{6,7},{7,6},{8,9},{9,8},{10,11... | collective-permute-start | bytes 983048 | tf_op jit(solution)/shard_map/ppermute | solution.py:38
  17.7 18.8 %collective-permute-start.6 = (bf16[2,256,256]{2,1,0:T(8,128)(2,1)S(1)}, bf16[2,256,256]{2,1,0:T(8,128)(2,1)S(1)}, u32[]{:S(2)}, u32[]{:S(2)}) collective-permute-start(bf16[2,256,256]{2,1,0:T(8,128)(2,1)S(1)} %get-tuple-element.36.g0), channel_id=1, source_target_pairs={{0,12},{1,97},{4,0},{5,101},{8,4},{9,105},{12,8},{13,109},{32,44},... | collective-permute-start | bytes 786440 | tf_op jit(solution)/shard_map/ppermute | solution.py:34
  18.6 19.2 %collective-permute-start.5 = (bf16[2,256,256]{2,1,0:T(8,128)(2,1)S(1)}, bf16[2,256,256]{2,1,0:T(8,128)(2,1)S(1)}, u32[]{:S(2)}, u32[]{:S(2)}) collective-permute-start(bf16[2,256,256]{2,1,0:T(8,128)(2,1)S(1)} %get-tuple-element.36.g0), channel_id=1, source_target_pairs={{0,8},{1,65},{4,12},{5,69},{8,0},{9,73},{12,4},{13,77},{32,40},{33... | collective-permute-start | bytes 786440 | tf_op jit(solution)/shard_map/ppermute | solution.py:34
  19.7 18.1 %collective-permute-start.4 = (bf16[2,256,256]{2,1,0:T(8,128)(2,1)S(1)}, bf16[2,256,256]{2,1,0:T(8,128)(2,1)S(1)}, u32[]{:S(2)}, u32[]{:S(2)}) collective-permute-start(bf16[2,256,256]{2,1,0:T(8,128)(2,1)S(1)} %get-tuple-element.36.g0), channel_id=1, source_target_pairs={{0,4},{1,33},{4,8},{5,37},{8,12},{9,41},{12,0},{13,45},{32,36},{33... | collective-permute-start | bytes 786440 | tf_op jit(solution)/shard_map/ppermute | solution.py:34
  37.9 8.3 %collective-permute-start.12 = (bf16[2,256,256]{2,1,0:T(8,128)(2,1)S(1)}, bf16[2,256,256]{2,1,0:T(8,128)(2,1)S(1)}, u32[]{:S(2)}, u32[]{:S(2)}) collective-permute-start(bf16[2,256,256]{2,1,0:T(8,128)(2,1)S(1)} %get-tuple-element.50), channel_id=1, source_target_pairs={{1,0},{3,2},{5,4},{7,6},{9,8},{11,10},{13,12},{15,14},{17,16},{19,... | collective-permute-start | bytes 786440 | tf_op jit(solution)/shard_map/ppermute | solution.py:361
  40.5 15.0 %collective-permute-start.9 = (bf16[512,512]{1,0:T(8,128)(2,1)S(1)}, bf16[512,512]{1,0:T(8,128)(2,1)S(1)}, u32[]{:S(2)}, u32[]{:S(2)}) collective-permute-start(bf16[512,512]{1,0:T(8,128)(2,1)S(1)} %get-tuple-element.46), channel_id=1, source_target_pairs={{0,32},{1,5},{4,36},{5,9},{8,40},{9,13},{12,44},{13,1},{32,64},{33... | collective-permute-start | bytes 1572872 | tf_op jit(solution)/shard_map/ppermute | solution.py:34
  42.5 15.7 %collective-permute-start.10 = (bf16[512,512]{1,0:T(8,128)(2,1)S(1)}, bf16[512,512]{1,0:T(8,128)(2,1)S(1)}, u32[]{:S(2)}, u32[]{:S(2)}) collective-permute-start(bf16[512,512]{1,0:T(8,128)(2,1)S(1)} %get-tuple-element.47), channel_id=1, source_target_pairs={{0,64},{1,9},{4,68},{5,13},{8,72},{9,1},{12,76},{13,5},{32,96},{33... | collective-permute-start | bytes 1572872 | tf_op jit(solution)/shard_map/ppermute | solution.py:34
  43.6 14.8 %collective-permute-start.11 = (bf16[512,512]{1,0:T(8,128)(2,1)S(1)}, bf16[512,512]{1,0:T(8,128)(2,1)S(1)}, u32[]{:S(2)}, u32[]{:S(2)}) collective-permute-start(bf16[512,512]{1,0:T(8,128)(2,1)S(1)} %get-tuple-element.48), channel_id=1, source_target_pairs={{0,96},{1,13},{4,100},{5,1},{8,104},{9,5},{12,108},{13,9},{32,0},{... | collective-permute-start | bytes 1572872 | tf_op jit(solution)/shard_map/ppermute | solution.py:34
  46.2 6.5 %collective-permute-start.13 = (bf16[2,256,256]{2,1,0:T(8,128)(2,1)S(1)}, bf16[2,256,256]{2,1,0:T(8,128)(2,1)S(1)}, u32[]{:S(2)}, u32[]{:S(2)}) collective-permute-start(bf16[2,256,256]{2,1,0:T(8,128)(2,1)S(1)} %picked.1.a_ref.seed), channel_id=1, source_target_pairs={{0,16},{16,0},{1,17},{17,1},{2,18},{18,2},{3,19},{19,3},{4,20},{20... | collective-permute-start | bytes 786440 | tf_op jit(solution)/shard_map/ppermute | solution.py:38
  53.5 15.1 %collective-permute-start.14 = (bf16[4,256,256]{2,1,0:T(8,128)(2,1)}, bf16[4,256,256]{2,1,0:T(8,128)(2,1)S(1)}, u32[]{:S(2)}, u32[]{:S(2)}) collective-permute-start(bf16[4,256,256]{2,1,0:T(8,128)(2,1)} %paired.1), channel_id=1, source_target_pairs={{0,4},{4,8},{8,12},{12,0},{1,5},{5,9},{9,13},{13,1},{2,6},{6,10},{... | collective-permute-start | bytes 1572872 | tf_op jit(solution)/shard_map/ppermute | solution.py:365
  55.0 16.2 %collective-permute-start.16 = (bf16[4,256,256]{2,1,0:T(8,128)(2,1)}, bf16[4,256,256]{2,1,0:T(8,128)(2,1)S(1)}, u32[]{:S(2)}, u32[]{:S(2)}) collective-permute-start(bf16[4,256,256]{2,1,0:T(8,128)(2,1)} %paired.1), channel_id=1, source_target_pairs={{0,12},{4,0},{8,4},{12,8},{1,13},{5,1},{9,5},{13,9},{2,14},{6,2},{... | collective-permute-start | bytes 1572872 | tf_op jit(solution)/shard_map/ppermute | solution.py:365
  55.5 25.3 %collective-permute-start.15 = (bf16[4,256,256]{2,1,0:T(8,128)(2,1)}, bf16[4,256,256]{2,1,0:T(8,128)(2,1)}, u32[]{:S(2)}, u32[]{:S(2)}) collective-permute-start(bf16[4,256,256]{2,1,0:T(8,128)(2,1)} %paired.1), channel_id=1, source_target_pairs={{0,8},{4,12},{8,0},{12,4},{1,9},{5,13},{9,1},{13,5},{2,10},{6,14},... | collective-permute-start | bytes 1572872 | tf_op jit(solution)/shard_map/ppermute | solution.py:365
  59.5 25.0 %all-to-all-start = ((bf16[8,128,256]{2,1,0:T(8,128)(2,1)}), bf16[8,128,256]{2,1,0:T(8,128)(2,1)S(1)}, u32[]{:S(2)}, u32[]{:S(2)}) async-start(bf16[8,128,256]{2,1,0:T(8,128)(2,1)} %summed.1), calls=%async_computation | async-start | bytes 1048576 | tf_op jit(solution)/shard_map/all_to_all | solution.py:369

commit v10 on v9

--- a/solution.py
+++ b/solution.py
@@ -273,20 +273,31 @@
     )(for_core_0, for_core_1)
 
 
-def paired_body(a_ref, b_ref, o_ref):
+def paired_body(a_ref, b_ref, o_ref, one_ref):
     o_ref[0:2] = a_ref[...]
     o_ref[2:4] = b_ref[...]
+    odd = lax.axis_index("z") & 1
+    one_ref[...] = o_ref[pl.ds(2 * odd, 2)]
 
 
 def paired(a, b):
     return pl.pallas_call(
         paired_body,
-        out_shape=VM((4, 256, 256), BF),
+        out_shape=[VM((4, 256, 256), BF), VM((2, 256, 256), BF)],
         in_specs=[IN] * 2,
-        out_specs=IN,
-        compiler_params=LIMIT,
+        out_specs=[IN] * 2,
+        compiler_params=LIMIT,
+        cost_estimate=pl.CostEstimate(flops=int(5e9), bytes_accessed=1 << 20, transcendentals=0),
         name="paired",
     )(*kept(a, b))
+
+
+def z_pairs(value):
+    pairs = []
+    for z in range(4):
+        pairs.append((z * 2, (z ^ 1) * 2))
+        pairs.append((z * 2 + 1, (z + 1 if z & 1 else z + 3) % 4 * 2 + 1))
+    return lax.ppermute(value, ("z", "c"), pairs)
 
 
 def outer_into(blocks, h_ref, o_ref, buf, sems):
@@ -308,16 +319,17 @@
         copy.wait()
 
 
-def first_half_body(h_ref, seed, other, up, *refs):
+def first_half_body(h_ref, seed, other, far, far_pair, *refs):
     yl = lax.axis_index("yl")
-    blocks = [(yl, 0, seed), (1 - yl, 0, other), (yl, 1, up.at[0:2]), (1 - yl, 1, up.at[2:4])]
+    here = yl ^ (lax.axis_index("z") & 1)
+    blocks = [(yl, 0, seed), (1 - yl, 0, other), (here, 2, far), (1 - here, 2, far_pair)]
     outer_into(blocks, h_ref, *refs)
 
 
-def second_half_body(o_in, h_ref, far, down, *refs):
+def second_half_body(o_in, h_ref, up, down, *refs):
     yl = lax.axis_index("yl")
     blocks = []
-    for k, ref in ((3, down), (2, far)):
+    for k, ref in ((1, up), (3, down)):
         blocks += [(yl, k, ref.at[0:2]), (1 - yl, k, ref.at[2:4])]
     outer_into(blocks, h_ref, *refs)
 
@@ -355,21 +367,23 @@
     keep, give = plane_blocks(*plane)
     acc, keep, give = lax.optimization_barrier((acc, keep, give))
     sums = partial_sums(acc, r1, r2, g1, g2)
+    seed = picked(lax.ppermute(give, "c", [(1, 0)]), keep)
+    sums, seed = lax.optimization_barrier((sums, seed))
+    other = swap(seed, "yl")
     parts = [sums[0]] + [None] * 3
     for k in (1, 3, 2):
         parts[k] = shift(sums[k], second_axis_steps(k))
-    seed = picked(lax.ppermute(give, "c", [(1, 0)]), keep)
-    other = swap(seed, "yl")
-    both = paired(seed, other)
-    up, far, down = [
-        lax.ppermute(both, "x", [(i, (i + k) % 4) for i in range(4)]) for k in (1, 2, 3)
-    ]
+    both, one = paired(seed, other)
+    along_x = lambda value, k: lax.ppermute(value, "x", [(i, (i + k) % 4) for i in range(4)])
+    far = along_x(one, 2)
+    up, down = along_x(both, 1), along_x(both, 3)
+    far_pair = z_pairs(far)
 
     blocks = summed_blocks(parts)
     blocks = lax.all_to_all(blocks, ("yl", "yh", "c"), 0, 0, tiled=True)
-    half = outer_half(first_half_body, "first_half", (h, seed, other, up))
-    grad_weight = outer_half(second_half_body, "second_half", (h, far, down), half)
-    blocks, grad_weight = lax.optimization_barrier((blocks, grad_weight))
+    half = outer_half(first_half_body, "first_half", (h, seed, other, far, far_pair))
+    blocks, half = lax.optimization_barrier((blocks, half))
+    grad_weight = outer_half(second_half_body, "second_half", (h, up, down), half)
     return finished(blocks), grad_weight
 
 

time: 85.6 us -> 85.4 us (level)
  the two profiles are of different devices: /device:TPU:46 before, /device:TPU:1 now
where the time goes in v10:
time: 85.4 us; the launch traced here: 84.5 us
  starting transfers between devices  42.4 us (50%)
  waiting for transfers between devices  27.8 us (33%)
  Pallas kernels  13.3 us (16%)
  between operations  0.92 us (1%)
    ppermute x9, starting transfers between devices, shift(): return lax.ppermute(value, ('z', 'x', 'c'), pairs)  22.5 us
    ppermute x9, waiting for transfers between devices, shift(): return lax.ppermute(value, ('z', 'x', 'c'), pairs)  14.8 us
    ppermute x4, waiting for transfers between devices, swap(): return lax.ppermute(value, axis, [(0, 1), (1, 0)])  9.02 us
    ppermute x4, starting transfers between devices, swap(): return lax.ppermute(value, axis, [(0, 1), (1, 0)])  6.07 us
    pallas_call x2, Pallas kernels, outer_half(): pl.pallas_call(body, out_shape=jax.ShapeDtypeStruct((2048, 4, 256), BF),...  5.24 us
    ppermute x1, waiting for transfers between devices, z_pairs(): return lax.ppermute(value, ('z', 'c'), pairs)  4.05 us
    all_to_all x1, starting transfers between devices, per_device(): blocks = lax.all_to_all(blocks, ('yl', 'yh', 'c'), 0, 0, tiled=True)  4.01 us
    ppermute x3, starting transfers between devices, per_device(): lax.ppermute(value, 'x', [(i, (i + k) % 4) for i in range(4)])  3.79 us
  transfers between devices with their start and end apart: 19, of which 8 were waited for; matrix products, arithmetic and copies ran while one was open for 0% of the time, Pallas kernels for 10%

profile of v10, /device:TPU:1, one launch (start us, length us, event | category | flops | bytes accessed | tf_op | source)
XLA Modules:
  0.0 84.5 jit_solution(17158336621073065637)
XLA Ops:
  0.7 2.4 %scale.1 = (bf16[8,256,256]{2,1,0:T(8,128)(2,1)S(1)}, bf16[8,256,256]{2,1,0:T(8,128)(2,1)S(1)}, bf16[8,256,256]{2,1,0:T(8,128)(2,1)S(1)}, bf16[8,256,256]{2,1,0:T(8,128)(2,1)S(1)}) custom-call(bf16[4,2,4,256,256]{4,3,2,1,0:T(8,128)(2,1)} %bitcast.2, bf16[16,512]{1,0:T(8,128)(2,1)} %bitcast.3), custom_call_target="tpu_custom_call" | custom-call | tf_op jit(solution)/shard_map/scale/pallas_call | solution.py:96
  3.1 2.5 %collective-permute-start.3 = (bf16[8,256,256]{2,1,0:T(8,128)(2,1)S(1)}, bf16[8,256,256]{2,1,0:T(8,128)(2,1)S(1)}, u32[]{:S(2)}, u32[]{:S(2)}) collective-permute-start(bf16[8,256,256]{2,1,0:T(8,128)(2,1)S(1)} %get-tuple-element.39), channel_id=1, source_target_pairs={{0,4},{1,33},{4,8},{5,37},{8,12},{9,41},{12,0},{13,45},{32,36},{33... | collective-permute-start | bytes 3145736 | tf_op jit(solution)/shard_map/ppermute | solution.py:34
  5.6 2.2 %collective-permute-start.7 = (bf16[8,256,256]{2,1,0:T(8,128)(2,1)S(1)}, bf16[8,256,256]{2,1,0:T(8,128)(2,1)S(1)}, u32[]{:S(2)}, u32[]{:S(2)}) collective-permute-start(bf16[8,256,256]{2,1,0:T(8,128)(2,1)S(1)} %get-tuple-element.41), channel_id=1, source_target_pairs={{0,12},{1,97},{4,0},{5,101},{8,4},{9,105},{12,8},{13,109},{32,44},... | collective-permute-start | bytes 3145736 | tf_op jit(solution)/shard_map/ppermute | solution.py:34
  7.8 0.1 packed.1.p0
  7.9 3.0 %collective-permute-start.1 = (bf16[5,128,256]{2,1,0:T(8,128)(2,1)S(1)}, bf16[5,128,256]{2,1,0:T(8,128)(2,1)S(1)}, u32[]{:S(2)}, u32[]{:S(2)}) collective-permute-start(bf16[5,128,256]{2,1,0:T(8,128)(2,1)S(1)} %packed.1.p0), channel_id=1, source_target_pairs={{0,2},{2,0},{1,3},{3,1},{4,6},{6,4},{5,7},{7,5},{8,10},{10,8},{9,1... | collective-permute-start | bytes 983048 | tf_op jit(solution)/shard_map/ppermute | solution.py:38
  10.9 1.2 %collective-permute-start.8 = (bf16[8,256,256]{2,1,0:T(8,128)(2,1)S(1)}, bf16[8,256,256]{2,1,0:T(8,128)(2,1)S(1)}, u32[]{:S(2)}, u32[]{:S(2)}) collective-permute-start(bf16[8,256,256]{2,1,0:T(8,128)(2,1)S(1)} %get-tuple-element.51), channel_id=1, source_target_pairs={{0,8},{1,65},{4,12},{5,69},{8,0},{9,73},{12,4},{13,77},{32,40},{33... | collective-permute-start | bytes 3145736 | tf_op jit(solution)/shard_map/ppermute | solution.py:34
  12.1 0.9 %collective-permute-start = (bf16[5,128,256]{2,1,0:T(8,128)(2,1)S(1)}, bf16[5,128,256]{2,1,0:T(8,128)(2,1)S(1)}, u32[]{:S(2)}, u32[]{:S(2)}) collective-permute-start(bf16[5,128,256]{2,1,0:T(8,128)(2,1)S(1)} %packed.1.p0), channel_id=1, source_target_pairs={{0,1},{1,0},{2,3},{3,2},{4,5},{5,4},{6,7},{7,6},{8,9},{9,8},{10,11... | collective-permute-start | bytes 983048 | tf_op jit(solution)/shard_map/ppermute | solution.py:38
  13.0 5.8 %collective-permute-done.1.p2 = bf16[5,128,256]{2,1,0:T(8,128)(2,1)S(1)} collective-permute-done((bf16[5,128,256]{2,1,0:T(8,128)(2,1)S(1)}, bf16[5,128,256]{2,1,0:T(8,128)(2,1)S(1)}, u32[]{:S(2)}, u32[]{:S(2)}) %collective-permute-start.1) | collective-permute-done | bytes 327712 | tf_op jit(solution)/shard_map/ppermute | solution.py:38
  18.8 0.8 collective-permute-start.2
  19.6 0.0 collective-permute-done.p1
  19.6 1.3 %collective-permute-done.2.p3 = bf16[5,128,256]{2,1,0:T(8,128)(2,1)S(1)} collective-permute-done((bf16[5,128,256]{2,1,0:T(8,128)(2,1)S(1)}, bf16[5,128,256]{2,1,0:T(8,128)(2,1)S(1)}, u32[]{:S(2)}, u32[]{:S(2)}) %collective-permute-start.2) | collective-permute-done | bytes 327712 | tf_op jit(solution)/shard_map/ppermute | solution.py:38
  20.9 0.1 tokens.1
  21.0 1.5 %collective-permute-start.6 = (bf16[2,256,256]{2,1,0:T(8,128)(2,1)S(1)}, bf16[2,256,256]{2,1,0:T(8,128)(2,1)S(1)}, u32[]{:S(2)}, u32[]{:S(2)}) collective-permute-start(bf16[2,256,256]{2,1,0:T(8,128)(2,1)S(1)} %get-tuple-element.43.g0), channel_id=1, source_target_pairs={{0,12},{1,97},{4,0},{5,101},{8,4},{9,105},{12,8},{13,109},{32,44},... | collective-permute-start | bytes 786440 | tf_op jit(solution)/shard_map/ppermute | solution.py:34
  22.4 0.0 collective-permute-start.5
  22.4 0.0 collective-permute-done.3.r1
  22.5 10.6 %collective-permute-start.4 = (bf16[2,256,256]{2,1,0:T(8,128)(2,1)S(1)}, bf16[2,256,256]{2,1,0:T(8,128)(2,1)S(1)}, u32[]{:S(2)}, u32[]{:S(2)}) collective-permute-start(bf16[2,256,256]{2,1,0:T(8,128)(2,1)S(1)} %get-tuple-element.43.g0), channel_id=1, source_target_pairs={{0,4},{1,33},{4,8},{5,37},{8,12},{9,41},{12,0},{13,45},{32,36},{33... | collective-permute-start | bytes 786440 | tf_op jit(solution)/shard_map/ppermute | solution.py:34
  33.0 3.4 %collective-permute-done.6.g3 = bf16[2,256,256]{2,1,0:T(8,128)(2,1)S(1)} collective-permute-done((bf16[2,256,256]{2,1,0:T(8,128)(2,1)S(1)}, bf16[2,256,256]{2,1,0:T(8,128)(2,1)S(1)}, u32[]{:S(2)}, u32[]{:S(2)}) %collective-permute-start.6) | collective-permute-done | bytes 262176 | tf_op jit(solution)/shard_map/ppermute | solution.py:34
  36.4 0.0 collective-permute-done.7.r3
  36.4 1.3 %early.1.acc = f32[4,512,512]{2,1,0:T(8,128)S(1)} custom-call(bf16[8,256,256]{2,1,0:T(8,128)(2,1)S(1)} %get-tuple-element.35.r0, bf16[8,256,256]{2,1,0:T(8,128)(2,1)S(1)} %collective-permute-done.7.r3, bf16[2,256,256]{2,1,0:T(8,128)(2,1)S(1)} %get-tuple-element.43.g0, bf16[2,256,256]{2,1,0:T(8,128)(2,1)S(1)} %collective-permute-done.6.g3), custom_call_target="tpu_custom_call" | custom-call | flops 2000000000 | bytes 6291456 | tf_op jit(solution)/shard_map/early/pallas_call | solution.py:163
  37.7 0.0 collective-permute-done.5.g2
  37.7 0.4 collective-permute-done.4.g1
  38.1 0.1 plane.1
  38.2 2.3 %collective-permute-start.9 = (bf16[2,256,256]{2,1,0:T(8,128)(2,1)S(1)}, bf16[2,256,256]{2,1,0:T(8,128)(2,1)S(1)}, u32[]{:S(2)}, u32[]{:S(2)}) collective-permute-start(bf16[2,256,256]{2,1,0:T(8,128)(2,1)S(1)} %get-tuple-element.56), channel_id=1, source_target_pairs={{1,0},{3,2},{5,4},{7,6},{9,8},{11,10},{13,12},{15,14},{17,16},{19,... | collective-permute-start | bytes 786440 | tf_op jit(solution)/shard_map/ppermute | solution.py:370
  40.5 0.0 collective-permute-done.8.r2
  40.5 1.3 %partial.1 = (f32[512,512]{1,0:T(8,128)S(1)}, bf16[512,512]{1,0:T(8,128)(2,1)S(1)}, bf16[512,512]{1,0:T(8,128)(2,1)S(1)}, bf16[512,512]{1,0:T(8,128)(2,1)S(1)}) custom-call(f32[4,512,512]{2,1,0:T(8,128)S(1)} %early.1.acc, bf16[8,256,256]{2,1,0:T(8,128)(2,1)S(1)} %collective-permute-done.3.r1, bf16[8,256,256]{2,1,0:T(8,128)(2,1)S(1)} %collective-permute-done.8.r2, ...), custom_call_target="tpu_custom_call" | custom-call | tf_op jit(solution)/shard_map/partial/pallas_call | solution.py:208
  41.8 0.0 collective-permute-done.9.a_ref
  41.9 1.4 %collective-permute-start.13 = (bf16[2,256,256]{2,1,0:T(8,128)(2,1)S(1)}, bf16[2,256,256]{2,1,0:T(8,128)(2,1)S(1)}, u32[]{:S(2)}, u32[]{:S(2)}) collective-permute-start(bf16[2,256,256]{2,1,0:T(8,128)(2,1)S(1)} %picked.1.a_ref.seed), channel_id=1, source_target_pairs={{0,16},{16,0},{1,17},{17,1},{2,18},{18,2},{3,19},{19,3},{4,20},{20... | collective-permute-start | bytes 786440 | tf_op jit(solution)/shard_map/ppermute | solution.py:38
  43.2 1.2 %collective-permute-start.10 = (bf16[512,512]{1,0:T(8,128)(2,1)S(1)}, bf16[512,512]{1,0:T(8,128)(2,1)S(1)}, u32[]{:S(2)}, u32[]{:S(2)}) collective-permute-start(bf16[512,512]{1,0:T(8,128)(2,1)S(1)} %get-tuple-element.59), channel_id=1, source_target_pairs={{0,32},{1,5},{4,36},{5,9},{8,40},{9,13},{12,44},{13,1},{32,64},{33... | collective-permute-start | bytes 1572872 | tf_op jit(solution)/shard_map/ppermute | solution.py:34
  44.4 3.3 %collective-permute-start.11 = (bf16[512,512]{1,0:T(8,128)(2,1)S(1)}, bf16[512,512]{1,0:T(8,128)(2,1)S(1)}, u32[]{:S(2)}, u32[]{:S(2)}) collective-permute-start(bf16[512,512]{1,0:T(8,128)(2,1)S(1)} %get-tuple-element.60), channel_id=1, source_target_pairs={{0,64},{1,9},{4,68},{5,13},{8,72},{9,1},{12,76},{13,5},{32,96},{33... | collective-permute-start | bytes 1572872 | tf_op jit(solution)/shard_map/ppermute | solution.py:34
  47.7 0.0 collective-permute-start.12
  47.7 2.0 %collective-permute-done.13.b_ref.other = bf16[2,256,256]{2,1,0:T(8,128)(2,1)S(1)} collective-permute-done((bf16[2,256,256]{2,1,0:T(8,128)(2,1)S(1)}, bf16[2,256,256]{2,1,0:T(8,128)(2,1)S(1)}, u32[]{:S(2)}, u32[]{:S(2)}) %collective-permute-start.13) | collective-permute-done | bytes 262176 | tf_op jit(solution)/shard_map/ppermute | solution.py:38
  49.7 0.9 %paired.1 = (bf16[4,256,256]{2,1,0:T(8,128)(2,1)}, bf16[2,256,256]{2,1,0:T(8,128)(2,1)}) custom-call(bf16[2,256,256]{2,1,0:T(8,128)(2,1)S(1)} %picked.1.a_ref.seed, bf16[2,256,256]{2,1,0:T(8,128)(2,1)S(1)} %collective-permute-done.13.b_ref.other), custom_call_target="tpu_custom_call" | custom-call | flops 5000000000 | bytes 1048576 | tf_op jit(solution)/shard_map/paired/pallas_call | solution.py:284
  50.6 1.6 %collective-permute-start.14 = (bf16[2,256,256]{2,1,0:T(8,128)(2,1)}, bf16[2,256,256]{2,1,0:T(8,128)(2,1)S(1)}, u32[]{:S(2)}, u32[]{:S(2)}) collective-permute-start(bf16[2,256,256]{2,1,0:T(8,128)(2,1)} %get-tuple-element.64), channel_id=1, source_target_pairs={{0,8},{4,12},{8,0},{12,4},{1,9},{5,13},{9,1},{13,5},{2,10},{6,14},... | collective-permute-start | bytes 786440 | tf_op jit(solution)/shard_map/ppermute | solution.py:377
  52.2 2.0 %collective-permute-start.17 = (bf16[4,256,256]{2,1,0:T(8,128)(2,1)}, bf16[4,256,256]{2,1,0:T(8,128)(2,1)S(1)}, u32[]{:S(2)}, u32[]{:S(2)}) collective-permute-start(bf16[4,256,256]{2,1,0:T(8,128)(2,1)} %get-tuple-element.67), channel_id=1, source_target_pairs={{0,12},{4,0},{8,4},{12,8},{1,13},{5,1},{9,5},{13,9},{2,14},{6,2},{... | collective-permute-start | bytes 1572872 | tf_op jit(solution)/shard_map/ppermute | solution.py:377
  54.2 0.0 collective-permute-done.10.b
  54.2 0.2 collective-permute-start.16
  54.4 9.2 %collective-permute-done.11.c = bf16[512,512]{1,0:T(8,128)(2,1)S(1)} collective-permute-done((bf16[512,512]{1,0:T(8,128)(2,1)S(1)}, bf16[512,512]{1,0:T(8,128)(2,1)S(1)}, u32[]{:S(2)}, u32[]{:S(2)}) %collective-permute-start.11) | collective-permute-done | bytes 524320 | tf_op jit(solution)/shard_map/ppermute | solution.py:34
  63.6 1.8 %collective-permute-done.12.d = bf16[512,512]{1,0:T(8,128)(2,1)S(1)} collective-permute-done((bf16[512,512]{1,0:T(8,128)(2,1)S(1)}, bf16[512,512]{1,0:T(8,128)(2,1)S(1)}, u32[]{:S(2)}, u32[]{:S(2)}) %collective-permute-start.12) | collective-permute-done | bytes 524320 | tf_op jit(solution)/shard_map/ppermute | solution.py:34
  65.4 1.0 %summed.1 = bf16[8,128,256]{2,1,0:T(8,128)(2,1)} custom-call(f32[512,512]{1,0:T(8,128)S(1)} %get-tuple-element.58.a, bf16[512,512]{1,0:T(8,128)(2,1)S(1)} %collective-permute-done.10.b, bf16[512,512]{1,0:T(8,128)(2,1)S(1)} %collective-permute-done.11.c, bf16[512,512]{1,0:T(8,128)(2,1)S(1)} %collective-permute-done.12.d), custom_call_target="tpu_custom_call" | custom-call | tf_op jit(solution)/shard_map/summed/pallas_call | solution.py:229
  66.4 4.0 %all-to-all-start = ((bf16[8,128,256]{2,1,0:T(8,128)(2,1)}), bf16[8,128,256]{2,1,0:T(8,128)(2,1)S(1)}, u32[]{:S(2)}, u32[]{:S(2)}) async-start(bf16[8,128,256]{2,1,0:T(8,128)(2,1)} %summed.1), calls=%async_computation | async-start | bytes 1048576 | tf_op jit(solution)/shard_map/all_to_all | solution.py:383
  70.4 0.0 collective-permute-done.14.far
  70.4 3.8 %collective-permute-start.15 = (bf16[2,256,256]{2,1,0:T(8,128)(2,1)S(1)}, bf16[2,256,256]{2,1,0:T(8,128)(2,1)S(1)}, u32[]{:S(2)}, u32[]{:S(2)}) collective-permute-start(bf16[2,256,256]{2,1,0:T(8,128)(2,1)S(1)} %collective-permute-done.14.far), channel_id=1, source_target_pairs={{0,32},{1,97},{32,0},{33,65},{64,96},{65,33},{96,64},{97,1},{2,34}... | collective-permute-start | bytes 786440 | tf_op jit(solution)/shard_map/ppermute | solution.py:300
  74.2 4.1 %collective-permute-done.15.far_pair = bf16[2,256,256]{2,1,0:T(8,128)(2,1)S(1)} collective-permute-done((bf16[2,256,256]{2,1,0:T(8,128)(2,1)S(1)}, bf16[2,256,256]{2,1,0:T(8,128)(2,1)S(1)}, u32[]{:S(2)}, u32[]{:S(2)}) %collective-permute-start.15) | collective-permute-done | bytes 262176 | tf_op jit(solution)/shard_map/ppermute | solution.py:300
  78.2 2.6 %first_half.1.o_in = bf16[2048,4,256]{2,1,0:T(4,128)(2,1)} custom-call(bf16[512,1024]{1,0:T(8,128)(2,1)S(1)} %get-tuple-element.62.h_ref, bf16[2,256,256]{2,1,0:T(8,128)(2,1)S(1)} %picked.1.a_ref.seed, bf16[2,256,256]{2,1,0:T(8,128)(2,1)S(1)} %collective-permute-done.13.b_ref.other, bf16[2,256,256]{2,1,0:T(8,128)(2,1)S(1)} %collective-permute-done.14.far, ...), custom_call_target="tpu_custom_call" | custom-call | flops 1000000 | bytes 1024 | tf_op jit(solution)/shard_map/first_half/pallas_call | solution.py:339
  80.9 0.0 all-to-all-done.r_ref
  80.9 0.9 %finish.1 = bf16[128,4,256]{2,1,0:T(4,128)(2,1)} custom-call(bf16[8,128,256]{2,1,0:T(8,128)(2,1)S(1)} %all-to-all-done.r_ref), custom_call_target="tpu_custom_call" | custom-call | tf_op jit(solution)/shard_map/finish/pallas_call | solution.py:245
  81.7 0.0 collective-permute-done.17.down
  81.7 2.6 %second_half.1 = bf16[2048,4,256]{2,1,0:T(4,128)(2,1)} custom-call(bf16[2048,4,256]{2,1,0:T(4,128)(2,1)} %first_half.1.o_in, bf16[512,1024]{1,0:T(8,128)(2,1)S(1)} %get-tuple-element.62.h_ref, bf16[4,256,256]{2,1,0:T(8,128)(2,1)S(1)} %collective-permute-done.16.up, bf16[4,256,256]{2,1,0:T(8,128)(2,1)S(1)} %collective-permute-done.17.down), custom_call_target="tpu_custom_call", output_to_operand_aliasing={{}: (0, {})} | custom-call | flops 1000000 | bytes 1024 | tf_op jit(solution)/shard_map/second_half/pallas_call | solution.py:339
  (6 shorter events, 0.0 us)
Async XLA Ops:
  0.6 7.2 %copy-start.1 = (bf16[128,256]{1,0:T(8,128)(2,1)S(1)}, bf16[128,256]{1,0:T(8,128)(2,1)}, u32[]{:S(2)}) copy-start(bf16[128,256]{1,0:T(8,128)(2,1)} %g_ref) | copy-start | bytes 196612
  0.6 7.2 %copy-start = (bf16[128,4,256]{2,1,0:T(4,128)(2,1)S(1)}, bf16[128,4,256]{2,1,0:T(4,128)(2,1)}, u32[]{:S(2)}) copy-start(bf16[128,4,256]{2,1,0:T(4,128)(2,1)} %h_ref) | copy-start | bytes 786436
  3.1 19.4 %collective-permute-start.3 = (bf16[8,256,256]{2,1,0:T(8,128)(2,1)S(1)}, bf16[8,256,256]{2,1,0:T(8,128)(2,1)S(1)}, u32[]{:S(2)}, u32[]{:S(2)}) collective-permute-start(bf16[8,256,256]{2,1,0:T(8,128)(2,1)S(1)} %get-tuple-element.39), channel_id=1, source_target_pairs={{0,4},{1,33},{4,8},{5,37},{8,12},{9,41},{12,0},{13,45},{32,36},{33... | collective-permute-start | bytes 3145736 | tf_op jit(solution)/shard_map/ppermute | solution.py:34
  5.6 30.8 %collective-permute-start.7 = (bf16[8,256,256]{2,1,0:T(8,128)(2,1)S(1)}, bf16[8,256,256]{2,1,0:T(8,128)(2,1)S(1)}, u32[]{:S(2)}, u32[]{:S(2)}) collective-permute-start(bf16[8,256,256]{2,1,0:T(8,128)(2,1)S(1)} %get-tuple-element.41), channel_id=1, source_target_pairs={{0,12},{1,97},{4,0},{5,101},{8,4},{9,105},{12,8},{13,109},{32,44},... | collective-permute-start | bytes 3145736 | tf_op jit(solution)/shard_map/ppermute | solution.py:34
  7.9 10.9 %collective-permute-start.1 = (bf16[5,128,256]{2,1,0:T(8,128)(2,1)S(1)}, bf16[5,128,256]{2,1,0:T(8,128)(2,1)S(1)}, u32[]{:S(2)}, u32[]{:S(2)}) collective-permute-start(bf16[5,128,256]{2,1,0:T(8,128)(2,1)S(1)} %packed.1.p0), channel_id=1, source_target_pairs={{0,2},{2,0},{1,3},{3,1},{4,6},{6,4},{5,7},{7,5},{8,10},{10,8},{9,1... | collective-permute-start | bytes 983048 | tf_op jit(solution)/shard_map/ppermute | solution.py:38
  10.9 29.6 %collective-permute-start.8 = (bf16[8,256,256]{2,1,0:T(8,128)(2,1)S(1)}, bf16[8,256,256]{2,1,0:T(8,128)(2,1)S(1)}, u32[]{:S(2)}, u32[]{:S(2)}) collective-permute-start(bf16[8,256,256]{2,1,0:T(8,128)(2,1)S(1)} %get-tuple-element.51), channel_id=1, source_target_pairs={{0,8},{1,65},{4,12},{5,69},{8,0},{9,73},{12,4},{13,77},{32,40},{33... | collective-permute-start | bytes 3145736 | tf_op jit(solution)/shard_map/ppermute | solution.py:34
  12.1 7.5 %collective-permute-start = (bf16[5,128,256]{2,1,0:T(8,128)(2,1)S(1)}, bf16[5,128,256]{2,1,0:T(8,128)(2,1)S(1)}, u32[]{:S(2)}, u32[]{:S(2)}) collective-permute-start(bf16[5,128,256]{2,1,0:T(8,128)(2,1)S(1)} %packed.1.p0), channel_id=1, source_target_pairs={{0,1},{1,0},{2,3},{3,2},{4,5},{5,4},{6,7},{7,6},{8,9},{9,8},{10,11... | collective-permute-start | bytes 983048 | tf_op jit(solution)/shard_map/ppermute | solution.py:38
  18.8 2.0 %collective-permute-start.2 = (bf16[5,128,256]{2,1,0:T(8,128)(2,1)S(1)}, bf16[5,128,256]{2,1,0:T(8,128)(2,1)S(1)}, u32[]{:S(2)}, u32[]{:S(2)}) collective-permute-start(bf16[5,128,256]{2,1,0:T(8,128)(2,1)S(1)} %collective-permute-done.1.p2), channel_id=1, source_target_pairs={{0,1},{1,0},{2,3},{3,2},{4,5},{5,4},{6,7},{7,6},{8,9},{9,8},{10,11... | collective-permute-start | bytes 983048 | tf_op jit(solution)/shard_map/ppermute | solution.py:38
  21.0 15.4 %collective-permute-start.6 = (bf16[2,256,256]{2,1,0:T(8,128)(2,1)S(1)}, bf16[2,256,256]{2,1,0:T(8,128)(2,1)S(1)}, u32[]{:S(2)}, u32[]{:S(2)}) collective-permute-start(bf16[2,256,256]{2,1,0:T(8,128)(2,1)S(1)} %get-tuple-element.43.g0), channel_id=1, source_target_pairs={{0,12},{1,97},{4,0},{5,101},{8,4},{9,105},{12,8},{13,109},{32,44},... | collective-permute-start | bytes 786440 | tf_op jit(solution)/shard_map/ppermute | solution.py:34
  22.4 15.3 %collective-permute-start.5 = (bf16[2,256,256]{2,1,0:T(8,128)(2,1)S(1)}, bf16[2,256,256]{2,1,0:T(8,128)(2,1)S(1)}, u32[]{:S(2)}, u32[]{:S(2)}) collective-permute-start(bf16[2,256,256]{2,1,0:T(8,128)(2,1)S(1)} %get-tuple-element.43.g0), channel_id=1, source_target_pairs={{0,8},{1,65},{4,12},{5,69},{8,0},{9,73},{12,4},{13,77},{32,40},{33... | collective-permute-start | bytes 786440 | tf_op jit(solution)/shard_map/ppermute | solution.py:34
  22.5 15.6 %collective-permute-start.4 = (bf16[2,256,256]{2,1,0:T(8,128)(2,1)S(1)}, bf16[2,256,256]{2,1,0:T(8,128)(2,1)S(1)}, u32[]{:S(2)}, u32[]{:S(2)}) collective-permute-start(bf16[2,256,256]{2,1,0:T(8,128)(2,1)S(1)} %get-tuple-element.43.g0), channel_id=1, source_target_pairs={{0,4},{1,33},{4,8},{5,37},{8,12},{9,41},{12,0},{13,45},{32,36},{33... | collective-permute-start | bytes 786440 | tf_op jit(solution)/shard_map/ppermute | solution.py:34
  38.2 3.6 %collective-permute-start.9 = (bf16[2,256,256]{2,1,0:T(8,128)(2,1)S(1)}, bf16[2,256,256]{2,1,0:T(8,128)(2,1)S(1)}, u32[]{:S(2)}, u32[]{:S(2)}) collective-permute-start(bf16[2,256,256]{2,1,0:T(8,128)(2,1)S(1)} %get-tuple-element.56), channel_id=1, source_target_pairs={{1,0},{3,2},{5,4},{7,6},{9,8},{11,10},{13,12},{15,14},{17,16},{19,... | collective-permute-start | bytes 786440 | tf_op jit(solution)/shard_map/ppermute | solution.py:370
  41.9 7.8 %collective-permute-start.13 = (bf16[2,256,256]{2,1,0:T(8,128)(2,1)S(1)}, bf16[2,256,256]{2,1,0:T(8,128)(2,1)S(1)}, u32[]{:S(2)}, u32[]{:S(2)}) collective-permute-start(bf16[2,256,256]{2,1,0:T(8,128)(2,1)S(1)} %picked.1.a_ref.seed), channel_id=1, source_target_pairs={{0,16},{16,0},{1,17},{17,1},{2,18},{18,2},{3,19},{19,3},{4,20},{20... | collective-permute-start | bytes 786440 | tf_op jit(solution)/shard_map/ppermute | solution.py:38
  43.2 11.0 %collective-permute-start.10 = (bf16[512,512]{1,0:T(8,128)(2,1)S(1)}, bf16[512,512]{1,0:T(8,128)(2,1)S(1)}, u32[]{:S(2)}, u32[]{:S(2)}) collective-permute-start(bf16[512,512]{1,0:T(8,128)(2,1)S(1)} %get-tuple-element.59), channel_id=1, source_target_pairs={{0,32},{1,5},{4,36},{5,9},{8,40},{9,13},{12,44},{13,1},{32,64},{33... | collective-permute-start | bytes 1572872 | tf_op jit(solution)/shard_map/ppermute | solution.py:34
  44.4 19.2 %collective-permute-start.11 = (bf16[512,512]{1,0:T(8,128)(2,1)S(1)}, bf16[512,512]{1,0:T(8,128)(2,1)S(1)}, u32[]{:S(2)}, u32[]{:S(2)}) collective-permute-start(bf16[512,512]{1,0:T(8,128)(2,1)S(1)} %get-tuple-element.60), channel_id=1, source_target_pairs={{0,64},{1,9},{4,68},{5,13},{8,72},{9,1},{12,76},{13,5},{32,96},{33... | collective-permute-start | bytes 1572872 | tf_op jit(solution)/shard_map/ppermute | solution.py:34
  47.7 17.7 %collective-permute-start.12 = (bf16[512,512]{1,0:T(8,128)(2,1)S(1)}, bf16[512,512]{1,0:T(8,128)(2,1)S(1)}, u32[]{:S(2)}, u32[]{:S(2)}) collective-permute-start(bf16[512,512]{1,0:T(8,128)(2,1)S(1)} %get-tuple-element.61), channel_id=1, source_target_pairs={{0,96},{1,13},{4,100},{5,1},{8,104},{9,5},{12,108},{13,9},{32,0},{... | collective-permute-start | bytes 1572872 | tf_op jit(solution)/shard_map/ppermute | solution.py:34
  50.6 19.8 %collective-permute-start.14 = (bf16[2,256,256]{2,1,0:T(8,128)(2,1)}, bf16[2,256,256]{2,1,0:T(8,128)(2,1)S(1)}, u32[]{:S(2)}, u32[]{:S(2)}) collective-permute-start(bf16[2,256,256]{2,1,0:T(8,128)(2,1)} %get-tuple-element.64), channel_id=1, source_target_pairs={{0,8},{4,12},{8,0},{12,4},{1,9},{5,13},{9,1},{13,5},{2,10},{6,14},... | collective-permute-start | bytes 786440 | tf_op jit(solution)/shard_map/ppermute | solution.py:377
  52.2 29.6 %collective-permute-start.17 = (bf16[4,256,256]{2,1,0:T(8,128)(2,1)}, bf16[4,256,256]{2,1,0:T(8,128)(2,1)S(1)}, u32[]{:S(2)}, u32[]{:S(2)}) collective-permute-start(bf16[4,256,256]{2,1,0:T(8,128)(2,1)} %get-tuple-element.67), channel_id=1, source_target_pairs={{0,12},{4,0},{8,4},{12,8},{1,13},{5,1},{9,5},{13,9},{2,14},{6,2},{... | collective-permute-start | bytes 1572872 | tf_op jit(solution)/shard_map/ppermute | solution.py:377
  54.2 27.6 %collective-permute-start.16 = (bf16[4,256,256]{2,1,0:T(8,128)(2,1)}, bf16[4,256,256]{2,1,0:T(8,128)(2,1)S(1)}, u32[]{:S(2)}, u32[]{:S(2)}) collective-permute-start(bf16[4,256,256]{2,1,0:T(8,128)(2,1)} %get-tuple-element.67), channel_id=1, source_target_pairs={{0,4},{4,8},{8,12},{12,0},{1,5},{5,9},{9,13},{13,1},{2,6},{6,10},{... | collective-permute-start | bytes 1572872 | tf_op jit(solution)/shard_map/ppermute | solution.py:377
  66.4 14.4 %all-to-all-start = ((bf16[8,128,256]{2,1,0:T(8,128)(2,1)}), bf16[8,128,256]{2,1,0:T(8,128)(2,1)S(1)}, u32[]{:S(2)}, u32[]{:S(2)}) async-start(bf16[8,128,256]{2,1,0:T(8,128)(2,1)} %summed.1), calls=%async_computation | async-start | bytes 1048576 | tf_op jit(solution)/shard_map/all_to_all | solution.py:383
  70.4 7.8 %collective-permute-start.15 = (bf16[2,256,256]{2,1,0:T(8,128)(2,1)S(1)}, bf16[2,256,256]{2,1,0:T(8,128)(2,1)S(1)}, u32[]{:S(2)}, u32[]{:S(2)}) collective-permute-start(bf16[2,256,256]{2,1,0:T(8,128)(2,1)S(1)} %collective-permute-done.14.far), channel_id=1, source_target_pairs={{0,32},{1,97},{32,0},{33,65},{64,96},{65,33},{96,64},{97,1},{2,34}... | collective-permute-start | bytes 786440 | tf_op jit(solution)/shard_map/ppermute | solution.py:300

commit v11 on v10

--- a/solution.py
+++ b/solution.py
@@ -334,7 +334,7 @@
     outer_into(blocks, h_ref, *refs)
 
 
-def outer_half(body, name, operands, so_far=None):
+def outer_half(body, name, operands, so_far=None, flops=int(1e6)):
     aliased = so_far is not None
     return pl.pallas_call(
         body,
@@ -344,7 +344,7 @@
         scratch_shapes=[VM((4, 256, 4, 256), BF), pltpu.SemaphoreType.DMA((4,))],
         input_output_aliases={0: 0} if aliased else {},
         compiler_params=LIMIT,
-        cost_estimate=pl.CostEstimate(flops=int(1e6), bytes_accessed=1 << 10, transcendentals=0),
+        cost_estimate=pl.CostEstimate(flops=flops, bytes_accessed=1 << 10, transcendentals=0),
         name=name,
     )(*([so_far] if aliased else []), *kept(*operands))
 
@@ -376,12 +376,13 @@
     both, one = paired(seed, other)
     along_x = lambda value, k: lax.ppermute(value, "x", [(i, (i + k) % 4) for i in range(4)])
     far = along_x(one, 2)
+    both, *parts = lax.optimization_barrier((both, *parts))
     up, down = along_x(both, 1), along_x(both, 3)
     far_pair = z_pairs(far)
 
     blocks = summed_blocks(parts)
     blocks = lax.all_to_all(blocks, ("yl", "yh", "c"), 0, 0, tiled=True)
-    half = outer_half(first_half_body, "first_half", (h, seed, other, far, far_pair))
+    half = outer_half(first_half_body, "first_half", (h, seed, other, far, far_pair), flops=int(4e9))
     blocks, half = lax.optimization_barrier((blocks, half))
     grad_weight = outer_half(second_half_body, "second_half", (h, up, down), half)
     return finished(blocks), grad_weight

time: 85.4 us -> 89.3 us (1.046)
  waiting for transfers between devices: 27.8 us -> 30.6 us
  local copies, waits for them, and re-layouts: 0.01 us -> 1.6 us
    ppermute x3, waiting for transfers between devices: 0.01 us -> 13.7 us  [per_device(): lax.ppermute(value, 'x', [(i, (i + k) % 4) for i in range(4)])]
    ppermute x9, waiting for transfers between devices: 14.8 us -> 3.78 us  [shift(): return lax.ppermute(value, ('z', 'x', 'c'), pairs)]
    all_to_all x1, waiting for transfers between devices: 0.01 us -> 4.12 us  [per_device(): blocks = lax.all_to_all(blocks, ('yl', 'yh', 'c'), 0, 0, tiled=True)]
    ppermute x1, waiting for transfers between devices: 4.05 us -> 0.01 us  [z_pairs(): return lax.ppermute(value, ('z', 'c'), pairs)]
    unnamed x4 -> x8, local copies, waits for them, and re-layouts: 0.01 us -> 1.6 us
    pallas_call x2, Pallas kernels: 5.24 us -> 6.28 us  [outer_half(): pl.pallas_call(body, out_shape=jax.ShapeDtypeStruct((2048, 4, 256), BF),...]
  transfers between devices with their start and end apart: 19 -> 19, of which waited for: 8 -> 7; matrix products, arithmetic and copies ran while one was open for 0% -> 0% of each run, Pallas kernels for 10% -> 9%
where the time goes in v11:
time: 89.3 us; the launch traced here: 89 us
  starting transfers between devices  42.4 us (47%)
  waiting for transfers between devices  30.6 us (34%)
  Pallas kernels  13.5 us (15%)
  local copies, waits for them, and re-layouts  1.6 us (2%)
  between operations  0.93 us (1%)
    ppermute x9, starting transfers between devices, shift(): return lax.ppermute(value, ('z', 'x', 'c'), pairs)  22.5 us
    ppermute x3, waiting for transfers between devices, per_device(): lax.ppermute(value, 'x', [(i, (i + k) % 4) for i in range(4)])  13.7 us
    ppermute x4, waiting for transfers between devices, swap(): return lax.ppermute(value, axis, [(0, 1), (1, 0)])  9.02 us
    pallas_call x2, Pallas kernels, outer_half(): pl.pallas_call(body, out_shape=jax.ShapeDtypeStruct((2048, 4, 256), BF),...  6.28 us
    ppermute x4, starting transfers between devices, swap(): return lax.ppermute(value, axis, [(0, 1), (1, 0)])  6.07 us
    all_to_all x1, starting transfers between devices, per_device(): blocks = lax.all_to_all(blocks, ('yl', 'yh', 'c'), 0, 0, tiled=True)  4.29 us
    all_to_all x1, waiting for transfers between devices, per_device(): blocks = lax.all_to_all(blocks, ('yl', 'yh', 'c'), 0, 0, tiled=True)  4.12 us
    ppermute x9, waiting for transfers between devices, shift(): return lax.ppermute(value, ('z', 'x', 'c'), pairs)  3.78 us
  transfers between devices with their start and end apart: 19, of which 7 were waited for; matrix products, arithmetic and copies ran while one was open for 0% of the time, Pallas kernels for 9%

profile of v11, /device:TPU:1, one launch (start us, length us, event | category | flops | bytes accessed | tf_op | source)
XLA Modules:
  0.0 89.0 jit_solution(13326780340543792873)
XLA Ops:
  0.7 2.4 %scale.1 = (bf16[8,256,256]{2,1,0:T(8,128)(2,1)S(1)}, bf16[8,256,256]{2,1,0:T(8,128)(2,1)S(1)}, bf16[8,256,256]{2,1,0:T(8,128)(2,1)S(1)}, bf16[8,256,256]{2,1,0:T(8,128)(2,1)S(1)}) custom-call(bf16[4,2,4,256,256]{4,3,2,1,0:T(8,128)(2,1)} %bitcast.2, bf16[16,512]{1,0:T(8,128)(2,1)} %bitcast.3), custom_call_target="tpu_custom_call" | custom-call | tf_op jit(solution)/shard_map/scale/pallas_call | solution.py:96
  3.1 2.5 %collective-permute-start.3 = (bf16[8,256,256]{2,1,0:T(8,128)(2,1)S(1)}, bf16[8,256,256]{2,1,0:T(8,128)(2,1)S(1)}, u32[]{:S(2)}, u32[]{:S(2)}) collective-permute-start(bf16[8,256,256]{2,1,0:T(8,128)(2,1)S(1)} %get-tuple-element.44), channel_id=1, source_target_pairs={{0,4},{1,33},{4,8},{5,37},{8,12},{9,41},{12,0},{13,45},{32,36},{33... | collective-permute-start | bytes 3145736 | tf_op jit(solution)/shard_map/ppermute | solution.py:34
  5.6 2.2 %collective-permute-start.7 = (bf16[8,256,256]{2,1,0:T(8,128)(2,1)S(1)}, bf16[8,256,256]{2,1,0:T(8,128)(2,1)S(1)}, u32[]{:S(2)}, u32[]{:S(2)}) collective-permute-start(bf16[8,256,256]{2,1,0:T(8,128)(2,1)S(1)} %get-tuple-element.46), channel_id=1, source_target_pairs={{0,12},{1,97},{4,0},{5,101},{8,4},{9,105},{12,8},{13,109},{32,44},... | collective-permute-start | bytes 3145736 | tf_op jit(solution)/shard_map/ppermute | solution.py:34
  7.8 0.1 packed.1.p0
  7.9 3.0 %collective-permute-start.1 = (bf16[5,128,256]{2,1,0:T(8,128)(2,1)S(1)}, bf16[5,128,256]{2,1,0:T(8,128)(2,1)S(1)}, u32[]{:S(2)}, u32[]{:S(2)}) collective-permute-start(bf16[5,128,256]{2,1,0:T(8,128)(2,1)S(1)} %packed.1.p0), channel_id=1, source_target_pairs={{0,2},{2,0},{1,3},{3,1},{4,6},{6,4},{5,7},{7,5},{8,10},{10,8},{9,1... | collective-permute-start | bytes 983048 | tf_op jit(solution)/shard_map/ppermute | solution.py:38
  10.9 1.2 %collective-permute-start.8 = (bf16[8,256,256]{2,1,0:T(8,128)(2,1)S(1)}, bf16[8,256,256]{2,1,0:T(8,128)(2,1)S(1)}, u32[]{:S(2)}, u32[]{:S(2)}) collective-permute-start(bf16[8,256,256]{2,1,0:T(8,128)(2,1)S(1)} %get-tuple-element.56), channel_id=1, source_target_pairs={{0,8},{1,65},{4,12},{5,69},{8,0},{9,73},{12,4},{13,77},{32,40},{33... | collective-permute-start | bytes 3145736 | tf_op jit(solution)/shard_map/ppermute | solution.py:34
  12.1 0.9 %collective-permute-start = (bf16[5,128,256]{2,1,0:T(8,128)(2,1)S(1)}, bf16[5,128,256]{2,1,0:T(8,128)(2,1)S(1)}, u32[]{:S(2)}, u32[]{:S(2)}) collective-permute-start(bf16[5,128,256]{2,1,0:T(8,128)(2,1)S(1)} %packed.1.p0), channel_id=1, source_target_pairs={{0,1},{1,0},{2,3},{3,2},{4,5},{5,4},{6,7},{7,6},{8,9},{9,8},{10,11... | collective-permute-start | bytes 983048 | tf_op jit(solution)/shard_map/ppermute | solution.py:38
  13.0 5.8 %collective-permute-done.1.p2 = bf16[5,128,256]{2,1,0:T(8,128)(2,1)S(1)} collective-permute-done((bf16[5,128,256]{2,1,0:T(8,128)(2,1)S(1)}, bf16[5,128,256]{2,1,0:T(8,128)(2,1)S(1)}, u32[]{:S(2)}, u32[]{:S(2)}) %collective-permute-start.1) | collective-permute-done | bytes 327712 | tf_op jit(solution)/shard_map/ppermute | solution.py:38
  18.8 0.8 collective-permute-start.2
  19.6 0.0 collective-permute-done.p1
  19.6 1.3 %collective-permute-done.2.p3 = bf16[5,128,256]{2,1,0:T(8,128)(2,1)S(1)} collective-permute-done((bf16[5,128,256]{2,1,0:T(8,128)(2,1)S(1)}, bf16[5,128,256]{2,1,0:T(8,128)(2,1)S(1)}, u32[]{:S(2)}, u32[]{:S(2)}) %collective-permute-start.2) | collective-permute-done | bytes 327712 | tf_op jit(solution)/shard_map/ppermute | solution.py:38
  20.9 0.1 tokens.1
  21.0 1.5 %collective-permute-start.6 = (bf16[2,256,256]{2,1,0:T(8,128)(2,1)S(1)}, bf16[2,256,256]{2,1,0:T(8,128)(2,1)S(1)}, u32[]{:S(2)}, u32[]{:S(2)}) collective-permute-start(bf16[2,256,256]{2,1,0:T(8,128)(2,1)S(1)} %get-tuple-element.48.g0), channel_id=1, source_target_pairs={{0,12},{1,97},{4,0},{5,101},{8,4},{9,105},{12,8},{13,109},{32,44},... | collective-permute-start | bytes 786440 | tf_op jit(solution)/shard_map/ppermute | solution.py:34
  22.4 0.0 collective-permute-start.5
  22.4 0.0 collective-permute-done.3.r1
  22.5 10.6 %collective-permute-start.4 = (bf16[2,256,256]{2,1,0:T(8,128)(2,1)S(1)}, bf16[2,256,256]{2,1,0:T(8,128)(2,1)S(1)}, u32[]{:S(2)}, u32[]{:S(2)}) collective-permute-start(bf16[2,256,256]{2,1,0:T(8,128)(2,1)S(1)} %get-tuple-element.48.g0), channel_id=1, source_target_pairs={{0,4},{1,33},{4,8},{5,37},{8,12},{9,41},{12,0},{13,45},{32,36},{33... | collective-permute-start | bytes 786440 | tf_op jit(solution)/shard_map/ppermute | solution.py:34
  33.0 3.4 %collective-permute-done.6.g3 = bf16[2,256,256]{2,1,0:T(8,128)(2,1)S(1)} collective-permute-done((bf16[2,256,256]{2,1,0:T(8,128)(2,1)S(1)}, bf16[2,256,256]{2,1,0:T(8,128)(2,1)S(1)}, u32[]{:S(2)}, u32[]{:S(2)}) %collective-permute-start.6) | collective-permute-done | bytes 262176 | tf_op jit(solution)/shard_map/ppermute | solution.py:34
  36.4 0.0 collective-permute-done.7.r3
  36.4 1.3 %early.1.acc = f32[4,512,512]{2,1,0:T(8,128)S(1)} custom-call(bf16[8,256,256]{2,1,0:T(8,128)(2,1)S(1)} %get-tuple-element.40.r0, bf16[8,256,256]{2,1,0:T(8,128)(2,1)S(1)} %collective-permute-done.7.r3, bf16[2,256,256]{2,1,0:T(8,128)(2,1)S(1)} %get-tuple-element.48.g0, bf16[2,256,256]{2,1,0:T(8,128)(2,1)S(1)} %collective-permute-done.6.g3), custom_call_target="tpu_custom_call" | custom-call | flops 2000000000 | bytes 6291456 | tf_op jit(solution)/shard_map/early/pallas_call | solution.py:163
  37.7 0.0 collective-permute-done.5.g2
  37.7 0.4 collective-permute-done.4.g1
  38.1 0.1 plane.1
  38.2 2.3 %collective-permute-start.9 = (bf16[2,256,256]{2,1,0:T(8,128)(2,1)S(1)}, bf16[2,256,256]{2,1,0:T(8,128)(2,1)S(1)}, u32[]{:S(2)}, u32[]{:S(2)}) collective-permute-start(bf16[2,256,256]{2,1,0:T(8,128)(2,1)S(1)} %get-tuple-element.61), channel_id=1, source_target_pairs={{1,0},{3,2},{5,4},{7,6},{9,8},{11,10},{13,12},{15,14},{17,16},{19,... | collective-permute-start | bytes 786440 | tf_op jit(solution)/shard_map/ppermute | solution.py:370
  40.5 0.0 collective-permute-done.8.r2
  40.5 1.3 %partial.1 = (f32[512,512]{1,0:T(8,128)S(1)}, bf16[512,512]{1,0:T(8,128)(2,1)S(1)}, bf16[512,512]{1,0:T(8,128)(2,1)S(1)}, bf16[512,512]{1,0:T(8,128)(2,1)S(1)}) custom-call(f32[4,512,512]{2,1,0:T(8,128)S(1)} %early.1.acc, bf16[8,256,256]{2,1,0:T(8,128)(2,1)S(1)} %collective-permute-done.3.r1, bf16[8,256,256]{2,1,0:T(8,128)(2,1)S(1)} %collective-permute-done.8.r2, ...), custom_call_target="tpu_custom_call" | custom-call | tf_op jit(solution)/shard_map/partial/pallas_call | solution.py:208
  41.8 0.0 collective-permute-done.9.a_ref
  41.9 1.4 %collective-permute-start.10 = (bf16[2,256,256]{2,1,0:T(8,128)(2,1)S(1)}, bf16[2,256,256]{2,1,0:T(8,128)(2,1)S(1)}, u32[]{:S(2)}, u32[]{:S(2)}) collective-permute-start(bf16[2,256,256]{2,1,0:T(8,128)(2,1)S(1)} %picked.1.a_ref.seed), channel_id=1, source_target_pairs={{0,16},{16,0},{1,17},{17,1},{2,18},{18,2},{3,19},{19,3},{4,20},{20... | collective-permute-start | bytes 786440 | tf_op jit(solution)/shard_map/ppermute | solution.py:38
  43.2 1.2 %collective-permute-start.11 = (bf16[512,512]{1,0:T(8,128)(2,1)S(1)}, bf16[512,512]{1,0:T(8,128)(2,1)S(1)}, u32[]{:S(2)}, u32[]{:S(2)}) collective-permute-start(bf16[512,512]{1,0:T(8,128)(2,1)S(1)} %get-tuple-element.66), channel_id=1, source_target_pairs={{0,32},{1,5},{4,36},{5,9},{8,40},{9,13},{12,44},{13,1},{32,64},{33... | collective-permute-start | bytes 1572872 | tf_op jit(solution)/shard_map/ppermute | solution.py:34
  44.4 3.3 %collective-permute-start.12 = (bf16[512,512]{1,0:T(8,128)(2,1)S(1)}, bf16[512,512]{1,0:T(8,128)(2,1)S(1)}, u32[]{:S(2)}, u32[]{:S(2)}) collective-permute-start(bf16[512,512]{1,0:T(8,128)(2,1)S(1)} %get-tuple-element.67), channel_id=1, source_target_pairs={{0,64},{1,9},{4,68},{5,13},{8,72},{9,1},{12,76},{13,5},{32,96},{33... | collective-permute-start | bytes 1572872 | tf_op jit(solution)/shard_map/ppermute | solution.py:34
  47.7 0.0 collective-permute-start.13
  47.7 2.0 %collective-permute-done.10.b_ref.other = bf16[2,256,256]{2,1,0:T(8,128)(2,1)S(1)} collective-permute-done((bf16[2,256,256]{2,1,0:T(8,128)(2,1)S(1)}, bf16[2,256,256]{2,1,0:T(8,128)(2,1)S(1)}, u32[]{:S(2)}, u32[]{:S(2)}) %collective-permute-start.10) | collective-permute-done | bytes 262176 | tf_op jit(solution)/shard_map/ppermute | solution.py:38
  49.7 0.1 paired.1
  49.8 0.6 copy-done.2
  50.4 1.6 %collective-permute-start.14 = (bf16[2,256,256]{2,1,0:T(8,128)(2,1)S(1)}, bf16[2,256,256]{2,1,0:T(8,128)(2,1)}, u32[]{:S(2)}, u32[]{:S(2)}) collective-permute-start(bf16[2,256,256]{2,1,0:T(8,128)(2,1)S(1)} %get-tuple-element.74), channel_id=1, source_target_pairs={{0,8},{4,12},{8,0},{12,4},{1,9},{5,13},{9,1},{13,5},{2,10},{6,14},... | collective-permute-start | bytes 786440 | tf_op jit(solution)/shard_map/ppermute | solution.py:377
  52.0 13.6 %collective-permute-done.14.far = bf16[2,256,256]{2,1,0:T(8,128)(2,1)} collective-permute-done((bf16[2,256,256]{2,1,0:T(8,128)(2,1)S(1)}, bf16[2,256,256]{2,1,0:T(8,128)(2,1)}, u32[]{:S(2)}, u32[]{:S(2)}) %collective-permute-start.14) | collective-permute-done | bytes 262176 | tf_op jit(solution)/shard_map/ppermute | solution.py:377
  65.6 3.8 %collective-permute-start.15 = (bf16[2,256,256]{2,1,0:T(8,128)(2,1)}, bf16[2,256,256]{2,1,0:T(8,128)(2,1)}, u32[]{:S(2)}, u32[]{:S(2)}) collective-permute-start(bf16[2,256,256]{2,1,0:T(8,128)(2,1)} %collective-permute-done.14.far), channel_id=1, source_target_pairs={{0,32},{1,97},{32,0},{33,65},{64,96},{65,33},{96,64},{97,1},{2,34}... | collective-permute-start | bytes 786440 | tf_op jit(solution)/shard_map/ppermute | solution.py:300
  69.4 0.0 collective-permute-done.11.b
  69.4 0.0 collective-permute-done.12.c
  69.4 0.0 collective-permute-done.13.d
  69.4 1.9 %collective-permute-start.17 = (bf16[4,256,256]{2,1,0:T(8,128)(2,1)S(1)}, bf16[4,256,256]{2,1,0:T(8,128)(2,1)S(1)}, u32[]{:S(2)}, u32[]{:S(2)}) collective-permute-start(bf16[4,256,256]{2,1,0:T(8,128)(2,1)S(1)} %get-tuple-element.77), channel_id=1, source_target_pairs={{0,12},{4,0},{8,4},{12,8},{1,13},{5,1},{9,5},{13,9},{2,14},{6,2},{... | collective-permute-start | bytes 1572872 | tf_op jit(solution)/shard_map/ppermute | solution.py:377
  71.3 1.0 %summed.1 = bf16[8,128,256]{2,1,0:T(8,128)(2,1)} custom-call(f32[512,512]{1,0:T(8,128)S(1)} %get-tuple-element.69.a, bf16[512,512]{1,0:T(8,128)(2,1)S(1)} %collective-permute-done.11.b, bf16[512,512]{1,0:T(8,128)(2,1)S(1)} %collective-permute-done.12.c, bf16[512,512]{1,0:T(8,128)(2,1)S(1)} %collective-permute-done.13.d), custom_call_target="tpu_custom_call" | custom-call | tf_op jit(solution)/shard_map/summed/pallas_call | solution.py:229
  72.3 4.3 %all-to-all-start = ((bf16[8,128,256]{2,1,0:T(8,128)(2,1)}), bf16[8,128,256]{2,1,0:T(8,128)(2,1)S(1)}, u32[]{:S(2)}, u32[]{:S(2)}) async-start(bf16[8,128,256]{2,1,0:T(8,128)(2,1)} %summed.1), calls=%async_computation | async-start | bytes 1048576 | tf_op jit(solution)/shard_map/all_to_all | solution.py:384
  76.6 0.0 collective-permute-done.15.far_pair
  76.6 0.9 %copy-done.3 = bf16[2,256,256]{2,1,0:T(8,128)(2,1)S(1)} copy-done((bf16[2,256,256]{2,1,0:T(8,128)(2,1)S(1)}, bf16[2,256,256]{2,1,0:T(8,128)(2,1)}, u32[]{:S(2)}) %copy-start.3) | copy-done | bytes 262168
  77.6 3.7 %first_half.1.o_in = bf16[2048,4,256]{2,1,0:T(4,128)(2,1)} custom-call(bf16[512,1024]{1,0:T(8,128)(2,1)S(1)} %get-tuple-element.73.h_ref, bf16[2,256,256]{2,1,0:T(8,128)(2,1)S(1)} %picked.1.a_ref.seed, bf16[2,256,256]{2,1,0:T(8,128)(2,1)S(1)} %copy-done.3, bf16[2,256,256]{2,1,0:T(8,128)(2,1)} %collective-permute-done.14.far, ...), custom_call_target="tpu_custom_call" | custom-call | flops 4000000000 | bytes 1024 | tf_op jit(solution)/shard_map/first_half/pallas_call | solution.py:339
  81.2 4.1 %all-to-all-done.r_ref = bf16[8,128,256]{2,1,0:T(8,128)(2,1)S(1)} async-done(((bf16[8,128,256]{2,1,0:T(8,128)(2,1)}), bf16[8,128,256]{2,1,0:T(8,128)(2,1)S(1)}, u32[]{:S(2)}, u32[]{:S(2)}) %all-to-all-start) | async-done | bytes 524320 | tf_op jit(solution)/shard_map/all_to_all | solution.py:384
  85.4 0.9 finish.1
  86.2 2.6 %second_half.1 = bf16[2048,4,256]{2,1,0:T(4,128)(2,1)} custom-call(bf16[2048,4,256]{2,1,0:T(4,128)(2,1)} %first_half.1.o_in, bf16[512,1024]{1,0:T(8,128)(2,1)S(1)} %get-tuple-element.73.h_ref, bf16[4,256,256]{2,1,0:T(8,128)(2,1)S(1)} %collective-permute-done.16.up, bf16[4,256,256]{2,1,0:T(8,128)(2,1)S(1)} %collective-permute-done.17.down), custom_call_target="tpu_custom_call", output_to_operand_aliasing={{}: (0, {})} | custom-call | flops 1000000 | bytes 1024 | tf_op jit(solution)/shard_map/second_half/pallas_call | solution.py:339
  (10 shorter events, 0.1 us)
Async XLA Ops:
  0.6 7.2 %copy-start.1 = (bf16[128,256]{1,0:T(8,128)(2,1)S(1)}, bf16[128,256]{1,0:T(8,128)(2,1)}, u32[]{:S(2)}) copy-start(bf16[128,256]{1,0:T(8,128)(2,1)} %g_ref) | copy-start | bytes 196612
  0.6 7.2 %copy-start = (bf16[128,4,256]{2,1,0:T(4,128)(2,1)S(1)}, bf16[128,4,256]{2,1,0:T(4,128)(2,1)}, u32[]{:S(2)}) copy-start(bf16[128,4,256]{2,1,0:T(4,128)(2,1)} %h_ref) | copy-start | bytes 786436
  3.1 19.4 %collective-permute-start.3 = (bf16[8,256,256]{2,1,0:T(8,128)(2,1)S(1)}, bf16[8,256,256]{2,1,0:T(8,128)(2,1)S(1)}, u32[]{:S(2)}, u32[]{:S(2)}) collective-permute-start(bf16[8,256,256]{2,1,0:T(8,128)(2,1)S(1)} %get-tuple-element.44), channel_id=1, source_target_pairs={{0,4},{1,33},{4,8},{5,37},{8,12},{9,41},{12,0},{13,45},{32,36},{33... | collective-permute-start | bytes 3145736 | tf_op jit(solution)/shard_map/ppermute | solution.py:34
  5.6 30.8 %collective-permute-start.7 = (bf16[8,256,256]{2,1,0:T(8,128)(2,1)S(1)}, bf16[8,256,256]{2,1,0:T(8,128)(2,1)S(1)}, u32[]{:S(2)}, u32[]{:S(2)}) collective-permute-start(bf16[8,256,256]{2,1,0:T(8,128)(2,1)S(1)} %get-tuple-element.46), channel_id=1, source_target_pairs={{0,12},{1,97},{4,0},{5,101},{8,4},{9,105},{12,8},{13,109},{32,44},... | collective-permute-start | bytes 3145736 | tf_op jit(solution)/shard_map/ppermute | solution.py:34
  7.9 10.9 %collective-permute-start.1 = (bf16[5,128,256]{2,1,0:T(8,128)(2,1)S(1)}, bf16[5,128,256]{2,1,0:T(8,128)(2,1)S(1)}, u32[]{:S(2)}, u32[]{:S(2)}) collective-permute-start(bf16[5,128,256]{2,1,0:T(8,128)(2,1)S(1)} %packed.1.p0), channel_id=1, source_target_pairs={{0,2},{2,0},{1,3},{3,1},{4,6},{6,4},{5,7},{7,5},{8,10},{10,8},{9,1... | collective-permute-start | bytes 983048 | tf_op jit(solution)/shard_map/ppermute | solution.py:38
  10.9 29.6 %collective-permute-start.8 = (bf16[8,256,256]{2,1,0:T(8,128)(2,1)S(1)}, bf16[8,256,256]{2,1,0:T(8,128)(2,1)S(1)}, u32[]{:S(2)}, u32[]{:S(2)}) collective-permute-start(bf16[8,256,256]{2,1,0:T(8,128)(2,1)S(1)} %get-tuple-element.56), channel_id=1, source_target_pairs={{0,8},{1,65},{4,12},{5,69},{8,0},{9,73},{12,4},{13,77},{32,40},{33... | collective-permute-start | bytes 3145736 | tf_op jit(solution)/shard_map/ppermute | solution.py:34
  12.1 7.5 %collective-permute-start = (bf16[5,128,256]{2,1,0:T(8,128)(2,1)S(1)}, bf16[5,128,256]{2,1,0:T(8,128)(2,1)S(1)}, u32[]{:S(2)}, u32[]{:S(2)}) collective-permute-start(bf16[5,128,256]{2,1,0:T(8,128)(2,1)S(1)} %packed.1.p0), channel_id=1, source_target_pairs={{0,1},{1,0},{2,3},{3,2},{4,5},{5,4},{6,7},{7,6},{8,9},{9,8},{10,11... | collective-permute-start | bytes 983048 | tf_op jit(solution)/shard_map/ppermute | solution.py:38
  18.8 2.0 %collective-permute-start.2 = (bf16[5,128,256]{2,1,0:T(8,128)(2,1)S(1)}, bf16[5,128,256]{2,1,0:T(8,128)(2,1)S(1)}, u32[]{:S(2)}, u32[]{:S(2)}) collective-permute-start(bf16[5,128,256]{2,1,0:T(8,128)(2,1)S(1)} %collective-permute-done.1.p2), channel_id=1, source_target_pairs={{0,1},{1,0},{2,3},{3,2},{4,5},{5,4},{6,7},{7,6},{8,9},{9,8},{10,11... | collective-permute-start | bytes 983048 | tf_op jit(solution)/shard_map/ppermute | solution.py:38
  21.0 15.4 %collective-permute-start.6 = (bf16[2,256,256]{2,1,0:T(8,128)(2,1)S(1)}, bf16[2,256,256]{2,1,0:T(8,128)(2,1)S(1)}, u32[]{:S(2)}, u32[]{:S(2)}) collective-permute-start(bf16[2,256,256]{2,1,0:T(8,128)(2,1)S(1)} %get-tuple-element.48.g0), channel_id=1, source_target_pairs={{0,12},{1,97},{4,0},{5,101},{8,4},{9,105},{12,8},{13,109},{32,44},... | collective-permute-start | bytes 786440 | tf_op jit(solution)/shard_map/ppermute | solution.py:34
  22.4 15.3 %collective-permute-start.5 = (bf16[2,256,256]{2,1,0:T(8,128)(2,1)S(1)}, bf16[2,256,256]{2,1,0:T(8,128)(2,1)S(1)}, u32[]{:S(2)}, u32[]{:S(2)}) collective-permute-start(bf16[2,256,256]{2,1,0:T(8,128)(2,1)S(1)} %get-tuple-element.48.g0), channel_id=1, source_target_pairs={{0,8},{1,65},{4,12},{5,69},{8,0},{9,73},{12,4},{13,77},{32,40},{33... | collective-permute-start | bytes 786440 | tf_op jit(solution)/shard_map/ppermute | solution.py:34
  22.5 15.6 %collective-permute-start.4 = (bf16[2,256,256]{2,1,0:T(8,128)(2,1)S(1)}, bf16[2,256,256]{2,1,0:T(8,128)(2,1)S(1)}, u32[]{:S(2)}, u32[]{:S(2)}) collective-permute-start(bf16[2,256,256]{2,1,0:T(8,128)(2,1)S(1)} %get-tuple-element.48.g0), channel_id=1, source_target_pairs={{0,4},{1,33},{4,8},{5,37},{8,12},{9,41},{12,0},{13,45},{32,36},{33... | collective-permute-start | bytes 786440 | tf_op jit(solution)/shard_map/ppermute | solution.py:34
  38.2 3.6 %collective-permute-start.9 = (bf16[2,256,256]{2,1,0:T(8,128)(2,1)S(1)}, bf16[2,256,256]{2,1,0:T(8,128)(2,1)S(1)}, u32[]{:S(2)}, u32[]{:S(2)}) collective-permute-start(bf16[2,256,256]{2,1,0:T(8,128)(2,1)S(1)} %get-tuple-element.61), channel_id=1, source_target_pairs={{1,0},{3,2},{5,4},{7,6},{9,8},{11,10},{13,12},{15,14},{17,16},{19,... | collective-permute-start | bytes 786440 | tf_op jit(solution)/shard_map/ppermute | solution.py:370
  41.9 7.8 %collective-permute-start.10 = (bf16[2,256,256]{2,1,0:T(8,128)(2,1)S(1)}, bf16[2,256,256]{2,1,0:T(8,128)(2,1)S(1)}, u32[]{:S(2)}, u32[]{:S(2)}) collective-permute-start(bf16[2,256,256]{2,1,0:T(8,128)(2,1)S(1)} %picked.1.a_ref.seed), channel_id=1, source_target_pairs={{0,16},{16,0},{1,17},{17,1},{2,18},{18,2},{3,19},{19,3},{4,20},{20... | collective-permute-start | bytes 786440 | tf_op jit(solution)/shard_map/ppermute | solution.py:38
  43.2 26.2 %collective-permute-start.11 = (bf16[512,512]{1,0:T(8,128)(2,1)S(1)}, bf16[512,512]{1,0:T(8,128)(2,1)S(1)}, u32[]{:S(2)}, u32[]{:S(2)}) collective-permute-start(bf16[512,512]{1,0:T(8,128)(2,1)S(1)} %get-tuple-element.66), channel_id=1, source_target_pairs={{0,32},{1,5},{4,36},{5,9},{8,40},{9,13},{12,44},{13,1},{32,64},{33... | collective-permute-start | bytes 1572872 | tf_op jit(solution)/shard_map/ppermute | solution.py:34
  44.4 25.0 %collective-permute-start.12 = (bf16[512,512]{1,0:T(8,128)(2,1)S(1)}, bf16[512,512]{1,0:T(8,128)(2,1)S(1)}, u32[]{:S(2)}, u32[]{:S(2)}) collective-permute-start(bf16[512,512]{1,0:T(8,128)(2,1)S(1)} %get-tuple-element.67), channel_id=1, source_target_pairs={{0,64},{1,9},{4,68},{5,13},{8,72},{9,1},{12,76},{13,5},{32,96},{33... | collective-permute-start | bytes 1572872 | tf_op jit(solution)/shard_map/ppermute | solution.py:34
  47.7 21.7 %collective-permute-start.13 = (bf16[512,512]{1,0:T(8,128)(2,1)S(1)}, bf16[512,512]{1,0:T(8,128)(2,1)S(1)}, u32[]{:S(2)}, u32[]{:S(2)}) collective-permute-start(bf16[512,512]{1,0:T(8,128)(2,1)S(1)} %get-tuple-element.68), channel_id=1, source_target_pairs={{0,96},{1,13},{4,100},{5,1},{8,104},{9,5},{12,108},{13,9},{32,0},{... | collective-permute-start | bytes 1572872 | tf_op jit(solution)/shard_map/ppermute | solution.py:34
  49.7 0.7 copy-start.2
  50.4 15.2 %collective-permute-start.14 = (bf16[2,256,256]{2,1,0:T(8,128)(2,1)S(1)}, bf16[2,256,256]{2,1,0:T(8,128)(2,1)}, u32[]{:S(2)}, u32[]{:S(2)}) collective-permute-start(bf16[2,256,256]{2,1,0:T(8,128)(2,1)S(1)} %get-tuple-element.74), channel_id=1, source_target_pairs={{0,8},{4,12},{8,0},{12,4},{1,9},{5,13},{9,1},{13,5},{2,10},{6,14},... | collective-permute-start | bytes 786440 | tf_op jit(solution)/shard_map/ppermute | solution.py:377
  65.6 11.0 %collective-permute-start.15 = (bf16[2,256,256]{2,1,0:T(8,128)(2,1)}, bf16[2,256,256]{2,1,0:T(8,128)(2,1)}, u32[]{:S(2)}, u32[]{:S(2)}) collective-permute-start(bf16[2,256,256]{2,1,0:T(8,128)(2,1)} %collective-permute-done.14.far), channel_id=1, source_target_pairs={{0,32},{1,97},{32,0},{33,65},{64,96},{65,33},{96,64},{97,1},{2,34}... | collective-permute-start | bytes 786440 | tf_op jit(solution)/shard_map/ppermute | solution.py:300
  69.4 16.8 %collective-permute-start.17 = (bf16[4,256,256]{2,1,0:T(8,128)(2,1)S(1)}, bf16[4,256,256]{2,1,0:T(8,128)(2,1)S(1)}, u32[]{:S(2)}, u32[]{:S(2)}) collective-permute-start(bf16[4,256,256]{2,1,0:T(8,128)(2,1)S(1)} %get-tuple-element.77), channel_id=1, source_target_pairs={{0,12},{4,0},{8,4},{12,8},{1,13},{5,1},{9,5},{13,9},{2,14},{6,2},{... | collective-permute-start | bytes 1572872 | tf_op jit(solution)/shard_map/ppermute | solution.py:377
  71.3 14.9 %collective-permute-start.16 = (bf16[4,256,256]{2,1,0:T(8,128)(2,1)S(1)}, bf16[4,256,256]{2,1,0:T(8,128)(2,1)S(1)}, u32[]{:S(2)}, u32[]{:S(2)}) collective-permute-start(bf16[4,256,256]{2,1,0:T(8,128)(2,1)S(1)} %get-tuple-element.77), channel_id=1, source_target_pairs={{0,4},{4,8},{8,12},{12,0},{1,5},{5,9},{9,13},{13,1},{2,6},{6,10},{... | collective-permute-start | bytes 1572872 | tf_op jit(solution)/shard_map/ppermute | solution.py:377
  72.3 13.0 %all-to-all-start = ((bf16[8,128,256]{2,1,0:T(8,128)(2,1)}), bf16[8,128,256]{2,1,0:T(8,128)(2,1)S(1)}, u32[]{:S(2)}, u32[]{:S(2)}) async-start(bf16[8,128,256]{2,1,0:T(8,128)(2,1)} %summed.1), calls=%async_computation | async-start | bytes 1048576 | tf_op jit(solution)/shard_map/all_to_all | solution.py:384
  76.6 1.0 %copy-start.3 = (bf16[2,256,256]{2,1,0:T(8,128)(2,1)S(1)}, bf16[2,256,256]{2,1,0:T(8,128)(2,1)}, u32[]{:S(2)}) copy-start(bf16[2,256,256]{2,1,0:T(8,128)(2,1)} %copy-done.2) | copy-start | bytes 786436

commit v12 on v10

--- a/solution.py
+++ b/solution.py
@@ -287,7 +287,6 @@
         in_specs=[IN] * 2,
         out_specs=[IN] * 2,
         compiler_params=LIMIT,
-        cost_estimate=pl.CostEstimate(flops=int(5e9), bytes_accessed=1 << 20, transcendentals=0),
         name="paired",
     )(*kept(a, b))
 
@@ -319,29 +318,28 @@
         copy.wait()
 
 
-def first_half_body(h_ref, seed, other, far, far_pair, *refs):
+def first_part_body(h_ref, seed, other, *refs):
+    yl = lax.axis_index("yl")
+    outer_into([(yl, 0, seed), (1 - yl, 0, other)], h_ref, *refs)
+
+
+def second_part_body(o_in, h_ref, up, down, far, far_pair, *refs):
     yl = lax.axis_index("yl")
     here = yl ^ (lax.axis_index("z") & 1)
-    blocks = [(yl, 0, seed), (1 - yl, 0, other), (here, 2, far), (1 - here, 2, far_pair)]
-    outer_into(blocks, h_ref, *refs)
-
-
-def second_half_body(o_in, h_ref, up, down, *refs):
-    yl = lax.axis_index("yl")
     blocks = []
     for k, ref in ((1, up), (3, down)):
         blocks += [(yl, k, ref.at[0:2]), (1 - yl, k, ref.at[2:4])]
-    outer_into(blocks, h_ref, *refs)
-
-
-def outer_half(body, name, operands, so_far=None):
+    outer_into(blocks + [(here, 2, far), (1 - here, 2, far_pair)], h_ref, *refs)
+
+
+def outer_part(body, name, operands, so_far=None):
     aliased = so_far is not None
     return pl.pallas_call(
         body,
         out_shape=jax.ShapeDtypeStruct((2048, 4, 256), BF),
         in_specs=[HBM] * aliased + [IN] * len(operands),
         out_specs=HBM,
-        scratch_shapes=[VM((4, 256, 4, 256), BF), pltpu.SemaphoreType.DMA((4,))],
+        scratch_shapes=[VM((6, 256, 4, 256), BF), pltpu.SemaphoreType.DMA((6,))],
         input_output_aliases={0: 0} if aliased else {},
         compiler_params=LIMIT,
         cost_estimate=pl.CostEstimate(flops=int(1e6), bytes_accessed=1 << 10, transcendentals=0),
@@ -368,7 +366,6 @@
     acc, keep, give = lax.optimization_barrier((acc, keep, give))
     sums = partial_sums(acc, r1, r2, g1, g2)
     seed = picked(lax.ppermute(give, "c", [(1, 0)]), keep)
-    sums, seed = lax.optimization_barrier((sums, seed))
     other = swap(seed, "yl")
     parts = [sums[0]] + [None] * 3
     for k in (1, 3, 2):
@@ -381,9 +378,9 @@
 
     blocks = summed_blocks(parts)
     blocks = lax.all_to_all(blocks, ("yl", "yh", "c"), 0, 0, tiled=True)
-    half = outer_half(first_half_body, "first_half", (h, seed, other, far, far_pair))
-    blocks, half = lax.optimization_barrier((blocks, half))
-    grad_weight = outer_half(second_half_body, "second_half", (h, up, down), half)
+    part = outer_part(first_part_body, "first_part", (h, seed, other))
+    blocks, part = lax.optimization_barrier((blocks, part))
+    grad_weight = outer_part(second_part_body, "second_part", (h, up, down, far, far_pair), part)
     return finished(blocks), grad_weight
 
 

time: 85.4 us -> 80.9 us (0.947)
  waiting for transfers between devices: 27.8 us -> 19.3 us
  starting transfers between devices: 42.4 us -> 45.7 us
  Pallas kernels: 13.3 us -> 14.3 us
    ppermute x9, waiting for transfers between devices: 14.8 us -> 4.77 us  [shift(): return lax.ppermute(value, ('z', 'x', 'c'), pairs)]
    ppermute x1, waiting for transfers between devices: 4.05 us -> 0.01 us  [z_pairs(): return lax.ppermute(value, ('z', 'c'), pairs)]
    ppermute x4, waiting for transfers between devices: 9.02 us -> 12 us  [swap(): return lax.ppermute(value, axis, [(0, 1), (1, 0)])]
    all_to_all x1, waiting for transfers between devices: 0.01 us -> 2.54 us  [per_device(): blocks = lax.all_to_all(blocks, ('yl', 'yh', 'c'), 0, 0, tiled=True)]
    all_to_all x1, starting transfers between devices: 4.01 us -> 6.25 us  [per_device(): blocks = lax.all_to_all(blocks, ('yl', 'yh', 'c'), 0, 0, tiled=True)]
    pallas_call x2, Pallas kernels: 5.24 us -> 6.24 us  [outer_part(): pl.pallas_call(body, out_shape=jax.ShapeDtypeStruct((2048, 4, 256), BF),...]
  transfers between devices with their start and end apart: 19 -> 19, of which waited for: 8 -> 7; matrix products, arithmetic and copies ran while one was open for 0% -> 0% of each run, Pallas kernels for 10% -> 9%
where the time goes in v12:
time: 80.9 us; the launch traced here: 80.2 us
  starting transfers between devices  45.7 us (56%)
  waiting for transfers between devices  19.3 us (24%)
  Pallas kernels  14.3 us (18%)
  between operations  0.91 us (1%)
    ppermute x9, starting transfers between devices, shift(): return lax.ppermute(value, ('z', 'x', 'c'), pairs)  22.5 us
    ppermute x4, waiting for transfers between devices, swap(): return lax.ppermute(value, axis, [(0, 1), (1, 0)])  12 us
    all_to_all x1, starting transfers between devices, per_device(): blocks = lax.all_to_all(blocks, ('yl', 'yh', 'c'), 0, 0, tiled=True)  6.25 us
    pallas_call x2, Pallas kernels, outer_part(): pl.pallas_call(body, out_shape=jax.ShapeDtypeStruct((2048, 4, 256), BF),...  6.24 us
    ppermute x4, starting transfers between devices, swap(): return lax.ppermute(value, axis, [(0, 1), (1, 0)])  6.16 us
    ppermute x9, waiting for transfers between devices, shift(): return lax.ppermute(value, ('z', 'x', 'c'), pairs)  4.77 us
    ppermute x1, starting transfers between devices, z_pairs(): return lax.ppermute(value, ('z', 'c'), pairs)  4.37 us
    ppermute x3, starting transfers between devices, per_device(): lax.ppermute(value, 'x', [(i, (i + k) % 4) for i in range(4)])  4.13 us
  transfers between devices with their start and end apart: 19, of which 7 were waited for; matrix products, arithmetic and copies ran while one was open for 0% of the time, Pallas kernels for 9%

profile of v12, /device:TPU:1, one launch (start us, length us, event | category | flops | bytes accessed | tf_op | source)
XLA Modules:
  0.0 80.2 jit_solution(2080463801164459148)
XLA Ops:
  0.7 2.4 %scale.1 = (bf16[8,256,256]{2,1,0:T(8,128)(2,1)S(1)}, bf16[8,256,256]{2,1,0:T(8,128)(2,1)S(1)}, bf16[8,256,256]{2,1,0:T(8,128)(2,1)S(1)}, bf16[8,256,256]{2,1,0:T(8,128)(2,1)S(1)}) custom-call(bf16[4,2,4,256,256]{4,3,2,1,0:T(8,128)(2,1)} %bitcast.2, bf16[16,512]{1,0:T(8,128)(2,1)} %bitcast.3), custom_call_target="tpu_custom_call" | custom-call | tf_op jit(solution)/shard_map/scale/pallas_call | solution.py:96
  3.1 2.5 %collective-permute-start.3 = (bf16[8,256,256]{2,1,0:T(8,128)(2,1)S(1)}, bf16[8,256,256]{2,1,0:T(8,128)(2,1)S(1)}, u32[]{:S(2)}, u32[]{:S(2)}) collective-permute-start(bf16[8,256,256]{2,1,0:T(8,128)(2,1)S(1)} %get-tuple-element.34), channel_id=1, source_target_pairs={{0,4},{1,33},{4,8},{5,37},{8,12},{9,41},{12,0},{13,45},{32,36},{33... | collective-permute-start | bytes 3145736 | tf_op jit(solution)/shard_map/ppermute | solution.py:34
  5.6 2.2 %collective-permute-start.7 = (bf16[8,256,256]{2,1,0:T(8,128)(2,1)S(1)}, bf16[8,256,256]{2,1,0:T(8,128)(2,1)S(1)}, u32[]{:S(2)}, u32[]{:S(2)}) collective-permute-start(bf16[8,256,256]{2,1,0:T(8,128)(2,1)S(1)} %get-tuple-element.36), channel_id=1, source_target_pairs={{0,12},{1,97},{4,0},{5,101},{8,4},{9,105},{12,8},{13,109},{32,44},... | collective-permute-start | bytes 3145736 | tf_op jit(solution)/shard_map/ppermute | solution.py:34
  7.8 0.1 packed.1.p0
  7.9 3.0 %collective-permute-start.1 = (bf16[5,128,256]{2,1,0:T(8,128)(2,1)S(1)}, bf16[5,128,256]{2,1,0:T(8,128)(2,1)S(1)}, u32[]{:S(2)}, u32[]{:S(2)}) collective-permute-start(bf16[5,128,256]{2,1,0:T(8,128)(2,1)S(1)} %packed.1.p0), channel_id=1, source_target_pairs={{0,2},{2,0},{1,3},{3,1},{4,6},{6,4},{5,7},{7,5},{8,10},{10,8},{9,1... | collective-permute-start | bytes 983048 | tf_op jit(solution)/shard_map/ppermute | solution.py:38
  10.9 1.2 %collective-permute-start.8 = (bf16[8,256,256]{2,1,0:T(8,128)(2,1)S(1)}, bf16[8,256,256]{2,1,0:T(8,128)(2,1)S(1)}, u32[]{:S(2)}, u32[]{:S(2)}) collective-permute-start(bf16[8,256,256]{2,1,0:T(8,128)(2,1)S(1)} %get-tuple-element.46), channel_id=1, source_target_pairs={{0,8},{1,65},{4,12},{5,69},{8,0},{9,73},{12,4},{13,77},{32,40},{33... | collective-permute-start | bytes 3145736 | tf_op jit(solution)/shard_map/ppermute | solution.py:34
  12.1 0.9 %collective-permute-start = (bf16[5,128,256]{2,1,0:T(8,128)(2,1)S(1)}, bf16[5,128,256]{2,1,0:T(8,128)(2,1)S(1)}, u32[]{:S(2)}, u32[]{:S(2)}) collective-permute-start(bf16[5,128,256]{2,1,0:T(8,128)(2,1)S(1)} %packed.1.p0), channel_id=1, source_target_pairs={{0,1},{1,0},{2,3},{3,2},{4,5},{5,4},{6,7},{7,6},{8,9},{9,8},{10,11... | collective-permute-start | bytes 983048 | tf_op jit(solution)/shard_map/ppermute | solution.py:38
  13.0 5.8 %collective-permute-done.1.p2 = bf16[5,128,256]{2,1,0:T(8,128)(2,1)S(1)} collective-permute-done((bf16[5,128,256]{2,1,0:T(8,128)(2,1)S(1)}, bf16[5,128,256]{2,1,0:T(8,128)(2,1)S(1)}, u32[]{:S(2)}, u32[]{:S(2)}) %collective-permute-start.1) | collective-permute-done | bytes 327712 | tf_op jit(solution)/shard_map/ppermute | solution.py:38
  18.8 0.8 collective-permute-start.2
  19.6 0.0 collective-permute-done.p1
  19.6 1.3 %collective-permute-done.2.p3 = bf16[5,128,256]{2,1,0:T(8,128)(2,1)S(1)} collective-permute-done((bf16[5,128,256]{2,1,0:T(8,128)(2,1)S(1)}, bf16[5,128,256]{2,1,0:T(8,128)(2,1)S(1)}, u32[]{:S(2)}, u32[]{:S(2)}) %collective-permute-start.2) | collective-permute-done | bytes 327712 | tf_op jit(solution)/shard_map/ppermute | solution.py:38
  20.9 0.1 tokens.1
  21.0 1.5 %collective-permute-start.6 = (bf16[2,256,256]{2,1,0:T(8,128)(2,1)S(1)}, bf16[2,256,256]{2,1,0:T(8,128)(2,1)S(1)}, u32[]{:S(2)}, u32[]{:S(2)}) collective-permute-start(bf16[2,256,256]{2,1,0:T(8,128)(2,1)S(1)} %get-tuple-element.38.g0), channel_id=1, source_target_pairs={{0,12},{1,97},{4,0},{5,101},{8,4},{9,105},{12,8},{13,109},{32,44},... | collective-permute-start | bytes 786440 | tf_op jit(solution)/shard_map/ppermute | solution.py:34
  22.4 0.0 collective-permute-start.5
  22.4 0.0 collective-permute-done.3.r1
  22.5 10.6 %collective-permute-start.4 = (bf16[2,256,256]{2,1,0:T(8,128)(2,1)S(1)}, bf16[2,256,256]{2,1,0:T(8,128)(2,1)S(1)}, u32[]{:S(2)}, u32[]{:S(2)}) collective-permute-start(bf16[2,256,256]{2,1,0:T(8,128)(2,1)S(1)} %get-tuple-element.38.g0), channel_id=1, source_target_pairs={{0,4},{1,33},{4,8},{5,37},{8,12},{9,41},{12,0},{13,45},{32,36},{33... | collective-permute-start | bytes 786440 | tf_op jit(solution)/shard_map/ppermute | solution.py:34
  33.0 3.4 %collective-permute-done.6.g3 = bf16[2,256,256]{2,1,0:T(8,128)(2,1)S(1)} collective-permute-done((bf16[2,256,256]{2,1,0:T(8,128)(2,1)S(1)}, bf16[2,256,256]{2,1,0:T(8,128)(2,1)S(1)}, u32[]{:S(2)}, u32[]{:S(2)}) %collective-permute-start.6) | collective-permute-done | bytes 262176 | tf_op jit(solution)/shard_map/ppermute | solution.py:34
  36.4 0.0 collective-permute-done.7.r3
  36.4 1.3 %early.1.acc = f32[4,512,512]{2,1,0:T(8,128)S(1)} custom-call(bf16[8,256,256]{2,1,0:T(8,128)(2,1)S(1)} %get-tuple-element.30.r0, bf16[8,256,256]{2,1,0:T(8,128)(2,1)S(1)} %collective-permute-done.7.r3, bf16[2,256,256]{2,1,0:T(8,128)(2,1)S(1)} %get-tuple-element.38.g0, bf16[2,256,256]{2,1,0:T(8,128)(2,1)S(1)} %collective-permute-done.6.g3), custom_call_target="tpu_custom_call" | custom-call | flops 2000000000 | bytes 6291456 | tf_op jit(solution)/shard_map/early/pallas_call | solution.py:163
  37.7 0.0 collective-permute-done.5.g2
  37.7 0.4 collective-permute-done.4.g1
  38.1 0.1 plane.1
  38.2 2.3 %collective-permute-start.12 = (bf16[2,256,256]{2,1,0:T(8,128)(2,1)S(1)}, bf16[2,256,256]{2,1,0:T(8,128)(2,1)S(1)}, u32[]{:S(2)}, u32[]{:S(2)}) collective-permute-start(bf16[2,256,256]{2,1,0:T(8,128)(2,1)S(1)} %get-tuple-element.52), channel_id=1, source_target_pairs={{1,0},{3,2},{5,4},{7,6},{9,8},{11,10},{13,12},{15,14},{17,16},{19,... | collective-permute-start | bytes 786440 | tf_op jit(solution)/shard_map/ppermute | solution.py:368
  40.5 0.0 collective-permute-done.8.r2
  40.5 1.3 %partial.1 = (f32[512,512]{1,0:T(8,128)S(1)}, bf16[512,512]{1,0:T(8,128)(2,1)S(1)}, bf16[512,512]{1,0:T(8,128)(2,1)S(1)}, bf16[512,512]{1,0:T(8,128)(2,1)S(1)}) custom-call(f32[4,512,512]{2,1,0:T(8,128)S(1)} %early.1.acc, bf16[8,256,256]{2,1,0:T(8,128)(2,1)S(1)} %collective-permute-done.3.r1, bf16[8,256,256]{2,1,0:T(8,128)(2,1)S(1)} %collective-permute-done.8.r2, ...), custom_call_target="tpu_custom_call" | custom-call | tf_op jit(solution)/shard_map/partial/pallas_call | solution.py:208
  41.8 1.3 %collective-permute-start.9 = (bf16[512,512]{1,0:T(8,128)(2,1)S(1)}, bf16[512,512]{1,0:T(8,128)(2,1)S(1)}, u32[]{:S(2)}, u32[]{:S(2)}) collective-permute-start(bf16[512,512]{1,0:T(8,128)(2,1)S(1)} %get-tuple-element.48), channel_id=1, source_target_pairs={{0,32},{1,5},{4,36},{5,9},{8,40},{9,13},{12,44},{13,1},{32,64},{33... | collective-permute-start | bytes 1572872 | tf_op jit(solution)/shard_map/ppermute | solution.py:34
  43.1 3.2 %collective-permute-start.10 = (bf16[512,512]{1,0:T(8,128)(2,1)S(1)}, bf16[512,512]{1,0:T(8,128)(2,1)S(1)}, u32[]{:S(2)}, u32[]{:S(2)}) collective-permute-start(bf16[512,512]{1,0:T(8,128)(2,1)S(1)} %get-tuple-element.49), channel_id=1, source_target_pairs={{0,64},{1,9},{4,68},{5,13},{8,72},{9,1},{12,76},{13,5},{32,96},{33... | collective-permute-start | bytes 1572872 | tf_op jit(solution)/shard_map/ppermute | solution.py:34
  46.3 0.0 collective-permute-start.11
  46.3 0.0 collective-permute-done.12.a_ref
  46.3 1.5 %collective-permute-start.13 = (bf16[2,256,256]{2,1,0:T(8,128)(2,1)S(1)}, bf16[2,256,256]{2,1,0:T(8,128)(2,1)S(1)}, u32[]{:S(2)}, u32[]{:S(2)}) collective-permute-start(bf16[2,256,256]{2,1,0:T(8,128)(2,1)S(1)} %picked.1.seed.a_ref), channel_id=1, source_target_pairs={{0,16},{16,0},{1,17},{17,1},{2,18},{18,2},{3,19},{19,3},{4,20},{20... | collective-permute-start | bytes 786440 | tf_op jit(solution)/shard_map/ppermute | solution.py:38
  47.8 4.9 %collective-permute-done.13.other.b_ref = bf16[2,256,256]{2,1,0:T(8,128)(2,1)S(1)} collective-permute-done((bf16[2,256,256]{2,1,0:T(8,128)(2,1)S(1)}, bf16[2,256,256]{2,1,0:T(8,128)(2,1)S(1)}, u32[]{:S(2)}, u32[]{:S(2)}) %collective-permute-start.13) | collective-permute-done | bytes 262176 | tf_op jit(solution)/shard_map/ppermute | solution.py:38
  52.7 0.9 %paired.1 = (bf16[4,256,256]{2,1,0:T(8,128)(2,1)}, bf16[2,256,256]{2,1,0:T(8,128)(2,1)}) custom-call(bf16[2,256,256]{2,1,0:T(8,128)(2,1)S(1)} %picked.1.seed.a_ref, bf16[2,256,256]{2,1,0:T(8,128)(2,1)S(1)} %collective-permute-done.13.other.b_ref), custom_call_target="tpu_custom_call" | custom-call | tf_op jit(solution)/shard_map/paired/pallas_call | solution.py:284
  53.6 2.0 %collective-permute-start.16 = (bf16[2,256,256]{2,1,0:T(8,128)(2,1)}, bf16[2,256,256]{2,1,0:T(8,128)(2,1)S(1)}, u32[]{:S(2)}, u32[]{:S(2)}) collective-permute-start(bf16[2,256,256]{2,1,0:T(8,128)(2,1)} %get-tuple-element.57), channel_id=1, source_target_pairs={{0,8},{4,12},{8,0},{12,4},{1,9},{5,13},{9,1},{13,5},{2,10},{6,14},... | collective-permute-start | bytes 786440 | tf_op jit(solution)/shard_map/ppermute | solution.py:374
  55.7 2.1 %collective-permute-start.15 = (bf16[4,256,256]{2,1,0:T(8,128)(2,1)}, bf16[4,256,256]{2,1,0:T(8,128)(2,1)S(1)}, u32[]{:S(2)}, u32[]{:S(2)}) collective-permute-start(bf16[4,256,256]{2,1,0:T(8,128)(2,1)} %get-tuple-element.56), channel_id=1, source_target_pairs={{0,12},{4,0},{8,4},{12,8},{1,13},{5,1},{9,5},{13,9},{2,14},{6,2},{... | collective-permute-start | bytes 1572872 | tf_op jit(solution)/shard_map/ppermute | solution.py:374
  57.8 0.0 collective-permute-done.9.b
  57.8 0.0 collective-permute-start.14
  57.8 1.0 %collective-permute-done.10.c = bf16[512,512]{1,0:T(8,128)(2,1)S(1)} collective-permute-done((bf16[512,512]{1,0:T(8,128)(2,1)S(1)}, bf16[512,512]{1,0:T(8,128)(2,1)S(1)}, u32[]{:S(2)}, u32[]{:S(2)}) %collective-permute-start.10) | collective-permute-done | bytes 524320 | tf_op jit(solution)/shard_map/ppermute | solution.py:34
  58.8 0.0 collective-permute-done.11.d
  58.8 1.0 %summed.1 = bf16[8,128,256]{2,1,0:T(8,128)(2,1)} custom-call(f32[512,512]{1,0:T(8,128)S(1)} %get-tuple-element.47.a, bf16[512,512]{1,0:T(8,128)(2,1)S(1)} %collective-permute-done.9.b, bf16[512,512]{1,0:T(8,128)(2,1)S(1)} %collective-permute-done.10.c, bf16[512,512]{1,0:T(8,128)(2,1)S(1)} %collective-permute-done.11.d), custom_call_target="tpu_custom_call" | custom-call | tf_op jit(solution)/shard_map/summed/pallas_call | solution.py:229
  59.8 6.3 %all-to-all-start = ((bf16[8,128,256]{2,1,0:T(8,128)(2,1)}), bf16[8,128,256]{2,1,0:T(8,128)(2,1)S(1)}, u32[]{:S(2)}, u32[]{:S(2)}) async-start(bf16[8,128,256]{2,1,0:T(8,128)(2,1)} %summed.1), calls=%async_computation | async-start | bytes 1048576 | tf_op jit(solution)/shard_map/all_to_all | solution.py:380
  66.0 4.4 %collective-permute-start.17 = (bf16[2,256,256]{2,1,0:T(8,128)(2,1)S(1)}, bf16[2,256,256]{2,1,0:T(8,128)(2,1)}, u32[]{:S(2)}, u32[]{:S(2)}) collective-permute-start(bf16[2,256,256]{2,1,0:T(8,128)(2,1)S(1)} %collective-permute-done.16.far), channel_id=1, source_target_pairs={{0,32},{1,97},{32,0},{33,65},{64,96},{65,33},{96,64},{97,1},{2,34}... | collective-permute-start | bytes 786440 | tf_op jit(solution)/shard_map/ppermute | solution.py:299
  70.4 1.8 %first_part.1.o_in = bf16[2048,4,256]{2,1,0:T(4,128)(2,1)} custom-call(bf16[512,1024]{1,0:T(8,128)(2,1)S(1)} %get-tuple-element.51.h_ref, bf16[2,256,256]{2,1,0:T(8,128)(2,1)S(1)} %picked.1.seed.a_ref, bf16[2,256,256]{2,1,0:T(8,128)(2,1)S(1)} %collective-permute-done.13.other.b_ref), custom_call_target="tpu_custom_call" | custom-call | flops 1000000 | bytes 1024 | tf_op jit(solution)/shard_map/first_part/pallas_call | solution.py:337
  72.2 2.5 %all-to-all-done.r_ref = bf16[8,128,256]{2,1,0:T(8,128)(2,1)S(1)} async-done(((bf16[8,128,256]{2,1,0:T(8,128)(2,1)}), bf16[8,128,256]{2,1,0:T(8,128)(2,1)S(1)}, u32[]{:S(2)}, u32[]{:S(2)}) %all-to-all-start) | async-done | bytes 524320 | tf_op jit(solution)/shard_map/all_to_all | solution.py:380
  74.8 0.9 %finish.1 = bf16[128,4,256]{2,1,0:T(4,128)(2,1)} custom-call(bf16[8,128,256]{2,1,0:T(8,128)(2,1)S(1)} %all-to-all-done.r_ref), custom_call_target="tpu_custom_call" | custom-call | tf_op jit(solution)/shard_map/finish/pallas_call | solution.py:245
  75.6 0.0 collective-permute-done.17.far_pair
  75.6 0.0 collective-permute-done.15.down
  75.6 0.0 collective-permute-done.14.up
  75.6 4.4 %second_part.1 = bf16[2048,4,256]{2,1,0:T(4,128)(2,1)} custom-call(bf16[2048,4,256]{2,1,0:T(4,128)(2,1)} %first_part.1.o_in, bf16[512,1024]{1,0:T(8,128)(2,1)S(1)} %get-tuple-element.51.h_ref, bf16[4,256,256]{2,1,0:T(8,128)(2,1)S(1)} %collective-permute-done.14.up, ...), custom_call_target="tpu_custom_call", output_to_operand_aliasing={{}: (0, {})} | custom-call | flops 1000000 | bytes 1024 | tf_op jit(solution)/shard_map/second_part/pallas_call | solution.py:337
  (6 shorter events, 0.0 us)
Async XLA Ops:
  0.6 7.2 %copy-start.1 = (bf16[128,256]{1,0:T(8,128)(2,1)S(1)}, bf16[128,256]{1,0:T(8,128)(2,1)}, u32[]{:S(2)}) copy-start(bf16[128,256]{1,0:T(8,128)(2,1)} %g_ref) | copy-start | bytes 196612
  0.6 7.2 %copy-start = (bf16[128,4,256]{2,1,0:T(4,128)(2,1)S(1)}, bf16[128,4,256]{2,1,0:T(4,128)(2,1)}, u32[]{:S(2)}) copy-start(bf16[128,4,256]{2,1,0:T(4,128)(2,1)} %h_ref) | copy-start | bytes 786436
  3.1 19.4 %collective-permute-start.3 = (bf16[8,256,256]{2,1,0:T(8,128)(2,1)S(1)}, bf16[8,256,256]{2,1,0:T(8,128)(2,1)S(1)}, u32[]{:S(2)}, u32[]{:S(2)}) collective-permute-start(bf16[8,256,256]{2,1,0:T(8,128)(2,1)S(1)} %get-tuple-element.34), channel_id=1, source_target_pairs={{0,4},{1,33},{4,8},{5,37},{8,12},{9,41},{12,0},{13,45},{32,36},{33... | collective-permute-start | bytes 3145736 | tf_op jit(solution)/shard_map/ppermute | solution.py:34
  5.6 30.8 %collective-permute-start.7 = (bf16[8,256,256]{2,1,0:T(8,128)(2,1)S(1)}, bf16[8,256,256]{2,1,0:T(8,128)(2,1)S(1)}, u32[]{:S(2)}, u32[]{:S(2)}) collective-permute-start(bf16[8,256,256]{2,1,0:T(8,128)(2,1)S(1)} %get-tuple-element.36), channel_id=1, source_target_pairs={{0,12},{1,97},{4,0},{5,101},{8,4},{9,105},{12,8},{13,109},{32,44},... | collective-permute-start | bytes 3145736 | tf_op jit(solution)/shard_map/ppermute | solution.py:34
  7.9 10.9 %collective-permute-start.1 = (bf16[5,128,256]{2,1,0:T(8,128)(2,1)S(1)}, bf16[5,128,256]{2,1,0:T(8,128)(2,1)S(1)}, u32[]{:S(2)}, u32[]{:S(2)}) collective-permute-start(bf16[5,128,256]{2,1,0:T(8,128)(2,1)S(1)} %packed.1.p0), channel_id=1, source_target_pairs={{0,2},{2,0},{1,3},{3,1},{4,6},{6,4},{5,7},{7,5},{8,10},{10,8},{9,1... | collective-permute-start | bytes 983048 | tf_op jit(solution)/shard_map/ppermute | solution.py:38
  10.9 29.6 %collective-permute-start.8 = (bf16[8,256,256]{2,1,0:T(8,128)(2,1)S(1)}, bf16[8,256,256]{2,1,0:T(8,128)(2,1)S(1)}, u32[]{:S(2)}, u32[]{:S(2)}) collective-permute-start(bf16[8,256,256]{2,1,0:T(8,128)(2,1)S(1)} %get-tuple-element.46), channel_id=1, source_target_pairs={{0,8},{1,65},{4,12},{5,69},{8,0},{9,73},{12,4},{13,77},{32,40},{33... | collective-permute-start | bytes 3145736 | tf_op jit(solution)/shard_map/ppermute | solution.py:34
  12.1 7.5 %collective-permute-start = (bf16[5,128,256]{2,1,0:T(8,128)(2,1)S(1)}, bf16[5,128,256]{2,1,0:T(8,128)(2,1)S(1)}, u32[]{:S(2)}, u32[]{:S(2)}) collective-permute-start(bf16[5,128,256]{2,1,0:T(8,128)(2,1)S(1)} %packed.1.p0), channel_id=1, source_target_pairs={{0,1},{1,0},{2,3},{3,2},{4,5},{5,4},{6,7},{7,6},{8,9},{9,8},{10,11... | collective-permute-start | bytes 983048 | tf_op jit(solution)/shard_map/ppermute | solution.py:38
  18.8 2.0 %collective-permute-start.2 = (bf16[5,128,256]{2,1,0:T(8,128)(2,1)S(1)}, bf16[5,128,256]{2,1,0:T(8,128)(2,1)S(1)}, u32[]{:S(2)}, u32[]{:S(2)}) collective-permute-start(bf16[5,128,256]{2,1,0:T(8,128)(2,1)S(1)} %collective-permute-done.1.p2), channel_id=1, source_target_pairs={{0,1},{1,0},{2,3},{3,2},{4,5},{5,4},{6,7},{7,6},{8,9},{9,8},{10,11... | collective-permute-start | bytes 983048 | tf_op jit(solution)/shard_map/ppermute | solution.py:38
  21.0 15.4 %collective-permute-start.6 = (bf16[2,256,256]{2,1,0:T(8,128)(2,1)S(1)}, bf16[2,256,256]{2,1,0:T(8,128)(2,1)S(1)}, u32[]{:S(2)}, u32[]{:S(2)}) collective-permute-start(bf16[2,256,256]{2,1,0:T(8,128)(2,1)S(1)} %get-tuple-element.38.g0), channel_id=1, source_target_pairs={{0,12},{1,97},{4,0},{5,101},{8,4},{9,105},{12,8},{13,109},{32,44},... | collective-permute-start | bytes 786440 | tf_op jit(solution)/shard_map/ppermute | solution.py:34
  22.4 15.3 %collective-permute-start.5 = (bf16[2,256,256]{2,1,0:T(8,128)(2,1)S(1)}, bf16[2,256,256]{2,1,0:T(8,128)(2,1)S(1)}, u32[]{:S(2)}, u32[]{:S(2)}) collective-permute-start(bf16[2,256,256]{2,1,0:T(8,128)(2,1)S(1)} %get-tuple-element.38.g0), channel_id=1, source_target_pairs={{0,8},{1,65},{4,12},{5,69},{8,0},{9,73},{12,4},{13,77},{32,40},{33... | collective-permute-start | bytes 786440 | tf_op jit(solution)/shard_map/ppermute | solution.py:34
  22.5 15.6 %collective-permute-start.4 = (bf16[2,256,256]{2,1,0:T(8,128)(2,1)S(1)}, bf16[2,256,256]{2,1,0:T(8,128)(2,1)S(1)}, u32[]{:S(2)}, u32[]{:S(2)}) collective-permute-start(bf16[2,256,256]{2,1,0:T(8,128)(2,1)S(1)} %get-tuple-element.38.g0), channel_id=1, source_target_pairs={{0,4},{1,33},{4,8},{5,37},{8,12},{9,41},{12,0},{13,45},{32,36},{33... | collective-permute-start | bytes 786440 | tf_op jit(solution)/shard_map/ppermute | solution.py:34
  38.2 8.1 %collective-permute-start.12 = (bf16[2,256,256]{2,1,0:T(8,128)(2,1)S(1)}, bf16[2,256,256]{2,1,0:T(8,128)(2,1)S(1)}, u32[]{:S(2)}, u32[]{:S(2)}) collective-permute-start(bf16[2,256,256]{2,1,0:T(8,128)(2,1)S(1)} %get-tuple-element.52), channel_id=1, source_target_pairs={{1,0},{3,2},{5,4},{7,6},{9,8},{11,10},{13,12},{15,14},{17,16},{19,... | collective-permute-start | bytes 786440 | tf_op jit(solution)/shard_map/ppermute | solution.py:368
  41.8 15.9 %collective-permute-start.9 = (bf16[512,512]{1,0:T(8,128)(2,1)S(1)}, bf16[512,512]{1,0:T(8,128)(2,1)S(1)}, u32[]{:S(2)}, u32[]{:S(2)}) collective-permute-start(bf16[512,512]{1,0:T(8,128)(2,1)S(1)} %get-tuple-element.48), channel_id=1, source_target_pairs={{0,32},{1,5},{4,36},{5,9},{8,40},{9,13},{12,44},{13,1},{32,64},{33... | collective-permute-start | bytes 1572872 | tf_op jit(solution)/shard_map/ppermute | solution.py:34
  43.1 15.7 %collective-permute-start.10 = (bf16[512,512]{1,0:T(8,128)(2,1)S(1)}, bf16[512,512]{1,0:T(8,128)(2,1)S(1)}, u32[]{:S(2)}, u32[]{:S(2)}) collective-permute-start(bf16[512,512]{1,0:T(8,128)(2,1)S(1)} %get-tuple-element.49), channel_id=1, source_target_pairs={{0,64},{1,9},{4,68},{5,13},{8,72},{9,1},{12,76},{13,5},{32,96},{33... | collective-permute-start | bytes 1572872 | tf_op jit(solution)/shard_map/ppermute | solution.py:34
  46.3 12.5 %collective-permute-start.11 = (bf16[512,512]{1,0:T(8,128)(2,1)S(1)}, bf16[512,512]{1,0:T(8,128)(2,1)S(1)}, u32[]{:S(2)}, u32[]{:S(2)}) collective-permute-start(bf16[512,512]{1,0:T(8,128)(2,1)S(1)} %get-tuple-element.50), channel_id=1, source_target_pairs={{0,96},{1,13},{4,100},{5,1},{8,104},{9,5},{12,108},{13,9},{32,0},{... | collective-permute-start | bytes 1572872 | tf_op jit(solution)/shard_map/ppermute | solution.py:34
  46.3 6.4 %collective-permute-start.13 = (bf16[2,256,256]{2,1,0:T(8,128)(2,1)S(1)}, bf16[2,256,256]{2,1,0:T(8,128)(2,1)S(1)}, u32[]{:S(2)}, u32[]{:S(2)}) collective-permute-start(bf16[2,256,256]{2,1,0:T(8,128)(2,1)S(1)} %picked.1.seed.a_ref), channel_id=1, source_target_pairs={{0,16},{16,0},{1,17},{17,1},{2,18},{18,2},{3,19},{19,3},{4,20},{20... | collective-permute-start | bytes 786440 | tf_op jit(solution)/shard_map/ppermute | solution.py:38
  53.6 12.4 %collective-permute-start.16 = (bf16[2,256,256]{2,1,0:T(8,128)(2,1)}, bf16[2,256,256]{2,1,0:T(8,128)(2,1)S(1)}, u32[]{:S(2)}, u32[]{:S(2)}) collective-permute-start(bf16[2,256,256]{2,1,0:T(8,128)(2,1)} %get-tuple-element.57), channel_id=1, source_target_pairs={{0,8},{4,12},{8,0},{12,4},{1,9},{5,13},{9,1},{13,5},{2,10},{6,14},... | collective-permute-start | bytes 786440 | tf_op jit(solution)/shard_map/ppermute | solution.py:374
  55.7 20.0 %collective-permute-start.15 = (bf16[4,256,256]{2,1,0:T(8,128)(2,1)}, bf16[4,256,256]{2,1,0:T(8,128)(2,1)S(1)}, u32[]{:S(2)}, u32[]{:S(2)}) collective-permute-start(bf16[4,256,256]{2,1,0:T(8,128)(2,1)} %get-tuple-element.56), channel_id=1, source_target_pairs={{0,12},{4,0},{8,4},{12,8},{1,13},{5,1},{9,5},{13,9},{2,14},{6,2},{... | collective-permute-start | bytes 1572872 | tf_op jit(solution)/shard_map/ppermute | solution.py:374
  57.8 17.9 %collective-permute-start.14 = (bf16[4,256,256]{2,1,0:T(8,128)(2,1)}, bf16[4,256,256]{2,1,0:T(8,128)(2,1)S(1)}, u32[]{:S(2)}, u32[]{:S(2)}) collective-permute-start(bf16[4,256,256]{2,1,0:T(8,128)(2,1)} %get-tuple-element.56), channel_id=1, source_target_pairs={{0,4},{4,8},{8,12},{12,0},{1,5},{5,9},{9,13},{13,1},{2,6},{6,10},{... | collective-permute-start | bytes 1572872 | tf_op jit(solution)/shard_map/ppermute | solution.py:374
  59.8 15.0 %all-to-all-start = ((bf16[8,128,256]{2,1,0:T(8,128)(2,1)}), bf16[8,128,256]{2,1,0:T(8,128)(2,1)S(1)}, u32[]{:S(2)}, u32[]{:S(2)}) async-start(bf16[8,128,256]{2,1,0:T(8,128)(2,1)} %summed.1), calls=%async_computation | async-start | bytes 1048576 | tf_op jit(solution)/shard_map/all_to_all | solution.py:380
  66.0 9.6 %collective-permute-start.17 = (bf16[2,256,256]{2,1,0:T(8,128)(2,1)S(1)}, bf16[2,256,256]{2,1,0:T(8,128)(2,1)}, u32[]{:S(2)}, u32[]{:S(2)}) collective-permute-start(bf16[2,256,256]{2,1,0:T(8,128)(2,1)S(1)} %collective-permute-done.16.far), channel_id=1, source_target_pairs={{0,32},{1,97},{32,0},{33,65},{64,96},{65,33},{96,64},{97,1},{2,34}... | collective-permute-start | bytes 786440 | tf_op jit(solution)/shard_map/ppermute | solution.py:299

commit v13 on v12

--- a/solution.py
+++ b/solution.py
@@ -323,13 +323,17 @@
     outer_into([(yl, 0, seed), (1 - yl, 0, other)], h_ref, *refs)
 
 
-def second_part_body(o_in, h_ref, up, down, far, far_pair, *refs):
+def second_part_body(o_in, h_ref, far, far_pair, *refs):
+    here = lax.axis_index("yl") ^ (lax.axis_index("z") & 1)
+    outer_into([(here, 2, far), (1 - here, 2, far_pair)], h_ref, *refs)
+
+
+def third_part_body(o_in, h_ref, up, down, *refs):
     yl = lax.axis_index("yl")
-    here = yl ^ (lax.axis_index("z") & 1)
     blocks = []
     for k, ref in ((1, up), (3, down)):
         blocks += [(yl, k, ref.at[0:2]), (1 - yl, k, ref.at[2:4])]
-    outer_into(blocks + [(here, 2, far), (1 - here, 2, far_pair)], h_ref, *refs)
+    outer_into(blocks, h_ref, *refs)
 
 
 def outer_part(body, name, operands, so_far=None):
@@ -339,7 +343,7 @@
         out_shape=jax.ShapeDtypeStruct((2048, 4, 256), BF),
         in_specs=[HBM] * aliased + [IN] * len(operands),
         out_specs=HBM,
-        scratch_shapes=[VM((6, 256, 4, 256), BF), pltpu.SemaphoreType.DMA((6,))],
+        scratch_shapes=[VM((4, 256, 4, 256), BF), pltpu.SemaphoreType.DMA((4,))],
         input_output_aliases={0: 0} if aliased else {},
         compiler_params=LIMIT,
         cost_estimate=pl.CostEstimate(flops=int(1e6), bytes_accessed=1 << 10, transcendentals=0),
@@ -379,8 +383,9 @@
     blocks = summed_blocks(parts)
     blocks = lax.all_to_all(blocks, ("yl", "yh", "c"), 0, 0, tiled=True)
     part = outer_part(first_part_body, "first_part", (h, seed, other))
+    part = outer_part(second_part_body, "second_part", (h, far, far_pair), part)
     blocks, part = lax.optimization_barrier((blocks, part))
-    grad_weight = outer_part(second_part_body, "second_part", (h, up, down, far, far_pair), part)
+    grad_weight = outer_part(third_part_body, "third_part", (h, up, down), part)
     return finished(blocks), grad_weight
 
 

time: 80.9 us -> 80.2 us (level)
  waiting for transfers between devices: 19.3 us -> 18.4 us
    all_to_all x1, waiting for transfers between devices: 2.54 us -> 0.01 us  [per_device(): blocks = lax.all_to_all(blocks, ('yl', 'yh', 'c'), 0, 0, tiled=True)]
    ppermute x1, waiting for transfers between devices: 0.01 us -> 2.25 us  [z_pairs(): return lax.ppermute(value, ('z', 'c'), pairs)]
    pallas_call x2 -> x3, Pallas kernels: 6.24 us -> 6.22 us  [outer_part(): pl.pallas_call(body, out_shape=jax.ShapeDtypeStruct((2048, 4, 256), BF),...]
  transfers between devices with their start and end apart: 19 -> 19, of which waited for: 7 -> 7; matrix products, arithmetic and copies ran while one was open for 0% -> 0% of each run, Pallas kernels for 9% -> 12%
where the time goes in v13:
time: 80.2 us; the launch traced here: 80 us
  starting transfers between devices  46.3 us (58%)
  waiting for transfers between devices  18.4 us (23%)
  Pallas kernels  14.3 us (18%)
  between operations  0.92 us (1%)
    ppermute x9, starting transfers between devices, shift(): return lax.ppermute(value, ('z', 'x', 'c'), pairs)  22.5 us
    ppermute x4, waiting for transfers between devices, swap(): return lax.ppermute(value, axis, [(0, 1), (1, 0)])  12 us
    all_to_all x1, starting transfers between devices, per_device(): blocks = lax.all_to_all(blocks, ('yl', 'yh', 'c'), 0, 0, tiled=True)  6.61 us
    pallas_call x3, Pallas kernels, outer_part(): pl.pallas_call(body, out_shape=jax.ShapeDtypeStruct((2048, 4, 256), BF),...  6.22 us
    ppermute x4, starting transfers between devices, swap(): return lax.ppermute(value, axis, [(0, 1), (1, 0)])  6.16 us
    ppermute x3, starting transfers between devices, per_device(): lax.ppermute(value, 'x', [(i, (i + k) % 4) for i in range(4)])  4.71 us
    ppermute x9, waiting for transfers between devices, shift(): return lax.ppermute(value, ('z', 'x', 'c'), pairs)  4.19 us
    ppermute x1, starting transfers between devices, z_pairs(): return lax.ppermute(value, ('z', 'c'), pairs)  4.05 us
  transfers between devices with their start and end apart: 19, of which 7 were waited for; matrix products, arithmetic and copies ran while one was open for 0% of the time, Pallas kernels for 12%

profile of v13, /device:TPU:1, one launch (start us, length us, event | category | flops | bytes accessed | tf_op | source)
XLA Modules:
  0.0 80.0 jit_solution(17745968240394226386)
XLA Ops:
  0.7 2.4 %scale.1 = (bf16[8,256,256]{2,1,0:T(8,128)(2,1)S(1)}, bf16[8,256,256]{2,1,0:T(8,128)(2,1)S(1)}, bf16[8,256,256]{2,1,0:T(8,128)(2,1)S(1)}, bf16[8,256,256]{2,1,0:T(8,128)(2,1)S(1)}) custom-call(bf16[4,2,4,256,256]{4,3,2,1,0:T(8,128)(2,1)} %bitcast.2, bf16[16,512]{1,0:T(8,128)(2,1)} %bitcast.3), custom_call_target="tpu_custom_call" | custom-call | tf_op jit(solution)/shard_map/scale/pallas_call | solution.py:96
  3.1 2.5 %collective-permute-start.3 = (bf16[8,256,256]{2,1,0:T(8,128)(2,1)S(1)}, bf16[8,256,256]{2,1,0:T(8,128)(2,1)S(1)}, u32[]{:S(2)}, u32[]{:S(2)}) collective-permute-start(bf16[8,256,256]{2,1,0:T(8,128)(2,1)S(1)} %get-tuple-element.34), channel_id=1, source_target_pairs={{0,4},{1,33},{4,8},{5,37},{8,12},{9,41},{12,0},{13,45},{32,36},{33... | collective-permute-start | bytes 3145736 | tf_op jit(solution)/shard_map/ppermute | solution.py:34
  5.6 2.2 %collective-permute-start.7 = (bf16[8,256,256]{2,1,0:T(8,128)(2,1)S(1)}, bf16[8,256,256]{2,1,0:T(8,128)(2,1)S(1)}, u32[]{:S(2)}, u32[]{:S(2)}) collective-permute-start(bf16[8,256,256]{2,1,0:T(8,128)(2,1)S(1)} %get-tuple-element.36), channel_id=1, source_target_pairs={{0,12},{1,97},{4,0},{5,101},{8,4},{9,105},{12,8},{13,109},{32,44},... | collective-permute-start | bytes 3145736 | tf_op jit(solution)/shard_map/ppermute | solution.py:34
  7.8 0.1 packed.1.p0
  7.9 3.0 %collective-permute-start.1 = (bf16[5,128,256]{2,1,0:T(8,128)(2,1)S(1)}, bf16[5,128,256]{2,1,0:T(8,128)(2,1)S(1)}, u32[]{:S(2)}, u32[]{:S(2)}) collective-permute-start(bf16[5,128,256]{2,1,0:T(8,128)(2,1)S(1)} %packed.1.p0), channel_id=1, source_target_pairs={{0,2},{2,0},{1,3},{3,1},{4,6},{6,4},{5,7},{7,5},{8,10},{10,8},{9,1... | collective-permute-start | bytes 983048 | tf_op jit(solution)/shard_map/ppermute | solution.py:38
  10.9 1.2 %collective-permute-start.8 = (bf16[8,256,256]{2,1,0:T(8,128)(2,1)S(1)}, bf16[8,256,256]{2,1,0:T(8,128)(2,1)S(1)}, u32[]{:S(2)}, u32[]{:S(2)}) collective-permute-start(bf16[8,256,256]{2,1,0:T(8,128)(2,1)S(1)} %get-tuple-element.46), channel_id=1, source_target_pairs={{0,8},{1,65},{4,12},{5,69},{8,0},{9,73},{12,4},{13,77},{32,40},{33... | collective-permute-start | bytes 3145736 | tf_op jit(solution)/shard_map/ppermute | solution.py:34
  12.1 0.9 %collective-permute-start = (bf16[5,128,256]{2,1,0:T(8,128)(2,1)S(1)}, bf16[5,128,256]{2,1,0:T(8,128)(2,1)S(1)}, u32[]{:S(2)}, u32[]{:S(2)}) collective-permute-start(bf16[5,128,256]{2,1,0:T(8,128)(2,1)S(1)} %packed.1.p0), channel_id=1, source_target_pairs={{0,1},{1,0},{2,3},{3,2},{4,5},{5,4},{6,7},{7,6},{8,9},{9,8},{10,11... | collective-permute-start | bytes 983048 | tf_op jit(solution)/shard_map/ppermute | solution.py:38
  13.0 5.8 %collective-permute-done.1.p2 = bf16[5,128,256]{2,1,0:T(8,128)(2,1)S(1)} collective-permute-done((bf16[5,128,256]{2,1,0:T(8,128)(2,1)S(1)}, bf16[5,128,256]{2,1,0:T(8,128)(2,1)S(1)}, u32[]{:S(2)}, u32[]{:S(2)}) %collective-permute-start.1) | collective-permute-done | bytes 327712 | tf_op jit(solution)/shard_map/ppermute | solution.py:38
  18.8 0.8 collective-permute-start.2
  19.6 0.0 collective-permute-done.p1
  19.6 1.3 %collective-permute-done.2.p3 = bf16[5,128,256]{2,1,0:T(8,128)(2,1)S(1)} collective-permute-done((bf16[5,128,256]{2,1,0:T(8,128)(2,1)S(1)}, bf16[5,128,256]{2,1,0:T(8,128)(2,1)S(1)}, u32[]{:S(2)}, u32[]{:S(2)}) %collective-permute-start.2) | collective-permute-done | bytes 327712 | tf_op jit(solution)/shard_map/ppermute | solution.py:38
  20.9 0.1 tokens.1
  21.0 1.5 %collective-permute-start.6 = (bf16[2,256,256]{2,1,0:T(8,128)(2,1)S(1)}, bf16[2,256,256]{2,1,0:T(8,128)(2,1)S(1)}, u32[]{:S(2)}, u32[]{:S(2)}) collective-permute-start(bf16[2,256,256]{2,1,0:T(8,128)(2,1)S(1)} %get-tuple-element.38.g0), channel_id=1, source_target_pairs={{0,12},{1,97},{4,0},{5,101},{8,4},{9,105},{12,8},{13,109},{32,44},... | collective-permute-start | bytes 786440 | tf_op jit(solution)/shard_map/ppermute | solution.py:34
  22.4 0.0 collective-permute-start.5
  22.4 0.0 collective-permute-done.3.r1
  22.5 10.6 %collective-permute-start.4 = (bf16[2,256,256]{2,1,0:T(8,128)(2,1)S(1)}, bf16[2,256,256]{2,1,0:T(8,128)(2,1)S(1)}, u32[]{:S(2)}, u32[]{:S(2)}) collective-permute-start(bf16[2,256,256]{2,1,0:T(8,128)(2,1)S(1)} %get-tuple-element.38.g0), channel_id=1, source_target_pairs={{0,4},{1,33},{4,8},{5,37},{8,12},{9,41},{12,0},{13,45},{32,36},{33... | collective-permute-start | bytes 786440 | tf_op jit(solution)/shard_map/ppermute | solution.py:34
  33.0 3.4 %collective-permute-done.6.g3 = bf16[2,256,256]{2,1,0:T(8,128)(2,1)S(1)} collective-permute-done((bf16[2,256,256]{2,1,0:T(8,128)(2,1)S(1)}, bf16[2,256,256]{2,1,0:T(8,128)(2,1)S(1)}, u32[]{:S(2)}, u32[]{:S(2)}) %collective-permute-start.6) | collective-permute-done | bytes 262176 | tf_op jit(solution)/shard_map/ppermute | solution.py:34
  36.4 0.0 collective-permute-done.7.r3
  36.4 1.3 %early.1.acc = f32[4,512,512]{2,1,0:T(8,128)S(1)} custom-call(bf16[8,256,256]{2,1,0:T(8,128)(2,1)S(1)} %get-tuple-element.30.r0, bf16[8,256,256]{2,1,0:T(8,128)(2,1)S(1)} %collective-permute-done.7.r3, bf16[2,256,256]{2,1,0:T(8,128)(2,1)S(1)} %get-tuple-element.38.g0, bf16[2,256,256]{2,1,0:T(8,128)(2,1)S(1)} %collective-permute-done.6.g3), custom_call_target="tpu_custom_call" | custom-call | flops 2000000000 | bytes 6291456 | tf_op jit(solution)/shard_map/early/pallas_call | solution.py:163
  37.7 0.0 collective-permute-done.5.g2
  37.7 0.4 collective-permute-done.4.g1
  38.1 0.1 plane.1
  38.2 2.3 %collective-permute-start.12 = (bf16[2,256,256]{2,1,0:T(8,128)(2,1)S(1)}, bf16[2,256,256]{2,1,0:T(8,128)(2,1)S(1)}, u32[]{:S(2)}, u32[]{:S(2)}) collective-permute-start(bf16[2,256,256]{2,1,0:T(8,128)(2,1)S(1)} %get-tuple-element.52), channel_id=1, source_target_pairs={{1,0},{3,2},{5,4},{7,6},{9,8},{11,10},{13,12},{15,14},{17,16},{19,... | collective-permute-start | bytes 786440 | tf_op jit(solution)/shard_map/ppermute | solution.py:372
  40.5 0.0 collective-permute-done.8.r2
  40.5 1.3 %partial.1 = (f32[512,512]{1,0:T(8,128)S(1)}, bf16[512,512]{1,0:T(8,128)(2,1)S(1)}, bf16[512,512]{1,0:T(8,128)(2,1)S(1)}, bf16[512,512]{1,0:T(8,128)(2,1)S(1)}) custom-call(f32[4,512,512]{2,1,0:T(8,128)S(1)} %early.1.acc, bf16[8,256,256]{2,1,0:T(8,128)(2,1)S(1)} %collective-permute-done.3.r1, bf16[8,256,256]{2,1,0:T(8,128)(2,1)S(1)} %collective-permute-done.8.r2, ...), custom_call_target="tpu_custom_call" | custom-call | tf_op jit(solution)/shard_map/partial/pallas_call | solution.py:208
  41.8 1.3 %collective-permute-start.9 = (bf16[512,512]{1,0:T(8,128)(2,1)S(1)}, bf16[512,512]{1,0:T(8,128)(2,1)S(1)}, u32[]{:S(2)}, u32[]{:S(2)}) collective-permute-start(bf16[512,512]{1,0:T(8,128)(2,1)S(1)} %get-tuple-element.48), channel_id=1, source_target_pairs={{0,32},{1,5},{4,36},{5,9},{8,40},{9,13},{12,44},{13,1},{32,64},{33... | collective-permute-start | bytes 1572872 | tf_op jit(solution)/shard_map/ppermute | solution.py:34
  43.1 3.2 %collective-permute-start.10 = (bf16[512,512]{1,0:T(8,128)(2,1)S(1)}, bf16[512,512]{1,0:T(8,128)(2,1)S(1)}, u32[]{:S(2)}, u32[]{:S(2)}) collective-permute-start(bf16[512,512]{1,0:T(8,128)(2,1)S(1)} %get-tuple-element.49), channel_id=1, source_target_pairs={{0,64},{1,9},{4,68},{5,13},{8,72},{9,1},{12,76},{13,5},{32,96},{33... | collective-permute-start | bytes 1572872 | tf_op jit(solution)/shard_map/ppermute | solution.py:34
  46.3 0.0 collective-permute-start.11
  46.3 0.0 collective-permute-done.12.a_ref
  46.3 1.5 %collective-permute-start.13 = (bf16[2,256,256]{2,1,0:T(8,128)(2,1)S(1)}, bf16[2,256,256]{2,1,0:T(8,128)(2,1)S(1)}, u32[]{:S(2)}, u32[]{:S(2)}) collective-permute-start(bf16[2,256,256]{2,1,0:T(8,128)(2,1)S(1)} %picked.1.seed.a_ref), channel_id=1, source_target_pairs={{0,16},{16,0},{1,17},{17,1},{2,18},{18,2},{3,19},{19,3},{4,20},{20... | collective-permute-start | bytes 786440 | tf_op jit(solution)/shard_map/ppermute | solution.py:38
  47.8 4.9 %collective-permute-done.13.other.b_ref = bf16[2,256,256]{2,1,0:T(8,128)(2,1)S(1)} collective-permute-done((bf16[2,256,256]{2,1,0:T(8,128)(2,1)S(1)}, bf16[2,256,256]{2,1,0:T(8,128)(2,1)S(1)}, u32[]{:S(2)}, u32[]{:S(2)}) %collective-permute-start.13) | collective-permute-done | bytes 262176 | tf_op jit(solution)/shard_map/ppermute | solution.py:38
  52.7 0.9 %paired.1 = (bf16[4,256,256]{2,1,0:T(8,128)(2,1)}, bf16[2,256,256]{2,1,0:T(8,128)(2,1)}) custom-call(bf16[2,256,256]{2,1,0:T(8,128)(2,1)S(1)} %picked.1.seed.a_ref, bf16[2,256,256]{2,1,0:T(8,128)(2,1)S(1)} %collective-permute-done.13.other.b_ref), custom_call_target="tpu_custom_call" | custom-call | tf_op jit(solution)/shard_map/paired/pallas_call | solution.py:284
  53.6 2.0 %collective-permute-start.14 = (bf16[2,256,256]{2,1,0:T(8,128)(2,1)}, bf16[2,256,256]{2,1,0:T(8,128)(2,1)S(1)}, u32[]{:S(2)}, u32[]{:S(2)}) collective-permute-start(bf16[2,256,256]{2,1,0:T(8,128)(2,1)} %get-tuple-element.54), channel_id=1, source_target_pairs={{0,8},{4,12},{8,0},{12,4},{1,9},{5,13},{9,1},{13,5},{2,10},{6,14},... | collective-permute-start | bytes 786440 | tf_op jit(solution)/shard_map/ppermute | solution.py:378
  55.7 0.0 collective-permute-start.16
  55.7 0.0 collective-permute-done.9.b
  55.7 2.7 %collective-permute-start.17 = (bf16[4,256,256]{2,1,0:T(8,128)(2,1)}, bf16[4,256,256]{2,1,0:T(8,128)(2,1)S(1)}, u32[]{:S(2)}, u32[]{:S(2)}) collective-permute-start(bf16[4,256,256]{2,1,0:T(8,128)(2,1)} %get-tuple-element.57), channel_id=1, source_target_pairs={{0,12},{4,0},{8,4},{12,8},{1,13},{5,1},{9,5},{13,9},{2,14},{6,2},{... | collective-permute-start | bytes 1572872 | tf_op jit(solution)/shard_map/ppermute | solution.py:378
  58.3 0.4 collective-permute-done.10.c
  58.8 0.0 collective-permute-done.11.d
  58.8 1.0 %summed.1 = bf16[8,128,256]{2,1,0:T(8,128)(2,1)} custom-call(f32[512,512]{1,0:T(8,128)S(1)} %get-tuple-element.47.a, bf16[512,512]{1,0:T(8,128)(2,1)S(1)} %collective-permute-done.9.b, bf16[512,512]{1,0:T(8,128)(2,1)S(1)} %collective-permute-done.10.c, bf16[512,512]{1,0:T(8,128)(2,1)S(1)} %collective-permute-done.11.d), custom_call_target="tpu_custom_call" | custom-call | tf_op jit(solution)/shard_map/summed/pallas_call | solution.py:229
  59.8 6.6 %all-to-all-start = ((bf16[8,128,256]{2,1,0:T(8,128)(2,1)}), bf16[8,128,256]{2,1,0:T(8,128)(2,1)S(1)}, u32[]{:S(2)}, u32[]{:S(2)}) async-start(bf16[8,128,256]{2,1,0:T(8,128)(2,1)} %summed.1), calls=%async_computation | async-start | bytes 1048576 | tf_op jit(solution)/shard_map/all_to_all | solution.py:384
  66.4 0.0 collective-permute-done.14.far
  66.4 4.1 %collective-permute-start.15 = (bf16[2,256,256]{2,1,0:T(8,128)(2,1)S(1)}, bf16[2,256,256]{2,1,0:T(8,128)(2,1)S(1)}, u32[]{:S(2)}, u32[]{:S(2)}) collective-permute-start(bf16[2,256,256]{2,1,0:T(8,128)(2,1)S(1)} %collective-permute-done.14.far), channel_id=1, source_target_pairs={{0,32},{1,97},{32,0},{33,65},{64,96},{65,33},{96,64},{97,1},{2,34}... | collective-permute-start | bytes 786440 | tf_op jit(solution)/shard_map/ppermute | solution.py:299
  70.5 1.8 %first_part.1.o_in = bf16[2048,4,256]{2,1,0:T(4,128)(2,1)} custom-call(bf16[512,1024]{1,0:T(8,128)(2,1)S(1)} %get-tuple-element.51.h_ref, bf16[2,256,256]{2,1,0:T(8,128)(2,1)S(1)} %picked.1.seed.a_ref, bf16[2,256,256]{2,1,0:T(8,128)(2,1)S(1)} %collective-permute-done.13.other.b_ref), custom_call_target="tpu_custom_call" | custom-call | flops 1000000 | bytes 1024 | tf_op jit(solution)/shard_map/first_part/pallas_call | solution.py:341
  72.3 2.2 %collective-permute-done.15.far_pair = bf16[2,256,256]{2,1,0:T(8,128)(2,1)S(1)} collective-permute-done((bf16[2,256,256]{2,1,0:T(8,128)(2,1)S(1)}, bf16[2,256,256]{2,1,0:T(8,128)(2,1)S(1)}, u32[]{:S(2)}, u32[]{:S(2)}) %collective-permute-start.15) | collective-permute-done | bytes 262176 | tf_op jit(solution)/shard_map/ppermute | solution.py:299
  74.5 1.8 %second_part.1.o_in = bf16[2048,4,256]{2,1,0:T(4,128)(2,1)} custom-call(bf16[2048,4,256]{2,1,0:T(4,128)(2,1)} %first_part.1.o_in, bf16[512,1024]{1,0:T(8,128)(2,1)S(1)} %get-tuple-element.51.h_ref, bf16[2,256,256]{2,1,0:T(8,128)(2,1)S(1)} %collective-permute-done.14.far, ...), custom_call_target="tpu_custom_call", output_to_operand_aliasing={{}: (0, {})} | custom-call | flops 1000000 | bytes 1024 | tf_op jit(solution)/shard_map/second_part/pallas_call | solution.py:341
  76.3 0.0 all-to-all-done.r_ref
  76.3 0.9 %finish.1 = bf16[128,4,256]{2,1,0:T(4,128)(2,1)} custom-call(bf16[8,128,256]{2,1,0:T(8,128)(2,1)S(1)} %all-to-all-done.r_ref), custom_call_target="tpu_custom_call" | custom-call | tf_op jit(solution)/shard_map/finish/pallas_call | solution.py:245
  77.2 2.6 %third_part.1 = bf16[2048,4,256]{2,1,0:T(4,128)(2,1)} custom-call(bf16[2048,4,256]{2,1,0:T(4,128)(2,1)} %second_part.1.o_in, bf16[512,1024]{1,0:T(8,128)(2,1)S(1)} %get-tuple-element.51.h_ref, bf16[4,256,256]{2,1,0:T(8,128)(2,1)S(1)} %collective-permute-done.16.up, bf16[4,256,256]{2,1,0:T(8,128)(2,1)S(1)} %collective-permute-done.17.down), custom_call_target="tpu_custom_call", output_to_operand_aliasing={{}: (0, {})} | custom-call | flops 1000000 | bytes 1024 | tf_op jit(solution)/shard_map/third_part/pallas_call | solution.py:341
  (7 shorter events, 0.0 us)
Async XLA Ops:
  0.6 7.2 %copy-start.1 = (bf16[128,256]{1,0:T(8,128)(2,1)S(1)}, bf16[128,256]{1,0:T(8,128)(2,1)}, u32[]{:S(2)}) copy-start(bf16[128,256]{1,0:T(8,128)(2,1)} %g_ref) | copy-start | bytes 196612
  0.6 7.2 %copy-start = (bf16[128,4,256]{2,1,0:T(4,128)(2,1)S(1)}, bf16[128,4,256]{2,1,0:T(4,128)(2,1)}, u32[]{:S(2)}) copy-start(bf16[128,4,256]{2,1,0:T(4,128)(2,1)} %h_ref) | copy-start | bytes 786436
  3.1 19.4 %collective-permute-start.3 = (bf16[8,256,256]{2,1,0:T(8,128)(2,1)S(1)}, bf16[8,256,256]{2,1,0:T(8,128)(2,1)S(1)}, u32[]{:S(2)}, u32[]{:S(2)}) collective-permute-start(bf16[8,256,256]{2,1,0:T(8,128)(2,1)S(1)} %get-tuple-element.34), channel_id=1, source_target_pairs={{0,4},{1,33},{4,8},{5,37},{8,12},{9,41},{12,0},{13,45},{32,36},{33... | collective-permute-start | bytes 3145736 | tf_op jit(solution)/shard_map/ppermute | solution.py:34
  5.6 30.8 %collective-permute-start.7 = (bf16[8,256,256]{2,1,0:T(8,128)(2,1)S(1)}, bf16[8,256,256]{2,1,0:T(8,128)(2,1)S(1)}, u32[]{:S(2)}, u32[]{:S(2)}) collective-permute-start(bf16[8,256,256]{2,1,0:T(8,128)(2,1)S(1)} %get-tuple-element.36), channel_id=1, source_target_pairs={{0,12},{1,97},{4,0},{5,101},{8,4},{9,105},{12,8},{13,109},{32,44},... | collective-permute-start | bytes 3145736 | tf_op jit(solution)/shard_map/ppermute | solution.py:34
  7.9 10.9 %collective-permute-start.1 = (bf16[5,128,256]{2,1,0:T(8,128)(2,1)S(1)}, bf16[5,128,256]{2,1,0:T(8,128)(2,1)S(1)}, u32[]{:S(2)}, u32[]{:S(2)}) collective-permute-start(bf16[5,128,256]{2,1,0:T(8,128)(2,1)S(1)} %packed.1.p0), channel_id=1, source_target_pairs={{0,2},{2,0},{1,3},{3,1},{4,6},{6,4},{5,7},{7,5},{8,10},{10,8},{9,1... | collective-permute-start | bytes 983048 | tf_op jit(solution)/shard_map/ppermute | solution.py:38
  10.9 29.6 %collective-permute-start.8 = (bf16[8,256,256]{2,1,0:T(8,128)(2,1)S(1)}, bf16[8,256,256]{2,1,0:T(8,128)(2,1)S(1)}, u32[]{:S(2)}, u32[]{:S(2)}) collective-permute-start(bf16[8,256,256]{2,1,0:T(8,128)(2,1)S(1)} %get-tuple-element.46), channel_id=1, source_target_pairs={{0,8},{1,65},{4,12},{5,69},{8,0},{9,73},{12,4},{13,77},{32,40},{33... | collective-permute-start | bytes 3145736 | tf_op jit(solution)/shard_map/ppermute | solution.py:34
  12.1 7.5 %collective-permute-start = (bf16[5,128,256]{2,1,0:T(8,128)(2,1)S(1)}, bf16[5,128,256]{2,1,0:T(8,128)(2,1)S(1)}, u32[]{:S(2)}, u32[]{:S(2)}) collective-permute-start(bf16[5,128,256]{2,1,0:T(8,128)(2,1)S(1)} %packed.1.p0), channel_id=1, source_target_pairs={{0,1},{1,0},{2,3},{3,2},{4,5},{5,4},{6,7},{7,6},{8,9},{9,8},{10,11... | collective-permute-start | bytes 983048 | tf_op jit(solution)/shard_map/ppermute | solution.py:38
  18.8 2.0 %collective-permute-start.2 = (bf16[5,128,256]{2,1,0:T(8,128)(2,1)S(1)}, bf16[5,128,256]{2,1,0:T(8,128)(2,1)S(1)}, u32[]{:S(2)}, u32[]{:S(2)}) collective-permute-start(bf16[5,128,256]{2,1,0:T(8,128)(2,1)S(1)} %collective-permute-done.1.p2), channel_id=1, source_target_pairs={{0,1},{1,0},{2,3},{3,2},{4,5},{5,4},{6,7},{7,6},{8,9},{9,8},{10,11... | collective-permute-start | bytes 983048 | tf_op jit(solution)/shard_map/ppermute | solution.py:38
  21.0 15.4 %collective-permute-start.6 = (bf16[2,256,256]{2,1,0:T(8,128)(2,1)S(1)}, bf16[2,256,256]{2,1,0:T(8,128)(2,1)S(1)}, u32[]{:S(2)}, u32[]{:S(2)}) collective-permute-start(bf16[2,256,256]{2,1,0:T(8,128)(2,1)S(1)} %get-tuple-element.38.g0), channel_id=1, source_target_pairs={{0,12},{1,97},{4,0},{5,101},{8,4},{9,105},{12,8},{13,109},{32,44},... | collective-permute-start | bytes 786440 | tf_op jit(solution)/shard_map/ppermute | solution.py:34
  22.4 15.3 %collective-permute-start.5 = (bf16[2,256,256]{2,1,0:T(8,128)(2,1)S(1)}, bf16[2,256,256]{2,1,0:T(8,128)(2,1)S(1)}, u32[]{:S(2)}, u32[]{:S(2)}) collective-permute-start(bf16[2,256,256]{2,1,0:T(8,128)(2,1)S(1)} %get-tuple-element.38.g0), channel_id=1, source_target_pairs={{0,8},{1,65},{4,12},{5,69},{8,0},{9,73},{12,4},{13,77},{32,40},{33... | collective-permute-start | bytes 786440 | tf_op jit(solution)/shard_map/ppermute | solution.py:34
  22.5 15.6 %collective-permute-start.4 = (bf16[2,256,256]{2,1,0:T(8,128)(2,1)S(1)}, bf16[2,256,256]{2,1,0:T(8,128)(2,1)S(1)}, u32[]{:S(2)}, u32[]{:S(2)}) collective-permute-start(bf16[2,256,256]{2,1,0:T(8,128)(2,1)S(1)} %get-tuple-element.38.g0), channel_id=1, source_target_pairs={{0,4},{1,33},{4,8},{5,37},{8,12},{9,41},{12,0},{13,45},{32,36},{33... | collective-permute-start | bytes 786440 | tf_op jit(solution)/shard_map/ppermute | solution.py:34
  38.2 8.1 %collective-permute-start.12 = (bf16[2,256,256]{2,1,0:T(8,128)(2,1)S(1)}, bf16[2,256,256]{2,1,0:T(8,128)(2,1)S(1)}, u32[]{:S(2)}, u32[]{:S(2)}) collective-permute-start(bf16[2,256,256]{2,1,0:T(8,128)(2,1)S(1)} %get-tuple-element.52), channel_id=1, source_target_pairs={{1,0},{3,2},{5,4},{7,6},{9,8},{11,10},{13,12},{15,14},{17,16},{19,... | collective-permute-start | bytes 786440 | tf_op jit(solution)/shard_map/ppermute | solution.py:372
  41.8 13.9 %collective-permute-start.9 = (bf16[512,512]{1,0:T(8,128)(2,1)S(1)}, bf16[512,512]{1,0:T(8,128)(2,1)S(1)}, u32[]{:S(2)}, u32[]{:S(2)}) collective-permute-start(bf16[512,512]{1,0:T(8,128)(2,1)S(1)} %get-tuple-element.48), channel_id=1, source_target_pairs={{0,32},{1,5},{4,36},{5,9},{8,40},{9,13},{12,44},{13,1},{32,64},{33... | collective-permute-start | bytes 1572872 | tf_op jit(solution)/shard_map/ppermute | solution.py:34
  43.1 15.7 %collective-permute-start.10 = (bf16[512,512]{1,0:T(8,128)(2,1)S(1)}, bf16[512,512]{1,0:T(8,128)(2,1)S(1)}, u32[]{:S(2)}, u32[]{:S(2)}) collective-permute-start(bf16[512,512]{1,0:T(8,128)(2,1)S(1)} %get-tuple-element.49), channel_id=1, source_target_pairs={{0,64},{1,9},{4,68},{5,13},{8,72},{9,1},{12,76},{13,5},{32,96},{33... | collective-permute-start | bytes 1572872 | tf_op jit(solution)/shard_map/ppermute | solution.py:34
  46.3 12.5 %collective-permute-start.11 = (bf16[512,512]{1,0:T(8,128)(2,1)S(1)}, bf16[512,512]{1,0:T(8,128)(2,1)S(1)}, u32[]{:S(2)}, u32[]{:S(2)}) collective-permute-start(bf16[512,512]{1,0:T(8,128)(2,1)S(1)} %get-tuple-element.50), channel_id=1, source_target_pairs={{0,96},{1,13},{4,100},{5,1},{8,104},{9,5},{12,108},{13,9},{32,0},{... | collective-permute-start | bytes 1572872 | tf_op jit(solution)/shard_map/ppermute | solution.py:34
  46.3 6.4 %collective-permute-start.13 = (bf16[2,256,256]{2,1,0:T(8,128)(2,1)S(1)}, bf16[2,256,256]{2,1,0:T(8,128)(2,1)S(1)}, u32[]{:S(2)}, u32[]{:S(2)}) collective-permute-start(bf16[2,256,256]{2,1,0:T(8,128)(2,1)S(1)} %picked.1.seed.a_ref), channel_id=1, source_target_pairs={{0,16},{16,0},{1,17},{17,1},{2,18},{18,2},{3,19},{19,3},{4,20},{20... | collective-permute-start | bytes 786440 | tf_op jit(solution)/shard_map/ppermute | solution.py:38
  53.6 12.8 %collective-permute-start.14 = (bf16[2,256,256]{2,1,0:T(8,128)(2,1)}, bf16[2,256,256]{2,1,0:T(8,128)(2,1)S(1)}, u32[]{:S(2)}, u32[]{:S(2)}) collective-permute-start(bf16[2,256,256]{2,1,0:T(8,128)(2,1)} %get-tuple-element.54), channel_id=1, source_target_pairs={{0,8},{4,12},{8,0},{12,4},{1,9},{5,13},{9,1},{13,5},{2,10},{6,14},... | collective-permute-start | bytes 786440 | tf_op jit(solution)/shard_map/ppermute | solution.py:378
  55.7 21.5 %collective-permute-start.16 = (bf16[4,256,256]{2,1,0:T(8,128)(2,1)}, bf16[4,256,256]{2,1,0:T(8,128)(2,1)S(1)}, u32[]{:S(2)}, u32[]{:S(2)}) collective-permute-start(bf16[4,256,256]{2,1,0:T(8,128)(2,1)} %get-tuple-element.57), channel_id=1, source_target_pairs={{0,4},{4,8},{8,12},{12,0},{1,5},{5,9},{9,13},{13,1},{2,6},{6,10},{... | collective-permute-start | bytes 1572872 | tf_op jit(solution)/shard_map/ppermute | solution.py:378
  55.7 21.5 %collective-permute-start.17 = (bf16[4,256,256]{2,1,0:T(8,128)(2,1)}, bf16[4,256,256]{2,1,0:T(8,128)(2,1)S(1)}, u32[]{:S(2)}, u32[]{:S(2)}) collective-permute-start(bf16[4,256,256]{2,1,0:T(8,128)(2,1)} %get-tuple-element.57), channel_id=1, source_target_pairs={{0,12},{4,0},{8,4},{12,8},{1,13},{5,1},{9,5},{13,9},{2,14},{6,2},{... | collective-permute-start | bytes 1572872 | tf_op jit(solution)/shard_map/ppermute | solution.py:378
  59.8 16.5 %all-to-all-start = ((bf16[8,128,256]{2,1,0:T(8,128)(2,1)}), bf16[8,128,256]{2,1,0:T(8,128)(2,1)S(1)}, u32[]{:S(2)}, u32[]{:S(2)}) async-start(bf16[8,128,256]{2,1,0:T(8,128)(2,1)} %summed.1), calls=%async_computation | async-start | bytes 1048576 | tf_op jit(solution)/shard_map/all_to_all | solution.py:384
  66.4 8.1 %collective-permute-start.15 = (bf16[2,256,256]{2,1,0:T(8,128)(2,1)S(1)}, bf16[2,256,256]{2,1,0:T(8,128)(2,1)S(1)}, u32[]{:S(2)}, u32[]{:S(2)}) collective-permute-start(bf16[2,256,256]{2,1,0:T(8,128)(2,1)S(1)} %collective-permute-done.14.far), channel_id=1, source_target_pairs={{0,32},{1,97},{32,0},{33,65},{64,96},{65,33},{96,64},{97,1},{2,34}... | collective-permute-start | bytes 786440 | tf_op jit(solution)/shard_map/ppermute | solution.py:299

commit v14 on v13

--- a/solution.py
+++ b/solution.py
@@ -67,37 +67,36 @@
     scales = pltpu.make_async_copy(s_ref, narrow_ref, sems.at[16])
     scales.start()
     copies = []
-    for j, (k, o_ref) in enumerate(outs):
+    for j, (k, buffers) in enumerate(outs):
         p = (first + k) & 3
-        for i in range(4):
+        places = [r.at[pl.ds(i, 2)] for r in buffers for i in range(0, r.shape[0], 2)]
+        for i, o_ref in enumerate(places):
             z, x = c * p + (1 - c) * i, c * i + (1 - c) * p
-            copy = pltpu.make_async_copy(
-                w_ref.at[z, :, x], o_ref.at[pl.ds(2 * i, 2)], sems.at[j * 4 + i]
-            )
+            copy = pltpu.make_async_copy(w_ref.at[z, :, x], o_ref, sems.at[j * 4 + i])
             copy.start()
-            copies.append((copy, o_ref, i, z, x))
+            copies.append((copy, o_ref, z, x))
     scales.wait()
     spread_scales(narrow_ref, wide_ref)
-    for copy, o_ref, i, z, x in copies:
+    for copy, o_ref, z, x in copies:
         copy.wait()
         for yl in range(2):
             r = pl.multiple_of((z * 8 + yl * 4 + x) * 16, 16)
             s = wide_ref[pl.ds(r, 16), :]
-            w = o_ref[2 * i + yl].astype(F32).reshape(16, 16, 256)
-            o_ref[2 * i + yl] = (w * s[:, None, :]).reshape(256, 256).astype(BF)
-
-
-def scale_body(w_ref, s_ref, *refs):
-    outs, scratch = refs[:4], refs[4:]
-    scale_into([(k, outs[k]) for k in (1, 3, 2, 0)], w_ref, s_ref, *scratch)
+            w = o_ref[yl].astype(F32).reshape(16, 16, 256)
+            o_ref[yl] = (w * s[:, None, :]).reshape(256, 256).astype(BF)
+
+
+def scale_body(w_ref, s_ref, o0, o1a, o1b, o2, o3, *scratch):
+    outs = [(1, (o1a, o1b)), (3, (o3,)), (2, (o2,)), (0, (o0,))]
+    scale_into(outs, w_ref, s_ref, *scratch)
 
 
 def scaled_rows(w5, scales_t):
     return pl.pallas_call(
         scale_body,
-        out_shape=[VM((8, 256, 256), BF)] * 4,
+        out_shape=[VM((n, 256, 256), BF) for n in (8, 6, 2, 8, 8)],
         in_specs=[HBM, HBM],
-        out_specs=[IN] * 4,
+        out_specs=[IN] * 5,
         scratch_shapes=[VM((16, 512), BF), VM((512, 256), F32), pltpu.SemaphoreType.DMA((17,))],
         compiler_params=LIMIT,
         name="scale",
@@ -122,7 +121,7 @@
     )(grad_out, hidden)
 
 
-def tokens_body(p0, p1, p2, p3, g_ref, h_ref):
+def tokens_body(rows_ref, p0, p1, p2, p3, g_ref, h_ref, o_ref):
     n = lax.axis_index("yh") * 2 + lax.axis_index("c")
     for r, p in enumerate((p0, p1, p2, p3)):
         t = n ^ r
@@ -130,19 +129,22 @@
         rows = pl.ds(pl.multiple_of(t * 128, 128), 128)
         for m in range(4):
             h_ref[rows, m * 256 : (m + 1) * 256] = p[1 + m]
-
-
-def all_tokens(own):
+    o_ref[0:2] = rows_ref[...]
+    o_ref[2:4] = g_ref[...]
+
+
+def all_tokens(own, rows):
     far = swap(own, "yh")
     pieces = [own, swap(own, "c"), far, swap(far, "c")]
     return pl.pallas_call(
         tokens_body,
-        out_shape=[VM((2, 256, 256), BF), VM((512, 1024), BF)],
-        in_specs=[IN] * 4,
-        out_specs=[IN] * 2,
-        compiler_params=LIMIT,
+        out_shape=[VM((2, 256, 256), BF), VM((512, 1024), BF), VM((4, 256, 256), BF)],
+        in_specs=[IN] * 5,
+        out_specs=[IN] * 3,
+        compiler_params=LIMIT,
+        cost_estimate=pl.CostEstimate(flops=1000, bytes_accessed=1000, transcendentals=0),
         name="tokens",
-    )(*kept(*pieces))
+    )(*kept(rows, *pieces))
 
 
 def block_product(g, w, q):
@@ -171,9 +173,9 @@
     )(*kept(*operands))
 
 
-def plane_body(g0, g1, g2, g3, keep, give):
+def plane_body(g0, r1b, g2, g3, keep, give):
     z, yh = lax.axis_index("z"), lax.axis_index("yh")
-    g = (g0, g1, g2, g3)
+    g = (g0, r1b.at[2:4], g2, g3)
     for k in range(4):
 
         @pl.when(((z - 2 * yh) & 3) == k)
@@ -196,7 +198,11 @@
     )(*kept(*grads))
 
 
-def partial_body(acc, r1, r2, g1, g2, *outs):
+def partial_body(acc, r1a, r1b, r2, g2, *outs):
+    outs, r1 = outs[:4], outs[4]
+    r1[0:6] = r1a[...]
+    r1[6:8] = r1b[0:2]
+    g1 = r1b.at[2:4]
     _, _, second = roles()
     for k in (2, 1, 3, 0):
         q = (second + k) & 3
@@ -211,6 +217,7 @@
         + [VM((512, 512), BF)] * 3,
         in_specs=[IN] * 5,
         out_specs=[IN] * 4,
+        scratch_shapes=[VM((8, 256, 256), BF)],
         compiler_params=LIMIT,
         name="partial",
     )(*kept(*operands))
@@ -355,20 +362,20 @@
     w5 = pltpu.with_memory_space_constraint(weight_base.reshape(4, 2, 4, 256, 256), pltpu.HBM)
     scales_t = pltpu.with_memory_space_constraint(block_scale.T, pltpu.HBM)
 
-    sent = scaled_rows(w5, scales_t)
-    r0 = sent[0]
-    r1, r2, r3 = [shift(sent[k], first_axis_steps(k)) for k in (1, 2, 3)]
+    r0, sent1a, sent1b, sent2, sent3 = scaled_rows(w5, scales_t)
+    r1a = shift(sent1a, first_axis_steps(1))
+    r2, r3 = shift(sent2, first_axis_steps(2)), shift(sent3, first_axis_steps(3))
     grad_out, hidden, _ = lax.optimization_barrier((grad_out, hidden, r0))
-    g0, h = all_tokens(packed(grad_out, hidden))
+    g0, h, sent1b = all_tokens(packed(grad_out, hidden), sent1b)
+    sent1b, g0, r1a = lax.optimization_barrier((sent1b, g0, r1a))
+    r1b = shift(sent1b, first_axis_steps(1))
     g2, g3 = [shift(g0, first_axis_steps(k)) for k in (2, 3)]
-    later, r1 = lax.optimization_barrier((g0, r1))
-    g1 = shift(later, first_axis_steps(1))
 
     acc = early_sums(r0, r3, g0, g3)
-    plane, acc = lax.optimization_barrier(((g0, g1, g2, g3), acc))
+    plane, acc = lax.optimization_barrier(((g0, r1b, g2, g3), acc))
     keep, give = plane_blocks(*plane)
     acc, keep, give = lax.optimization_barrier((acc, keep, give))
-    sums = partial_sums(acc, r1, r2, g1, g2)
+    sums = partial_sums(acc, r1a, r1b, r2, g2)
     seed = picked(lax.ppermute(give, "c", [(1, 0)]), keep)
     other = swap(seed, "yl")
     parts = [sums[0]] + [None] * 3

time: 80.2 us -> 80.2 us (level)
  starting transfers between devices: 46.3 us -> 42.6 us
  waiting for transfers between devices: 18.4 us -> 22 us
    ppermute x9, waiting for transfers between devices: 4.19 us -> 7.06 us  [shift(): return lax.ppermute(value, ('z', 'x', 'c'), pairs)]
    ppermute x9, starting transfers between devices: 22.5 us -> 21.2 us  [shift(): return lax.ppermute(value, ('z', 'x', 'c'), pairs)]
    ppermute x3, starting transfers between devices: 4.71 us -> 3.46 us  [per_device(): lax.ppermute(value, 'x', [(i, (i + k) % 4) for i in range(4)])]
    ppermute x1, starting transfers between devices: 2.31 us -> 1.31 us  [per_device(): seed = picked(lax.ppermute(give, 'c', [(1, 0)]), keep)]
where the time goes in v14:
time: 80.2 us; the launch traced here: 79.9 us
  starting transfers between devices  42.6 us (53%)
  waiting for transfers between devices  22 us (27%)
  Pallas kernels  14.4 us (18%)
  between operations  0.92 us (1%)
    ppermute x9, starting transfers between devices, shift(): return lax.ppermute(value, ('z', 'x', 'c'), pairs)  21.2 us
    ppermute x4, waiting for transfers between devices, swap(): return lax.ppermute(value, axis, [(0, 1), (1, 0)])  12.7 us
    ppermute x9, waiting for transfers between devices, shift(): return lax.ppermute(value, ('z', 'x', 'c'), pairs)  7.06 us
    all_to_all x1, starting transfers between devices, per_device(): blocks = lax.all_to_all(blocks, ('yl', 'yh', 'c'), 0, 0, tiled=True)  6.61 us
    pallas_call x3, Pallas kernels, outer_part(): pl.pallas_call(body, out_shape=jax.ShapeDtypeStruct((2048, 4, 256), BF),...  6.22 us
    ppermute x4, starting transfers between devices, swap(): return lax.ppermute(value, axis, [(0, 1), (1, 0)])  6.07 us
    ppermute x1, starting transfers between devices, z_pairs(): return lax.ppermute(value, ('z', 'c'), pairs)  3.96 us
    ppermute x3, starting transfers between devices, per_device(): lax.ppermute(value, 'x', [(i, (i + k) % 4) for i in range(4)])  3.46 us
  transfers between devices with their start and end apart: 19, of which 7 were waited for; matrix products, arithmetic and copies ran while one was open for 0% of the time, Pallas kernels for 12%

profile of v14, /device:TPU:1, one launch (start us, length us, event | category | flops | bytes accessed | tf_op | source)
XLA Modules:
  0.0 79.9 jit_solution(11434657120693649511)
XLA Ops:
  0.7 2.4 %scale.1 = (bf16[8,256,256]{2,1,0:T(8,128)(2,1)S(1)}, bf16[6,256,256]{2,1,0:T(8,128)(2,1)S(1)}, bf16[2,256,256]{2,1,0:T(8,128)(2,1)S(1)}, bf16[8,256,256]{2,1,0:T(8,128)(2,1)S(1)}, bf16[8,256,256]{2,1,0:T(8,128)(2,1)S(1)}) custom-call(bf16[4,2,4,256,256]{4,3,2,1,0:T(8,128)(2,1)} %bitcast.2, bf16[16,512]{1,0:T(8,128)(2,1)} %bitcast.3), custom_call_target="tpu_custom_call" | custom-call | tf_op jit(solution)/shard_map/scale/pallas_call | solution.py:95
  3.1 2.5 %collective-permute-start.3 = (bf16[6,256,256]{2,1,0:T(8,128)(2,1)S(1)}, bf16[6,256,256]{2,1,0:T(8,128)(2,1)S(1)}, u32[]{:S(2)}, u32[]{:S(2)}) collective-permute-start(bf16[6,256,256]{2,1,0:T(8,128)(2,1)S(1)} %get-tuple-element.39), channel_id=1, source_target_pairs={{0,4},{1,33},{4,8},{5,37},{8,12},{9,41},{12,0},{13,45},{32,36},{33... | collective-permute-start | bytes 2359304 | tf_op jit(solution)/shard_map/ppermute | solution.py:34
  5.6 2.2 %collective-permute-start.7 = (bf16[8,256,256]{2,1,0:T(8,128)(2,1)S(1)}, bf16[8,256,256]{2,1,0:T(8,128)(2,1)S(1)}, u32[]{:S(2)}, u32[]{:S(2)}) collective-permute-start(bf16[8,256,256]{2,1,0:T(8,128)(2,1)S(1)} %get-tuple-element.42), channel_id=1, source_target_pairs={{0,12},{1,97},{4,0},{5,101},{8,4},{9,105},{12,8},{13,109},{32,44},... | collective-permute-start | bytes 3145736 | tf_op jit(solution)/shard_map/ppermute | solution.py:34
  7.8 0.1 packed.1.p0
  7.9 3.0 %collective-permute-start.1 = (bf16[5,128,256]{2,1,0:T(8,128)(2,1)S(1)}, bf16[5,128,256]{2,1,0:T(8,128)(2,1)S(1)}, u32[]{:S(2)}, u32[]{:S(2)}) collective-permute-start(bf16[5,128,256]{2,1,0:T(8,128)(2,1)S(1)} %packed.1.p0), channel_id=1, source_target_pairs={{0,2},{2,0},{1,3},{3,1},{4,6},{6,4},{5,7},{7,5},{8,10},{10,8},{9,1... | collective-permute-start | bytes 983048 | tf_op jit(solution)/shard_map/ppermute | solution.py:38
  10.9 1.2 %collective-permute-start.8 = (bf16[8,256,256]{2,1,0:T(8,128)(2,1)S(1)}, bf16[8,256,256]{2,1,0:T(8,128)(2,1)S(1)}, u32[]{:S(2)}, u32[]{:S(2)}) collective-permute-start(bf16[8,256,256]{2,1,0:T(8,128)(2,1)S(1)} %get-tuple-element.52), channel_id=1, source_target_pairs={{0,8},{1,65},{4,12},{5,69},{8,0},{9,73},{12,4},{13,77},{32,40},{33... | collective-permute-start | bytes 3145736 | tf_op jit(solution)/shard_map/ppermute | solution.py:34
  12.1 0.9 %collective-permute-start = (bf16[5,128,256]{2,1,0:T(8,128)(2,1)S(1)}, bf16[5,128,256]{2,1,0:T(8,128)(2,1)S(1)}, u32[]{:S(2)}, u32[]{:S(2)}) collective-permute-start(bf16[5,128,256]{2,1,0:T(8,128)(2,1)S(1)} %packed.1.p0), channel_id=1, source_target_pairs={{0,1},{1,0},{2,3},{3,2},{4,5},{5,4},{6,7},{7,6},{8,9},{9,8},{10,11... | collective-permute-start | bytes 983048 | tf_op jit(solution)/shard_map/ppermute | solution.py:38
  13.0 5.8 %collective-permute-done.1.p2 = bf16[5,128,256]{2,1,0:T(8,128)(2,1)S(1)} collective-permute-done((bf16[5,128,256]{2,1,0:T(8,128)(2,1)S(1)}, bf16[5,128,256]{2,1,0:T(8,128)(2,1)S(1)}, u32[]{:S(2)}, u32[]{:S(2)}) %collective-permute-start.1) | collective-permute-done | bytes 327712 | tf_op jit(solution)/shard_map/ppermute | solution.py:38
  18.8 0.8 collective-permute-start.2
  19.6 0.0 collective-permute-done.p1
  19.6 1.3 %collective-permute-done.2.p3 = bf16[5,128,256]{2,1,0:T(8,128)(2,1)S(1)} collective-permute-done((bf16[5,128,256]{2,1,0:T(8,128)(2,1)S(1)}, bf16[5,128,256]{2,1,0:T(8,128)(2,1)S(1)}, u32[]{:S(2)}, u32[]{:S(2)}) %collective-permute-start.2) | collective-permute-done | bytes 327712 | tf_op jit(solution)/shard_map/ppermute | solution.py:38
  20.9 0.2 tokens.1
  21.0 0.0 collective-permute-done.3.r1a
  21.0 6.4 %collective-permute-start.4 = (bf16[4,256,256]{2,1,0:T(8,128)(2,1)S(1)}, bf16[4,256,256]{2,1,0:T(8,128)(2,1)S(1)}, u32[]{:S(2)}, u32[]{:S(2)}) collective-permute-start(bf16[4,256,256]{2,1,0:T(8,128)(2,1)S(1)} %get-tuple-element.41), channel_id=1, source_target_pairs={{0,4},{1,33},{4,8},{5,37},{8,12},{9,41},{12,0},{13,45},{32,36},{33... | collective-permute-start | bytes 1572872 | tf_op jit(solution)/shard_map/ppermute | solution.py:34
  27.4 0.0 collective-permute-start.6
  27.4 4.0 %collective-permute-start.5 = (bf16[2,256,256]{2,1,0:T(8,128)(2,1)S(1)}, bf16[2,256,256]{2,1,0:T(8,128)(2,1)S(1)}, u32[]{:S(2)}, u32[]{:S(2)}) collective-permute-start(bf16[2,256,256]{2,1,0:T(8,128)(2,1)S(1)} %get-tuple-element.44.g0), channel_id=1, source_target_pairs={{0,8},{1,65},{4,12},{5,69},{8,0},{9,73},{12,4},{13,77},{32,40},{33... | collective-permute-start | bytes 786440 | tf_op jit(solution)/shard_map/ppermute | solution.py:34
  31.4 5.0 %collective-permute-done.6.g3 = bf16[2,256,256]{2,1,0:T(8,128)(2,1)S(1)} collective-permute-done((bf16[2,256,256]{2,1,0:T(8,128)(2,1)S(1)}, bf16[2,256,256]{2,1,0:T(8,128)(2,1)S(1)}, u32[]{:S(2)}, u32[]{:S(2)}) %collective-permute-start.6) | collective-permute-done | bytes 262176 | tf_op jit(solution)/shard_map/ppermute | solution.py:34
  36.4 0.0 collective-permute-done.7.r3
  36.4 1.3 %early.1.acc = f32[4,512,512]{2,1,0:T(8,128)S(1)} custom-call(bf16[8,256,256]{2,1,0:T(8,128)(2,1)S(1)} %get-tuple-element.34.r0, bf16[8,256,256]{2,1,0:T(8,128)(2,1)S(1)} %collective-permute-done.7.r3, bf16[2,256,256]{2,1,0:T(8,128)(2,1)S(1)} %get-tuple-element.44.g0, bf16[2,256,256]{2,1,0:T(8,128)(2,1)S(1)} %collective-permute-done.6.g3), custom_call_target="tpu_custom_call" | custom-call | flops 2000000000 | bytes 6291456 | tf_op jit(solution)/shard_map/early/pallas_call | solution.py:165
  37.7 1.6 %collective-permute-done.5.g2 = bf16[2,256,256]{2,1,0:T(8,128)(2,1)S(1)} collective-permute-done((bf16[2,256,256]{2,1,0:T(8,128)(2,1)S(1)}, bf16[2,256,256]{2,1,0:T(8,128)(2,1)S(1)}, u32[]{:S(2)}, u32[]{:S(2)}) %collective-permute-start.5) | collective-permute-done | bytes 262176 | tf_op jit(solution)/shard_map/ppermute | solution.py:34
  39.3 0.0 collective-permute-done.4.r1b
  39.3 0.1 plane.1
  39.4 1.3 %collective-permute-start.12 = (bf16[2,256,256]{2,1,0:T(8,128)(2,1)S(1)}, bf16[2,256,256]{2,1,0:T(8,128)(2,1)S(1)}, u32[]{:S(2)}, u32[]{:S(2)}) collective-permute-start(bf16[2,256,256]{2,1,0:T(8,128)(2,1)S(1)} %get-tuple-element.58), channel_id=1, source_target_pairs={{1,0},{3,2},{5,4},{7,6},{9,8},{11,10},{13,12},{15,14},{17,16},{19,... | collective-permute-start | bytes 786440 | tf_op jit(solution)/shard_map/ppermute | solution.py:379
  40.7 0.0 collective-permute-done.8.r2
  40.7 1.3 %partial.1 = (f32[512,512]{1,0:T(8,128)S(1)}, bf16[512,512]{1,0:T(8,128)(2,1)S(1)}, bf16[512,512]{1,0:T(8,128)(2,1)S(1)}, bf16[512,512]{1,0:T(8,128)(2,1)S(1)}) custom-call(f32[4,512,512]{2,1,0:T(8,128)S(1)} %early.1.acc, bf16[6,256,256]{2,1,0:T(8,128)(2,1)S(1)} %collective-permute-done.3.r1a, bf16[4,256,256]{2,1,0:T(8,128)(2,1)S(1)} %collective-permute-done.4.r1b, ...), custom_call_target="tpu_custom_call" | custom-call | tf_op jit(solution)/shard_map/partial/pallas_call | solution.py:214
  42.1 1.3 %collective-permute-start.9 = (bf16[512,512]{1,0:T(8,128)(2,1)S(1)}, bf16[512,512]{1,0:T(8,128)(2,1)S(1)}, u32[]{:S(2)}, u32[]{:S(2)}) collective-permute-start(bf16[512,512]{1,0:T(8,128)(2,1)S(1)} %get-tuple-element.54), channel_id=1, source_target_pairs={{0,32},{1,5},{4,36},{5,9},{8,40},{9,13},{12,44},{13,1},{32,64},{33... | collective-permute-start | bytes 1572872 | tf_op jit(solution)/shard_map/ppermute | solution.py:34
  43.3 3.0 %collective-permute-start.10 = (bf16[512,512]{1,0:T(8,128)(2,1)S(1)}, bf16[512,512]{1,0:T(8,128)(2,1)S(1)}, u32[]{:S(2)}, u32[]{:S(2)}) collective-permute-start(bf16[512,512]{1,0:T(8,128)(2,1)S(1)} %get-tuple-element.55), channel_id=1, source_target_pairs={{0,64},{1,9},{4,68},{5,13},{8,72},{9,1},{12,76},{13,5},{32,96},{33... | collective-permute-start | bytes 1572872 | tf_op jit(solution)/shard_map/ppermute | solution.py:34
  46.3 0.6 collective-permute-start.11
  47.0 0.0 collective-permute-done.12.a_ref
  47.0 1.4 %collective-permute-start.13 = (bf16[2,256,256]{2,1,0:T(8,128)(2,1)S(1)}, bf16[2,256,256]{2,1,0:T(8,128)(2,1)S(1)}, u32[]{:S(2)}, u32[]{:S(2)}) collective-permute-start(bf16[2,256,256]{2,1,0:T(8,128)(2,1)S(1)} %picked.1.seed.a_ref), channel_id=1, source_target_pairs={{0,16},{16,0},{1,17},{17,1},{2,18},{18,2},{3,19},{19,3},{4,20},{20... | collective-permute-start | bytes 786440 | tf_op jit(solution)/shard_map/ppermute | solution.py:38
  48.4 5.6 %collective-permute-done.13.other.b_ref = bf16[2,256,256]{2,1,0:T(8,128)(2,1)S(1)} collective-permute-done((bf16[2,256,256]{2,1,0:T(8,128)(2,1)S(1)}, bf16[2,256,256]{2,1,0:T(8,128)(2,1)S(1)}, u32[]{:S(2)}, u32[]{:S(2)}) %collective-permute-start.13) | collective-permute-done | bytes 262176 | tf_op jit(solution)/shard_map/ppermute | solution.py:38
  54.0 0.9 %paired.1 = (bf16[4,256,256]{2,1,0:T(8,128)(2,1)}, bf16[2,256,256]{2,1,0:T(8,128)(2,1)}) custom-call(bf16[2,256,256]{2,1,0:T(8,128)(2,1)S(1)} %picked.1.seed.a_ref, bf16[2,256,256]{2,1,0:T(8,128)(2,1)S(1)} %collective-permute-done.13.other.b_ref), custom_call_target="tpu_custom_call" | custom-call | tf_op jit(solution)/shard_map/paired/pallas_call | solution.py:291
  54.9 0.8 collective-permute-start.14
  55.7 0.0 collective-permute-start.16
  55.7 0.0 collective-permute-done.9.b
  55.7 2.7 %collective-permute-start.17 = (bf16[4,256,256]{2,1,0:T(8,128)(2,1)}, bf16[4,256,256]{2,1,0:T(8,128)(2,1)S(1)}, u32[]{:S(2)}, u32[]{:S(2)}) collective-permute-start(bf16[4,256,256]{2,1,0:T(8,128)(2,1)} %get-tuple-element.63), channel_id=1, source_target_pairs={{0,12},{4,0},{8,4},{12,8},{1,13},{5,1},{9,5},{13,9},{2,14},{6,2},{... | collective-permute-start | bytes 1572872 | tf_op jit(solution)/shard_map/ppermute | solution.py:385
  58.4 0.4 collective-permute-done.10.c
  58.8 0.0 collective-permute-done.11.d
  58.8 1.0 %summed.1 = bf16[8,128,256]{2,1,0:T(8,128)(2,1)} custom-call(f32[512,512]{1,0:T(8,128)S(1)} %get-tuple-element.53.a, bf16[512,512]{1,0:T(8,128)(2,1)S(1)} %collective-permute-done.9.b, bf16[512,512]{1,0:T(8,128)(2,1)S(1)} %collective-permute-done.10.c, bf16[512,512]{1,0:T(8,128)(2,1)S(1)} %collective-permute-done.11.d), custom_call_target="tpu_custom_call" | custom-call | tf_op jit(solution)/shard_map/summed/pallas_call | solution.py:236
  59.8 6.6 %all-to-all-start = ((bf16[8,128,256]{2,1,0:T(8,128)(2,1)}), bf16[8,128,256]{2,1,0:T(8,128)(2,1)S(1)}, u32[]{:S(2)}, u32[]{:S(2)}) async-start(bf16[8,128,256]{2,1,0:T(8,128)(2,1)} %summed.1), calls=%async_computation | async-start | bytes 1048576 | tf_op jit(solution)/shard_map/all_to_all | solution.py:391
  66.4 4.0 %collective-permute-start.15 = (bf16[2,256,256]{2,1,0:T(8,128)(2,1)S(1)}, bf16[2,256,256]{2,1,0:T(8,128)(2,1)S(1)}, u32[]{:S(2)}, u32[]{:S(2)}) collective-permute-start(bf16[2,256,256]{2,1,0:T(8,128)(2,1)S(1)} %collective-permute-done.14.far), channel_id=1, source_target_pairs={{0,32},{1,97},{32,0},{33,65},{64,96},{65,33},{96,64},{97,1},{2,34}... | collective-permute-start | bytes 786440 | tf_op jit(solution)/shard_map/ppermute | solution.py:306
  70.4 1.8 %first_part.1.o_in = bf16[2048,4,256]{2,1,0:T(4,128)(2,1)} custom-call(bf16[512,1024]{1,0:T(8,128)(2,1)S(1)} %get-tuple-element.57.h_ref, bf16[2,256,256]{2,1,0:T(8,128)(2,1)S(1)} %picked.1.seed.a_ref, bf16[2,256,256]{2,1,0:T(8,128)(2,1)S(1)} %collective-permute-done.13.other.b_ref), custom_call_target="tpu_custom_call" | custom-call | flops 1000000 | bytes 1024 | tf_op jit(solution)/shard_map/first_part/pallas_call | solution.py:348
  72.2 2.2 %collective-permute-done.15.far_pair = bf16[2,256,256]{2,1,0:T(8,128)(2,1)S(1)} collective-permute-done((bf16[2,256,256]{2,1,0:T(8,128)(2,1)S(1)}, bf16[2,256,256]{2,1,0:T(8,128)(2,1)S(1)}, u32[]{:S(2)}, u32[]{:S(2)}) %collective-permute-start.15) | collective-permute-done | bytes 262176 | tf_op jit(solution)/shard_map/ppermute | solution.py:306
  74.5 1.8 %second_part.1.o_in = bf16[2048,4,256]{2,1,0:T(4,128)(2,1)} custom-call(bf16[2048,4,256]{2,1,0:T(4,128)(2,1)} %first_part.1.o_in, bf16[512,1024]{1,0:T(8,128)(2,1)S(1)} %get-tuple-element.57.h_ref, bf16[2,256,256]{2,1,0:T(8,128)(2,1)S(1)} %collective-permute-done.14.far, ...), custom_call_target="tpu_custom_call", output_to_operand_aliasing={{}: (0, {})} | custom-call | flops 1000000 | bytes 1024 | tf_op jit(solution)/shard_map/second_part/pallas_call | solution.py:348
  76.3 0.9 %finish.1 = bf16[128,4,256]{2,1,0:T(4,128)(2,1)} custom-call(bf16[8,128,256]{2,1,0:T(8,128)(2,1)S(1)} %all-to-all-done.r_ref), custom_call_target="tpu_custom_call" | custom-call | tf_op jit(solution)/shard_map/finish/pallas_call | solution.py:252
  77.1 0.0 collective-permute-done.16.up
  77.2 0.0 collective-permute-done.17.down
  77.2 2.6 %third_part.1 = bf16[2048,4,256]{2,1,0:T(4,128)(2,1)} custom-call(bf16[2048,4,256]{2,1,0:T(4,128)(2,1)} %second_part.1.o_in, bf16[512,1024]{1,0:T(8,128)(2,1)S(1)} %get-tuple-element.57.h_ref, bf16[4,256,256]{2,1,0:T(8,128)(2,1)S(1)} %collective-permute-done.16.up, bf16[4,256,256]{2,1,0:T(8,128)(2,1)S(1)} %collective-permute-done.17.down), custom_call_target="tpu_custom_call", output_to_operand_aliasing={{}: (0, {})} | custom-call | flops 1000000 | bytes 1024 | tf_op jit(solution)/shard_map/third_part/pallas_call | solution.py:348
  (7 shorter events, 0.0 us)
Async XLA Ops:
  0.6 7.2 %copy-start.1 = (bf16[128,256]{1,0:T(8,128)(2,1)S(1)}, bf16[128,256]{1,0:T(8,128)(2,1)}, u32[]{:S(2)}) copy-start(bf16[128,256]{1,0:T(8,128)(2,1)} %g_ref) | copy-start | bytes 196612
  0.6 7.2 %copy-start = (bf16[128,4,256]{2,1,0:T(4,128)(2,1)S(1)}, bf16[128,4,256]{2,1,0:T(4,128)(2,1)}, u32[]{:S(2)}) copy-start(bf16[128,4,256]{2,1,0:T(4,128)(2,1)} %h_ref) | copy-start | bytes 786436
  3.1 18.0 %collective-permute-start.3 = (bf16[6,256,256]{2,1,0:T(8,128)(2,1)S(1)}, bf16[6,256,256]{2,1,0:T(8,128)(2,1)S(1)}, u32[]{:S(2)}, u32[]{:S(2)}) collective-permute-start(bf16[6,256,256]{2,1,0:T(8,128)(2,1)S(1)} %get-tuple-element.39), channel_id=1, source_target_pairs={{0,4},{1,33},{4,8},{5,37},{8,12},{9,41},{12,0},{13,45},{32,36},{33... | collective-permute-start | bytes 2359304 | tf_op jit(solution)/shard_map/ppermute | solution.py:34
  5.6 30.8 %collective-permute-start.7 = (bf16[8,256,256]{2,1,0:T(8,128)(2,1)S(1)}, bf16[8,256,256]{2,1,0:T(8,128)(2,1)S(1)}, u32[]{:S(2)}, u32[]{:S(2)}) collective-permute-start(bf16[8,256,256]{2,1,0:T(8,128)(2,1)S(1)} %get-tuple-element.42), channel_id=1, source_target_pairs={{0,12},{1,97},{4,0},{5,101},{8,4},{9,105},{12,8},{13,109},{32,44},... | collective-permute-start | bytes 3145736 | tf_op jit(solution)/shard_map/ppermute | solution.py:34
  7.9 10.9 %collective-permute-start.1 = (bf16[5,128,256]{2,1,0:T(8,128)(2,1)S(1)}, bf16[5,128,256]{2,1,0:T(8,128)(2,1)S(1)}, u32[]{:S(2)}, u32[]{:S(2)}) collective-permute-start(bf16[5,128,256]{2,1,0:T(8,128)(2,1)S(1)} %packed.1.p0), channel_id=1, source_target_pairs={{0,2},{2,0},{1,3},{3,1},{4,6},{6,4},{5,7},{7,5},{8,10},{10,8},{9,1... | collective-permute-start | bytes 983048 | tf_op jit(solution)/shard_map/ppermute | solution.py:38
  10.9 29.8 %collective-permute-start.8 = (bf16[8,256,256]{2,1,0:T(8,128)(2,1)S(1)}, bf16[8,256,256]{2,1,0:T(8,128)(2,1)S(1)}, u32[]{:S(2)}, u32[]{:S(2)}) collective-permute-start(bf16[8,256,256]{2,1,0:T(8,128)(2,1)S(1)} %get-tuple-element.52), channel_id=1, source_target_pairs={{0,8},{1,65},{4,12},{5,69},{8,0},{9,73},{12,4},{13,77},{32,40},{33... | collective-permute-start | bytes 3145736 | tf_op jit(solution)/shard_map/ppermute | solution.py:34
  12.1 7.5 %collective-permute-start = (bf16[5,128,256]{2,1,0:T(8,128)(2,1)S(1)}, bf16[5,128,256]{2,1,0:T(8,128)(2,1)S(1)}, u32[]{:S(2)}, u32[]{:S(2)}) collective-permute-start(bf16[5,128,256]{2,1,0:T(8,128)(2,1)S(1)} %packed.1.p0), channel_id=1, source_target_pairs={{0,1},{1,0},{2,3},{3,2},{4,5},{5,4},{6,7},{7,6},{8,9},{9,8},{10,11... | collective-permute-start | bytes 983048 | tf_op jit(solution)/shard_map/ppermute | solution.py:38
  18.8 2.0 %collective-permute-start.2 = (bf16[5,128,256]{2,1,0:T(8,128)(2,1)S(1)}, bf16[5,128,256]{2,1,0:T(8,128)(2,1)S(1)}, u32[]{:S(2)}, u32[]{:S(2)}) collective-permute-start(bf16[5,128,256]{2,1,0:T(8,128)(2,1)S(1)} %collective-permute-done.1.p2), channel_id=1, source_target_pairs={{0,1},{1,0},{2,3},{3,2},{4,5},{5,4},{6,7},{7,6},{8,9},{9,8},{10,11... | collective-permute-start | bytes 983048 | tf_op jit(solution)/shard_map/ppermute | solution.py:38
  21.0 18.3 %collective-permute-start.4 = (bf16[4,256,256]{2,1,0:T(8,128)(2,1)S(1)}, bf16[4,256,256]{2,1,0:T(8,128)(2,1)S(1)}, u32[]{:S(2)}, u32[]{:S(2)}) collective-permute-start(bf16[4,256,256]{2,1,0:T(8,128)(2,1)S(1)} %get-tuple-element.41), channel_id=1, source_target_pairs={{0,4},{1,33},{4,8},{5,37},{8,12},{9,41},{12,0},{13,45},{32,36},{33... | collective-permute-start | bytes 1572872 | tf_op jit(solution)/shard_map/ppermute | solution.py:34
  27.4 9.0 %collective-permute-start.6 = (bf16[2,256,256]{2,1,0:T(8,128)(2,1)S(1)}, bf16[2,256,256]{2,1,0:T(8,128)(2,1)S(1)}, u32[]{:S(2)}, u32[]{:S(2)}) collective-permute-start(bf16[2,256,256]{2,1,0:T(8,128)(2,1)S(1)} %get-tuple-element.44.g0), channel_id=1, source_target_pairs={{0,12},{1,97},{4,0},{5,101},{8,4},{9,105},{12,8},{13,109},{32,44},... | collective-permute-start | bytes 786440 | tf_op jit(solution)/shard_map/ppermute | solution.py:34
  27.4 11.9 %collective-permute-start.5 = (bf16[2,256,256]{2,1,0:T(8,128)(2,1)S(1)}, bf16[2,256,256]{2,1,0:T(8,128)(2,1)S(1)}, u32[]{:S(2)}, u32[]{:S(2)}) collective-permute-start(bf16[2,256,256]{2,1,0:T(8,128)(2,1)S(1)} %get-tuple-element.44.g0), channel_id=1, source_target_pairs={{0,8},{1,65},{4,12},{5,69},{8,0},{9,73},{12,4},{13,77},{32,40},{33... | collective-permute-start | bytes 786440 | tf_op jit(solution)/shard_map/ppermute | solution.py:34
  39.4 7.6 %collective-permute-start.12 = (bf16[2,256,256]{2,1,0:T(8,128)(2,1)S(1)}, bf16[2,256,256]{2,1,0:T(8,128)(2,1)S(1)}, u32[]{:S(2)}, u32[]{:S(2)}) collective-permute-start(bf16[2,256,256]{2,1,0:T(8,128)(2,1)S(1)} %get-tuple-element.58), channel_id=1, source_target_pairs={{1,0},{3,2},{5,4},{7,6},{9,8},{11,10},{13,12},{15,14},{17,16},{19,... | collective-permute-start | bytes 786440 | tf_op jit(solution)/shard_map/ppermute | solution.py:379
  42.1 13.6 %collective-permute-start.9 = (bf16[512,512]{1,0:T(8,128)(2,1)S(1)}, bf16[512,512]{1,0:T(8,128)(2,1)S(1)}, u32[]{:S(2)}, u32[]{:S(2)}) collective-permute-start(bf16[512,512]{1,0:T(8,128)(2,1)S(1)} %get-tuple-element.54), channel_id=1, source_target_pairs={{0,32},{1,5},{4,36},{5,9},{8,40},{9,13},{12,44},{13,1},{32,64},{33... | collective-permute-start | bytes 1572872 | tf_op jit(solution)/shard_map/ppermute | solution.py:34
  43.3 15.5 %collective-permute-start.10 = (bf16[512,512]{1,0:T(8,128)(2,1)S(1)}, bf16[512,512]{1,0:T(8,128)(2,1)S(1)}, u32[]{:S(2)}, u32[]{:S(2)}) collective-permute-start(bf16[512,512]{1,0:T(8,128)(2,1)S(1)} %get-tuple-element.55), channel_id=1, source_target_pairs={{0,64},{1,9},{4,68},{5,13},{8,72},{9,1},{12,76},{13,5},{32,96},{33... | collective-permute-start | bytes 1572872 | tf_op jit(solution)/shard_map/ppermute | solution.py:34
  46.3 12.5 %collective-permute-start.11 = (bf16[512,512]{1,0:T(8,128)(2,1)S(1)}, bf16[512,512]{1,0:T(8,128)(2,1)S(1)}, u32[]{:S(2)}, u32[]{:S(2)}) collective-permute-start(bf16[512,512]{1,0:T(8,128)(2,1)S(1)} %get-tuple-element.56), channel_id=1, source_target_pairs={{0,96},{1,13},{4,100},{5,1},{8,104},{9,5},{12,108},{13,9},{32,0},{... | collective-permute-start | bytes 1572872 | tf_op jit(solution)/shard_map/ppermute | solution.py:34
  47.0 7.0 %collective-permute-start.13 = (bf16[2,256,256]{2,1,0:T(8,128)(2,1)S(1)}, bf16[2,256,256]{2,1,0:T(8,128)(2,1)S(1)}, u32[]{:S(2)}, u32[]{:S(2)}) collective-permute-start(bf16[2,256,256]{2,1,0:T(8,128)(2,1)S(1)} %picked.1.seed.a_ref), channel_id=1, source_target_pairs={{0,16},{16,0},{1,17},{17,1},{2,18},{18,2},{3,19},{19,3},{4,20},{20... | collective-permute-start | bytes 786440 | tf_op jit(solution)/shard_map/ppermute | solution.py:38
  54.9 11.5 %collective-permute-start.14 = (bf16[2,256,256]{2,1,0:T(8,128)(2,1)}, bf16[2,256,256]{2,1,0:T(8,128)(2,1)S(1)}, u32[]{:S(2)}, u32[]{:S(2)}) collective-permute-start(bf16[2,256,256]{2,1,0:T(8,128)(2,1)} %get-tuple-element.60), channel_id=1, source_target_pairs={{0,8},{4,12},{8,0},{12,4},{1,9},{5,13},{9,1},{13,5},{2,10},{6,14},... | collective-permute-start | bytes 786440 | tf_op jit(solution)/shard_map/ppermute | solution.py:385
  55.7 21.5 %collective-permute-start.16 = (bf16[4,256,256]{2,1,0:T(8,128)(2,1)}, bf16[4,256,256]{2,1,0:T(8,128)(2,1)S(1)}, u32[]{:S(2)}, u32[]{:S(2)}) collective-permute-start(bf16[4,256,256]{2,1,0:T(8,128)(2,1)} %get-tuple-element.63), channel_id=1, source_target_pairs={{0,4},{4,8},{8,12},{12,0},{1,5},{5,9},{9,13},{13,1},{2,6},{6,10},{... | collective-permute-start | bytes 1572872 | tf_op jit(solution)/shard_map/ppermute | solution.py:385
  55.7 21.5 %collective-permute-start.17 = (bf16[4,256,256]{2,1,0:T(8,128)(2,1)}, bf16[4,256,256]{2,1,0:T(8,128)(2,1)S(1)}, u32[]{:S(2)}, u32[]{:S(2)}) collective-permute-start(bf16[4,256,256]{2,1,0:T(8,128)(2,1)} %get-tuple-element.63), channel_id=1, source_target_pairs={{0,12},{4,0},{8,4},{12,8},{1,13},{5,1},{9,5},{13,9},{2,14},{6,2},{... | collective-permute-start | bytes 1572872 | tf_op jit(solution)/shard_map/ppermute | solution.py:385
  59.8 16.4 %all-to-all-start = ((bf16[8,128,256]{2,1,0:T(8,128)(2,1)}), bf16[8,128,256]{2,1,0:T(8,128)(2,1)S(1)}, u32[]{:S(2)}, u32[]{:S(2)}) async-start(bf16[8,128,256]{2,1,0:T(8,128)(2,1)} %summed.1), calls=%async_computation | async-start | bytes 1048576 | tf_op jit(solution)/shard_map/all_to_all | solution.py:391
  66.4 8.0 %collective-permute-start.15 = (bf16[2,256,256]{2,1,0:T(8,128)(2,1)S(1)}, bf16[2,256,256]{2,1,0:T(8,128)(2,1)S(1)}, u32[]{:S(2)}, u32[]{:S(2)}) collective-permute-start(bf16[2,256,256]{2,1,0:T(8,128)(2,1)S(1)} %collective-permute-done.14.far), channel_id=1, source_target_pairs={{0,32},{1,97},{32,0},{33,65},{64,96},{65,33},{96,64},{97,1},{2,34}... | collective-permute-start | bytes 786440 | tf_op jit(solution)/shard_map/ppermute | solution.py:306

commit v15 on v14

--- a/solution.py
+++ b/solution.py
@@ -243,22 +243,6 @@
     )(parts[0], *kept(*parts[1:]))
 
 
-def finish_body(r_ref, o_ref):
-    r = [(r_ref[n].astype(F32) + r_ref[4 + n].astype(F32)).astype(BF) for n in range(4)]
-    o_ref[...] = jnp.concatenate(r, axis=1).reshape(128, 4, 256)
-
-
-def finished(blocks):
-    return pl.pallas_call(
-        finish_body,
-        out_shape=jax.ShapeDtypeStruct((128, 4, 256), BF),
-        in_specs=[IN],
-        out_specs=IN,
-        compiler_params=LIMIT,
-        name="finish",
-    )(*kept(blocks))
-
-
 def picked_body(a_ref, b_ref, o_ref):
     @pl.when(lax.axis_index("c") == 0)
     def _():
@@ -335,12 +319,38 @@
     outer_into([(here, 2, far), (1 - here, 2, far_pair)], h_ref, *refs)
 
 
-def third_part_body(o_in, h_ref, up, down, *refs):
+def last_part_body(o_in, h_ref, up, down, r_ref, o_ref, d_ref, buf, sems, d_buf, d_sem):
+    r = [(r_ref[n].astype(F32) + r_ref[4 + n].astype(F32)).astype(BF) for n in range(4)]
+    d_buf[...] = jnp.concatenate(r, axis=1).reshape(128, 4, 256)
+    copy = pltpu.make_async_copy(d_buf, d_ref, d_sem.at[0])
+    copy.start()
     yl = lax.axis_index("yl")
     blocks = []
     for k, ref in ((1, up), (3, down)):
         blocks += [(yl, k, ref.at[0:2]), (1 - yl, k, ref.at[2:4])]
-    outer_into(blocks, h_ref, *refs)
+    outer_into(blocks, h_ref, o_ref, buf, sems)
+    copy.wait()
+
+
+def last_part(operands, so_far):
+    return pl.pallas_call(
+        last_part_body,
+        out_shape=[
+            jax.ShapeDtypeStruct((2048, 4, 256), BF),
+            jax.ShapeDtypeStruct((128, 4, 256), BF),
+        ],
+        in_specs=[HBM] + [IN] * len(operands),
+        out_specs=[HBM, HBM],
+        scratch_shapes=[
+            VM((4, 256, 4, 256), BF),
+            pltpu.SemaphoreType.DMA((4,)),
+            VM((128, 4, 256), BF),
+            pltpu.SemaphoreType.DMA((1,)),
+        ],
+        input_output_aliases={0: 0},
+        compiler_params=LIMIT,
+        name="last_part",
+    )(so_far, *kept(*operands))
 
 
 def outer_part(body, name, operands, so_far=None):
@@ -391,9 +401,8 @@
     blocks = lax.all_to_all(blocks, ("yl", "yh", "c"), 0, 0, tiled=True)
     part = outer_part(first_part_body, "first_part", (h, seed, other))
     part = outer_part(second_part_body, "second_part", (h, far, far_pair), part)
-    blocks, part = lax.optimization_barrier((blocks, part))
-    grad_weight = outer_part(third_part_body, "third_part", (h, up, down), part)
-    return finished(blocks), grad_weight
+    grad_weight, grad_hidden = last_part((h, up, down, blocks), part)
+    return grad_hidden, grad_weight
 
 
 def solution(mesh):

time: 80.2 us -> 79.5 us (level)
    pallas_call x3 -> x2, Pallas kernels: 6.22 us -> 3.6 us  [outer_part(): pl.pallas_call(body, out_shape=jax.ShapeDtypeStruct((2048, 4, 256), BF),...]
    pallas_call x1, Pallas kernels: 0.86 us -> 2.76 us  [last_part(): pl.pallas_call(last_part_body, out_shape=[jax.ShapeDtypeStruct((2048, 4,...]
  transfers between devices with their start and end apart: 19 -> 19, of which waited for: 7 -> 7; matrix products, arithmetic and copies ran while one was open for 0% -> 0% of each run, Pallas kernels for 12% -> 11%
where the time goes in v15:
time: 79.5 us; the launch traced here: 79.2 us
  starting transfers between devices  42.6 us (54%)
  waiting for transfers between devices  22 us (28%)
  Pallas kernels  13.7 us (17%)
  between operations  0.93 us (1%)
    ppermute x9, starting transfers between devices, shift(): return lax.ppermute(value, ('z', 'x', 'c'), pairs)  21.2 us
    ppermute x4, waiting for transfers between devices, swap(): return lax.ppermute(value, axis, [(0, 1), (1, 0)])  12.7 us
    ppermute x9, waiting for transfers between devices, shift(): return lax.ppermute(value, ('z', 'x', 'c'), pairs)  7.06 us
    all_to_all x1, starting transfers between devices, per_device(): blocks = lax.all_to_all(blocks, ('yl', 'yh', 'c'), 0, 0, tiled=True)  6.61 us
    ppermute x4, starting transfers between devices, swap(): return lax.ppermute(value, axis, [(0, 1), (1, 0)])  6.08 us
    ppermute x1, starting transfers between devices, z_pairs(): return lax.ppermute(value, ('z', 'c'), pairs)  3.98 us
    pallas_call x2, Pallas kernels, outer_part(): pl.pallas_call(body, out_shape=jax.ShapeDtypeStruct((2048, 4, 256), BF),...  3.6 us
    ppermute x3, starting transfers between devices, per_device(): lax.ppermute(value, 'x', [(i, (i + k) % 4) for i in range(4)])  3.48 us
  transfers between devices with their start and end apart: 19, of which 7 were waited for; matrix products, arithmetic and copies ran while one was open for 0% of the time, Pallas kernels for 11%

profile of v15, /device:TPU:1, one launch (start us, length us, event | category | flops | bytes accessed | tf_op | source)
XLA Modules:
  0.0 79.2 jit_solution(3764265562769829112)
XLA Ops:
  0.7 2.4 %scale.1 = (bf16[8,256,256]{2,1,0:T(8,128)(2,1)S(1)}, bf16[6,256,256]{2,1,0:T(8,128)(2,1)S(1)}, bf16[2,256,256]{2,1,0:T(8,128)(2,1)S(1)}, bf16[8,256,256]{2,1,0:T(8,128)(2,1)S(1)}, bf16[8,256,256]{2,1,0:T(8,128)(2,1)S(1)}) custom-call(bf16[4,2,4,256,256]{4,3,2,1,0:T(8,128)(2,1)} %bitcast.2, bf16[16,512]{1,0:T(8,128)(2,1)} %bitcast.3), custom_call_target="tpu_custom_call" | custom-call | tf_op jit(solution)/shard_map/scale/pallas_call | solution.py:95
  3.1 2.5 %collective-permute-start.3 = (bf16[6,256,256]{2,1,0:T(8,128)(2,1)S(1)}, bf16[6,256,256]{2,1,0:T(8,128)(2,1)S(1)}, u32[]{:S(2)}, u32[]{:S(2)}) collective-permute-start(bf16[6,256,256]{2,1,0:T(8,128)(2,1)S(1)} %get-tuple-element.40), channel_id=1, source_target_pairs={{0,4},{1,33},{4,8},{5,37},{8,12},{9,41},{12,0},{13,45},{32,36},{33... | collective-permute-start | bytes 2359304 | tf_op jit(solution)/shard_map/ppermute | solution.py:34
  5.6 2.2 %collective-permute-start.7 = (bf16[8,256,256]{2,1,0:T(8,128)(2,1)S(1)}, bf16[8,256,256]{2,1,0:T(8,128)(2,1)S(1)}, u32[]{:S(2)}, u32[]{:S(2)}) collective-permute-start(bf16[8,256,256]{2,1,0:T(8,128)(2,1)S(1)} %get-tuple-element.43), channel_id=1, source_target_pairs={{0,12},{1,97},{4,0},{5,101},{8,4},{9,105},{12,8},{13,109},{32,44},... | collective-permute-start | bytes 3145736 | tf_op jit(solution)/shard_map/ppermute | solution.py:34
  7.8 0.1 packed.1.p0
  7.9 3.0 %collective-permute-start.1 = (bf16[5,128,256]{2,1,0:T(8,128)(2,1)S(1)}, bf16[5,128,256]{2,1,0:T(8,128)(2,1)S(1)}, u32[]{:S(2)}, u32[]{:S(2)}) collective-permute-start(bf16[5,128,256]{2,1,0:T(8,128)(2,1)S(1)} %packed.1.p0), channel_id=1, source_target_pairs={{0,2},{2,0},{1,3},{3,1},{4,6},{6,4},{5,7},{7,5},{8,10},{10,8},{9,1... | collective-permute-start | bytes 983048 | tf_op jit(solution)/shard_map/ppermute | solution.py:38
  10.9 1.2 %collective-permute-start.14 = (bf16[8,256,256]{2,1,0:T(8,128)(2,1)S(1)}, bf16[8,256,256]{2,1,0:T(8,128)(2,1)S(1)}, u32[]{:S(2)}, u32[]{:S(2)}) collective-permute-start(bf16[8,256,256]{2,1,0:T(8,128)(2,1)S(1)} %get-tuple-element.57), channel_id=1, source_target_pairs={{0,8},{1,65},{4,12},{5,69},{8,0},{9,73},{12,4},{13,77},{32,40},{33... | collective-permute-start | bytes 3145736 | tf_op jit(solution)/shard_map/ppermute | solution.py:34
  12.1 0.9 %collective-permute-start = (bf16[5,128,256]{2,1,0:T(8,128)(2,1)S(1)}, bf16[5,128,256]{2,1,0:T(8,128)(2,1)S(1)}, u32[]{:S(2)}, u32[]{:S(2)}) collective-permute-start(bf16[5,128,256]{2,1,0:T(8,128)(2,1)S(1)} %packed.1.p0), channel_id=1, source_target_pairs={{0,1},{1,0},{2,3},{3,2},{4,5},{5,4},{6,7},{7,6},{8,9},{9,8},{10,11... | collective-permute-start | bytes 983048 | tf_op jit(solution)/shard_map/ppermute | solution.py:38
  13.0 5.8 %collective-permute-done.1.p2 = bf16[5,128,256]{2,1,0:T(8,128)(2,1)S(1)} collective-permute-done((bf16[5,128,256]{2,1,0:T(8,128)(2,1)S(1)}, bf16[5,128,256]{2,1,0:T(8,128)(2,1)S(1)}, u32[]{:S(2)}, u32[]{:S(2)}) %collective-permute-start.1) | collective-permute-done | bytes 327712 | tf_op jit(solution)/shard_map/ppermute | solution.py:38
  18.8 0.8 collective-permute-start.2
  19.6 0.0 collective-permute-done.p1
  19.6 1.3 %collective-permute-done.2.p3 = bf16[5,128,256]{2,1,0:T(8,128)(2,1)S(1)} collective-permute-done((bf16[5,128,256]{2,1,0:T(8,128)(2,1)S(1)}, bf16[5,128,256]{2,1,0:T(8,128)(2,1)S(1)}, u32[]{:S(2)}, u32[]{:S(2)}) %collective-permute-start.2) | collective-permute-done | bytes 327712 | tf_op jit(solution)/shard_map/ppermute | solution.py:38
  20.9 0.2 tokens.1
  21.0 0.0 collective-permute-done.3.r1a
  21.0 6.4 %collective-permute-start.4 = (bf16[4,256,256]{2,1,0:T(8,128)(2,1)S(1)}, bf16[4,256,256]{2,1,0:T(8,128)(2,1)S(1)}, u32[]{:S(2)}, u32[]{:S(2)}) collective-permute-start(bf16[4,256,256]{2,1,0:T(8,128)(2,1)S(1)} %get-tuple-element.42), channel_id=1, source_target_pairs={{0,4},{1,33},{4,8},{5,37},{8,12},{9,41},{12,0},{13,45},{32,36},{33... | collective-permute-start | bytes 1572872 | tf_op jit(solution)/shard_map/ppermute | solution.py:34
  27.4 0.0 collective-permute-start.6
  27.4 4.0 %collective-permute-start.5 = (bf16[2,256,256]{2,1,0:T(8,128)(2,1)S(1)}, bf16[2,256,256]{2,1,0:T(8,128)(2,1)S(1)}, u32[]{:S(2)}, u32[]{:S(2)}) collective-permute-start(bf16[2,256,256]{2,1,0:T(8,128)(2,1)S(1)} %get-tuple-element.45.g0), channel_id=1, source_target_pairs={{0,8},{1,65},{4,12},{5,69},{8,0},{9,73},{12,4},{13,77},{32,40},{33... | collective-permute-start | bytes 786440 | tf_op jit(solution)/shard_map/ppermute | solution.py:34
  31.4 5.0 %collective-permute-done.6.g3 = bf16[2,256,256]{2,1,0:T(8,128)(2,1)S(1)} collective-permute-done((bf16[2,256,256]{2,1,0:T(8,128)(2,1)S(1)}, bf16[2,256,256]{2,1,0:T(8,128)(2,1)S(1)}, u32[]{:S(2)}, u32[]{:S(2)}) %collective-permute-start.6) | collective-permute-done | bytes 262176 | tf_op jit(solution)/shard_map/ppermute | solution.py:34
  36.4 0.0 collective-permute-done.7.r3
  36.4 1.3 %early.1.acc = f32[4,512,512]{2,1,0:T(8,128)S(1)} custom-call(bf16[8,256,256]{2,1,0:T(8,128)(2,1)S(1)} %get-tuple-element.34.r0, bf16[8,256,256]{2,1,0:T(8,128)(2,1)S(1)} %collective-permute-done.7.r3, bf16[2,256,256]{2,1,0:T(8,128)(2,1)S(1)} %get-tuple-element.45.g0, bf16[2,256,256]{2,1,0:T(8,128)(2,1)S(1)} %collective-permute-done.6.g3), custom_call_target="tpu_custom_call" | custom-call | flops 2000000000 | bytes 6291456 | tf_op jit(solution)/shard_map/early/pallas_call | solution.py:165
  37.7 1.6 %collective-permute-done.5.g2 = bf16[2,256,256]{2,1,0:T(8,128)(2,1)S(1)} collective-permute-done((bf16[2,256,256]{2,1,0:T(8,128)(2,1)S(1)}, bf16[2,256,256]{2,1,0:T(8,128)(2,1)S(1)}, u32[]{:S(2)}, u32[]{:S(2)}) %collective-permute-start.5) | collective-permute-done | bytes 262176 | tf_op jit(solution)/shard_map/ppermute | solution.py:34
  39.3 0.0 collective-permute-done.4.r1b
  39.3 0.1 plane.1
  39.4 1.3 %collective-permute-start.8 = (bf16[2,256,256]{2,1,0:T(8,128)(2,1)S(1)}, bf16[2,256,256]{2,1,0:T(8,128)(2,1)S(1)}, u32[]{:S(2)}, u32[]{:S(2)}) collective-permute-start(bf16[2,256,256]{2,1,0:T(8,128)(2,1)S(1)} %get-tuple-element.51), channel_id=1, source_target_pairs={{1,0},{3,2},{5,4},{7,6},{9,8},{11,10},{13,12},{15,14},{17,16},{19,... | collective-permute-start | bytes 786440 | tf_op jit(solution)/shard_map/ppermute | solution.py:389
  40.7 0.0 collective-permute-done.14.r2
  40.7 1.3 %partial.1 = (f32[512,512]{1,0:T(8,128)S(1)}, bf16[512,512]{1,0:T(8,128)(2,1)S(1)}, bf16[512,512]{1,0:T(8,128)(2,1)S(1)}, bf16[512,512]{1,0:T(8,128)(2,1)S(1)}) custom-call(f32[4,512,512]{2,1,0:T(8,128)S(1)} %early.1.acc, bf16[6,256,256]{2,1,0:T(8,128)(2,1)S(1)} %collective-permute-done.3.r1a, bf16[4,256,256]{2,1,0:T(8,128)(2,1)S(1)} %collective-permute-done.4.r1b, ...), custom_call_target="tpu_custom_call" | custom-call | tf_op jit(solution)/shard_map/partial/pallas_call | solution.py:214
  42.1 1.3 %collective-permute-start.15 = (bf16[512,512]{1,0:T(8,128)(2,1)S(1)}, bf16[512,512]{1,0:T(8,128)(2,1)S(1)}, u32[]{:S(2)}, u32[]{:S(2)}) collective-permute-start(bf16[512,512]{1,0:T(8,128)(2,1)S(1)} %get-tuple-element.59), channel_id=1, source_target_pairs={{0,32},{1,5},{4,36},{5,9},{8,40},{9,13},{12,44},{13,1},{32,64},{33... | collective-permute-start | bytes 1572872 | tf_op jit(solution)/shard_map/ppermute | solution.py:34
  43.3 3.0 %collective-permute-start.16 = (bf16[512,512]{1,0:T(8,128)(2,1)S(1)}, bf16[512,512]{1,0:T(8,128)(2,1)S(1)}, u32[]{:S(2)}, u32[]{:S(2)}) collective-permute-start(bf16[512,512]{1,0:T(8,128)(2,1)S(1)} %get-tuple-element.60), channel_id=1, source_target_pairs={{0,64},{1,9},{4,68},{5,13},{8,72},{9,1},{12,76},{13,5},{32,96},{33... | collective-permute-start | bytes 1572872 | tf_op jit(solution)/shard_map/ppermute | solution.py:34
  46.3 0.6 collective-permute-start.17
  46.9 0.0 collective-permute-done.8.a_ref
  47.0 1.4 %collective-permute-start.9 = (bf16[2,256,256]{2,1,0:T(8,128)(2,1)S(1)}, bf16[2,256,256]{2,1,0:T(8,128)(2,1)S(1)}, u32[]{:S(2)}, u32[]{:S(2)}) collective-permute-start(bf16[2,256,256]{2,1,0:T(8,128)(2,1)S(1)} %picked.1.seed.a_ref), channel_id=1, source_target_pairs={{0,16},{16,0},{1,17},{17,1},{2,18},{18,2},{3,19},{19,3},{4,20},{20... | collective-permute-start | bytes 786440 | tf_op jit(solution)/shard_map/ppermute | solution.py:38
  48.3 5.6 %collective-permute-done.9.other.b_ref = bf16[2,256,256]{2,1,0:T(8,128)(2,1)S(1)} collective-permute-done((bf16[2,256,256]{2,1,0:T(8,128)(2,1)S(1)}, bf16[2,256,256]{2,1,0:T(8,128)(2,1)S(1)}, u32[]{:S(2)}, u32[]{:S(2)}) %collective-permute-start.9) | collective-permute-done | bytes 262176 | tf_op jit(solution)/shard_map/ppermute | solution.py:38
  54.0 0.9 %paired.1 = (bf16[4,256,256]{2,1,0:T(8,128)(2,1)}, bf16[2,256,256]{2,1,0:T(8,128)(2,1)}) custom-call(bf16[2,256,256]{2,1,0:T(8,128)(2,1)S(1)} %picked.1.seed.a_ref, bf16[2,256,256]{2,1,0:T(8,128)(2,1)S(1)} %collective-permute-done.9.other.b_ref), custom_call_target="tpu_custom_call" | custom-call | tf_op jit(solution)/shard_map/paired/pallas_call | solution.py:275
  54.9 0.8 %collective-permute-start.10 = (bf16[2,256,256]{2,1,0:T(8,128)(2,1)}, bf16[2,256,256]{2,1,0:T(8,128)(2,1)S(1)}, u32[]{:S(2)}, u32[]{:S(2)}) collective-permute-start(bf16[2,256,256]{2,1,0:T(8,128)(2,1)} %get-tuple-element.53), channel_id=1, source_target_pairs={{0,8},{4,12},{8,0},{12,4},{1,9},{5,13},{9,1},{13,5},{2,10},{6,14},... | collective-permute-start | bytes 786440 | tf_op jit(solution)/shard_map/ppermute | solution.py:395
  55.7 0.0 collective-permute-start.12
  55.7 0.0 collective-permute-done.15.b
  55.7 2.7 %collective-permute-start.13 = (bf16[4,256,256]{2,1,0:T(8,128)(2,1)}, bf16[4,256,256]{2,1,0:T(8,128)(2,1)S(1)}, u32[]{:S(2)}, u32[]{:S(2)}) collective-permute-start(bf16[4,256,256]{2,1,0:T(8,128)(2,1)} %get-tuple-element.54), channel_id=1, source_target_pairs={{0,12},{4,0},{8,4},{12,8},{1,13},{5,1},{9,5},{13,9},{2,14},{6,2},{... | collective-permute-start | bytes 1572872 | tf_op jit(solution)/shard_map/ppermute | solution.py:395
  58.4 0.4 collective-permute-done.16.c
  58.8 0.0 collective-permute-done.17.d
  58.8 1.0 %summed.1 = bf16[8,128,256]{2,1,0:T(8,128)(2,1)} custom-call(f32[512,512]{1,0:T(8,128)S(1)} %get-tuple-element.58.a, bf16[512,512]{1,0:T(8,128)(2,1)S(1)} %collective-permute-done.15.b, bf16[512,512]{1,0:T(8,128)(2,1)S(1)} %collective-permute-done.16.c, bf16[512,512]{1,0:T(8,128)(2,1)S(1)} %collective-permute-done.17.d), custom_call_target="tpu_custom_call" | custom-call | tf_op jit(solution)/shard_map/summed/pallas_call | solution.py:236
  59.8 6.6 %all-to-all-start = ((bf16[8,128,256]{2,1,0:T(8,128)(2,1)}), bf16[8,128,256]{2,1,0:T(8,128)(2,1)S(1)}, u32[]{:S(2)}, u32[]{:S(2)}) async-start(bf16[8,128,256]{2,1,0:T(8,128)(2,1)} %summed.1), calls=%async_computation | async-start | bytes 1048576 | tf_op jit(solution)/shard_map/all_to_all | solution.py:401
  66.4 0.0 collective-permute-done.10.far
  66.4 4.0 %collective-permute-start.11 = (bf16[2,256,256]{2,1,0:T(8,128)(2,1)S(1)}, bf16[2,256,256]{2,1,0:T(8,128)(2,1)S(1)}, u32[]{:S(2)}, u32[]{:S(2)}) collective-permute-start(bf16[2,256,256]{2,1,0:T(8,128)(2,1)S(1)} %collective-permute-done.10.far), channel_id=1, source_target_pairs={{0,32},{1,97},{32,0},{33,65},{64,96},{65,33},{96,64},{97,1},{2,34}... | collective-permute-start | bytes 786440 | tf_op jit(solution)/shard_map/ppermute | solution.py:290
  70.4 1.8 %first_part.1.o_in = bf16[2048,4,256]{2,1,0:T(4,128)(2,1)} custom-call(bf16[512,1024]{1,0:T(8,128)(2,1)S(1)} %get-tuple-element.37.h_ref, bf16[2,256,256]{2,1,0:T(8,128)(2,1)S(1)} %picked.1.seed.a_ref, bf16[2,256,256]{2,1,0:T(8,128)(2,1)S(1)} %collective-permute-done.9.other.b_ref), custom_call_target="tpu_custom_call" | custom-call | flops 1000000 | bytes 1024 | tf_op jit(solution)/shard_map/first_part/pallas_call | solution.py:358
  72.2 2.2 %collective-permute-done.11.far_pair = bf16[2,256,256]{2,1,0:T(8,128)(2,1)S(1)} collective-permute-done((bf16[2,256,256]{2,1,0:T(8,128)(2,1)S(1)}, bf16[2,256,256]{2,1,0:T(8,128)(2,1)S(1)}, u32[]{:S(2)}, u32[]{:S(2)}) %collective-permute-start.11) | collective-permute-done | bytes 262176 | tf_op jit(solution)/shard_map/ppermute | solution.py:290
  74.5 1.8 %second_part.1.o_in = bf16[2048,4,256]{2,1,0:T(4,128)(2,1)} custom-call(bf16[2048,4,256]{2,1,0:T(4,128)(2,1)} %first_part.1.o_in, bf16[512,1024]{1,0:T(8,128)(2,1)S(1)} %get-tuple-element.37.h_ref, bf16[2,256,256]{2,1,0:T(8,128)(2,1)S(1)} %collective-permute-done.10.far, ...), custom_call_target="tpu_custom_call", output_to_operand_aliasing={{}: (0, {})} | custom-call | flops 1000000 | bytes 1024 | tf_op jit(solution)/shard_map/second_part/pallas_call | solution.py:358
  76.3 0.0 all-to-all-done.r_ref
  76.3 0.0 collective-permute-done.12.up
  76.3 2.8 %last_part.1 = (bf16[2048,4,256]{2,1,0:T(4,128)(2,1)}, bf16[128,4,256]{2,1,0:T(4,128)(2,1)}) custom-call(bf16[2048,4,256]{2,1,0:T(4,128)(2,1)} %second_part.1.o_in, bf16[512,1024]{1,0:T(8,128)(2,1)S(1)} %get-tuple-element.37.h_ref, bf16[4,256,256]{2,1,0:T(8,128)(2,1)S(1)} %collective-permute-done.12.up, ...), custom_call_target="tpu_custom_call", output_to_operand_aliasing={{0}: (0, {})} | custom-call | tf_op jit(solution)/shard_map/last_part/pallas_call | solution.py:336
  (6 shorter events, 0.0 us)
Async XLA Ops:
  0.6 7.2 %copy-start = (bf16[128,4,256]{2,1,0:T(4,128)(2,1)S(1)}, bf16[128,4,256]{2,1,0:T(4,128)(2,1)}, u32[]{:S(2)}) copy-start(bf16[128,4,256]{2,1,0:T(4,128)(2,1)} %h_ref) | copy-start | bytes 786436
  0.6 7.2 %copy-start.1 = (bf16[128,256]{1,0:T(8,128)(2,1)S(1)}, bf16[128,256]{1,0:T(8,128)(2,1)}, u32[]{:S(2)}) copy-start(bf16[128,256]{1,0:T(8,128)(2,1)} %g_ref) | copy-start | bytes 196612
  3.1 18.0 %collective-permute-start.3 = (bf16[6,256,256]{2,1,0:T(8,128)(2,1)S(1)}, bf16[6,256,256]{2,1,0:T(8,128)(2,1)S(1)}, u32[]{:S(2)}, u32[]{:S(2)}) collective-permute-start(bf16[6,256,256]{2,1,0:T(8,128)(2,1)S(1)} %get-tuple-element.40), channel_id=1, source_target_pairs={{0,4},{1,33},{4,8},{5,37},{8,12},{9,41},{12,0},{13,45},{32,36},{33... | collective-permute-start | bytes 2359304 | tf_op jit(solution)/shard_map/ppermute | solution.py:34
  5.6 30.8 %collective-permute-start.7 = (bf16[8,256,256]{2,1,0:T(8,128)(2,1)S(1)}, bf16[8,256,256]{2,1,0:T(8,128)(2,1)S(1)}, u32[]{:S(2)}, u32[]{:S(2)}) collective-permute-start(bf16[8,256,256]{2,1,0:T(8,128)(2,1)S(1)} %get-tuple-element.43), channel_id=1, source_target_pairs={{0,12},{1,97},{4,0},{5,101},{8,4},{9,105},{12,8},{13,109},{32,44},... | collective-permute-start | bytes 3145736 | tf_op jit(solution)/shard_map/ppermute | solution.py:34
  7.9 10.9 %collective-permute-start.1 = (bf16[5,128,256]{2,1,0:T(8,128)(2,1)S(1)}, bf16[5,128,256]{2,1,0:T(8,128)(2,1)S(1)}, u32[]{:S(2)}, u32[]{:S(2)}) collective-permute-start(bf16[5,128,256]{2,1,0:T(8,128)(2,1)S(1)} %packed.1.p0), channel_id=1, source_target_pairs={{0,2},{2,0},{1,3},{3,1},{4,6},{6,4},{5,7},{7,5},{8,10},{10,8},{9,1... | collective-permute-start | bytes 983048 | tf_op jit(solution)/shard_map/ppermute | solution.py:38
  10.9 29.8 %collective-permute-start.14 = (bf16[8,256,256]{2,1,0:T(8,128)(2,1)S(1)}, bf16[8,256,256]{2,1,0:T(8,128)(2,1)S(1)}, u32[]{:S(2)}, u32[]{:S(2)}) collective-permute-start(bf16[8,256,256]{2,1,0:T(8,128)(2,1)S(1)} %get-tuple-element.57), channel_id=1, source_target_pairs={{0,8},{1,65},{4,12},{5,69},{8,0},{9,73},{12,4},{13,77},{32,40},{33... | collective-permute-start | bytes 3145736 | tf_op jit(solution)/shard_map/ppermute | solution.py:34
  12.1 7.5 %collective-permute-start = (bf16[5,128,256]{2,1,0:T(8,128)(2,1)S(1)}, bf16[5,128,256]{2,1,0:T(8,128)(2,1)S(1)}, u32[]{:S(2)}, u32[]{:S(2)}) collective-permute-start(bf16[5,128,256]{2,1,0:T(8,128)(2,1)S(1)} %packed.1.p0), channel_id=1, source_target_pairs={{0,1},{1,0},{2,3},{3,2},{4,5},{5,4},{6,7},{7,6},{8,9},{9,8},{10,11... | collective-permute-start | bytes 983048 | tf_op jit(solution)/shard_map/ppermute | solution.py:38
  18.8 2.0 %collective-permute-start.2 = (bf16[5,128,256]{2,1,0:T(8,128)(2,1)S(1)}, bf16[5,128,256]{2,1,0:T(8,128)(2,1)S(1)}, u32[]{:S(2)}, u32[]{:S(2)}) collective-permute-start(bf16[5,128,256]{2,1,0:T(8,128)(2,1)S(1)} %collective-permute-done.1.p2), channel_id=1, source_target_pairs={{0,1},{1,0},{2,3},{3,2},{4,5},{5,4},{6,7},{7,6},{8,9},{9,8},{10,11... | collective-permute-start | bytes 983048 | tf_op jit(solution)/shard_map/ppermute | solution.py:38
  21.0 18.3 %collective-permute-start.4 = (bf16[4,256,256]{2,1,0:T(8,128)(2,1)S(1)}, bf16[4,256,256]{2,1,0:T(8,128)(2,1)S(1)}, u32[]{:S(2)}, u32[]{:S(2)}) collective-permute-start(bf16[4,256,256]{2,1,0:T(8,128)(2,1)S(1)} %get-tuple-element.42), channel_id=1, source_target_pairs={{0,4},{1,33},{4,8},{5,37},{8,12},{9,41},{12,0},{13,45},{32,36},{33... | collective-permute-start | bytes 1572872 | tf_op jit(solution)/shard_map/ppermute | solution.py:34
  27.4 9.0 %collective-permute-start.6 = (bf16[2,256,256]{2,1,0:T(8,128)(2,1)S(1)}, bf16[2,256,256]{2,1,0:T(8,128)(2,1)S(1)}, u32[]{:S(2)}, u32[]{:S(2)}) collective-permute-start(bf16[2,256,256]{2,1,0:T(8,128)(2,1)S(1)} %get-tuple-element.45.g0), channel_id=1, source_target_pairs={{0,12},{1,97},{4,0},{5,101},{8,4},{9,105},{12,8},{13,109},{32,44},... | collective-permute-start | bytes 786440 | tf_op jit(solution)/shard_map/ppermute | solution.py:34
  27.4 11.9 %collective-permute-start.5 = (bf16[2,256,256]{2,1,0:T(8,128)(2,1)S(1)}, bf16[2,256,256]{2,1,0:T(8,128)(2,1)S(1)}, u32[]{:S(2)}, u32[]{:S(2)}) collective-permute-start(bf16[2,256,256]{2,1,0:T(8,128)(2,1)S(1)} %get-tuple-element.45.g0), channel_id=1, source_target_pairs={{0,8},{1,65},{4,12},{5,69},{8,0},{9,73},{12,4},{13,77},{32,40},{33... | collective-permute-start | bytes 786440 | tf_op jit(solution)/shard_map/ppermute | solution.py:34
  39.4 7.6 %collective-permute-start.8 = (bf16[2,256,256]{2,1,0:T(8,128)(2,1)S(1)}, bf16[2,256,256]{2,1,0:T(8,128)(2,1)S(1)}, u32[]{:S(2)}, u32[]{:S(2)}) collective-permute-start(bf16[2,256,256]{2,1,0:T(8,128)(2,1)S(1)} %get-tuple-element.51), channel_id=1, source_target_pairs={{1,0},{3,2},{5,4},{7,6},{9,8},{11,10},{13,12},{15,14},{17,16},{19,... | collective-permute-start | bytes 786440 | tf_op jit(solution)/shard_map/ppermute | solution.py:389
  42.1 13.6 %collective-permute-start.15 = (bf16[512,512]{1,0:T(8,128)(2,1)S(1)}, bf16[512,512]{1,0:T(8,128)(2,1)S(1)}, u32[]{:S(2)}, u32[]{:S(2)}) collective-permute-start(bf16[512,512]{1,0:T(8,128)(2,1)S(1)} %get-tuple-element.59), channel_id=1, source_target_pairs={{0,32},{1,5},{4,36},{5,9},{8,40},{9,13},{12,44},{13,1},{32,64},{33... | collective-permute-start | bytes 1572872 | tf_op jit(solution)/shard_map/ppermute | solution.py:34
  43.3 15.5 %collective-permute-start.16 = (bf16[512,512]{1,0:T(8,128)(2,1)S(1)}, bf16[512,512]{1,0:T(8,128)(2,1)S(1)}, u32[]{:S(2)}, u32[]{:S(2)}) collective-permute-start(bf16[512,512]{1,0:T(8,128)(2,1)S(1)} %get-tuple-element.60), channel_id=1, source_target_pairs={{0,64},{1,9},{4,68},{5,13},{8,72},{9,1},{12,76},{13,5},{32,96},{33... | collective-permute-start | bytes 1572872 | tf_op jit(solution)/shard_map/ppermute | solution.py:34
  46.3 12.5 %collective-permute-start.17 = (bf16[512,512]{1,0:T(8,128)(2,1)S(1)}, bf16[512,512]{1,0:T(8,128)(2,1)S(1)}, u32[]{:S(2)}, u32[]{:S(2)}) collective-permute-start(bf16[512,512]{1,0:T(8,128)(2,1)S(1)} %get-tuple-element.61), channel_id=1, source_target_pairs={{0,96},{1,13},{4,100},{5,1},{8,104},{9,5},{12,108},{13,9},{32,0},{... | collective-permute-start | bytes 1572872 | tf_op jit(solution)/shard_map/ppermute | solution.py:34
  47.0 7.0 %collective-permute-start.9 = (bf16[2,256,256]{2,1,0:T(8,128)(2,1)S(1)}, bf16[2,256,256]{2,1,0:T(8,128)(2,1)S(1)}, u32[]{:S(2)}, u32[]{:S(2)}) collective-permute-start(bf16[2,256,256]{2,1,0:T(8,128)(2,1)S(1)} %picked.1.seed.a_ref), channel_id=1, source_target_pairs={{0,16},{16,0},{1,17},{17,1},{2,18},{18,2},{3,19},{19,3},{4,20},{20... | collective-permute-start | bytes 786440 | tf_op jit(solution)/shard_map/ppermute | solution.py:38
  54.9 11.5 %collective-permute-start.10 = (bf16[2,256,256]{2,1,0:T(8,128)(2,1)}, bf16[2,256,256]{2,1,0:T(8,128)(2,1)S(1)}, u32[]{:S(2)}, u32[]{:S(2)}) collective-permute-start(bf16[2,256,256]{2,1,0:T(8,128)(2,1)} %get-tuple-element.53), channel_id=1, source_target_pairs={{0,8},{4,12},{8,0},{12,4},{1,9},{5,13},{9,1},{13,5},{2,10},{6,14},... | collective-permute-start | bytes 786440 | tf_op jit(solution)/shard_map/ppermute | solution.py:395
  55.7 20.6 %collective-permute-start.12 = (bf16[4,256,256]{2,1,0:T(8,128)(2,1)}, bf16[4,256,256]{2,1,0:T(8,128)(2,1)S(1)}, u32[]{:S(2)}, u32[]{:S(2)}) collective-permute-start(bf16[4,256,256]{2,1,0:T(8,128)(2,1)} %get-tuple-element.54), channel_id=1, source_target_pairs={{0,4},{4,8},{8,12},{12,0},{1,5},{5,9},{9,13},{13,1},{2,6},{6,10},{... | collective-permute-start | bytes 1572872 | tf_op jit(solution)/shard_map/ppermute | solution.py:395
  55.7 20.6 %collective-permute-start.13 = (bf16[4,256,256]{2,1,0:T(8,128)(2,1)}, bf16[4,256,256]{2,1,0:T(8,128)(2,1)S(1)}, u32[]{:S(2)}, u32[]{:S(2)}) collective-permute-start(bf16[4,256,256]{2,1,0:T(8,128)(2,1)} %get-tuple-element.54), channel_id=1, source_target_pairs={{0,12},{4,0},{8,4},{12,8},{1,13},{5,1},{9,5},{13,9},{2,14},{6,2},{... | collective-permute-start | bytes 1572872 | tf_op jit(solution)/shard_map/ppermute | solution.py:395
  59.8 16.5 %all-to-all-start = ((bf16[8,128,256]{2,1,0:T(8,128)(2,1)}), bf16[8,128,256]{2,1,0:T(8,128)(2,1)S(1)}, u32[]{:S(2)}, u32[]{:S(2)}) async-start(bf16[8,128,256]{2,1,0:T(8,128)(2,1)} %summed.1), calls=%async_computation | async-start | bytes 1048576 | tf_op jit(solution)/shard_map/all_to_all | solution.py:401
  66.4 8.0 %collective-permute-start.11 = (bf16[2,256,256]{2,1,0:T(8,128)(2,1)S(1)}, bf16[2,256,256]{2,1,0:T(8,128)(2,1)S(1)}, u32[]{:S(2)}, u32[]{:S(2)}) collective-permute-start(bf16[2,256,256]{2,1,0:T(8,128)(2,1)S(1)} %collective-permute-done.10.far), channel_id=1, source_target_pairs={{0,32},{1,97},{32,0},{33,65},{64,96},{65,33},{96,64},{97,1},{2,34}... | collective-permute-start | bytes 786440 | tf_op jit(solution)/shard_map/ppermute | solution.py:290

commit v16 on v15

--- a/solution.py
+++ b/solution.py
@@ -309,14 +309,18 @@
         copy.wait()
 
 
-def first_part_body(h_ref, seed, other, *refs):
+def own_part_body(h_ref, seed, *refs):
+    outer_into([(lax.axis_index("yl"), 0, seed)], h_ref, *refs)
+
+
+def first_part_body(o_in, h_ref, other, far, *refs):
     yl = lax.axis_index("yl")
-    outer_into([(yl, 0, seed), (1 - yl, 0, other)], h_ref, *refs)
-
-
-def second_part_body(o_in, h_ref, far, far_pair, *refs):
+    outer_into([(1 - yl, 0, other), (yl ^ (lax.axis_index("z") & 1), 2, far)], h_ref, *refs)
+
+
+def second_part_body(o_in, h_ref, far_pair, *refs):
     here = lax.axis_index("yl") ^ (lax.axis_index("z") & 1)
-    outer_into([(here, 2, far), (1 - here, 2, far_pair)], h_ref, *refs)
+    outer_into([(1 - here, 2, far_pair)], h_ref, *refs)
 
 
 def last_part_body(o_in, h_ref, up, down, r_ref, o_ref, d_ref, buf, sems, d_buf, d_sem):
@@ -391,6 +395,8 @@
     parts = [sums[0]] + [None] * 3
     for k in (1, 3, 2):
         parts[k] = shift(sums[k], second_axis_steps(k))
+    part = outer_part(own_part_body, "own_part", (h, seed))
+    other, part = lax.optimization_barrier((other, part))
     both, one = paired(seed, other)
     along_x = lambda value, k: lax.ppermute(value, "x", [(i, (i + k) % 4) for i in range(4)])
     far = along_x(one, 2)
@@ -399,8 +405,8 @@
 
     blocks = summed_blocks(parts)
     blocks = lax.all_to_all(blocks, ("yl", "yh", "c"), 0, 0, tiled=True)
-    part = outer_part(first_part_body, "first_part", (h, seed, other))
-    part = outer_part(second_part_body, "second_part", (h, far, far_pair), part)
+    part = outer_part(first_part_body, "first_part", (h, other, far), part)
+    part = outer_part(second_part_body, "second_part", (h, far_pair), part)
     grad_weight, grad_hidden = last_part((h, up, down, blocks), part)
     return grad_hidden, grad_weight
 

time: 79.5 us -> 79.3 us (level)
  Pallas kernels: 13.7 us -> 14.6 us
  waiting for transfers between devices: 22 us -> 21.2 us
    ppermute x4, waiting for transfers between devices: 12.7 us -> 11.3 us  [swap(): return lax.ppermute(value, axis, [(0, 1), (1, 0)])]
    pallas_call x2 -> x3, Pallas kernels: 3.6 us -> 4.59 us  [outer_part(): pl.pallas_call(body, out_shape=jax.ShapeDtypeStruct((2048, 4, 256), BF),...]
  transfers between devices with their start and end apart: 19 -> 19, of which waited for: 7 -> 7; matrix products, arithmetic and copies ran while one was open for 0% -> 0% of each run, Pallas kernels for 11% -> 12%
where the time goes in v16:
time: 79.3 us; the launch traced here: 79.1 us
  starting transfers between devices  42.3 us (53%)
  waiting for transfers between devices  21.2 us (27%)
  Pallas kernels  14.6 us (18%)
  between operations  0.94 us (1%)
    ppermute x9, starting transfers between devices, shift(): return lax.ppermute(value, ('z', 'x', 'c'), pairs)  21.2 us
    ppermute x4, waiting for transfers between devices, swap(): return lax.ppermute(value, axis, [(0, 1), (1, 0)])  11.3 us
    ppermute x9, waiting for transfers between devices, shift(): return lax.ppermute(value, ('z', 'x', 'c'), pairs)  7.68 us
    all_to_all x1, starting transfers between devices, per_device(): blocks = lax.all_to_all(blocks, ('yl', 'yh', 'c'), 0, 0, tiled=True)  6.19 us
    ppermute x4, starting transfers between devices, swap(): return lax.ppermute(value, axis, [(0, 1), (1, 0)])  6.07 us
    ppermute x1, starting transfers between devices, z_pairs(): return lax.ppermute(value, ('z', 'c'), pairs)  4.62 us
    pallas_call x3, Pallas kernels, outer_part(): pl.pallas_call(body, out_shape=jax.ShapeDtypeStruct((2048, 4, 256), BF),...  4.59 us
    ppermute x3, starting transfers between devices, per_device(): lax.ppermute(value, 'x', [(i, (i + k) % 4) for i in range(4)])  2.91 us
  transfers between devices with their start and end apart: 19, of which 7 were waited for; matrix products, arithmetic and copies ran while one was open for 0% of the time, Pallas kernels for 12%

profile of v16, /device:TPU:1, one launch (start us, length us, event | category | flops | bytes accessed | tf_op | source)
XLA Modules:
  0.0 79.1 jit_solution(6745833213167292745)
XLA Ops:
  0.7 2.4 %scale.1 = (bf16[8,256,256]{2,1,0:T(8,128)(2,1)S(1)}, bf16[6,256,256]{2,1,0:T(8,128)(2,1)S(1)}, bf16[2,256,256]{2,1,0:T(8,128)(2,1)S(1)}, bf16[8,256,256]{2,1,0:T(8,128)(2,1)S(1)}, bf16[8,256,256]{2,1,0:T(8,128)(2,1)S(1)}) custom-call(bf16[4,2,4,256,256]{4,3,2,1,0:T(8,128)(2,1)} %bitcast.2, bf16[16,512]{1,0:T(8,128)(2,1)} %bitcast.3), custom_call_target="tpu_custom_call" | custom-call | tf_op jit(solution)/shard_map/scale/pallas_call | solution.py:95
  3.1 2.5 %collective-permute-start.3 = (bf16[6,256,256]{2,1,0:T(8,128)(2,1)S(1)}, bf16[6,256,256]{2,1,0:T(8,128)(2,1)S(1)}, u32[]{:S(2)}, u32[]{:S(2)}) collective-permute-start(bf16[6,256,256]{2,1,0:T(8,128)(2,1)S(1)} %get-tuple-element.41), channel_id=1, source_target_pairs={{0,4},{1,33},{4,8},{5,37},{8,12},{9,41},{12,0},{13,45},{32,36},{33... | collective-permute-start | bytes 2359304 | tf_op jit(solution)/shard_map/ppermute | solution.py:34
  5.6 2.2 %collective-permute-start.7 = (bf16[8,256,256]{2,1,0:T(8,128)(2,1)S(1)}, bf16[8,256,256]{2,1,0:T(8,128)(2,1)S(1)}, u32[]{:S(2)}, u32[]{:S(2)}) collective-permute-start(bf16[8,256,256]{2,1,0:T(8,128)(2,1)S(1)} %get-tuple-element.44), channel_id=1, source_target_pairs={{0,12},{1,97},{4,0},{5,101},{8,4},{9,105},{12,8},{13,109},{32,44},... | collective-permute-start | bytes 3145736 | tf_op jit(solution)/shard_map/ppermute | solution.py:34
  7.8 0.1 packed.1.p0
  7.9 3.0 %collective-permute-start.1 = (bf16[5,128,256]{2,1,0:T(8,128)(2,1)S(1)}, bf16[5,128,256]{2,1,0:T(8,128)(2,1)S(1)}, u32[]{:S(2)}, u32[]{:S(2)}) collective-permute-start(bf16[5,128,256]{2,1,0:T(8,128)(2,1)S(1)} %packed.1.p0), channel_id=1, source_target_pairs={{0,2},{2,0},{1,3},{3,1},{4,6},{6,4},{5,7},{7,5},{8,10},{10,8},{9,1... | collective-permute-start | bytes 983048 | tf_op jit(solution)/shard_map/ppermute | solution.py:38
  10.9 1.2 %collective-permute-start.14 = (bf16[8,256,256]{2,1,0:T(8,128)(2,1)S(1)}, bf16[8,256,256]{2,1,0:T(8,128)(2,1)S(1)}, u32[]{:S(2)}, u32[]{:S(2)}) collective-permute-start(bf16[8,256,256]{2,1,0:T(8,128)(2,1)S(1)} %get-tuple-element.61), channel_id=1, source_target_pairs={{0,8},{1,65},{4,12},{5,69},{8,0},{9,73},{12,4},{13,77},{32,40},{33... | collective-permute-start | bytes 3145736 | tf_op jit(solution)/shard_map/ppermute | solution.py:34
  12.1 0.9 %collective-permute-start = (bf16[5,128,256]{2,1,0:T(8,128)(2,1)S(1)}, bf16[5,128,256]{2,1,0:T(8,128)(2,1)S(1)}, u32[]{:S(2)}, u32[]{:S(2)}) collective-permute-start(bf16[5,128,256]{2,1,0:T(8,128)(2,1)S(1)} %packed.1.p0), channel_id=1, source_target_pairs={{0,1},{1,0},{2,3},{3,2},{4,5},{5,4},{6,7},{7,6},{8,9},{9,8},{10,11... | collective-permute-start | bytes 983048 | tf_op jit(solution)/shard_map/ppermute | solution.py:38
  13.0 5.8 %collective-permute-done.1.p2 = bf16[5,128,256]{2,1,0:T(8,128)(2,1)S(1)} collective-permute-done((bf16[5,128,256]{2,1,0:T(8,128)(2,1)S(1)}, bf16[5,128,256]{2,1,0:T(8,128)(2,1)S(1)}, u32[]{:S(2)}, u32[]{:S(2)}) %collective-permute-start.1) | collective-permute-done | bytes 327712 | tf_op jit(solution)/shard_map/ppermute | solution.py:38
  18.8 0.8 collective-permute-start.2
  19.6 0.0 collective-permute-done.p1
  19.6 1.3 %collective-permute-done.2.p3 = bf16[5,128,256]{2,1,0:T(8,128)(2,1)S(1)} collective-permute-done((bf16[5,128,256]{2,1,0:T(8,128)(2,1)S(1)}, bf16[5,128,256]{2,1,0:T(8,128)(2,1)S(1)}, u32[]{:S(2)}, u32[]{:S(2)}) %collective-permute-start.2) | collective-permute-done | bytes 327712 | tf_op jit(solution)/shard_map/ppermute | solution.py:38
  20.9 0.2 tokens.1
  21.0 0.0 collective-permute-done.3.r1a
  21.0 6.4 %collective-permute-start.4 = (bf16[4,256,256]{2,1,0:T(8,128)(2,1)S(1)}, bf16[4,256,256]{2,1,0:T(8,128)(2,1)S(1)}, u32[]{:S(2)}, u32[]{:S(2)}) collective-permute-start(bf16[4,256,256]{2,1,0:T(8,128)(2,1)S(1)} %get-tuple-element.43), channel_id=1, source_target_pairs={{0,4},{1,33},{4,8},{5,37},{8,12},{9,41},{12,0},{13,45},{32,36},{33... | collective-permute-start | bytes 1572872 | tf_op jit(solution)/shard_map/ppermute | solution.py:34
  27.4 0.0 collective-permute-start.6
  27.4 4.0 %collective-permute-start.5 = (bf16[2,256,256]{2,1,0:T(8,128)(2,1)S(1)}, bf16[2,256,256]{2,1,0:T(8,128)(2,1)S(1)}, u32[]{:S(2)}, u32[]{:S(2)}) collective-permute-start(bf16[2,256,256]{2,1,0:T(8,128)(2,1)S(1)} %get-tuple-element.46.g0), channel_id=1, source_target_pairs={{0,8},{1,65},{4,12},{5,69},{8,0},{9,73},{12,4},{13,77},{32,40},{33... | collective-permute-start | bytes 786440 | tf_op jit(solution)/shard_map/ppermute | solution.py:34
  31.4 5.0 %collective-permute-done.6.g3 = bf16[2,256,256]{2,1,0:T(8,128)(2,1)S(1)} collective-permute-done((bf16[2,256,256]{2,1,0:T(8,128)(2,1)S(1)}, bf16[2,256,256]{2,1,0:T(8,128)(2,1)S(1)}, u32[]{:S(2)}, u32[]{:S(2)}) %collective-permute-start.6) | collective-permute-done | bytes 262176 | tf_op jit(solution)/shard_map/ppermute | solution.py:34
  36.4 0.0 collective-permute-done.7.r3
  36.4 1.3 %early.1.acc = f32[4,512,512]{2,1,0:T(8,128)S(1)} custom-call(bf16[8,256,256]{2,1,0:T(8,128)(2,1)S(1)} %get-tuple-element.36.r0, bf16[8,256,256]{2,1,0:T(8,128)(2,1)S(1)} %collective-permute-done.7.r3, bf16[2,256,256]{2,1,0:T(8,128)(2,1)S(1)} %get-tuple-element.46.g0, bf16[2,256,256]{2,1,0:T(8,128)(2,1)S(1)} %collective-permute-done.6.g3), custom_call_target="tpu_custom_call" | custom-call | flops 2000000000 | bytes 6291456 | tf_op jit(solution)/shard_map/early/pallas_call | solution.py:165
  37.7 1.6 %collective-permute-done.5.g2 = bf16[2,256,256]{2,1,0:T(8,128)(2,1)S(1)} collective-permute-done((bf16[2,256,256]{2,1,0:T(8,128)(2,1)S(1)}, bf16[2,256,256]{2,1,0:T(8,128)(2,1)S(1)}, u32[]{:S(2)}, u32[]{:S(2)}) %collective-permute-start.5) | collective-permute-done | bytes 262176 | tf_op jit(solution)/shard_map/ppermute | solution.py:34
  39.3 0.0 collective-permute-done.4.r1b
  39.3 0.1 plane.1
  39.4 1.3 %collective-permute-start.8 = (bf16[2,256,256]{2,1,0:T(8,128)(2,1)S(1)}, bf16[2,256,256]{2,1,0:T(8,128)(2,1)S(1)}, u32[]{:S(2)}, u32[]{:S(2)}) collective-permute-start(bf16[2,256,256]{2,1,0:T(8,128)(2,1)S(1)} %get-tuple-element.52), channel_id=1, source_target_pairs={{1,0},{3,2},{5,4},{7,6},{9,8},{11,10},{13,12},{15,14},{17,16},{19,... | collective-permute-start | bytes 786440 | tf_op jit(solution)/shard_map/ppermute | solution.py:393
  40.7 0.0 collective-permute-done.14.r2
  40.7 1.3 %partial.1 = (f32[512,512]{1,0:T(8,128)S(1)}, bf16[512,512]{1,0:T(8,128)(2,1)S(1)}, bf16[512,512]{1,0:T(8,128)(2,1)S(1)}, bf16[512,512]{1,0:T(8,128)(2,1)S(1)}) custom-call(f32[4,512,512]{2,1,0:T(8,128)S(1)} %early.1.acc, bf16[6,256,256]{2,1,0:T(8,128)(2,1)S(1)} %collective-permute-done.3.r1a, bf16[4,256,256]{2,1,0:T(8,128)(2,1)S(1)} %collective-permute-done.4.r1b, ...), custom_call_target="tpu_custom_call" | custom-call | tf_op jit(solution)/shard_map/partial/pallas_call | solution.py:214
  42.1 1.3 %collective-permute-start.15 = (bf16[512,512]{1,0:T(8,128)(2,1)S(1)}, bf16[512,512]{1,0:T(8,128)(2,1)S(1)}, u32[]{:S(2)}, u32[]{:S(2)}) collective-permute-start(bf16[512,512]{1,0:T(8,128)(2,1)S(1)} %get-tuple-element.63), channel_id=1, source_target_pairs={{0,32},{1,5},{4,36},{5,9},{8,40},{9,13},{12,44},{13,1},{32,64},{33... | collective-permute-start | bytes 1572872 | tf_op jit(solution)/shard_map/ppermute | solution.py:34
  43.3 3.0 %collective-permute-start.16 = (bf16[512,512]{1,0:T(8,128)(2,1)S(1)}, bf16[512,512]{1,0:T(8,128)(2,1)S(1)}, u32[]{:S(2)}, u32[]{:S(2)}) collective-permute-start(bf16[512,512]{1,0:T(8,128)(2,1)S(1)} %get-tuple-element.64), channel_id=1, source_target_pairs={{0,64},{1,9},{4,68},{5,13},{8,72},{9,1},{12,76},{13,5},{32,96},{33... | collective-permute-start | bytes 1572872 | tf_op jit(solution)/shard_map/ppermute | solution.py:34
  46.3 0.6 collective-permute-start.17
  47.0 0.0 collective-permute-done.8.a_ref
  47.0 1.4 %collective-permute-start.9 = (bf16[2,256,256]{2,1,0:T(8,128)(2,1)S(1)}, bf16[2,256,256]{2,1,0:T(8,128)(2,1)S(1)}, u32[]{:S(2)}, u32[]{:S(2)}) collective-permute-start(bf16[2,256,256]{2,1,0:T(8,128)(2,1)S(1)} %picked.1.seed.a_ref), channel_id=1, source_target_pairs={{0,16},{16,0},{1,17},{17,1},{2,18},{18,2},{3,19},{19,3},{4,20},{20... | collective-permute-start | bytes 786440 | tf_op jit(solution)/shard_map/ppermute | solution.py:38
  48.4 1.4 %own_part.1.o_in = bf16[2048,4,256]{2,1,0:T(4,128)(2,1)} custom-call(bf16[512,1024]{1,0:T(8,128)(2,1)S(1)} %get-tuple-element.54.h_ref, bf16[2,256,256]{2,1,0:T(8,128)(2,1)S(1)} %picked.1.seed.a_ref), custom_call_target="tpu_custom_call" | custom-call | flops 1000000 | bytes 1024 | tf_op jit(solution)/shard_map/own_part/pallas_call | solution.py:362
  49.8 4.2 %collective-permute-done.9.b_ref.other = bf16[2,256,256]{2,1,0:T(8,128)(2,1)S(1)} collective-permute-done((bf16[2,256,256]{2,1,0:T(8,128)(2,1)S(1)}, bf16[2,256,256]{2,1,0:T(8,128)(2,1)S(1)}, u32[]{:S(2)}, u32[]{:S(2)}) %collective-permute-start.9) | collective-permute-done | bytes 262176 | tf_op jit(solution)/shard_map/ppermute | solution.py:38
  54.0 0.8 %paired.1 = (bf16[4,256,256]{2,1,0:T(8,128)(2,1)}, bf16[2,256,256]{2,1,0:T(8,128)(2,1)S(1)}) custom-call(bf16[2,256,256]{2,1,0:T(8,128)(2,1)S(1)} %picked.1.seed.a_ref, bf16[2,256,256]{2,1,0:T(8,128)(2,1)S(1)} %collective-permute-done.9.b_ref.other), custom_call_target="tpu_custom_call" | custom-call | tf_op jit(solution)/shard_map/paired/pallas_call | solution.py:275
  54.8 0.8 collective-permute-start.10
  55.6 2.1 %collective-permute-start.13 = (bf16[4,256,256]{2,1,0:T(8,128)(2,1)}, bf16[4,256,256]{2,1,0:T(8,128)(2,1)S(1)}, u32[]{:S(2)}, u32[]{:S(2)}) collective-permute-start(bf16[4,256,256]{2,1,0:T(8,128)(2,1)} %get-tuple-element.58), channel_id=1, source_target_pairs={{0,12},{4,0},{8,4},{12,8},{1,13},{5,1},{9,5},{13,9},{2,14},{6,2},{... | collective-permute-start | bytes 1572872 | tf_op jit(solution)/shard_map/ppermute | solution.py:401
  57.7 0.0 collective-permute-done.15.b
  57.7 0.0 collective-permute-start.12
  57.8 1.0 %collective-permute-done.16.c = bf16[512,512]{1,0:T(8,128)(2,1)S(1)} collective-permute-done((bf16[512,512]{1,0:T(8,128)(2,1)S(1)}, bf16[512,512]{1,0:T(8,128)(2,1)S(1)}, u32[]{:S(2)}, u32[]{:S(2)}) %collective-permute-start.16) | collective-permute-done | bytes 524320 | tf_op jit(solution)/shard_map/ppermute | solution.py:34
  58.8 1.0 %summed.1 = bf16[8,128,256]{2,1,0:T(8,128)(2,1)} custom-call(f32[512,512]{1,0:T(8,128)S(1)} %get-tuple-element.62.a, bf16[512,512]{1,0:T(8,128)(2,1)S(1)} %collective-permute-done.15.b, bf16[512,512]{1,0:T(8,128)(2,1)S(1)} %collective-permute-done.16.c, bf16[512,512]{1,0:T(8,128)(2,1)S(1)} %collective-permute-done.17.d), custom_call_target="tpu_custom_call" | custom-call | tf_op jit(solution)/shard_map/summed/pallas_call | solution.py:236
  59.8 6.2 %all-to-all-start = ((bf16[8,128,256]{2,1,0:T(8,128)(2,1)}), bf16[8,128,256]{2,1,0:T(8,128)(2,1)S(1)}, u32[]{:S(2)}, u32[]{:S(2)}) async-start(bf16[8,128,256]{2,1,0:T(8,128)(2,1)} %summed.1), calls=%async_computation | async-start | bytes 1048576 | tf_op jit(solution)/shard_map/all_to_all | solution.py:407
  66.0 0.0 collective-permute-done.10.far
  66.0 4.6 %collective-permute-start.11 = (bf16[2,256,256]{2,1,0:T(8,128)(2,1)S(1)}, bf16[2,256,256]{2,1,0:T(8,128)(2,1)S(1)}, u32[]{:S(2)}, u32[]{:S(2)}) collective-permute-start(bf16[2,256,256]{2,1,0:T(8,128)(2,1)S(1)} %collective-permute-done.10.far), channel_id=1, source_target_pairs={{0,32},{1,97},{32,0},{33,65},{64,96},{65,33},{96,64},{97,1},{2,34}... | collective-permute-start | bytes 786440 | tf_op jit(solution)/shard_map/ppermute | solution.py:290
  70.6 1.8 %first_part.1.o_in = bf16[2048,4,256]{2,1,0:T(4,128)(2,1)} custom-call(bf16[2048,4,256]{2,1,0:T(4,128)(2,1)} %own_part.1.o_in, bf16[512,1024]{1,0:T(8,128)(2,1)S(1)} %get-tuple-element.54.h_ref, bf16[2,256,256]{2,1,0:T(8,128)(2,1)S(1)} %collective-permute-done.9.b_ref.other, ...), custom_call_target="tpu_custom_call", output_to_operand_aliasing={{}: (0, {})} | custom-call | flops 1000000 | bytes 1024 | tf_op jit(solution)/shard_map/first_part/pallas_call | solution.py:362
  72.5 2.2 %collective-permute-done.11.far_pair = bf16[2,256,256]{2,1,0:T(8,128)(2,1)S(1)} collective-permute-done((bf16[2,256,256]{2,1,0:T(8,128)(2,1)S(1)}, bf16[2,256,256]{2,1,0:T(8,128)(2,1)S(1)}, u32[]{:S(2)}, u32[]{:S(2)}) %collective-permute-start.11) | collective-permute-done | bytes 262176 | tf_op jit(solution)/shard_map/ppermute | solution.py:290
  74.7 1.4 %second_part.1.o_in = bf16[2048,4,256]{2,1,0:T(4,128)(2,1)} custom-call(bf16[2048,4,256]{2,1,0:T(4,128)(2,1)} %first_part.1.o_in, bf16[512,1024]{1,0:T(8,128)(2,1)S(1)} %get-tuple-element.54.h_ref, bf16[2,256,256]{2,1,0:T(8,128)(2,1)S(1)} %collective-permute-done.11.far_pair), custom_call_target="tpu_custom_call", output_to_operand_aliasing={{}: (0, {})} | custom-call | flops 1000000 | bytes 1024 | tf_op jit(solution)/shard_map/second_part/pallas_call | solution.py:362
  76.1 0.0 all-to-all-done.r_ref
  76.1 0.0 collective-permute-done.13.down
  76.1 2.8 %last_part.1 = (bf16[2048,4,256]{2,1,0:T(4,128)(2,1)}, bf16[128,4,256]{2,1,0:T(4,128)(2,1)}) custom-call(bf16[2048,4,256]{2,1,0:T(4,128)(2,1)} %second_part.1.o_in, bf16[512,1024]{1,0:T(8,128)(2,1)S(1)} %get-tuple-element.54.h_ref, bf16[4,256,256]{2,1,0:T(8,128)(2,1)S(1)} %collective-permute-done.12.up, ...), custom_call_target="tpu_custom_call", output_to_operand_aliasing={{0}: (0, {})} | custom-call | tf_op jit(solution)/shard_map/last_part/pallas_call | solution.py:340
  (7 shorter events, 0.0 us)
Async XLA Ops:
  0.6 7.2 %copy-start.1 = (bf16[128,256]{1,0:T(8,128)(2,1)S(1)}, bf16[128,256]{1,0:T(8,128)(2,1)}, u32[]{:S(2)}) copy-start(bf16[128,256]{1,0:T(8,128)(2,1)} %g_ref) | copy-start | bytes 196612
  0.6 7.2 %copy-start = (bf16[128,4,256]{2,1,0:T(4,128)(2,1)S(1)}, bf16[128,4,256]{2,1,0:T(4,128)(2,1)}, u32[]{:S(2)}) copy-start(bf16[128,4,256]{2,1,0:T(4,128)(2,1)} %h_ref) | copy-start | bytes 786436
  3.1 18.0 %collective-permute-start.3 = (bf16[6,256,256]{2,1,0:T(8,128)(2,1)S(1)}, bf16[6,256,256]{2,1,0:T(8,128)(2,1)S(1)}, u32[]{:S(2)}, u32[]{:S(2)}) collective-permute-start(bf16[6,256,256]{2,1,0:T(8,128)(2,1)S(1)} %get-tuple-element.41), channel_id=1, source_target_pairs={{0,4},{1,33},{4,8},{5,37},{8,12},{9,41},{12,0},{13,45},{32,36},{33... | collective-permute-start | bytes 2359304 | tf_op jit(solution)/shard_map/ppermute | solution.py:34
  5.6 30.8 %collective-permute-start.7 = (bf16[8,256,256]{2,1,0:T(8,128)(2,1)S(1)}, bf16[8,256,256]{2,1,0:T(8,128)(2,1)S(1)}, u32[]{:S(2)}, u32[]{:S(2)}) collective-permute-start(bf16[8,256,256]{2,1,0:T(8,128)(2,1)S(1)} %get-tuple-element.44), channel_id=1, source_target_pairs={{0,12},{1,97},{4,0},{5,101},{8,4},{9,105},{12,8},{13,109},{32,44},... | collective-permute-start | bytes 3145736 | tf_op jit(solution)/shard_map/ppermute | solution.py:34
  7.9 10.9 %collective-permute-start.1 = (bf16[5,128,256]{2,1,0:T(8,128)(2,1)S(1)}, bf16[5,128,256]{2,1,0:T(8,128)(2,1)S(1)}, u32[]{:S(2)}, u32[]{:S(2)}) collective-permute-start(bf16[5,128,256]{2,1,0:T(8,128)(2,1)S(1)} %packed.1.p0), channel_id=1, source_target_pairs={{0,2},{2,0},{1,3},{3,1},{4,6},{6,4},{5,7},{7,5},{8,10},{10,8},{9,1... | collective-permute-start | bytes 983048 | tf_op jit(solution)/shard_map/ppermute | solution.py:38
  10.9 29.8 %collective-permute-start.14 = (bf16[8,256,256]{2,1,0:T(8,128)(2,1)S(1)}, bf16[8,256,256]{2,1,0:T(8,128)(2,1)S(1)}, u32[]{:S(2)}, u32[]{:S(2)}) collective-permute-start(bf16[8,256,256]{2,1,0:T(8,128)(2,1)S(1)} %get-tuple-element.61), channel_id=1, source_target_pairs={{0,8},{1,65},{4,12},{5,69},{8,0},{9,73},{12,4},{13,77},{32,40},{33... | collective-permute-start | bytes 3145736 | tf_op jit(solution)/shard_map/ppermute | solution.py:34
  12.1 7.5 %collective-permute-start = (bf16[5,128,256]{2,1,0:T(8,128)(2,1)S(1)}, bf16[5,128,256]{2,1,0:T(8,128)(2,1)S(1)}, u32[]{:S(2)}, u32[]{:S(2)}) collective-permute-start(bf16[5,128,256]{2,1,0:T(8,128)(2,1)S(1)} %packed.1.p0), channel_id=1, source_target_pairs={{0,1},{1,0},{2,3},{3,2},{4,5},{5,4},{6,7},{7,6},{8,9},{9,8},{10,11... | collective-permute-start | bytes 983048 | tf_op jit(solution)/shard_map/ppermute | solution.py:38
  18.8 2.0 %collective-permute-start.2 = (bf16[5,128,256]{2,1,0:T(8,128)(2,1)S(1)}, bf16[5,128,256]{2,1,0:T(8,128)(2,1)S(1)}, u32[]{:S(2)}, u32[]{:S(2)}) collective-permute-start(bf16[5,128,256]{2,1,0:T(8,128)(2,1)S(1)} %collective-permute-done.1.p2), channel_id=1, source_target_pairs={{0,1},{1,0},{2,3},{3,2},{4,5},{5,4},{6,7},{7,6},{8,9},{9,8},{10,11... | collective-permute-start | bytes 983048 | tf_op jit(solution)/shard_map/ppermute | solution.py:38
  21.0 18.3 %collective-permute-start.4 = (bf16[4,256,256]{2,1,0:T(8,128)(2,1)S(1)}, bf16[4,256,256]{2,1,0:T(8,128)(2,1)S(1)}, u32[]{:S(2)}, u32[]{:S(2)}) collective-permute-start(bf16[4,256,256]{2,1,0:T(8,128)(2,1)S(1)} %get-tuple-element.43), channel_id=1, source_target_pairs={{0,4},{1,33},{4,8},{5,37},{8,12},{9,41},{12,0},{13,45},{32,36},{33... | collective-permute-start | bytes 1572872 | tf_op jit(solution)/shard_map/ppermute | solution.py:34
  27.4 9.0 %collective-permute-start.6 = (bf16[2,256,256]{2,1,0:T(8,128)(2,1)S(1)}, bf16[2,256,256]{2,1,0:T(8,128)(2,1)S(1)}, u32[]{:S(2)}, u32[]{:S(2)}) collective-permute-start(bf16[2,256,256]{2,1,0:T(8,128)(2,1)S(1)} %get-tuple-element.46.g0), channel_id=1, source_target_pairs={{0,12},{1,97},{4,0},{5,101},{8,4},{9,105},{12,8},{13,109},{32,44},... | collective-permute-start | bytes 786440 | tf_op jit(solution)/shard_map/ppermute | solution.py:34
  27.4 11.9 %collective-permute-start.5 = (bf16[2,256,256]{2,1,0:T(8,128)(2,1)S(1)}, bf16[2,256,256]{2,1,0:T(8,128)(2,1)S(1)}, u32[]{:S(2)}, u32[]{:S(2)}) collective-permute-start(bf16[2,256,256]{2,1,0:T(8,128)(2,1)S(1)} %get-tuple-element.46.g0), channel_id=1, source_target_pairs={{0,8},{1,65},{4,12},{5,69},{8,0},{9,73},{12,4},{13,77},{32,40},{33... | collective-permute-start | bytes 786440 | tf_op jit(solution)/shard_map/ppermute | solution.py:34
  39.4 7.6 %collective-permute-start.8 = (bf16[2,256,256]{2,1,0:T(8,128)(2,1)S(1)}, bf16[2,256,256]{2,1,0:T(8,128)(2,1)S(1)}, u32[]{:S(2)}, u32[]{:S(2)}) collective-permute-start(bf16[2,256,256]{2,1,0:T(8,128)(2,1)S(1)} %get-tuple-element.52), channel_id=1, source_target_pairs={{1,0},{3,2},{5,4},{7,6},{9,8},{11,10},{13,12},{15,14},{17,16},{19,... | collective-permute-start | bytes 786440 | tf_op jit(solution)/shard_map/ppermute | solution.py:393
  42.1 15.7 %collective-permute-start.15 = (bf16[512,512]{1,0:T(8,128)(2,1)S(1)}, bf16[512,512]{1,0:T(8,128)(2,1)S(1)}, u32[]{:S(2)}, u32[]{:S(2)}) collective-permute-start(bf16[512,512]{1,0:T(8,128)(2,1)S(1)} %get-tuple-element.63), channel_id=1, source_target_pairs={{0,32},{1,5},{4,36},{5,9},{8,40},{9,13},{12,44},{13,1},{32,64},{33... | collective-permute-start | bytes 1572872 | tf_op jit(solution)/shard_map/ppermute | solution.py:34
  43.3 15.5 %collective-permute-start.16 = (bf16[512,512]{1,0:T(8,128)(2,1)S(1)}, bf16[512,512]{1,0:T(8,128)(2,1)S(1)}, u32[]{:S(2)}, u32[]{:S(2)}) collective-permute-start(bf16[512,512]{1,0:T(8,128)(2,1)S(1)} %get-tuple-element.64), channel_id=1, source_target_pairs={{0,64},{1,9},{4,68},{5,13},{8,72},{9,1},{12,76},{13,5},{32,96},{33... | collective-permute-start | bytes 1572872 | tf_op jit(solution)/shard_map/ppermute | solution.py:34
  46.3 12.5 %collective-permute-start.17 = (bf16[512,512]{1,0:T(8,128)(2,1)S(1)}, bf16[512,512]{1,0:T(8,128)(2,1)S(1)}, u32[]{:S(2)}, u32[]{:S(2)}) collective-permute-start(bf16[512,512]{1,0:T(8,128)(2,1)S(1)} %get-tuple-element.65), channel_id=1, source_target_pairs={{0,96},{1,13},{4,100},{5,1},{8,104},{9,5},{12,108},{13,9},{32,0},{... | collective-permute-start | bytes 1572872 | tf_op jit(solution)/shard_map/ppermute | solution.py:34
  47.0 7.0 %collective-permute-start.9 = (bf16[2,256,256]{2,1,0:T(8,128)(2,1)S(1)}, bf16[2,256,256]{2,1,0:T(8,128)(2,1)S(1)}, u32[]{:S(2)}, u32[]{:S(2)}) collective-permute-start(bf16[2,256,256]{2,1,0:T(8,128)(2,1)S(1)} %picked.1.seed.a_ref), channel_id=1, source_target_pairs={{0,16},{16,0},{1,17},{17,1},{2,18},{18,2},{3,19},{19,3},{4,20},{20... | collective-permute-start | bytes 786440 | tf_op jit(solution)/shard_map/ppermute | solution.py:38
  54.8 11.2 %collective-permute-start.10 = (bf16[2,256,256]{2,1,0:T(8,128)(2,1)S(1)}, bf16[2,256,256]{2,1,0:T(8,128)(2,1)S(1)}, u32[]{:S(2)}, u32[]{:S(2)}) collective-permute-start(bf16[2,256,256]{2,1,0:T(8,128)(2,1)S(1)} %get-tuple-element.57), channel_id=1, source_target_pairs={{0,8},{4,12},{8,0},{12,4},{1,9},{5,13},{9,1},{13,5},{2,10},{6,14},... | collective-permute-start | bytes 786440 | tf_op jit(solution)/shard_map/ppermute | solution.py:401
  55.6 20.5 %collective-permute-start.13 = (bf16[4,256,256]{2,1,0:T(8,128)(2,1)}, bf16[4,256,256]{2,1,0:T(8,128)(2,1)S(1)}, u32[]{:S(2)}, u32[]{:S(2)}) collective-permute-start(bf16[4,256,256]{2,1,0:T(8,128)(2,1)} %get-tuple-element.58), channel_id=1, source_target_pairs={{0,12},{4,0},{8,4},{12,8},{1,13},{5,1},{9,5},{13,9},{2,14},{6,2},{... | collective-permute-start | bytes 1572872 | tf_op jit(solution)/shard_map/ppermute | solution.py:401
  57.7 18.4 %collective-permute-start.12 = (bf16[4,256,256]{2,1,0:T(8,128)(2,1)}, bf16[4,256,256]{2,1,0:T(8,128)(2,1)S(1)}, u32[]{:S(2)}, u32[]{:S(2)}) collective-permute-start(bf16[4,256,256]{2,1,0:T(8,128)(2,1)} %get-tuple-element.58), channel_id=1, source_target_pairs={{0,4},{4,8},{8,12},{12,0},{1,5},{5,9},{9,13},{13,1},{2,6},{6,10},{... | collective-permute-start | bytes 1572872 | tf_op jit(solution)/shard_map/ppermute | solution.py:401
  59.8 16.3 %all-to-all-start = ((bf16[8,128,256]{2,1,0:T(8,128)(2,1)}), bf16[8,128,256]{2,1,0:T(8,128)(2,1)S(1)}, u32[]{:S(2)}, u32[]{:S(2)}) async-start(bf16[8,128,256]{2,1,0:T(8,128)(2,1)} %summed.1), calls=%async_computation | async-start | bytes 1048576 | tf_op jit(solution)/shard_map/all_to_all | solution.py:407
  66.0 8.7 %collective-permute-start.11 = (bf16[2,256,256]{2,1,0:T(8,128)(2,1)S(1)}, bf16[2,256,256]{2,1,0:T(8,128)(2,1)S(1)}, u32[]{:S(2)}, u32[]{:S(2)}) collective-permute-start(bf16[2,256,256]{2,1,0:T(8,128)(2,1)S(1)} %collective-permute-done.10.far), channel_id=1, source_target_pairs={{0,32},{1,97},{32,0},{33,65},{64,96},{65,33},{96,64},{97,1},{2,34}... | collective-permute-start | bytes 786440 | tf_op jit(solution)/shard_map/ppermute | solution.py:290
